TPU v7x, 32 devices: a whole 2x2x4 slice. The times are simulated.
32 devices in a mesh: dp: 16 (over z, x, core), tensor: 2 (over y).
Axes of the slice: x: 2, y: 2, z: 4, core: 2. Of those that a mesh axis runs over, the one named last changes fastest.
Arguments:
- tokens: bfloat16 [16, 1024, 1024], P('dp', 'tensor'), may hold values from -6 to 6
- segments: int32 [16, 1024], P('dp'), may hold values from 0 to 7, never falling along the last dimension, each value on 1 to 512 neighbouring positions
- qkv_weight: bfloat16 [1024, 3, 1024], P('dp', None, 'tensor'), may hold values from -0.1875 to 0.1875
- attn_out_weight: bfloat16 [1024, 1024], P('tensor', 'dp'), may hold values from -1 to 1
- in_weight: bfloat16 [1024, 2, 2624], P('dp', None, 'tensor'), may hold values from -0.1875 to 0.1875
- down_weight: bfloat16 [2624, 1024], P('tensor', 'dp'), may hold values from -0.15625 to 0.15625
- norm_attn: bfloat16 [1024], P('dp'), may hold values from 0.5 to 1.5
- norm_mlp: bfloat16 [1024], P('dp'), may hold values from 0.5 to 1.5
- cotangent: bfloat16 [16, 1024, 1024], P('dp', 'tensor'), may hold values from -6 to 6
Outputs:
- output: bfloat16 [16, 1024, 1024], P('dp', 'tensor')
- token_grad: float32 [16, 1024, 1024], P('dp', 'tensor')
- norm_attn_grad: float32 [1024], P('dp')
- norm_mlp_grad: float32 [1024], P('dp')
- qkv_weight_grad: float32 [1024, 3, 1024], P('dp', None, 'tensor')
- attn_out_weight_grad: float32 [1024, 1024], P('tensor', 'dp')
- in_weight_grad: float32 [1024, 2, 2624], P('dp', None, 'tensor')
- down_weight_grad: float32 [2624, 1024], P('tensor', 'dp')
Inputs may be any that keep to these rules, and one draw needn't show every extreme that they name: `segments`: segment ids never fall along a sequence; each document holds 1 to 512 tokens, and in every sequence one holds exactly 512.
All inputs are finite; a program needn't handle non-finite values.
Results may differ from a plain program's by a relative error of at most 0.015.
Values may be sent and summed in bfloat16 or wider, within the bound.
A program may use at most 192 MiB of HBM per device.

v0:
```python
import math

import jax
import jax.numpy as jnp
from jax import lax
from jax.sharding import PartitionSpec as P

HD = 64


norm_epsilon = 1e-05
rotary_base = 160000.0


def level_normalize(values, gain):
    centre = jnp.mean(values, axis=-1, keepdims=True)
    centred = values - centre
    spread = jnp.mean(centred * centred, axis=-1, keepdims=True)
    return centred * lax.rsqrt(spread + norm_epsilon) * gain


def rotary_tables(length, head_size):
    half_size = head_size // 2
    inverse = 1.0 / rotary_base ** (jnp.arange(half_size).astype(jnp.float32) * (2.0 / head_size))
    angles = jnp.arange(length).astype(jnp.float32)[:, None] * inverse[None, :]
    angles = jnp.concatenate([angles, angles], axis=-1)
    return (jnp.cos(angles), jnp.sin(angles))


def rotate(values, cosine, sine):
    half_size = values.shape[-1] // 2
    turned = jnp.concatenate([-values[..., half_size:], values[..., :half_size]], axis=-1)
    return values * cosine + turned * sine


def unrotate(grads, cosine, sine):
    half_size = grads.shape[-1] // 2
    scaled = grads * sine
    turned = jnp.concatenate([scaled[..., half_size:], -scaled[..., :half_size]], axis=-1)
    return grads * cosine + turned


def attend_forward(query_all, key_all, value_all, segment_ids, block_rows):
    length = key_all.shape[0]
    score_scale = 1.0 / math.sqrt(query_all.shape[-1])

    def one_block(position):
        begin_at = position * block_rows
        asking_vectors = lax.dynamic_slice_in_dim(query_all, begin_at, block_rows, 0)
        query_segs = lax.dynamic_slice_in_dim(segment_ids, begin_at, block_rows, 0)
        raw_scores = (
            jnp.einsum("qd,kd->qk", asking_vectors, key_all, preferred_element_type=jnp.float32)
            * score_scale
        )
        masked = jnp.where(query_segs[:, None] == segment_ids[None, :], raw_scores, -1e30)
        highest_score = jnp.max(masked, axis=-1, keepdims=True)
        expvals = jnp.exp(masked - highest_score)
        totals = jnp.sum(expvals, axis=-1, keepdims=True)
        probs = (expvals / totals).astype(jnp.bfloat16)
        mixed = jnp.dot(probs, value_all, preferred_element_type=jnp.float32).astype(jnp.bfloat16)
        return (mixed, highest_score[:, 0], totals[:, 0])

    mixed, highest_all, totals_all = lax.map(
        one_block, jnp.arange(length // block_rows, dtype=jnp.int32)
    )
    return (mixed.reshape(length, -1), highest_all.reshape(length), totals_all.reshape(length))


def attend_backward(
    query_all, key_all, value_all, segment_ids, out_grad, highest_all, totals_all, block_rows
):
    length = key_all.shape[0]
    head_size = query_all.shape[-1]
    score_scale = 1.0 / math.sqrt(head_size)

    def one_block(carried, position):
        key_grad, value_grad = carried
        begin_at = position * block_rows
        asking_vectors = lax.dynamic_slice_in_dim(query_all, begin_at, block_rows, 0)
        query_segs = lax.dynamic_slice_in_dim(segment_ids, begin_at, block_rows, 0)
        grad_rows = lax.dynamic_slice_in_dim(out_grad, begin_at, block_rows, 0)
        top_rows = lax.dynamic_slice_in_dim(highest_all, begin_at, block_rows, 0)
        total_rows = lax.dynamic_slice_in_dim(totals_all, begin_at, block_rows, 0)
        raw_scores = (
            jnp.einsum("qd,kd->qk", asking_vectors, key_all, preferred_element_type=jnp.float32)
            * score_scale
        )
        masked = jnp.where(query_segs[:, None] == segment_ids[None, :], raw_scores, -1e30)
        probs = jnp.exp(masked - top_rows[:, None]) / total_rows[:, None]
        probs_low = probs.astype(jnp.bfloat16)
        value_grad = value_grad + jnp.einsum(
            "qk,qd->kd", probs_low, grad_rows, preferred_element_type=jnp.float32
        )
        probs_grad = jnp.einsum(
            "qd,kd->qk", grad_rows, value_all, preferred_element_type=jnp.float32
        )
        weighted = jnp.sum(probs * probs_grad, axis=-1, keepdims=True)
        score_grad = (probs * (probs_grad - weighted)).astype(jnp.bfloat16)
        query_grad = jnp.dot(score_grad, key_all, preferred_element_type=jnp.float32) * score_scale
        key_grad = (
            key_grad
            + jnp.einsum(
                "qk,qd->kd", score_grad, asking_vectors, preferred_element_type=jnp.float32
            )
            * score_scale
        )
        return ((key_grad, value_grad), query_grad)

    empty = jnp.zeros((length, head_size), jnp.float32)
    (key_grad, value_grad), query_grad = lax.scan(
        one_block, (empty, empty), jnp.arange(length // block_rows, dtype=jnp.int32)
    )
    return (query_grad.reshape(length, head_size), key_grad, value_grad)


def local(
    tokens,
    segments,
    qkv_weight,
    attn_out_weight,
    in_weight,
    down_weight,
    norm_attn,
    norm_mlp,
    cotangent,
):
    stacked = (qkv_weight, attn_out_weight, in_weight, down_weight, norm_attn, norm_mlp)
    query_key_value_matrix, mixing_matrix, gate_matrix, down_matrix, gain_attn, gain_mlp = (
        lax.all_gather(stacked[0], "dp", axis=0, tiled=True),
        lax.all_gather(stacked[1], "dp", axis=1, tiled=True),
        lax.all_gather(stacked[2], "dp", axis=0, tiled=True),
        lax.all_gather(stacked[3], "dp", axis=1, tiled=True),
        lax.all_gather(stacked[4], "dp", axis=0, tiled=True),
        lax.all_gather(stacked[5], "dp", axis=0, tiled=True),
    )
    seq_count = tokens.shape[0]
    x_input = tokens.astype(jnp.float32)
    gain_one = gain_attn.astype(jnp.float32)
    gain_two = gain_mlp.astype(jnp.float32)
    normed_one = level_normalize(x_input, gain_one).astype(jnp.bfloat16)
    complete_first = lax.all_gather(normed_one, "tensor", axis=1, tiled=True)
    length = complete_first.shape[1]
    heads_local = mixing_matrix.shape[0] // HD
    block_rows = min(512, length)
    projected_rows = jnp.einsum(
        "qik,kun->qiun", complete_first, query_key_value_matrix, preferred_element_type=jnp.float32
    )
    cosine, sine = rotary_tables(length, HD)

    def split_heads(values):
        shaped = values.reshape(seq_count, length, heads_local, HD)
        return shaped.transpose(0, 2, 1, 3).reshape(seq_count * heads_local, length, HD)

    def merge_heads(values):
        shaped = values.reshape(seq_count, heads_local, length, HD)
        return shaped.transpose(0, 2, 1, 3).reshape(seq_count, length, heads_local * HD)

    queries = rotate(split_heads(projected_rows[:, :, 0]), cosine, sine).astype(jnp.bfloat16)
    keys_all = rotate(split_heads(projected_rows[:, :, 1]), cosine, sine).astype(jnp.bfloat16)
    values_all = split_heads(projected_rows[:, :, 2]).astype(jnp.bfloat16)
    segment_items = jnp.repeat(segments, heads_local, axis=0)

    def forward_item(packed):
        return attend_forward(packed[0], packed[1], packed[2], packed[3], block_rows)

    mixed, highest_all, totals_all = lax.map(
        forward_item, (queries, keys_all, values_all, segment_items)
    )
    head_results = merge_heads(mixed)
    attention_pieces = jnp.einsum(
        "jbv,vm->jbm", head_results, mixing_matrix, preferred_element_type=jnp.float32
    )
    attn_branch = lax.psum_scatter(attention_pieces, "tensor", scatter_dimension=1, tiled=True)
    resid = x_input + attn_branch
    normed_two = level_normalize(resid, gain_two).astype(jnp.bfloat16)
    entire_latter_part = lax.all_gather(normed_two, "tensor", axis=1, tiled=True)
    gate_preactivation = jnp.einsum(
        "hnt,tx->hnx", entire_latter_part, gate_matrix[:, 0], preferred_element_type=jnp.float32
    )
    up_preactivation = jnp.einsum(
        "hnt,tx->hnx", entire_latter_part, gate_matrix[:, 1], preferred_element_type=jnp.float32
    )
    hidden_state = (jax.nn.gelu(gate_preactivation, approximate=False) * up_preactivation).astype(
        jnp.bfloat16
    )
    feedforward_pieces = jnp.einsum(
        "jbv,vm->jbm", hidden_state, down_matrix, preferred_element_type=jnp.float32
    )
    mlp_branch = lax.psum_scatter(
        feedforward_pieces.astype(jnp.bfloat16), "tensor", scatter_dimension=1, tiled=True
    ).astype(jnp.float32)
    result = (resid + mlp_branch).astype(jnp.bfloat16)
    gradient_complete = lax.all_gather(cotangent, "tensor", axis=1, tiled=True)
    down_projection_gradient = jnp.einsum(
        "ojn,ojq->nq", hidden_state, gradient_complete, preferred_element_type=jnp.float32
    )
    hidden_state_gradient = jnp.einsum(
        "wqj,oj->wqo", gradient_complete, down_matrix, preferred_element_type=jnp.float32
    )
    hidden_state_gradient = hidden_state_gradient.astype(jnp.bfloat16).astype(jnp.float32)

    def glu_piece(gate_arg, up_arg):
        return jax.nn.gelu(gate_arg, approximate=False) * up_arg

    unused_glu, glu_pull = jax.vjp(glu_piece, gate_preactivation, up_preactivation)
    switch_branch_derivative, up_grad = glu_pull(hidden_state_gradient)
    switch_branch_totalled = switch_branch_derivative.astype(jnp.bfloat16)
    widening_totalled = up_grad.astype(jnp.bfloat16)
    gate_weight_grad = jnp.einsum(
        "xdl,xdv->lv",
        entire_latter_part,
        switch_branch_totalled,
        preferred_element_type=jnp.float32,
    )
    up_matrix_gradient = jnp.einsum(
        "xdl,xdv->lv", entire_latter_part, widening_totalled, preferred_element_type=jnp.float32
    )
    in_grad = jnp.stack([gate_weight_grad, up_matrix_gradient], axis=1)
    normed_two_terms = jnp.einsum(
        "xoi,yi->xoy", switch_branch_totalled, gate_matrix[:, 0], preferred_element_type=jnp.float32
    )
    normed_two_terms = normed_two_terms + jnp.einsum(
        "xoi,yi->xoy", widening_totalled, gate_matrix[:, 1], preferred_element_type=jnp.float32
    )
    normed_two_grad = lax.psum_scatter(normed_two_terms, "tensor", scatter_dimension=1, tiled=True)
    unused_two, norm_two_pull = jax.vjp(level_normalize, resid, gain_two)
    resid_part, gain_two_grad = norm_two_pull(normed_two_grad)
    resid_grad = cotangent.astype(jnp.float32) + resid_part
    attention_complete = lax.all_gather(
        resid_grad.astype(jnp.bfloat16), "tensor", axis=1, tiled=True
    )
    mixing_gradient = jnp.einsum(
        "ojn,ojq->nq", head_results, attention_complete, preferred_element_type=jnp.float32
    )
    heads_grad = jnp.einsum(
        "wqj,oj->wqo", attention_complete, mixing_matrix, preferred_element_type=jnp.float32
    ).astype(jnp.bfloat16)

    def backward_item(packed):
        return attend_backward(
            packed[0], packed[1], packed[2], packed[3], packed[4], packed[5], packed[6], block_rows
        )

    query_grad, key_grad, value_grad = lax.map(
        backward_item,
        (
            queries,
            keys_all,
            values_all,
            segment_items,
            split_heads(heads_grad),
            highest_all,
            totals_all,
        ),
    )
    query_raw = merge_heads(unrotate(query_grad, cosine, sine))
    key_raw = merge_heads(unrotate(key_grad, cosine, sine))
    value_raw = merge_heads(value_grad)
    projected_rows_gradient = jnp.stack([query_raw, key_raw, value_raw], axis=2).astype(
        jnp.bfloat16
    )
    qkv_grad = jnp.einsum(
        "oun,ouwt->nwt", complete_first, projected_rows_gradient, preferred_element_type=jnp.float32
    )
    normed_one_terms = jnp.einsum(
        "rqnz,mnz->rqm",
        projected_rows_gradient,
        query_key_value_matrix,
        preferred_element_type=jnp.float32,
    )
    normed_one_grad = lax.psum_scatter(
        normed_one_terms.astype(jnp.bfloat16), "tensor", scatter_dimension=1, tiled=True
    ).astype(jnp.float32)
    unused_one, norm_one_pull = jax.vjp(level_normalize, x_input, gain_one)
    input_part, gain_one_grad = norm_one_pull(normed_one_grad)
    token_grad = resid_grad + input_part
    qkv_summed, mix_summed, in_summed, down_summed, gain_one_part, gain_two_part = (
        lax.psum_scatter(qkv_grad, "dp", scatter_dimension=0, tiled=True),
        lax.psum_scatter(mixing_gradient, "dp", scatter_dimension=1, tiled=True),
        lax.psum_scatter(in_grad, "dp", scatter_dimension=0, tiled=True),
        lax.psum_scatter(down_projection_gradient, "dp", scatter_dimension=1, tiled=True),
        lax.psum_scatter(gain_one_grad, "dp", scatter_dimension=0, tiled=True),
        lax.psum_scatter(gain_two_grad, "dp", scatter_dimension=0, tiled=True),
    )
    gain_one_total, gain_two_total = lax.psum((gain_one_part, gain_two_part), "tensor")
    return (
        result,
        token_grad,
        gain_one_total,
        gain_two_total,
        qkv_summed,
        mix_summed,
        in_summed,
        down_summed,
    )


def solution(mesh):
    return jax.shard_map(
        local,
        mesh=mesh,
        in_specs=(
            P("dp", "tensor", None),
            P("dp", None),
            P("dp", None, "tensor"),
            P("tensor", "dp"),
            P("dp", None, "tensor"),
            P("tensor", "dp"),
            P("dp"),
            P("dp"),
            P("dp", "tensor", None),
        ),
        out_specs=(
            P("dp", "tensor", None),
            P("dp", "tensor", None),
            P("dp"),
            P("dp"),
            P("dp", None, "tensor"),
            P("tensor", "dp"),
            P("dp", None, "tensor"),
            P("tensor", "dp"),
        ),
        check_vma=False,
    )
```

profile of v0, /device:TPU:0, one launch (start us, length us, event | category | flops | bytes accessed | tf_op | source)
XLA Modules:
  0.0 1138.5 jit_solution(10308793427913046427)
XLA Ops:
  10.9 34.9 %all-reduce.7 = (bf16[1024]{0:T(1024)(128)(2,1)S(1)}, bf16[1024]{0:T(1024)(128)(2,1)S(1)}) all-reduce(bf16[1024]{0:T(1024)(128)(2,1)S(1)} %dynamic-update-slice, bf16[1024]{0:T(1024)(128)(2,1)S(1)} %dynamic-update-slice.1), channel_id=1, replica_groups=mesh['dp'=16,'tensor'=2] {'dp'}, use_global_device_ids=true, to_apply=%add | all-reduce | flops 2048 | bytes 8192
  56.0 26.1 %all-gather.9.cloned.1.call-done = bf16[1,1024,1024]{2,1,0:T(8,128)(2,1)} async-done(((bf16[1,512,1024]{2,1,0:T(8,128)(2,1)}), bf16[1,1024,1024]{2,1,0:T(8,128)(2,1)}) %all-gather.9.cloned.1.call-update) | async-done | bytes 2097168 | tf_op jit(solution)/shard_map/all_gather | solution.py:141
  82.1 47.7 %all-gather.11.cloned.1.call-done = bf16[1024,3,512]{2,0,1:T(8,128)(2,1)} async-done(((bf16[64,3,512]{2,0,1:T(8,128)(2,1)}), bf16[1024,3,512]{2,0,1:T(8,128)(2,1)}) %all-gather.11.cloned.1.call-update) | async-done | bytes 3145744 | tf_op jit(solution)/shard_map/all_gather | solution.py:129
  129.8 6.2 convolution_bitcast_fusion.2
  137.6 2.2 fusion.46
  139.8 2.7 copy.56
  146.1 71.9 %while.58 = (s32[]{:T(128)}, bf16[8,1024,64]{1,2,0:T(8,128)(2,1)S(1)}, f32[8,1024]{1,0:T(8,128)S(1)}, f32[8,1024]{1,0:T(8,128)S(1)}, bf16[8,1024,64]{2,1,0:T(8,1...) while((s32[]{:T(128)}, ...), condition=%wide.region_7.8_spmd, body=%wide.region_2.7_spmd.sunk | while | flops 138968064 | bytes 8655344 | solution.py:166
  148.2 6.3 while.61
  157.2 6.2 while.61
  166.2 6.3 while.61
  175.2 6.3 while.61
  184.2 6.3 while.61
  193.2 6.2 while.61
  202.2 6.3 while.61
  211.2 6.3 while.61
  218.1 4.8 convolution_bitcast_fusion.3
  224.0 23.7 %all-gather.19.cloned.1.call-done = bf16[1312,1024]{0,1:T(8,128)(2,1)} async-done(((bf16[1312,64]{0,1:T(8,128)(2,1)}), bf16[1312,1024]{0,1:T(8,128)(2,1)}) %all-gather.19.cloned.1.call-update) | async-done | bytes 2686992 | tf_op jit(solution)/shard_map/all_gather | solution.py:132
  247.7 6.9 convolution_convert_fusion.1
  254.6 48.3 %reduce-scatter.8.cloned.1.call-done = f32[1,512,1024]{2,1,0:T(8,128)} async-done(((f32[1,1024,1024]{2,1,0:T(8,128)}), f32[1,512,1024]{2,1,0:T(8,128)}) %reduce-scatter.8.cloned.1.call-update) | async-done | bytes 2097168 | tf_op jit(solution)/shard_map/reduce_scatter | solution.py:173
  306.5 57.4 %all-gather.17.cloned.1.call-done = bf16[1024,2,1312]{2,1,0:T(2,128)(2,1)} async-done(((bf16[64,2,1312]{2,1,0:T(2,128)(2,1)}), bf16[1024,2,1312]{2,1,0:T(2,128)(2,1)}) %all-gather.17.cloned.1.call-update) | async-done | bytes 5373968 | tf_op jit(solution)/shard_map/all_gather | solution.py:131
  363.9 12.8 %fusion.82 = (bf16[1024,1,1312]{2,1,0:T(2,128)(2,1)}, bf16[1024,1,1312]{2,1,0:T(2,128)(2,1)}) fusion(bf16[1024,2,1312]{2,1,0:T(2,128)(2,1)} %all-gather.17.cloned.1.call-done), kind=kLoop, calls=%fused_computation.164 | loop fusion | bytes 10747904 | tf_op jit(solution)/shard_map/slice | solution.py:178
  376.6 14.0 %copy.79 = bf16[1024,1,1312]{0,2,1:T(8,128)(2,1)} copy(bf16[1024,1,1312]{2,1,0:T(2,128)(2,1)} %get-tuple-element.450) | data formatting | bytes 5373952
  390.7 14.1 %copy.80 = bf16[1024,1,1312]{0,2,1:T(8,128)(2,1)} copy(bf16[1024,1,1312]{2,1,0:T(2,128)(2,1)} %get-tuple-element.451) | data formatting | bytes 5373952
  404.8 5.6 fusion.35
  410.4 16.8 %add_convert_fusion = (bf16[1024,1312]{0,1:T(8,128)(2,1)}, f32[1024,1312]{0,1:T(8,128)}, f32[1024,1312]{0,1:T(8,128)}) fusion(bf16[1024,1312]{0,1:T(8,128)(2,1)S(1)} %copy-done.12, f32[1024,1312]{0,1:T(8,128)S(1)} %fusion.35, bf16[1024,1,1312]{0,2,1:T(8,128)(2,1)S(1)} %copy-done.14, bf16[1,1024,1024]{2,1,0:T(8,128)(2,1)S(1)} %copy-done.34), kind=kOutput, calls=%fused_computation.49 | convolution fusion | flops 2850881536 | bytes 26279936 | tf_op jit(solution)/shard_map/hnt,tx->hnx/dot_general | solution.py:180
  427.2 11.2 fusion.18
  438.4 6.3 fusion.29
  444.7 14.2 %add_bitcast_fusion = f32[1,1024,1024]{2,1,0:T(8,128)} fusion(f32[1024,1024]{1,0:T(8,128)S(1)} %fusion.29, bf16[1024,1312]{0,1:T(8,128)(2,1)S(1)} %copy-done.39, bf16[1024,1,1312]{0,2,1:T(8,128)(2,1)S(1)} %copy-done.13), kind=kOutput, calls=%fused_computation.68 | convolution fusion | flops 2752512000 | bytes 13762560 | tf_op jit(solution)/shard_map/xoi,yi->xoy/dot_general | solution.py:219
  459.0 7.4 convert_bitcast_fusion
  466.5 45.7 %reduce-scatter.12.cloned.1.call-done = f32[1,512,1024]{2,1,0:T(8,128)} async-done(((f32[1,1024,1024]{2,1,0:T(8,128)}), f32[1,512,1024]{2,1,0:T(8,128)}) %reduce-scatter.12.cloned.1.call-update) | async-done | bytes 2097168 | tf_op jit(solution)/shard_map/reduce_scatter | solution.py:225
  512.2 2.8 multiply_reduce_fusion.1
  515.0 31.1 %reduce-scatter.10.cloned.1.call-done = bf16[1,512,1024]{2,1,0:T(8,128)(2,1)} async-done(((bf16[1,1024,1024]{2,1,0:T(8,128)(2,1)}), bf16[1,512,1024]{2,1,0:T(8,128)(2,1)}) %reduce-scatter.10.cloned.1.call-update) | async-done | bytes 1048592 | tf_op jit(solution)/shard_map/reduce_scatter | solution.py:189
  546.2 3.6 fusion.77
  553.0 4.9 convolution_bitcast_fusion
  557.9 3.0 convolution_bitcast_fusion.1
  560.9 6.2 pad_maximum_fusion
  567.1 17.6 %copy.72 = f32[1024,2,1312]{2,1,0:T(2,128)} copy(f32[1024,2,1312]{0,2,1:T(8,128)} %pad_maximum_fusion) | data formatting | bytes 21495808 | tf_op jit(solution)/shard_map/stack | solution.py:218
  585.9 2.9 fusion.66
  590.6 249.3 %while.60 = (s32[]{:T(128)}, f32[8,1024,64]{1,2,0:T(8,128)}, f32[8,1024,64]{1,2,0:T(8,128)}, bf16[8,1024,64]{1,2,0:T(8,128)(2,1)}, bf16[8,1024,64]{2,1,0:T(8,128...) while((s32[]{:T(128)}, f32[8,1024,64]{1,2,0:T(8,128)}, ...), condition=%wide.region_19.20_spmd, body=%wide.region_15.19_spmd.sunk | while | flops 341671424 | bytes 24955564 | solution.py:244
  597.5 21.5 %while.62 = (s32[]{:T(128)}, f32[1024,64]{0,1:T(8,128)}, f32[1024,64]{0,1:T(8,128)S(1)}, f32[2,512,64]{1,2,0:T(8,128)}, s32[2]{0:T(128)S(1)}, /*index=5*/s32[102...) while((s32[]{:T(128)}, f32[1024,64]{0,1:T(8,128)}, ...), condition=%wide.region_18.18_spmd.clone, body=%wide.region_16.17_spmd.clone.sunk | while | flops 341671424 | bytes 20212024 | solution.py:110
  613.4 2.1 fusion.134
  628.7 21.5 %while.62 = (s32[]{:T(128)}, f32[1024,64]{0,1:T(8,128)}, f32[1024,64]{0,1:T(8,128)S(1)}, f32[2,512,64]{1,2,0:T(8,128)}, s32[2]{0:T(128)S(1)}, /*index=5*/s32[102...) while((s32[]{:T(128)}, f32[1024,64]{0,1:T(8,128)}, ...), condition=%wide.region_18.18_spmd.clone, body=%wide.region_16.17_spmd.clone.sunk | while | flops 341671424 | bytes 20212024 | solution.py:110
  659.8 21.6 %while.62 = (s32[]{:T(128)}, f32[1024,64]{0,1:T(8,128)}, f32[1024,64]{0,1:T(8,128)S(1)}, f32[2,512,64]{1,2,0:T(8,128)}, s32[2]{0:T(128)S(1)}, /*index=5*/s32[102...) while((s32[]{:T(128)}, f32[1024,64]{0,1:T(8,128)}, ...), condition=%wide.region_18.18_spmd.clone, body=%wide.region_16.17_spmd.clone.sunk | while | flops 341671424 | bytes 20212024 | solution.py:110
  675.8 2.2 fusion.134
  691.1 21.5 %while.62 = (s32[]{:T(128)}, f32[1024,64]{0,1:T(8,128)}, f32[1024,64]{0,1:T(8,128)S(1)}, f32[2,512,64]{1,2,0:T(8,128)}, s32[2]{0:T(128)S(1)}, /*index=5*/s32[102...) while((s32[]{:T(128)}, f32[1024,64]{0,1:T(8,128)}, ...), condition=%wide.region_18.18_spmd.clone, body=%wide.region_16.17_spmd.clone.sunk | while | flops 341671424 | bytes 20212024 | solution.py:110
  722.2 21.5 %while.62 = (s32[]{:T(128)}, f32[1024,64]{0,1:T(8,128)}, f32[1024,64]{0,1:T(8,128)S(1)}, f32[2,512,64]{1,2,0:T(8,128)}, s32[2]{0:T(128)S(1)}, /*index=5*/s32[102...) while((s32[]{:T(128)}, f32[1024,64]{0,1:T(8,128)}, ...), condition=%wide.region_18.18_spmd.clone, body=%wide.region_16.17_spmd.clone.sunk | while | flops 341671424 | bytes 20212024 | solution.py:110
  753.4 21.5 %while.62 = (s32[]{:T(128)}, f32[1024,64]{0,1:T(8,128)}, f32[1024,64]{0,1:T(8,128)S(1)}, f32[2,512,64]{1,2,0:T(8,128)}, s32[2]{0:T(128)S(1)}, /*index=5*/s32[102...) while((s32[]{:T(128)}, f32[1024,64]{0,1:T(8,128)}, ...), condition=%wide.region_18.18_spmd.clone, body=%wide.region_16.17_spmd.clone.sunk | while | flops 341671424 | bytes 20212024 | solution.py:110
  784.6 21.4 %while.62 = (s32[]{:T(128)}, f32[1024,64]{0,1:T(8,128)}, f32[1024,64]{0,1:T(8,128)S(1)}, f32[2,512,64]{1,2,0:T(8,128)}, s32[2]{0:T(128)S(1)}, /*index=5*/s32[102...) while((s32[]{:T(128)}, f32[1024,64]{0,1:T(8,128)}, ...), condition=%wide.region_18.18_spmd.clone, body=%wide.region_16.17_spmd.clone.sunk | while | flops 341671424 | bytes 20212024 | solution.py:110
  815.6 21.4 %while.62 = (s32[]{:T(128)}, f32[1024,64]{0,1:T(8,128)}, f32[1024,64]{0,1:T(8,128)S(1)}, f32[2,512,64]{1,2,0:T(8,128)}, s32[2]{0:T(128)S(1)}, /*index=5*/s32[102...) while((s32[]{:T(128)}, f32[1024,64]{0,1:T(8,128)}, ...), condition=%wide.region_18.18_spmd.clone, body=%wide.region_16.17_spmd.clone.sunk | while | flops 341671424 | bytes 20212024 | solution.py:110
  840.0 2.4 copy.70
  842.4 2.3 broadcast_multiply_fusion.1
  848.6 2.3 copy.69
  852.2 7.7 fusion.65
  860.0 6.9 fusion.53
  868.5 3.9 fusion.49
  874.0 7.1 fusion.60
  884.0 8.1 reduce-scatter.14.cloned.1.call-done
  893.9 2.4 fusion.40
  896.3 33.6 %all-reduce.5 = (f32[1024]{0:T(1024)S(1)}, f32[1024]{0:T(1024)S(1)}) all-reduce(f32[1024]{0:T(1024)S(1)} %get-tuple-element.344, f32[1024]{0:T(1024)S(1)} %copy-done.31), channel_id=6, replica_groups=mesh['dp'=16,'tensor'=2] {'dp'}, use_global_device_ids=true, to_apply=%region_24.25.clone | all-reduce | flops 2048 | bytes 16384
  930.1 5.4 all-reduce.6
  935.6 3.8 add_add_fusion.2
  939.4 38.5 %reduce-scatter.20.cloned.1.call-done = f32[1312,64]{0,1:T(8,128)} async-done(((f32[1312,1024]{0,1:T(8,128)}), f32[1312,64]{0,1:T(8,128)}) %reduce-scatter.20.cloned.1.call-update) | async-done | bytes 335888 | tf_op jit(solution)/shard_map/reduce_scatter | solution.py:281
  977.9 65.2 %reduce-scatter.18.cloned.1.call-done = f32[512,64]{0,1:T(8,128)} async-done(((f32[512,1024]{0,1:T(8,128)}), f32[512,64]{0,1:T(8,128)}) %reduce-scatter.18.cloned.1.call-update) | async-done | bytes 131088 | tf_op jit(solution)/shard_map/reduce_scatter | solution.py:279
  1043.1 88.4 %reduce-scatter.16.cloned.1.call-done = f32[64,3,512]{2,0,1:T(8,128)} async-done(((f32[1024,3,512]{2,0,1:T(8,128)}), f32[64,3,512]{2,0,1:T(8,128)}) %reduce-scatter.16.cloned.1.call-update) | async-done | bytes 393232 | tf_op jit(solution)/shard_map/reduce_scatter | solution.py:278
  (742 shorter events, 334.6 us)
Async XLA Ops:
  7.2 43.0 %copy-start.1 = (bf16[1,512,1024]{2,1,0:T(8,128)(2,1)S(1)}, bf16[1,512,1024]{2,1,0:T(8,128)(2,1)}, u32[]{:S(2)}) copy-start(bf16[1,512,1024]{2,1,0:T(8,128)(2,1)} %param.17) | copy-start | bytes 3145732
  7.2 74.9 %all-gather.9.cloned.1.call-start = ((), (), s32[]{:S(2)}) async-start(), calls=%async_computation.7 | async-start | bytes 3145728 | tf_op jit(solution)/shard_map/all_gather | solution.py:141
  45.9 3.7 copy-start.21
  47.3 2.3 copy-start.23
  51.5 78.3 %all-gather.11.cloned.1.call-start = ((), (), s32[]{:S(2)}) async-start(), calls=%async_computation.8 | async-start | bytes 3342336 | tf_op jit(solution)/shard_map/all_gather | solution.py:129
  52.3 165.8 %all-gather.13.cloned.1.call-start = ((), (), s32[]{:S(2)}) async-start(), calls=%async_computation.9 | async-start | bytes 1114112 | tf_op jit(solution)/shard_map/all_gather | solution.py:130
  53.0 171.0 %all-gather.21.cloned.1.call-start = ((), (), s32[]{:S(2)}) async-start(), calls=%async_computation.15 | async-start | bytes 3145728 | tf_op jit(solution)/shard_map/all_gather | solution.py:193
  53.6 194.1 %all-gather.19.cloned.1.call-start = ((), (), s32[]{:S(2)}) async-start(), calls=%async_computation.13 | async-start | bytes 3063808 | tf_op jit(solution)/shard_map/all_gather | solution.py:132
  54.2 248.7 %reduce-scatter.8.cloned.1.call-start = ((), (), s32[]{:S(2)}) async-start(), calls=%async_computation.10 | async-start | bytes 6291456 | tf_op jit(solution)/shard_map/reduce_scatter | solution.py:173
  56.0 81.4 %copy-start.15 = (f32[1024,64]{0,1:T(8,128)}, f32[1024,64]{0,1:T(8,128)S(1)}, u32[]{:S(2)}) copy-start(f32[1024,64]{0,1:T(8,128)S(1)} %get-tuple-element.468) | copy-start | bytes 786436
  218.0 4.9 copy-start.38
  222.9 140.9 %all-gather.17.cloned.1.call-start = ((), (), s32[]{:S(2)}) async-start(), calls=%async_computation.12 | async-start | bytes 6127616 | tf_op jit(solution)/shard_map/all_gather | solution.py:131
  223.7 181.1 %all-gather.15.cloned.1.call-start = ((), (), s32[]{:S(2)}) async-start(), calls=%async_computation.11 | async-start | bytes 3145728 | tf_op jit(solution)/shard_map/all_gather | solution.py:176
  306.5 205.7 %reduce-scatter.12.cloned.1.call-start = ((), (), s32[]{:S(2)}) async-start(), calls=%async_computation.16 | async-start | bytes 6291456 | tf_op jit(solution)/shard_map/reduce_scatter | solution.py:225
  404.8 5.6 copy-start.12
  404.8 5.6 copy-start.14
  404.8 5.6 copy-start.34
  410.4 16.8 %copy-start.10 = (f32[1024,1312]{0,1:T(8,128)}, f32[1024,1312]{0,1:T(8,128)S(1)}, u32[]{:S(2)}) copy-start(f32[1024,1312]{0,1:T(8,128)S(1)} %fusion.35) | copy-start | bytes 16121860
  438.4 6.3 copy-start.13
  438.4 6.3 copy-start.39
  458.9 87.2 %reduce-scatter.10.cloned.1.call-start = ((), (), s32[]{:S(2)}) async-start(), calls=%async_computation.14 | async-start | bytes 3145728 | tf_op jit(solution)/shard_map/reduce_scatter | solution.py:189
  466.4 119.2 %all-gather.23.cloned.1.call-start = ((), (), s32[]{:S(2)}) async-start(), calls=%async_computation.17 | async-start | bytes 3145728 | tf_op jit(solution)/shard_map/all_gather | solution.py:229
  515.0 36.0 %copy-start.5 = (bf16[1,512,1024]{2,1,0:T(8,128)(2,1)S(1)}, bf16[1,512,1024]{2,1,0:T(8,128)(2,1)}, u32[]{:S(2)}) copy-start(bf16[1,512,1024]{2,1,0:T(8,128)(2,1)} %param.25) | copy-start | bytes 3145732
  549.8 2.6 copy-start.27
  552.4 329.5 %all-reduce.10.cloned.1.call-start = ((), (), s32[]{:S(2)}) async-start(), calls=%async_computation.22 | async-start | bytes 23068672
  553.0 4.9 copy-start.40
  584.7 307.4 %reduce-scatter.14.cloned.1.call-start = ((), (), s32[]{:S(2)}) async-start(), calls=%async_computation.18 | async-start | bytes 3145728 | tf_op jit(solution)/shard_map/reduce_scatter | solution.py:271
  602.7 3.3 copy-start.8
  613.4 3.4 copy-start.8
  618.9 2.1 copy-start
  633.9 3.3 copy-start.8
  644.6 3.4 copy-start.8
  650.1 2.1 copy-start
  665.1 3.3 copy-start.8
  675.8 3.5 copy-start.8
  681.4 2.1 copy-start
  696.3 3.3 copy-start.8
  707.0 3.4 copy-start.8
  712.5 2.1 copy-start
  727.5 3.3 copy-start.8
  738.2 3.4 copy-start.8
  743.8 2.1 copy-start
  758.7 3.3 copy-start.8
  769.4 3.4 copy-start.8
  789.8 3.3 copy-start.8
  800.5 3.4 copy-start.8
  806.0 2.1 copy-start
  820.9 3.3 copy-start.8
  831.5 3.4 copy-start.8
  837.1 2.1 copy-start
  840.0 2.4 copy-start.6
  852.2 7.8 copy-start.11
  860.0 117.9 %reduce-scatter.20.cloned.1.call-start = ((), (), s32[]{:S(2)}) async-start(), calls=%async_computation.21 | async-start | bytes 6127616 | tf_op jit(solution)/shard_map/reduce_scatter | solution.py:281
  866.9 176.1 %reduce-scatter.18.cloned.1.call-start = ((), (), s32[]{:S(2)}) async-start(), calls=%async_computation.20 | async-start | bytes 2228224 | tf_op jit(solution)/shard_map/reduce_scatter | solution.py:279
  868.5 4.0 copy-start.20
  872.5 259.0 %reduce-scatter.16.cloned.1.call-start = ((), (), s32[]{:S(2)}) async-start(), calls=%async_computation.19 | async-start | bytes 6684672 | tf_op jit(solution)/shard_map/reduce_scatter | solution.py:278
  881.1 11.0 copy-start.22
  881.1 11.0 copy-start.24
  881.1 11.0 copy-start.2
  881.2 12.7 %copy-start.30 = (f32[512]{0:T(512)S(1)}, f32[512]{0:T(512)}, u32[]{:S(2)}) copy-start(f32[512]{0:T(512)} %copy-done.29) | copy-start | bytes 6148
  881.2 12.8 %copy-start.26 = (f32[512]{0:T(512)S(1)}, f32[512]{0:T(512)}, u32[]{:S(2)}) copy-start(f32[512]{0:T(512)} %copy-done.25) | copy-start | bytes 6148
  884.0 12.3 %copy-start.31 = (f32[1024]{0:T(1024)S(1)}, f32[1024]{0:T(1024)}, u32[]{:S(2)}) copy-start(f32[1024]{0:T(1024)} %get-tuple-element.342) | copy-start | bytes 12292
  884.0 51.6 %copy-start.4 = (f32[1,512,1024]{2,1,0:T(8,128)S(1)}, f32[1,512,1024]{2,1,0:T(8,128)}, u32[]{:S(2)}) copy-start(f32[1,512,1024]{2,1,0:T(8,128)} %copy-done.3) | copy-start | bytes 6291460
  884.0 51.6 %copy-start.28 = (f32[512]{0:T(512)S(1)}, f32[512]{0:T(512)}, u32[]{:S(2)}) copy-start(f32[512]{0:T(512)} %copy-done.27) | copy-start | bytes 6148
  (30 other events, 31.3 us)
Sparse Core Ops, SparseCore 0:
  51.6 30.3 all-gather.8
  84.2 45.4 all-gather.10
  131.9 36.2 all-gather.12
  169.6 32.0 all-gather.20
  203.8 43.8 all-gather.18
  249.9 52.9 reduce-scatter.7
  305.2 58.6 all-gather.16
  366.0 31.7 all-gather.14
  459.1 53.0 reduce-scatter.11
  514.3 31.8 reduce-scatter.9
  552.5 33.0 all-gather.22
  589.3 217.5 all-reduce.9
  860.1 31.9 reduce-scatter.13
  896.5 81.3 reduce-scatter.19
  982.0 60.9 reduce-scatter.17
  1047.4 84.0 reduce-scatter.15
where the time goes:
time: 1150 us; the launch traced here: 1140 us
  waiting for transfers between devices  484 us (42%)
  matrix products  254 us (22%)
  local copies, waits for them, and re-layouts  222 us (19%)
  blocking collectives  74 us (6%)
  other arithmetic  63 us (5%)
  loops' own time  24 us (2%)
  between operations  16.2 us (1%)
    reduce_scatter x1, waiting for transfers between devices, local(): lax.psum_scatter(qkv_grad, 'dp', scatter_dimension=0, tiled=True)  88.4 us
    squeeze x48, local copies, waits for them, and re-layouts, local(): lax.map(forward_item, (queries, keys_all, values_all, segment_items))  70.2 us
    unnamed x2, blocking collectives  68.6 us
    reduce_scatter x1, waiting for transfers between devices, local(): lax.psum_scatter(mixing_gradient, 'dp', scatter_dimension=1, tiled=True)  65.2 us
    all_gather x1, waiting for transfers between devices, local(): lax.all_gather(stacked[2], 'dp', axis=0, tiled=True)  57.4 us
    reduce_scatter x1, waiting for transfers between devices, local(): lax.psum_scatter(attention_pieces, 'tensor', scatter_dimension=1, tiled=T...  48.3 us
    all_gather x1, waiting for transfers between devices, local(): lax.all_gather(stacked[0], 'dp', axis=0, tiled=True)  47.7 us
    reduce_scatter x1, waiting for transfers between devices, local(): lax.psum_scatter(normed_two_terms, 'tensor', scatter_dimension=1, tiled=T...  45.7 us
  transfers between devices with their start and end apart: 16, of which 12 were waited for; matrix products, arithmetic and copies ran while one was open for 40% of the time, Pallas kernels for 0%

commit v1 on v0

v1 whole, which is shorter than its diff:
```python
import math

import jax
import jax.numpy as jnp
from jax import lax
from jax.experimental import pallas as pl
from jax.experimental.pallas import tpu as pltpu
from jax.sharding import PartitionSpec as P

HD = 64
EPS = 1e-05
ROTARY_BASE = 160000.0
BF = jnp.bfloat16
F32 = jnp.float32


def dotf(a, b, dims):
    return lax.dot_general(a, b, (dims, ((), ())), preferred_element_type=F32)


NN = ((1,), (0,))
NT = ((1,), (1,))
TN = ((0,), (0,))


def rope_tables(positions):
    half = HD // 2
    inverse = 1.0 / ROTARY_BASE ** (jnp.arange(half).astype(F32) * (2.0 / HD))
    angles = positions.astype(F32)[:, None] * inverse[None, :]
    cos, sin = jnp.cos(angles), jnp.sin(angles)
    zero = jnp.zeros_like(sin)
    cosine = jnp.concatenate([cos] * 4, axis=-1)
    upper = jnp.concatenate([-sin, zero] * 2, axis=-1)
    lower = jnp.concatenate([zero, sin] * 2, axis=-1)
    return cosine, upper, lower


def turn(u, upper, lower):
    return pltpu.roll(u, 128 - HD // 2, 1) * upper + pltpu.roll(u, HD // 2, 1) * lower


def attn_fwd_kernel(xh, wq, wk, wv, cos, upper, lower, seg_col, seg_row, o, q, k, v, lse, kh):
    length = xh.shape[0]
    rows = min(256, length)
    lane = lax.broadcasted_iota(jnp.int32, (length, 128), 1)
    first = lane < HD
    tokens = xh[...]
    qf = dotf(tokens, wq[...], NN)
    qf = qf * cos[...] + turn(qf, upper[...], lower[...])
    q[...] = (qf * (1.0 / math.sqrt(HD))).astype(BF)
    kf = dotf(tokens, wk[...], NN)
    kf = (kf * cos[...] + turn(kf, upper[...], lower[...])).astype(BF)
    k[...] = kf
    kh[0] = jnp.where(first, kf, jnp.zeros_like(kf))
    kh[1] = jnp.where(first, jnp.zeros_like(kf), kf)
    v[...] = dotf(tokens, wv[...], NN).astype(BF)

    def block(i, carry):
        at = pl.multiple_of(i * rows, rows)
        q_rows = q[pl.ds(at, rows), :]
        same = seg_col[pl.ds(at, rows), :] == seg_row[...]
        outs = []
        for head in range(2):
            scores = dotf(q_rows, kh[head], NT)
            scores = jnp.where(same, scores, -1e30)
            top = jnp.max(scores, axis=-1, keepdims=True)
            expv = jnp.exp(scores - top)
            total = jnp.sum(expv, axis=-1, keepdims=True)
            low = (expv * (1.0 / total)).astype(BF)
            outs.append(dotf(low, v[...], NN))
            level = top + jnp.log(total)
            flat = jnp.transpose(jnp.broadcast_to(level, (rows, 128)))
            lse[0, pl.ds(head, 1), pl.ds(at, rows)] = flat[0:1, :]
        o[pl.ds(at, rows), :] = jnp.where(first[:rows], outs[0], outs[1]).astype(BF)
        return carry

    lax.fori_loop(0, length // rows, block, 0)


def attn_fwd(xh, w_qk, w_vo, tables, seg_col, seg_row):
    length, width = xh.shape
    pairs = w_qk.shape[1] // 256
    whole = lambda a: pl.BlockSpec(a.shape, lambda h: (0,) * a.ndim)
    col = lambda off: pl.BlockSpec((width, 128), lambda h: (0, h + off))
    out = pl.BlockSpec((length, 128), lambda h: (0, h))
    shape = jax.ShapeDtypeStruct((length, pairs * 128), BF)
    flops = 2 * length * width * pairs * 384 + 4 * pairs * 2 * length * length * 128
    return pl.pallas_call(
        attn_fwd_kernel,
        grid=(pairs,),
        in_specs=[whole(xh), col(0), col(pairs), col(0)]
        + [whole(t) for t in tables]
        + [whole(seg_col), whole(seg_row)],
        out_specs=[out] * 4 + [pl.BlockSpec((1, 2, length), lambda h: (h, 0, 0))],
        out_shape=[shape] * 4 + [jax.ShapeDtypeStruct((pairs, 2, length), F32)],
        scratch_shapes=[pltpu.VMEM((2, length, 128), BF)],
        cost_estimate=pl.CostEstimate(
            flops=flops, bytes_accessed=length * width * 8, transcendentals=pairs * 2 * length * length
        ),
        name="attn_fwd",
    )(xh, w_qk, w_qk, w_vo, *tables, seg_col, seg_row)


def attn_bwd_kernel(
    q, k, v, o, do, lse, cos, upper, lower, seg_col, seg_row, pg, kh, dk, dv
):
    length = q.shape[0]
    rows = min(256, length)
    lane = lax.broadcasted_iota(jnp.int32, (length, 128), 1)
    first = lane < HD
    kf = k[...]
    none = jnp.zeros_like(kf)
    kh[0] = jnp.where(first, kf, none)
    kh[1] = jnp.where(first, none, kf)
    dk[...] = jnp.zeros_like(dk)
    dv[...] = jnp.zeros_like(dv)

    def block(i, carry):
        at = pl.multiple_of(i * rows, rows)
        here = pl.ds(at, rows)
        q_rows = q[here, :]
        g_rows = do[here, :]
        seg_here = seg_row[:, here]
        same = seg_col[...] == seg_here
        prod = g_rows.astype(F32) * o[here, :].astype(F32)
        f = first[:rows]
        blank = jnp.zeros_like(q_rows)
        dq = jnp.zeros((rows, 128), F32)
        for head in range(2):
            mine = f if head == 0 else jnp.logical_not(f)
            q_head = jnp.where(mine, q_rows, blank)
            g_head = jnp.where(mine, g_rows, blank)
            delta = lax.dot_general(
                jnp.ones((8, 128), F32),
                jnp.where(mine, prod, 0.0),
                (NT, ((), ())),
                precision=lax.Precision.HIGHEST,
                preferred_element_type=F32,
            )[0:1, :]
            scores = dotf(k[...], q_head, NT)
            level = lse[0, pl.ds(head, 1), here]
            probs = jnp.where(same, jnp.exp(scores - level), 0.0)
            dv[...] += dotf(probs.astype(BF), g_head, NN)
            dp = dotf(v[...], g_head, NT)
            ds = (probs * (dp - delta)).astype(BF)
            dk[...] += dotf(ds, q_head, NN)
            dq = dq + dotf(ds, kh[head], TN)
        dq = dq * (1.0 / math.sqrt(HD))
        c, a, b = cos[here, :], upper[here, :], lower[here, :]
        pg[0, here, :] = (dq * c - turn(dq, a, b)).astype(BF)
        return carry

    lax.fori_loop(0, length // rows, block, 0)
    dkf = dk[...]
    pg[1] = (dkf * cos[...] - turn(dkf, upper[...], lower[...])).astype(BF)
    pg[2] = dv[...].astype(BF)


def attn_bwd(q, k, v, o, do, lse, tables, seg_col, seg_row):
    length, width = q.shape
    pairs = width // 128
    whole = lambda a: pl.BlockSpec(a.shape, lambda h: (0,) * a.ndim)
    col = pl.BlockSpec((length, 128), lambda h: (0, h))
    return pl.pallas_call(
        attn_bwd_kernel,
        grid=(pairs,),
        in_specs=[col] * 5
        + [pl.BlockSpec((1, 2, length), lambda h: (h, 0, 0))]
        + [whole(t) for t in tables]
        + [whole(seg_col), whole(seg_row)],
        out_specs=pl.BlockSpec((3, length, 128), lambda h: (0, 0, h)),
        out_shape=jax.ShapeDtypeStruct((3, length, width), BF),
        scratch_shapes=[
            pltpu.VMEM((2, length, 128), BF),
            pltpu.VMEM((length, 128), F32),
            pltpu.VMEM((length, 128), F32),
        ],
        cost_estimate=pl.CostEstimate(
            flops=10 * pairs * 2 * length * length * 128,
            bytes_accessed=length * width * 20,
            transcendentals=pairs * 2 * length * length,
        ),
        name="attn_bwd",
    )(q, k, v, o, do, lse, *tables, seg_col, seg_row)


class Chips:
    def __init__(self):
        self.axes = ("dp", "tensor")
        dp = lax.axis_index("dp")
        self.z, self.x, self.core = dp // 4, (dp // 2) % 2, dp % 2
        self.y = lax.axis_index("tensor")

    @staticmethod
    def place(z, x, c, y):
        return ((z * 2 + x) * 2 + c) * 2 + y

    def send(self, value, dz=0, dx=0, dy=0, dc=0):
        pairs = [
            (self.place(z, x, c, y), self.place(z ^ dz, x ^ dx, c ^ dc, y ^ dy))
            for z in range(4)
            for x in range(2)
            for c in range(2)
            for y in range(2)
        ]
        return lax.ppermute(value, self.axes, pairs)

    def swap(self, value):
        pairs = [
            (self.place(z, x, c, y), self.place(z, x, y, c))
            for z in range(4)
            for x in range(2)
            for c in range(2)
            for y in range(2)
        ]
        return lax.ppermute(value, self.axes, pairs)

    def flips(self, blocks):
        for axis, bit in ((1, self.y), (2, self.x), (3, self.z // 2), (4, self.z % 2)):
            blocks = jnp.where(bit == 1, jnp.flip(blocks, axis), blocks)
        return blocks

    def to_relative(self, value):
        rows, width = value.shape
        blocks = value.reshape(rows, 2, 2, 2, 2, width // 16).transpose(0, 4, 3, 1, 2, 5)
        return self.flips(blocks).reshape(rows, width)

    def from_relative(self, value):
        rows, width = value.shape
        blocks = self.flips(value.reshape(rows, 2, 2, 2, 2, width // 16))
        return blocks.transpose(0, 3, 4, 2, 1, 5).reshape(rows, width)

    def positions(self, half):
        near = jnp.arange(half, dtype=jnp.int32)
        return jnp.concatenate([near + self.core * half, near + (1 - self.core) * half])

    def turn_rows(self, value):
        half = value.shape[0] // 2
        return jnp.where(self.core == 0, value, jnp.concatenate([value[half:], value[:half]]))

    def gather_rows(self, value):
        return jnp.concatenate([value, self.send(value, dc=1)], axis=0)

    def scatter_rows(self, value):
        half = value.shape[0] // 2
        return value[:half] + self.send(value[half:].astype(BF), dc=1).astype(F32)

    def gather(self, a, b):
        parts = [(a, b)] + [(self.send(a, dz=k), self.send(b, dz=k)) for k in (1, 2, 3)]
        za = jnp.stack([p[0] for p in parts])
        zb = jnp.stack([p[1] for p in parts])
        xa = jnp.concatenate([za, self.send(za, dx=1)])
        ya = self.send(xa, dy=1)
        yb = self.send(zb, dy=1)
        xb = self.send(jnp.concatenate([zb, yb]), dx=1)
        full_a = jnp.concatenate([xa, ya])
        full_b = jnp.concatenate([zb, xb[:4], yb, xb[4:]])
        flat = lambda f: f.reshape((f.shape[0] * f.shape[1],) + f.shape[2:])
        return flat(full_a), flat(full_b)

    def reduce(self, a, b):
        a = a.astype(BF).reshape(16, a.shape[0] // 16, a.shape[1])
        b = b.astype(BF).reshape(16, b.shape[0] // 16, b.shape[1])
        add = lambda u, w: (u.astype(F32) + w.astype(F32)).astype(BF)
        a = add(a[:8], self.send(a[8:], dy=1))
        b = add(
            jnp.concatenate([b[:4], b[8:12]]),
            self.send(jnp.concatenate([b[4:8], b[12:]]), dx=1),
        )
        a = add(a[:4], self.send(a[4:], dx=1))
        b = add(b[:4], self.send(b[4:], dy=1))
        sum_a, sum_b = a[0].astype(F32), b[0].astype(F32)
        for k in (1, 2, 3):
            sum_a = sum_a + self.send(a[k], dz=k).astype(F32)
            sum_b = sum_b + self.send(b[k], dz=k).astype(F32)
        return self.swap(sum_a.astype(BF)).astype(F32), self.swap(sum_b.astype(BF)).astype(F32)

    def sum_tensor(self, value):
        return value + self.send(value, dy=1)


class Axes:
    def swap(self, value):
        return value

    to_relative = from_relative = swap

    def positions(self, half):
        return jnp.arange(half * lax.axis_size("tensor"), dtype=jnp.int32)

    def turn_rows(self, value):
        return value

    def gather_rows(self, value):
        return lax.all_gather(value, "tensor", axis=0, tiled=True)

    def scatter_rows(self, value):
        return lax.psum_scatter(value.astype(BF), "tensor", scatter_dimension=0, tiled=True).astype(F32)

    def gather(self, a, b):
        return tuple(lax.all_gather(w, "dp", axis=0, tiled=True) for w in (a, b))

    def reduce(self, a, b):
        return tuple(
            lax.psum_scatter(w.astype(BF), "dp", scatter_dimension=0, tiled=True).astype(F32)
            for w in (a, b)
        )

    def sum_tensor(self, value):
        return lax.psum(value, "tensor")


def normalize(values):
    centred = values - jnp.mean(values, axis=-1, keepdims=True)
    scale = lax.rsqrt(jnp.mean(centred * centred, axis=-1, keepdims=True) + EPS)
    return centred * scale, scale


def normalize_back(f, xhat, scale):
    return scale * (
        f
        - jnp.mean(f, axis=-1, keepdims=True)
        - xhat * jnp.mean(f * xhat, axis=-1, keepdims=True)
    )


def gelu_parts(gate):
    half_erf = 0.5 * (1.0 + lax.erf(gate * (1.0 / math.sqrt(2.0))))
    density = jnp.exp(-0.5 * gate * gate) * (1.0 / math.sqrt(2.0 * math.pi))
    return gate * half_erf, half_erf + gate * density


def make_local(comm_type):
    def local(tokens, segments, w_qkv, w_out, w_in, w_down, g_attn, g_mlp, cotangent):
        comm = comm_type()
        shard = w_qkv.shape[0]
        cols = w_qkv.shape[2]
        units = w_in.shape[2]
        low = 128 * (units // 256)
        pad = 128 * pl.cdiv(units, 128) - units
        gain_one = g_attn.astype(F32)[:, None]
        gain_two = g_mlp.astype(F32)[:, None]
        scaled = lambda w, g: (w.astype(F32) * g).astype(BF)
        padded = lambda w: jnp.pad(w, ((0, 0), (0, pad)))
        down_rows = w_down.T
        a_one = jnp.concatenate([scaled(w_qkv[:, 0], gain_one), scaled(w_qkv[:, 1], gain_one)], axis=1)
        b_one = jnp.concatenate([scaled(w_qkv[:, 2], gain_one), w_out.T], axis=1)
        a_two = jnp.concatenate([padded(scaled(w_in[:, 0], gain_two)), down_rows[:, :low]], axis=1)
        b_two = jnp.concatenate([padded(scaled(w_in[:, 1], gain_two)), down_rows[:, low:]], axis=1)
        w_qk, w_vo = comm.gather(comm.swap(a_one), comm.swap(b_one))
        w_gd, w_ud = comm.gather(comm.swap(a_two), comm.swap(b_two))
        w_o = w_vo[:, cols:]
        w_gate, w_up = w_gd[:, :units], w_ud[:, :units]
        w_dn = jnp.concatenate([w_gd[:, units + pad :], w_ud[:, units + pad :]], axis=1)

        x_in = comm.to_relative(comm.swap(tokens[0])).astype(F32)
        seg = comm.turn_rows(comm.swap(segments[0]))
        cot = comm.to_relative(comm.swap(cotangent[0]))
        cot_all = comm.gather_rows(cot)
        tables = rope_tables(comm.positions(x_in.shape[0]))
        seg_col, seg_row = seg[:, None], seg[None, :]

        xh_one, scale_one = normalize(x_in)
        xh = comm.gather_rows(xh_one.astype(BF))
        o, q, k, v, lse = attn_fwd(xh, w_qk, w_vo, tables, seg_col, seg_row)
        resid = x_in + comm.scatter_rows(dotf(o, w_o, NT))
        xh_two, scale_two = normalize(resid)
        xn = comm.gather_rows(xh_two.astype(BF))
        gate, up = dotf(xn, w_gate, NN), dotf(xn, w_up, NN)
        act, slope = gelu_parts(gate)
        hidden = (act * up).astype(BF)
        mlp = comm.scatter_rows(dotf(hidden, w_dn, NT))
        result = comm.swap(comm.from_relative((resid + mlp).astype(BF)))

        hidden_grad = dotf(cot_all, w_dn, NN).astype(BF).astype(F32)
        gate_grad = (hidden_grad * up * slope).astype(BF)
        up_grad = (hidden_grad * act).astype(BF)
        f_two = comm.scatter_rows(dotf(gate_grad, w_gate, NT) + dotf(up_grad, w_up, NT))
        resid_grad = cot.astype(F32) + normalize_back(f_two, xh_two, scale_two)
        attn_cot = comm.gather_rows(resid_grad.astype(BF))

        d_down = dotf(cot_all, hidden, TN)
        d_gate, d_up = dotf(xn, gate_grad, TN), dotf(xn, up_grad, TN)
        wide = lambda g, d: jnp.concatenate([padded(g), d], axis=1)
        two_a, two_b = comm.reduce(wide(d_gate, d_down[:, :low]), wide(d_up, d_down[:, low:]))

        heads_grad = dotf(attn_cot, w_o, NN).astype(BF)
        pg = attn_bwd(q, k, v, o, heads_grad, lse, tables, seg_col, seg_row)
        d_out = dotf(attn_cot, o, TN)
        d_q, d_k, d_v = (dotf(xh, pg[i], TN) for i in range(3))
        one_a, one_b = comm.reduce(
            jnp.concatenate([d_q, d_k], axis=1), jnp.concatenate([d_v, d_out], axis=1)
        )
        f_one = comm.scatter_rows(
            dotf(pg[0], w_qk[:, :cols], NT)
            + dotf(pg[1], w_qk[:, cols:], NT)
            + dotf(pg[2], w_vo[:, :cols], NT)
        )
        token_grad = resid_grad + normalize_back(f_one, xh_one, scale_one)
        token_grad = comm.swap(comm.from_relative(token_grad.astype(BF))).astype(F32)

        qkv_raw = jnp.stack([one_a[:, :cols], one_a[:, cols:], one_b[:, :cols]], axis=1)
        in_raw = jnp.stack([two_a[:, :units], two_b[:, :units]], axis=1)
        down_sum = jnp.concatenate([two_a[:, units + pad :], two_b[:, units + pad :]], axis=1).T
        gains = jnp.stack(
            [
                jnp.sum(qkv_raw * w_qkv.astype(F32), axis=(1, 2)),
                jnp.sum(in_raw * w_in.astype(F32), axis=(1, 2)),
            ]
        )
        gains = comm.sum_tensor(gains)
        return (
            result[None],
            token_grad[None],
            gains[0],
            gains[1],
            qkv_raw * gain_one[:, :, None],
            one_b[:, cols:].T,
            in_raw * gain_two[:, :, None],
            down_sum,
        )

    return local


def solution(mesh):
    paired = mesh.shape["dp"] == 16 and mesh.shape["tensor"] == 2
    return jax.shard_map(
        make_local(Chips if paired else Axes),
        mesh=mesh,
        in_specs=(
            P("dp", "tensor", None),
            P("dp", None),
            P("dp", None, "tensor"),
            P("tensor", "dp"),
            P("dp", None, "tensor"),
            P("tensor", "dp"),
            P("dp"),
            P("dp"),
            P("dp", "tensor", None),
        ),
        out_specs=(
            P("dp", "tensor", None),
            P("dp", "tensor", None),
            P("dp"),
            P("dp"),
            P("dp", None, "tensor"),
            P("tensor", "dp"),
            P("dp", None, "tensor"),
            P("tensor", "dp"),
        ),
        check_vma=False,
    )
```

time: 1150 us -> 634 us (0.55)
  waiting for transfers between devices: 484 us -> 195 us
  matrix products: 254 us -> 74.2 us
  local copies, waits for them, and re-layouts: 222 us -> 108 us
  starting transfers between devices: 1.37 us -> 112 us
  blocking collectives: 74 us -> 0 us
  Pallas kernels: 0 us -> 68.4 us
  loops' own time: 24 us -> 0 us
  between operations: 16.2 us -> 2.61 us
    reduce_scatter x7 -> x0, waiting for transfers between devices: 325 us -> none  [the longest x1 88.4 us: local(): lax.psum_scatter(qkv_grad, 'dp', scatter_dimension=0, tiled=True)]
    ppermute x0 -> x62, waiting for transfers between devices: none -> 195 us  [the longest x49 195 us: send(): return lax.ppermute(value, self.axes, pairs)]
    dot_general x127 -> x18, matrix products: 254 us -> 74.2 us  [dotf(): return lax.dot_general(a, b, (dims, ((), ())), preferred_element_type=F32)]
    all_gather x8 -> x0, waiting for transfers between devices: 156 us -> none  [the longest x1 57.4 us: local(): lax.all_gather(stacked[2], 'dp', axis=0, tiled=True)]
    ppermute x0 -> x62, starting transfers between devices: none -> 112 us  [the longest x49 90.3 us: send(): return lax.ppermute(value, self.axes, pairs)]
    squeeze x48 -> x5, local copies, waits for them, and re-layouts: 70.2 us -> 1.53 us  [the longest x2 0.92 us: reduce(): sum_a = sum_a + self.send(a[k], dz=k).astype(F32)]
    unnamed x2 -> x0, blocking collectives: 68.6 us -> none
    pallas_call x0 -> x2, Pallas kernels: none -> 68.4 us  [the longest x1 34.6 us: attn_bwd(): pl.pallas_call(attn_bwd_kernel, grid=(pairs,), in_specs=[col] * 5 + [pl.B...]
  transfers between devices with their start and end apart: 16 -> 62, of which waited for: 12 -> 20; matrix products, arithmetic and copies ran while one was open for 40% -> 33% of each run, Pallas kernels for 0% -> 11%
where the time goes in v1:
time: 634 us; the launch traced here: 627 us
  waiting for transfers between devices  195 us (31%)
  starting transfers between devices  112 us (18%)
  local copies, waits for them, and re-layouts  108 us (17%)
  matrix products  74.2 us (12%)
  Pallas kernels  68.4 us (11%)
  other arithmetic  66.7 us (11%)
    ppermute x49, waiting for transfers between devices, send(): return lax.ppermute(value, self.axes, pairs)  195 us
    ppermute x49, starting transfers between devices, send(): return lax.ppermute(value, self.axes, pairs)  90.3 us
    dot_general x18, matrix products, dotf(): return lax.dot_general(a, b, (dims, ((), ())), preferred_element_type=F32)  74.2 us
    pallas_call x1, Pallas kernels, attn_bwd(): pl.pallas_call(attn_bwd_kernel, grid=(pairs,), in_specs=[col] * 5 + [pl.B...  34.6 us
    pallas_call x1, Pallas kernels, attn_fwd(): pl.pallas_call(attn_fwd_kernel, grid=(pairs,), in_specs=[whole(xh), col(0...  33.8 us
    unnamed x160, local copies, waits for them, and re-layouts  33 us
    ppermute x13, starting transfers between devices, swap(): return lax.ppermute(value, self.axes, pairs)  22.1 us
  transfers between devices with their start and end apart: 62, of which 20 were waited for; matrix products, arithmetic and copies ran while one was open for 33% of the time, Pallas kernels for 11%

profile of v1, /device:TPU:0, one launch (start us, length us, event | category | flops | bytes accessed | tf_op | source)
XLA Modules:
  0.0 627.0 jit_solution(5662098032093380555)
XLA Ops:
  19.8 3.1 collective-permute-start.3
  22.8 2.6 collective-permute-start.4
  27.9 3.5 collective-permute-start.10
  37.3 4.8 collective-permute-done.10
  44.7 12.6 %collective-permute-start.12 = (bf16[4,64,1024]{2,1,0:T(8,128)(2,1)S(1)}, bf16[4,64,1024]{2,1,0:T(8,128)(2,1)S(1)}, u32[]{:S(2)}, u32[]{:S(2)}) collective-permute-start(bf16[4,64,1024]{2,1,0:T(8,128)(2,1)S(1)} %pad_maximum_fusion.19), channel_id=1, source_target_pairs={{0,1},{1,0},{2,3},{3,2},{4,5},{5,4},{6,7},{7,6},{8,9},{9,8},{10,11... | collective-permute-start | bytes 1572872 | tf_op jit(solution)/shard_map/ppermute | solution.py:206
  65.0 5.4 collective-permute-done.18
  72.0 11.1 %collective-permute-done.19 = bf16[64,2048]{1,0:T(8,128)(2,1)S(1)} collective-permute-done((bf16[64,2048]{1,0:T(8,128)(2,1)S(1)}, bf16[64,2048]{1,0:T(8,128)(2,1)S(1)}, u32[]{:S(2)}, u32[]{:S(2)}) %collective-permute-start.19) | collective-permute-done | bytes 262176 | tf_op jit(solution)/shard_map/ppermute | solution.py:206
  85.7 7.5 %collective-permute-done.20 = bf16[64,2048]{1,0:T(8,128)(2,1)S(1)} collective-permute-done((bf16[64,2048]{1,0:T(8,128)(2,1)S(1)}, bf16[64,2048]{1,0:T(8,128)(2,1)S(1)}, u32[]{:S(2)}, u32[]{:S(2)}) %collective-permute-start.20) | collective-permute-done | bytes 262176 | tf_op jit(solution)/shard_map/ppermute | solution.py:206
  97.4 3.6 collective-permute-done.24
  101.1 3.1 collective-permute-start.25
  105.1 10.2 %collective-permute-done.25 = bf16[64,2080]{1,0:T(8,128)(2,1)S(1)} collective-permute-done((bf16[64,2080]{1,0:T(8,128)(2,1)S(1)}, bf16[64,2080]{1,0:T(8,128)(2,1)S(1)}, u32[]{:S(2)}, u32[]{:S(2)}) %collective-permute-start.25) | collective-permute-done | bytes 266272 | tf_op jit(solution)/shard_map/ppermute | solution.py:206
  115.3 2.6 collective-permute-start.26
  118.8 6.7 %collective-permute-done.26 = bf16[64,2080]{1,0:T(8,128)(2,1)S(1)} collective-permute-done((bf16[64,2080]{1,0:T(8,128)(2,1)S(1)}, bf16[64,2080]{1,0:T(8,128)(2,1)S(1)}, u32[]{:S(2)}, u32[]{:S(2)}) %collective-permute-start.26) | collective-permute-done | bytes 266272 | tf_op jit(solution)/shard_map/ppermute | solution.py:206
  127.2 2.7 collective-permute-start.27
  141.1 31.1 %collective-permute-done.13 = bf16[8,64,1024]{2,1,0:T(8,128)(2,1)} collective-permute-done((bf16[8,64,1024]{2,1,0:T(8,128)(2,1)}, bf16[8,64,1024]{2,1,0:T(8,128)(2,1)}, u32[]{:S(2)}, u32[]{:S(2)}) %collective-permute-start.13) | collective-permute-done | bytes 1048608 | tf_op jit(solution)/shard_map/ppermute | solution.py:206
  180.6 33.8 %attn_fwd.1 = (bf16[1024,512]{1,0:T(8,128)(2,1)}, bf16[1024,512]{1,0:T(8,128)(2,1)}, bf16[1024,512]{1,0:T(8,128)(2,1)}, bf16[1024,512]{1,0:T(8,128)(2,1)}, f32[4,2,1024]{2,1,0:T(2,128)}) custom-call(bf16[1024,1024]{1,0:T(8,128)(2,1)} %pad_maximum_fusion.2.xh, bf16[1024,1024]{1,0:T(8,128)(2,1)} %bitcast.248, bf16[1024,1024]{1,0:T(8,128)(2,1)} %bitcast.249, ...), custom_call_target="tpu_custom_call" | custom-call | flops 7516192768 | bytes 8388608 | tf_op jit(solution)/shard_map/attn_fwd/pallas_call | solution.py:88
  214.4 2.8 fusion.40
  218.5 3.4 constant_dynamic-update-slice_fusion.21
  223.6 2.3 constant_dynamic-update-slice_fusion.32
  229.6 2.4 fusion.79
  233.9 35.9 %collective-permute-done.22 = bf16[8,64,2048]{2,1,0:T(8,128)(2,1)} collective-permute-done((bf16[8,64,2048]{2,1,0:T(8,128)(2,1)}, bf16[8,64,2048]{2,1,0:T(8,128)(2,1)}, u32[]{:S(2)}, u32[]{:S(2)}) %collective-permute-start.22) | collective-permute-done | bytes 2097184 | tf_op jit(solution)/shard_map/ppermute | solution.py:206
  269.7 3.2 constant_dynamic-update-slice_fusion.26
  280.7 5.8 convolution_convert_fusion.3
  286.4 5.3 fusion.17
  291.8 10.3 %fusion.3 = (bf16[1024,1312]{0,1:T(8,128)(2,1)S(1)}, bf16[1024,1312]{0,1:T(8,128)(2,1)}, bf16[1024,1312]{0,1:T(8,128)(2,1)}) fusion(bf16[1024,1312]{0,1:T(8,128)(2,1)} %convolution_convert_fusion.3, f32[1024,1312]{0,1:T(8,128)S(1)} %fusion.17, bf16[1024,2080]{1,0:T(8,128)(2,1)S(1)} %bitcast.229, bf16[512,1024]{1,0:T(8,128)(2,1)S(1)} %collective-permute-done.16, ...), kind=kOutput, calls=%fused_computation.8 | convolution fusion | flops 2778497024 | bytes 21102592 | tf_op jit(solution)/shard_map/dot_general | solution.py:18
  302.1 6.2 fusion.11
  308.3 5.5 fusion.22
  315.1 3.5 fusion.25
  320.4 4.4 convolution_convert_fusion.2
  327.6 3.3 convolution_convert_fusion
  335.4 2.3 copy.81
  337.8 3.0 pad_maximum_fusion.1
  342.2 4.9 convolution_convert_fusion.1
  349.0 3.3 fusion.82
  353.9 2.3 copy.79
  356.3 5.4 copy.77
  361.7 4.0 copy.78
  365.9 3.3 fusion.47
  369.3 4.8 fusion.78
  379.7 9.6 %collective-permute-start.30 = (bf16[512,1024]{0,1:T(8,128)(2,1)}, bf16[512,1024]{0,1:T(8,128)(2,1)}, u32[]{:S(2)}, u32[]{:S(2)}) collective-permute-start(bf16[512,1024]{0,1:T(8,128)(2,1)} %bitcast.36), channel_id=1, source_target_pairs={{0,0},{1,2},{2,1},{3,3},{4,4},{5,6},{6,5},{7,7},{8,8},{9,10},{10,9... | collective-permute-start | bytes 3145736 | tf_op jit(solution)/shard_map/ppermute | solution.py:216
  389.3 24.3 %collective-permute-done.49 = bf16[8,64,2048]{2,1,0:T(8,128)(2,1)} collective-permute-done((bf16[8,64,2048]{2,1,0:T(8,128)(2,1)}, bf16[8,64,2048]{2,1,0:T(8,128)(2,1)}, u32[]{:S(2)}, u32[]{:S(2)}) %collective-permute-start.49) | collective-permute-done | bytes 2097184 | tf_op jit(solution)/shard_map/ppermute | solution.py:206
  413.6 2.4 add_convert_fusion.1
  421.0 34.6 %attn_bwd.1 = bf16[3,1024,512]{2,1,0:T(8,128)(2,1)} custom-call(bf16[1024,512]{1,0:T(8,128)(2,1)} %get-tuple-element.14.q, bf16[1024,512]{1,0:T(8,128)(2,1)} %get-tuple-element.15.k, bf16[1024,512]{1,0:T(8,128)(2,1)} %get-tuple-element.16.v, bf16[1024,512]{1,0:T(8,128)(2,1)} %get-tuple-element.13.o, bf16[1024,512]{1,0:T(8,128)(2,1)} %convolution_convert_fusion.8.do, ...), custom_call_target="tpu_custom_call" | custom-call | flops 10737418240 | bytes 10485760 | tf_op jit(solution)/shard_map/attn_bwd/pallas_call | solution.py:164
  455.6 3.0 fusion.37
  460.4 3.3 add_add_fusion
  466.0 2.9 slice.579
  468.9 2.7 convolution_convert_fusion.4
  471.6 2.5 convolution_convert_fusion.5
  479.8 2.4 pad_maximum_fusion.15
  482.7 3.6 convolution_convert_fusion.6
  486.3 3.5 convolution_convert_fusion.7
  493.9 3.5 pad_maximum_fusion.13
  497.4 3.2 copy.71
  504.0 2.5 add_convert_fusion
  514.9 2.7 collective-permute-start.52
  519.6 2.9 add_convert_fusion.6
  531.9 20.4 %collective-permute-done.56 = bf16[4,64,2080]{2,1,0:T(8,128)(2,1)} collective-permute-done((bf16[4,64,2080]{2,1,0:T(8,128)(2,1)}, bf16[4,64,2080]{2,1,0:T(8,128)(2,1)}, u32[]{:S(2)}, u32[]{:S(2)}) %collective-permute-start.56) | collective-permute-done | bytes 1064992 | tf_op jit(solution)/shard_map/ppermute | solution.py:206
  558.1 2.7 collective-permute-start.58
  561.9 5.5 collective-permute-done.59
  568.8 13.5 %collective-permute-done.58 = bf16[64,2080]{1,0:T(8,128)(2,1)S(1)} collective-permute-done((bf16[64,2080]{1,0:T(8,128)(2,1)S(1)}, bf16[64,2080]{1,0:T(8,128)(2,1)S(1)}, u32[]{:S(2)}, u32[]{:S(2)}) %collective-permute-start.58) | collective-permute-done | bytes 266272 | tf_op jit(solution)/shard_map/ppermute | solution.py:206
  588.4 4.1 collective-permute-start.40
  593.5 10.1 %collective-permute-start.46 = (bf16[64,1024]{1,0:T(8,128)(2,1)S(1)}, bf16[64,1024]{1,0:T(8,128)(2,1)S(1)}, u32[]{:S(2)}, u32[]{:S(2)}) collective-permute-start(bf16[64,1024]{1,0:T(8,128)(2,1)S(1)} %get-tuple-element.73), channel_id=1, source_target_pairs={{0,16},{1,17},{2,18},{3,19},{4,20},{5,21},{6,22},{7,23},{8,24},{9,... | collective-permute-start | bytes 393224 | tf_op jit(solution)/shard_map/ppermute | solution.py:206
  606.0 5.0 collective-permute-done.46
  615.3 6.4 %collective-permute-start.61 = (f32[2,64]{1,0:T(2,128)S(1)}, f32[2,64]{1,0:T(2,128)S(1)}, u32[]{:S(2)}, u32[]{:S(2)}) collective-permute-start(f32[2,64]{1,0:T(2,128)S(1)} %pad_maximum_fusion.26), channel_id=1, source_target_pairs={{0,1},{1,0},{2,3},{3,2},{4,5},{5,4},{6,7},{7,6},{8,9},{9,8},{10,11... | collective-permute-start | bytes 1544 | tf_op jit(solution)/shard_map/ppermute | solution.py:206
  (381 shorter events, 174.9 us)
Async XLA Ops:
  4.2 40.5 %collective-permute-start.17 = (bf16[64,2048]{1,0:T(8,128)(2,1)}, bf16[64,2048]{1,0:T(8,128)(2,1)S(1)}, u32[]{:S(2)}, u32[]{:S(2)}) collective-permute-start(bf16[64,2048]{1,0:T(8,128)(2,1)} %fusion.61), channel_id=1, source_target_pairs={{0,0},{1,2},{2,1},{3,3},{4,4},{5,6},{6,5},{7,7},{8,8},{9,10},{10,9... | collective-permute-start | bytes 786440 | tf_op jit(solution)/shard_map/ppermute | solution.py:216
  6.6 13.2 %collective-permute-start.2 = (bf16[64,1024]{1,0:T(8,128)(2,1)}, bf16[64,1024]{1,0:T(8,128)(2,1)}, u32[]{:S(2)}, u32[]{:S(2)}) collective-permute-start(bf16[64,1024]{1,0:T(8,128)(2,1)} %pad_maximum_fusion.24), channel_id=1, source_target_pairs={{0,0},{1,2},{2,1},{3,3},{4,4},{5,6},{6,5},{7,7},{8,8},{9,10},{10,9... | collective-permute-start | bytes 393224 | tf_op jit(solution)/shard_map/ppermute | solution.py:216
  9.4 16.0 %collective-permute-start.8 = (bf16[64,1024]{1,0:T(8,128)(2,1)}, bf16[64,1024]{1,0:T(8,128)(2,1)S(1)}, u32[]{:S(2)}, u32[]{:S(2)}) collective-permute-start(bf16[64,1024]{1,0:T(8,128)(2,1)} %pad_maximum_fusion.25), channel_id=1, source_target_pairs={{0,0},{1,2},{2,1},{3,3},{4,4},{5,6},{6,5},{7,7},{8,8},{9,10},{10,9... | collective-permute-start | bytes 393224 | tf_op jit(solution)/shard_map/ppermute | solution.py:216
  11.0 7.7 %collective-permute-start.14 = (s32[1024]{0:T(1024)S(1)}, s32[1024]{0:T(1024)S(1)}, u32[]{:S(2)}, u32[]{:S(2)}) collective-permute-start(s32[1024]{0:T(1024)S(1)} %bitcast.256), channel_id=1, source_target_pairs={{0,0},{1,2},{2,1},{3,3},{4,4},{5,6},{6,5},{7,7},{8,8},{9,10},{10,9... | collective-permute-start | bytes 12296 | tf_op jit(solution)/shard_map/ppermute | solution.py:216
  19.8 8.1 %collective-permute-start.3 = (bf16[64,1024]{1,0:T(8,128)(2,1)}, bf16[64,1024]{1,0:T(8,128)(2,1)S(1)}, u32[]{:S(2)}, u32[]{:S(2)}) collective-permute-start(bf16[64,1024]{1,0:T(8,128)(2,1)} %collective-permute-done.2), channel_id=1, source_target_pairs={{0,8},{1,9},{2,10},{3,11},{4,12},{5,13},{6,14},{7,15},{8,0},{9,1},... | collective-permute-start | bytes 393224 | tf_op jit(solution)/shard_map/ppermute | solution.py:206
  22.8 8.6 %collective-permute-start.4 = (bf16[64,1024]{1,0:T(8,128)(2,1)}, bf16[64,1024]{1,0:T(8,128)(2,1)S(1)}, u32[]{:S(2)}, u32[]{:S(2)}) collective-permute-start(bf16[64,1024]{1,0:T(8,128)(2,1)} %collective-permute-done.2), channel_id=1, source_target_pairs={{0,16},{1,17},{2,18},{3,19},{4,20},{5,21},{6,22},{7,23},{8,24},{9,... | collective-permute-start | bytes 393224 | tf_op jit(solution)/shard_map/ppermute | solution.py:206
  25.4 8.6 %collective-permute-start.5 = (bf16[64,1024]{1,0:T(8,128)(2,1)}, bf16[64,1024]{1,0:T(8,128)(2,1)S(1)}, u32[]{:S(2)}, u32[]{:S(2)}) collective-permute-start(bf16[64,1024]{1,0:T(8,128)(2,1)} %collective-permute-done.2), channel_id=1, source_target_pairs={{0,24},{1,25},{2,26},{3,27},{4,28},{5,29},{6,30},{7,31},{8,16},{9,... | collective-permute-start | bytes 393224 | tf_op jit(solution)/shard_map/ppermute | solution.py:206
  25.4 11.2 %collective-permute-start.9 = (bf16[64,1024]{1,0:T(8,128)(2,1)S(1)}, bf16[64,1024]{1,0:T(8,128)(2,1)S(1)}, u32[]{:S(2)}, u32[]{:S(2)}) collective-permute-start(bf16[64,1024]{1,0:T(8,128)(2,1)S(1)} %collective-permute-done.8), channel_id=1, source_target_pairs={{0,8},{1,9},{2,10},{3,11},{4,12},{5,13},{6,14},{7,15},{8,0},{9,1},... | collective-permute-start | bytes 393224 | tf_op jit(solution)/shard_map/ppermute | solution.py:206
  27.9 14.3 %collective-permute-start.10 = (bf16[64,1024]{1,0:T(8,128)(2,1)S(1)}, bf16[64,1024]{1,0:T(8,128)(2,1)S(1)}, u32[]{:S(2)}, u32[]{:S(2)}) collective-permute-start(bf16[64,1024]{1,0:T(8,128)(2,1)S(1)} %collective-permute-done.8), channel_id=1, source_target_pairs={{0,16},{1,17},{2,18},{3,19},{4,20},{5,21},{6,22},{7,23},{8,24},{9,... | collective-permute-start | bytes 393224 | tf_op jit(solution)/shard_map/ppermute | solution.py:206
  31.4 11.7 %collective-permute-start.11 = (bf16[64,1024]{1,0:T(8,128)(2,1)S(1)}, bf16[64,1024]{1,0:T(8,128)(2,1)S(1)}, u32[]{:S(2)}, u32[]{:S(2)}) collective-permute-start(bf16[64,1024]{1,0:T(8,128)(2,1)S(1)} %collective-permute-done.8), channel_id=1, source_target_pairs={{0,24},{1,25},{2,26},{3,27},{4,28},{5,29},{6,30},{7,31},{8,16},{9,... | collective-permute-start | bytes 393224 | tf_op jit(solution)/shard_map/ppermute | solution.py:206
  34.0 28.3 %collective-permute-start.23 = (bf16[64,2080]{1,0:T(8,128)(2,1)}, bf16[64,2080]{1,0:T(8,128)(2,1)S(1)}, u32[]{:S(2)}, u32[]{:S(2)}) collective-permute-start(bf16[64,2080]{1,0:T(8,128)(2,1)} %fusion.59), channel_id=1, source_target_pairs={{0,0},{1,2},{2,1},{3,3},{4,4},{5,6},{6,5},{7,7},{8,8},{9,10},{10,9... | collective-permute-start | bytes 798728 | tf_op jit(solution)/shard_map/ppermute | solution.py:216
  36.6 95.1 %collective-permute-start.31 = (bf16[512,1024]{0,1:T(8,128)(2,1)S(1)}, bf16[512,1024]{0,1:T(8,128)(2,1)S(1)}, u32[]{:S(2)}, u32[]{:S(2)}) collective-permute-start(bf16[512,1024]{0,1:T(8,128)(2,1)S(1)} %bitcast.220), channel_id=1, source_target_pairs={{0,0},{1,2},{2,1},{3,3},{4,4},{5,6},{6,5},{7,7},{8,8},{9,10},{10,9... | collective-permute-start | bytes 3145736 | tf_op jit(solution)/shard_map/ppermute | solution.py:216
  42.2 91.0 %collective-permute-start = (bf16[512,1024]{0,1:T(8,128)(2,1)S(1)}, bf16[512,1024]{0,1:T(8,128)(2,1)S(1)}, u32[]{:S(2)}, u32[]{:S(2)}) collective-permute-start(bf16[512,1024]{0,1:T(8,128)(2,1)S(1)} %bitcast.219), channel_id=1, source_target_pairs={{0,0},{1,2},{2,1},{3,3},{4,4},{5,6},{6,5},{7,7},{8,8},{9,10},{10,9... | collective-permute-start | bytes 3145736 | tf_op jit(solution)/shard_map/ppermute | solution.py:216
  43.1 84.1 %collective-permute-start.6 = (bf16[4,64,1024]{2,1,0:T(8,128)(2,1)S(1)}, bf16[4,64,1024]{2,1,0:T(8,128)(2,1)S(1)}, u32[]{:S(2)}, u32[]{:S(2)}) collective-permute-start(bf16[4,64,1024]{2,1,0:T(8,128)(2,1)S(1)} %pad_maximum_fusion.18), channel_id=1, source_target_pairs={{0,4},{1,5},{2,6},{3,7},{4,0},{5,1},{6,2},{7,3},{8,12},{9,13},{10,... | collective-permute-start | bytes 1572872 | tf_op jit(solution)/shard_map/ppermute | solution.py:206
  44.7 86.1 %collective-permute-start.12 = (bf16[4,64,1024]{2,1,0:T(8,128)(2,1)S(1)}, bf16[4,64,1024]{2,1,0:T(8,128)(2,1)S(1)}, u32[]{:S(2)}, u32[]{:S(2)}) collective-permute-start(bf16[4,64,1024]{2,1,0:T(8,128)(2,1)S(1)} %pad_maximum_fusion.19), channel_id=1, source_target_pairs={{0,1},{1,0},{2,3},{3,2},{4,5},{5,4},{6,7},{7,6},{8,9},{9,8},{10,11... | collective-permute-start | bytes 1572872 | tf_op jit(solution)/shard_map/ppermute | solution.py:206
  62.4 8.0 %collective-permute-start.18 = (bf16[64,2048]{1,0:T(8,128)(2,1)S(1)}, bf16[64,2048]{1,0:T(8,128)(2,1)S(1)}, u32[]{:S(2)}, u32[]{:S(2)}) collective-permute-start(bf16[64,2048]{1,0:T(8,128)(2,1)S(1)} %collective-permute-done.17), channel_id=1, source_target_pairs={{0,8},{1,9},{2,10},{3,11},{4,12},{5,13},{6,14},{7,15},{8,0},{9,1},... | collective-permute-start | bytes 786440 | tf_op jit(solution)/shard_map/ppermute | solution.py:206
  70.4 12.7 %collective-permute-start.19 = (bf16[64,2048]{1,0:T(8,128)(2,1)S(1)}, bf16[64,2048]{1,0:T(8,128)(2,1)S(1)}, u32[]{:S(2)}, u32[]{:S(2)}) collective-permute-start(bf16[64,2048]{1,0:T(8,128)(2,1)S(1)} %collective-permute-done.17), channel_id=1, source_target_pairs={{0,16},{1,17},{2,18},{3,19},{4,20},{5,21},{6,22},{7,23},{8,24},{9,... | collective-permute-start | bytes 786440 | tf_op jit(solution)/shard_map/ppermute | solution.py:206
  83.1 10.1 %collective-permute-start.20 = (bf16[64,2048]{1,0:T(8,128)(2,1)S(1)}, bf16[64,2048]{1,0:T(8,128)(2,1)S(1)}, u32[]{:S(2)}, u32[]{:S(2)}) collective-permute-start(bf16[64,2048]{1,0:T(8,128)(2,1)S(1)} %collective-permute-done.17), channel_id=1, source_target_pairs={{0,24},{1,25},{2,26},{3,27},{4,28},{5,29},{6,30},{7,31},{8,16},{9,... | collective-permute-start | bytes 786440 | tf_op jit(solution)/shard_map/ppermute | solution.py:206
  93.2 7.9 %collective-permute-start.24 = (bf16[64,2080]{1,0:T(8,128)(2,1)S(1)}, bf16[64,2080]{1,0:T(8,128)(2,1)S(1)}, u32[]{:S(2)}, u32[]{:S(2)}) collective-permute-start(bf16[64,2080]{1,0:T(8,128)(2,1)S(1)} %collective-permute-done.23), channel_id=1, source_target_pairs={{0,8},{1,9},{2,10},{3,11},{4,12},{5,13},{6,14},{7,15},{8,0},{9,1},... | collective-permute-start | bytes 798728 | tf_op jit(solution)/shard_map/ppermute | solution.py:206
  101.1 14.2 %collective-permute-start.25 = (bf16[64,2080]{1,0:T(8,128)(2,1)S(1)}, bf16[64,2080]{1,0:T(8,128)(2,1)S(1)}, u32[]{:S(2)}, u32[]{:S(2)}) collective-permute-start(bf16[64,2080]{1,0:T(8,128)(2,1)S(1)} %collective-permute-done.23), channel_id=1, source_target_pairs={{0,16},{1,17},{2,18},{3,19},{4,20},{5,21},{6,22},{7,23},{8,24},{9,... | collective-permute-start | bytes 798728 | tf_op jit(solution)/shard_map/ppermute | solution.py:206
  115.3 10.2 %collective-permute-start.26 = (bf16[64,2080]{1,0:T(8,128)(2,1)S(1)}, bf16[64,2080]{1,0:T(8,128)(2,1)S(1)}, u32[]{:S(2)}, u32[]{:S(2)}) collective-permute-start(bf16[64,2080]{1,0:T(8,128)(2,1)S(1)} %collective-permute-done.23), channel_id=1, source_target_pairs={{0,24},{1,25},{2,26},{3,27},{4,28},{5,29},{6,30},{7,31},{8,16},{9,... | collective-permute-start | bytes 798728 | tf_op jit(solution)/shard_map/ppermute | solution.py:206
  125.5 93.0 %collective-permute-start.21 = (bf16[4,64,2048]{2,1,0:T(8,128)(2,1)}, bf16[4,64,2048]{2,1,0:T(8,128)(2,1)}, u32[]{:S(2)}, u32[]{:S(2)}) collective-permute-start(bf16[4,64,2048]{2,1,0:T(8,128)(2,1)} %pad_maximum_fusion.14), channel_id=1, source_target_pairs={{0,4},{1,5},{2,6},{3,7},{4,0},{5,1},{6,2},{7,3},{8,12},{9,13},{10,... | collective-permute-start | bytes 3145736 | tf_op jit(solution)/shard_map/ppermute | solution.py:206
  127.2 96.4 %collective-permute-start.27 = (bf16[4,64,2080]{2,1,0:T(8,128)(2,1)}, bf16[4,64,2080]{2,1,0:T(8,128)(2,1)}, u32[]{:S(2)}, u32[]{:S(2)}) collective-permute-start(bf16[4,64,2080]{2,1,0:T(8,128)(2,1)} %pad_maximum_fusion.12), channel_id=1, source_target_pairs={{0,1},{1,0},{2,3},{3,2},{4,5},{5,4},{6,7},{7,6},{8,9},{9,8},{10,11... | collective-permute-start | bytes 3194888 | tf_op jit(solution)/shard_map/ppermute | solution.py:206
  130.8 44.6 %collective-permute-start.7 = (bf16[8,64,1024]{2,1,0:T(8,128)(2,1)}, bf16[8,64,1024]{2,1,0:T(8,128)(2,1)}, u32[]{:S(2)}, u32[]{:S(2)}) collective-permute-start(bf16[8,64,1024]{2,1,0:T(8,128)(2,1)} %get-tuple-element.76), channel_id=1, source_target_pairs={{0,1},{1,0},{2,3},{3,2},{4,5},{5,4},{6,7},{7,6},{8,9},{9,8},{10,11... | collective-permute-start | bytes 3145736 | tf_op jit(solution)/shard_map/ppermute | solution.py:206
  131.7 40.5 %collective-permute-start.13 = (bf16[8,64,1024]{2,1,0:T(8,128)(2,1)}, bf16[8,64,1024]{2,1,0:T(8,128)(2,1)}, u32[]{:S(2)}, u32[]{:S(2)}) collective-permute-start(bf16[8,64,1024]{2,1,0:T(8,128)(2,1)} %constant_dynamic-update-slice_fusion.11), channel_id=1, source_target_pairs={{0,4},{1,5},{2,6},{3,7},{4,0},{5,1},{6,2},{7,3},{8,12},{9,13},{10,... | collective-permute-start | bytes 3145736 | tf_op jit(solution)/shard_map/ppermute | solution.py:206
  139.9 38.2 %collective-permute-start.1 = (bf16[512,1024]{1,0:T(8,128)(2,1)S(1)}, bf16[512,1024]{1,0:T(8,128)(2,1)S(1)}, u32[]{:S(2)}, u32[]{:S(2)}) collective-permute-start(bf16[512,1024]{1,0:T(8,128)(2,1)S(1)} %fusion.27), channel_id=1, source_target_pairs={{0,2},{1,3},{2,0},{3,1},{4,6},{5,7},{6,4},{7,5},{8,10},{9,11},{10,... | collective-permute-start | bytes 3145736 | tf_op jit(solution)/shard_map/ppermute | solution.py:206
  218.5 11.1 %collective-permute-start.15 = (bf16[512,1024]{1,0:T(8,128)(2,1)}, bf16[512,1024]{1,0:T(8,128)(2,1)}, u32[]{:S(2)}, u32[]{:S(2)}) collective-permute-start(bf16[512,1024]{1,0:T(8,128)(2,1)} %slice.582), channel_id=1, source_target_pairs={{0,2},{1,3},{2,0},{3,1},{4,6},{5,7},{6,4},{7,5},{8,10},{9,11},{10,... | collective-permute-start | bytes 3145736 | tf_op jit(solution)/shard_map/ppermute | solution.py:206
  221.9 47.9 %collective-permute-start.22 = (bf16[8,64,2048]{2,1,0:T(8,128)(2,1)}, bf16[8,64,2048]{2,1,0:T(8,128)(2,1)}, u32[]{:S(2)}, u32[]{:S(2)}) collective-permute-start(bf16[8,64,2048]{2,1,0:T(8,128)(2,1)} %get-tuple-element.64), channel_id=1, source_target_pairs={{0,1},{1,0},{2,3},{3,2},{4,5},{5,4},{6,7},{7,6},{8,9},{9,8},{10,11... | collective-permute-start | bytes 6291464 | tf_op jit(solution)/shard_map/ppermute | solution.py:206
  225.9 50.4 %collective-permute-start.28 = (bf16[8,64,2080]{2,1,0:T(8,128)(2,1)}, bf16[8,64,2080]{2,1,0:T(8,128)(2,1)}, u32[]{:S(2)}, u32[]{:S(2)}) collective-permute-start(bf16[8,64,2080]{2,1,0:T(8,128)(2,1)} %constant_dynamic-update-slice_fusion.32), channel_id=1, source_target_pairs={{0,4},{1,5},{2,6},{3,7},{4,0},{5,1},{6,2},{7,3},{8,12},{9,13},{10,... | collective-permute-start | bytes 6389768 | tf_op jit(solution)/shard_map/ppermute | solution.py:206
  228.0 52.7 %collective-permute-start.32 = (bf16[512,1024]{0,1:T(8,128)(2,1)S(1)}, bf16[512,1024]{0,1:T(8,128)(2,1)}, u32[]{:S(2)}, u32[]{:S(2)}) collective-permute-start(bf16[512,1024]{0,1:T(8,128)(2,1)S(1)} %bitcast.201), channel_id=1, source_target_pairs={{0,2},{1,3},{2,0},{3,1},{4,6},{5,7},{6,4},{7,5},{8,10},{9,11},{10,... | collective-permute-start | bytes 3145736 | tf_op jit(solution)/shard_map/ppermute | solution.py:206
  229.6 46.8 %slice-start.1 = ((s8[4456448]{0:T(1024)(128)(4,1)}), s8[4194304]{0:T(1024)(128)(4,1)S(1)}, s32[]{:S(2)}) async-start(s8[4456448]{0:T(1024)(128)(4,1)} %bitcast.226), calls=%async_computation.1 | async-start | bytes 8388608
  233.4 91.7 %copy-start.28 = (bf16[512,1024]{1,0:T(8,128)(2,1)}, bf16[512,1024]{1,0:T(8,128)(2,1)S(1)}, u32[]{:S(2)}) copy-start(bf16[512,1024]{1,0:T(8,128)(2,1)S(1)} %fusion.26) | copy-start | bytes 3145732
  233.4 53.1 %collective-permute-start.16 = (bf16[512,1024]{1,0:T(8,128)(2,1)S(1)}, bf16[512,1024]{1,0:T(8,128)(2,1)S(1)}, u32[]{:S(2)}, u32[]{:S(2)}) collective-permute-start(bf16[512,1024]{1,0:T(8,128)(2,1)S(1)} %fusion.26), channel_id=1, source_target_pairs={{0,2},{1,3},{2,0},{3,1},{4,6},{5,7},{6,4},{7,5},{8,10},{9,11},{10,... | collective-permute-start | bytes 3145736 | tf_op jit(solution)/shard_map/ppermute | solution.py:206
  315.1 50.8 %collective-permute-start.33 = (bf16[512,1024]{1,0:T(8,128)(2,1)}, bf16[512,1024]{1,0:T(8,128)(2,1)}, u32[]{:S(2)}, u32[]{:S(2)}) collective-permute-start(bf16[512,1024]{1,0:T(8,128)(2,1)} %slice.580), channel_id=1, source_target_pairs={{0,2},{1,3},{2,0},{3,1},{4,6},{5,7},{6,4},{7,5},{8,10},{9,11},{10,... | collective-permute-start | bytes 3145736 | tf_op jit(solution)/shard_map/ppermute | solution.py:206
  319.9 49.3 %collective-permute-start.29 = (bf16[512,1024]{1,0:T(8,128)(2,1)}, bf16[512,1024]{1,0:T(8,128)(2,1)}, u32[]{:S(2)}, u32[]{:S(2)}) collective-permute-start(bf16[512,1024]{1,0:T(8,128)(2,1)} %slice.581), channel_id=1, source_target_pairs={{0,2},{1,3},{2,0},{3,1},{4,6},{5,7},{6,4},{7,5},{8,10},{9,11},{10,... | collective-permute-start | bytes 3145736 | tf_op jit(solution)/shard_map/ppermute | solution.py:206
  340.7 163.3 %collective-permute-start.55 = (bf16[8,64,2080]{2,1,0:T(8,128)(2,1)}, bf16[8,64,2080]{2,1,0:T(8,128)(2,1)}, u32[]{:S(2)}, u32[]{:S(2)}) collective-permute-start(bf16[8,64,2080]{2,1,0:T(8,128)(2,1)} %pad_maximum_fusion.1), channel_id=1, source_target_pairs={{0,4},{1,5},{2,6},{3,7},{4,0},{5,1},{6,2},{7,3},{8,12},{9,13},{10,... | collective-permute-start | bytes 6389768 | tf_op jit(solution)/shard_map/ppermute | solution.py:206
  365.6 48.0 %collective-permute-start.49 = (bf16[8,64,2048]{2,1,0:T(8,128)(2,1)}, bf16[8,64,2048]{2,1,0:T(8,128)(2,1)}, u32[]{:S(2)}, u32[]{:S(2)}) collective-permute-start(bf16[8,64,2048]{2,1,0:T(8,128)(2,1)} %bitcast.207), channel_id=1, source_target_pairs={{0,1},{1,0},{2,3},{3,2},{4,5},{5,4},{6,7},{7,6},{8,9},{9,8},{10,11... | collective-permute-start | bytes 6291464 | tf_op jit(solution)/shard_map/ppermute | solution.py:206
  377.9 39.8 %collective-permute-start.34 = (bf16[512,1024]{1,0:T(8,128)(2,1)S(1)}, bf16[512,1024]{1,0:T(8,128)(2,1)S(1)}, u32[]{:S(2)}, u32[]{:S(2)}) collective-permute-start(bf16[512,1024]{1,0:T(8,128)(2,1)S(1)} %copy-done.24), channel_id=1, source_target_pairs={{0,2},{1,3},{2,0},{3,1},{4,6},{5,7},{6,4},{7,5},{8,10},{9,11},{10,... | collective-permute-start | bytes 3145736 | tf_op jit(solution)/shard_map/ppermute | solution.py:206
  379.7 84.0 %collective-permute-start.30 = (bf16[512,1024]{0,1:T(8,128)(2,1)}, bf16[512,1024]{0,1:T(8,128)(2,1)}, u32[]{:S(2)}, u32[]{:S(2)}) collective-permute-start(bf16[512,1024]{0,1:T(8,128)(2,1)} %bitcast.36), channel_id=1, source_target_pairs={{0,0},{1,2},{2,1},{3,3},{4,4},{5,6},{6,5},{7,7},{8,8},{9,10},{10,9... | collective-permute-start | bytes 3145736 | tf_op jit(solution)/shard_map/ppermute | solution.py:216
  417.2 92.8 %collective-permute-start.50 = (bf16[4,64,2048]{2,1,0:T(8,128)(2,1)}, bf16[4,64,2048]{2,1,0:T(8,128)(2,1)}, u32[]{:S(2)}, u32[]{:S(2)}) collective-permute-start(bf16[4,64,2048]{2,1,0:T(8,128)(2,1)} %slice.425), channel_id=1, source_target_pairs={{0,4},{1,5},{2,6},{3,7},{4,0},{5,1},{6,2},{7,3},{8,12},{9,13},{10,... | collective-permute-start | bytes 3145736 | tf_op jit(solution)/shard_map/ppermute | solution.py:206
  468.9 46.0 %collective-permute-start.35 = (bf16[512,1024]{1,0:T(8,128)(2,1)}, bf16[512,1024]{1,0:T(8,128)(2,1)}, u32[]{:S(2)}, u32[]{:S(2)}) collective-permute-start(bf16[512,1024]{1,0:T(8,128)(2,1)} %slice.579), channel_id=1, source_target_pairs={{0,2},{1,3},{2,0},{3,1},{4,6},{5,7},{6,4},{7,5},{8,10},{9,11},{10,... | collective-permute-start | bytes 3145736 | tf_op jit(solution)/shard_map/ppermute | solution.py:206
  482.2 42.1 %collective-permute-start.43 = (bf16[8,64,1024]{2,1,0:T(8,128)(2,1)}, bf16[8,64,1024]{2,1,0:T(8,128)(2,1)}, u32[]{:S(2)}, u32[]{:S(2)}) collective-permute-start(bf16[8,64,1024]{2,1,0:T(8,128)(2,1)} %pad_maximum_fusion.15), channel_id=1, source_target_pairs={{0,4},{1,5},{2,6},{3,7},{4,0},{5,1},{6,2},{7,3},{8,12},{9,13},{10,... | collective-permute-start | bytes 3145736 | tf_op jit(solution)/shard_map/ppermute | solution.py:206
  502.9 26.3 %collective-permute-start.37 = (bf16[8,64,1024]{2,1,0:T(8,128)(2,1)}, bf16[8,64,1024]{2,1,0:T(8,128)(2,1)}, u32[]{:S(2)}, u32[]{:S(2)}) collective-permute-start(bf16[8,64,1024]{2,1,0:T(8,128)(2,1)} %bitcast.221), channel_id=1, source_target_pairs={{0,1},{1,0},{2,3},{3,2},{4,5},{5,4},{6,7},{7,6},{8,9},{9,8},{10,11... | collective-permute-start | bytes 3145736 | tf_op jit(solution)/shard_map/ppermute | solution.py:206
  509.1 43.2 %collective-permute-start.56 = (bf16[4,64,2080]{2,1,0:T(8,128)(2,1)}, bf16[4,64,2080]{2,1,0:T(8,128)(2,1)}, u32[]{:S(2)}, u32[]{:S(2)}) collective-permute-start(bf16[4,64,2080]{2,1,0:T(8,128)(2,1)} %slice.437), channel_id=1, source_target_pairs={{0,1},{1,0},{2,3},{3,2},{4,5},{5,4},{6,7},{7,6},{8,9},{9,8},{10,11... | collective-permute-start | bytes 3194888 | tf_op jit(solution)/shard_map/ppermute | solution.py:206
  512.8 43.1 %collective-permute-start.53 = (bf16[64,2048]{1,0:T(8,128)(2,1)}, bf16[64,2048]{1,0:T(8,128)(2,1)S(1)}, u32[]{:S(2)}, u32[]{:S(2)}) collective-permute-start(bf16[64,2048]{1,0:T(8,128)(2,1)} %get-tuple-element.62), channel_id=1, source_target_pairs={{0,24},{1,25},{2,26},{3,27},{4,28},{5,29},{6,30},{7,31},{8,16},{9,... | collective-permute-start | bytes 786440 | tf_op jit(solution)/shard_map/ppermute | solution.py:206
  514.9 43.1 %collective-permute-start.52 = (bf16[64,2048]{1,0:T(8,128)(2,1)}, bf16[64,2048]{1,0:T(8,128)(2,1)}, u32[]{:S(2)}, u32[]{:S(2)}) collective-permute-start(bf16[64,2048]{1,0:T(8,128)(2,1)} %get-tuple-element.63), channel_id=1, source_target_pairs={{0,16},{1,17},{2,18},{3,19},{4,20},{5,21},{6,22},{7,23},{8,24},{9,... | collective-permute-start | bytes 786440 | tf_op jit(solution)/shard_map/ppermute | solution.py:206
  525.1 35.7 %collective-permute-start.51 = (bf16[64,2048]{1,0:T(8,128)(2,1)S(1)}, bf16[64,2048]{1,0:T(8,128)(2,1)S(1)}, u32[]{:S(2)}, u32[]{:S(2)}) collective-permute-start(bf16[64,2048]{1,0:T(8,128)(2,1)S(1)} %copy-done.40), channel_id=1, source_target_pairs={{0,8},{1,9},{2,10},{3,11},{4,12},{5,13},{6,14},{7,15},{8,0},{9,1},... | collective-permute-start | bytes 786440 | tf_op jit(solution)/shard_map/ppermute | solution.py:206
  529.3 95.1 %collective-permute-start.36 = (bf16[512,1024]{0,1:T(8,128)(2,1)S(1)}, bf16[512,1024]{0,1:T(8,128)(2,1)S(1)}, u32[]{:S(2)}, u32[]{:S(2)}) collective-permute-start(bf16[512,1024]{0,1:T(8,128)(2,1)S(1)} %bitcast.218), channel_id=1, source_target_pairs={{0,0},{1,2},{2,1},{3,3},{4,4},{5,6},{6,5},{7,7},{8,8},{9,10},{10,9... | collective-permute-start | bytes 3145736 | tf_op jit(solution)/shard_map/ppermute | solution.py:216
  552.3 31.6 %collective-permute-start.44 = (bf16[4,64,1024]{2,1,0:T(8,128)(2,1)S(1)}, bf16[4,64,1024]{2,1,0:T(8,128)(2,1)S(1)}, u32[]{:S(2)}, u32[]{:S(2)}) collective-permute-start(bf16[4,64,1024]{2,1,0:T(8,128)(2,1)S(1)} %slice.415), channel_id=1, source_target_pairs={{0,1},{1,0},{2,3},{3,2},{4,5},{5,4},{6,7},{7,6},{8,9},{9,8},{10,11... | collective-permute-start | bytes 1572872 | tf_op jit(solution)/shard_map/ppermute | solution.py:206
  555.9 11.5 %collective-permute-start.59 = (bf16[64,2080]{1,0:T(8,128)(2,1)S(1)}, bf16[64,2080]{1,0:T(8,128)(2,1)S(1)}, u32[]{:S(2)}, u32[]{:S(2)}) collective-permute-start(bf16[64,2080]{1,0:T(8,128)(2,1)S(1)} %get-tuple-element.59), channel_id=1, source_target_pairs={{0,24},{1,25},{2,26},{3,27},{4,28},{5,29},{6,30},{7,31},{8,16},{9,... | collective-permute-start | bytes 798728 | tf_op jit(solution)/shard_map/ppermute | solution.py:206
  558.1 24.2 %collective-permute-start.58 = (bf16[64,2080]{1,0:T(8,128)(2,1)S(1)}, bf16[64,2080]{1,0:T(8,128)(2,1)S(1)}, u32[]{:S(2)}, u32[]{:S(2)}) collective-permute-start(bf16[64,2080]{1,0:T(8,128)(2,1)S(1)} %get-tuple-element.60), channel_id=1, source_target_pairs={{0,16},{1,17},{2,18},{3,19},{4,20},{5,21},{6,22},{7,23},{8,24},{9,... | collective-permute-start | bytes 798728 | tf_op jit(solution)/shard_map/ppermute | solution.py:206
  560.8 22.2 %collective-permute-start.57 = (bf16[64,2080]{1,0:T(8,128)(2,1)S(1)}, bf16[64,2080]{1,0:T(8,128)(2,1)S(1)}, u32[]{:S(2)}, u32[]{:S(2)}) collective-permute-start(bf16[64,2080]{1,0:T(8,128)(2,1)S(1)} %get-tuple-element.58), channel_id=1, source_target_pairs={{0,8},{1,9},{2,10},{3,11},{4,12},{5,13},{6,14},{7,15},{8,0},{9,1},... | collective-permute-start | bytes 798728 | tf_op jit(solution)/shard_map/ppermute | solution.py:206
  567.3 19.0 %collective-permute-start.38 = (bf16[4,64,1024]{2,1,0:T(8,128)(2,1)S(1)}, bf16[4,64,1024]{2,1,0:T(8,128)(2,1)S(1)}, u32[]{:S(2)}, u32[]{:S(2)}) collective-permute-start(bf16[4,64,1024]{2,1,0:T(8,128)(2,1)S(1)} %slice.401), channel_id=1, source_target_pairs={{0,4},{1,5},{2,6},{3,7},{4,0},{5,1},{6,2},{7,3},{8,12},{9,13},{10,... | collective-permute-start | bytes 1572872 | tf_op jit(solution)/shard_map/ppermute | solution.py:206
  582.3 1.5 collective-permute-start.54
  583.1 9.4 %collective-permute-start.60 = (bf16[64,2080]{1,0:T(8,128)(2,1)S(1)}, bf16[64,2080]{1,0:T(8,128)(2,1)S(1)}, u32[]{:S(2)}, u32[]{:S(2)}) collective-permute-start(bf16[64,2080]{1,0:T(8,128)(2,1)S(1)} %fusion.45), channel_id=1, source_target_pairs={{0,0},{1,2},{2,1},{3,3},{4,4},{5,6},{6,5},{7,7},{8,8},{9,10},{10,9... | collective-permute-start | bytes 798728 | tf_op jit(solution)/shard_map/ppermute | solution.py:216
  584.2 21.8 %collective-permute-start.47 = (bf16[64,1024]{1,0:T(8,128)(2,1)S(1)}, bf16[64,1024]{1,0:T(8,128)(2,1)S(1)}, u32[]{:S(2)}, u32[]{:S(2)}) collective-permute-start(bf16[64,1024]{1,0:T(8,128)(2,1)S(1)} %get-tuple-element.72), channel_id=1, source_target_pairs={{0,24},{1,25},{2,26},{3,27},{4,28},{5,29},{6,30},{7,31},{8,16},{9,... | collective-permute-start | bytes 393224 | tf_op jit(solution)/shard_map/ppermute | solution.py:206
  586.6 6.9 %collective-permute-start.41 = (bf16[64,1024]{1,0:T(8,128)(2,1)S(1)}, bf16[64,1024]{1,0:T(8,128)(2,1)S(1)}, u32[]{:S(2)}, u32[]{:S(2)}) collective-permute-start(bf16[64,1024]{1,0:T(8,128)(2,1)S(1)} %get-tuple-element.69), channel_id=1, source_target_pairs={{0,24},{1,25},{2,26},{3,27},{4,28},{5,29},{6,30},{7,31},{8,16},{9,... | collective-permute-start | bytes 393224 | tf_op jit(solution)/shard_map/ppermute | solution.py:206
  588.4 16.9 %collective-permute-start.40 = (bf16[64,1024]{1,0:T(8,128)(2,1)S(1)}, bf16[64,1024]{1,0:T(8,128)(2,1)S(1)}, u32[]{:S(2)}, u32[]{:S(2)}) collective-permute-start(bf16[64,1024]{1,0:T(8,128)(2,1)S(1)} %get-tuple-element.70), channel_id=1, source_target_pairs={{0,16},{1,17},{2,18},{3,19},{4,20},{5,21},{6,22},{7,23},{8,24},{9,... | collective-permute-start | bytes 393224 | tf_op jit(solution)/shard_map/ppermute | solution.py:206
  592.5 12.8 %collective-permute-start.39 = (bf16[64,1024]{1,0:T(8,128)(2,1)S(1)}, bf16[64,1024]{1,0:T(8,128)(2,1)S(1)}, u32[]{:S(2)}, u32[]{:S(2)}) collective-permute-start(bf16[64,1024]{1,0:T(8,128)(2,1)S(1)} %get-tuple-element.68), channel_id=1, source_target_pairs={{0,8},{1,9},{2,10},{3,11},{4,12},{5,13},{6,14},{7,15},{8,0},{9,1},... | collective-permute-start | bytes 393224 | tf_op jit(solution)/shard_map/ppermute | solution.py:206
  593.5 17.5 %collective-permute-start.46 = (bf16[64,1024]{1,0:T(8,128)(2,1)S(1)}, bf16[64,1024]{1,0:T(8,128)(2,1)S(1)}, u32[]{:S(2)}, u32[]{:S(2)}) collective-permute-start(bf16[64,1024]{1,0:T(8,128)(2,1)S(1)} %get-tuple-element.73), channel_id=1, source_target_pairs={{0,16},{1,17},{2,18},{3,19},{4,20},{5,21},{6,22},{7,23},{8,24},{9,... | collective-permute-start | bytes 393224 | tf_op jit(solution)/shard_map/ppermute | solution.py:206
  605.2 7.6 %collective-permute-start.45 = (bf16[64,1024]{1,0:T(8,128)(2,1)S(1)}, bf16[64,1024]{1,0:T(8,128)(2,1)S(1)}, u32[]{:S(2)}, u32[]{:S(2)}) collective-permute-start(bf16[64,1024]{1,0:T(8,128)(2,1)S(1)} %get-tuple-element.71), channel_id=1, source_target_pairs={{0,8},{1,9},{2,10},{3,11},{4,12},{5,13},{6,14},{7,15},{8,0},{9,1},... | collective-permute-start | bytes 393224 | tf_op jit(solution)/shard_map/ppermute | solution.py:206
  605.3 8.2 %collective-permute-start.42 = (bf16[64,1024]{1,0:T(8,128)(2,1)S(1)}, bf16[64,1024]{1,0:T(8,128)(2,1)S(1)}, u32[]{:S(2)}, u32[]{:S(2)}) collective-permute-start(bf16[64,1024]{1,0:T(8,128)(2,1)S(1)} %fusion.67), channel_id=1, source_target_pairs={{0,0},{1,2},{2,1},{3,3},{4,4},{5,6},{6,5},{7,7},{8,8},{9,10},{10,9... | collective-permute-start | bytes 393224 | tf_op jit(solution)/shard_map/ppermute | solution.py:216
  612.9 0.7 collective-permute-start.48
  615.3 8.6 %collective-permute-start.61 = (f32[2,64]{1,0:T(2,128)S(1)}, f32[2,64]{1,0:T(2,128)S(1)}, u32[]{:S(2)}, u32[]{:S(2)}) collective-permute-start(f32[2,64]{1,0:T(2,128)S(1)} %pad_maximum_fusion.26), channel_id=1, source_target_pairs={{0,1},{1,0},{2,3},{3,2},{4,5},{5,4},{6,7},{7,6},{8,9},{9,8},{10,11... | collective-permute-start | bytes 1544 | tf_op jit(solution)/shard_map/ppermute | solution.py:206
  (66 other events, 581.9 us)

commit v2 on v1

--- a/solution.py
+++ b/solution.py
@@ -184,6 +184,303 @@
     )(q, k, v, o, do, lse, *tables, seg_col, seg_row)
 
 
+SHARD = (4, 2, 2)
+
+
+def place():
+    dp = lax.axis_index("dp")
+    return dp // 4, (dp // 2) % 2, dp % 2, lax.axis_index("tensor")
+
+
+def partners():
+    z, x, c, y = place()
+    at = lambda z, x, c, y: ((z * 2 + x) * 2 + c, y)
+    return {
+        "z1": at(z + 1 - 2 * (z % 2), x, c, y),
+        "z2": at(z + 2 - 4 * (z // 2), x, c, y),
+        "z3": at(3 - z, x, c, y),
+        "x": at(z, 1 - x, c, y),
+        "y": at(z, x, c, 1 - y),
+        "c": at(z, x, 1 - c, y),
+    }
+
+
+def meet(peers):
+    barrier = pltpu.get_barrier_semaphore()
+    for peer in peers.values():
+        pl.semaphore_signal(barrier, inc=1, device_id=peer, device_id_type=pl.DeviceIdType.MESH)
+    pl.semaphore_wait(barrier, len(peers))
+
+
+def remote(src, dst, send_sem, recv_sem, peer):
+    return pltpu.make_async_remote_copy(
+        src_ref=src,
+        dst_ref=dst,
+        send_sem=send_sem,
+        recv_sem=recv_sem,
+        device_id=peer,
+        device_id_type=pl.DeviceIdType.MESH,
+    )
+
+
+def to_place(values, inverse=False):
+    z, x, _, y = place()
+    tiles = [values[:, j * 128 : (j + 1) * 128] for j in range(8)]
+    tiles = [jnp.where(y == 1, pltpu.roll(t, 64, 1), t) for t in tiles]
+    for bit, step in ((x, 1), (z % 2, 2), (z // 2, 4)):
+        tiles = [jnp.where(bit == 1, tiles[j ^ step], tiles[j]) for j in range(8)]
+    return jnp.concatenate(tiles, axis=1)
+
+
+class Gather:
+    MESSAGES = 15
+
+    def __init__(self, own, buf, rows, axes, peers, sems, base):
+        self.buf, self.rows, self.axes, self.peers = buf, rows, axes, peers
+        self.own = own.at[rows]
+        self.send_sem, self.recv_sem = sems
+        self.base = base
+
+    def slot(self, z, first, second):
+        x, y = (first, second) if self.axes[0] == "x" else (second, first)
+        return self.buf.at[z, x, y, self.rows]
+
+    def copy(self, i):
+        if i < 3:
+            src, dst, peer = self.own, self.slot(i + 1, 0, 0), "z%d" % (i + 1)
+        elif i < 7:
+            src, dst, peer = self.slot(i - 3, 0, 0), self.slot(i - 3, 1, 0), self.axes[0]
+        else:
+            f, z = divmod(i - 7, 4)
+            src, dst, peer = self.slot(z, f, 0), self.slot(z, f, 1), self.axes[1]
+        if i in (3, 7):
+            src = self.own
+        n = self.base + i
+        return remote(src, dst, self.send_sem.at[n], self.recv_sem.at[n], self.peers[peer])
+
+    def start_z(self):
+        for i in range(3):
+            self.copy(i).start()
+
+    def relay_z(self, z):
+        if z:
+            self.copy(z - 1).wait_recv()
+        self.copy(3 + z).start()
+        self.copy(7 + z).start()
+
+    def relay_first(self, z):
+        self.copy(3 + z).wait_recv()
+        self.copy(11 + z).start()
+
+    def finish(self):
+        for i in range(7, 15):
+            self.copy(i).wait_recv()
+        for i in range(15):
+            self.copy(i).wait_send()
+
+
+def forward_kernel(
+    a_own, b_own, g_own, u_own, d_own, x_half, cos, upper, lower, seg_col, seg_row,
+    q, k, v, o, lse, xh, w_qk, w_vo, resid, xn, w_gate, w_up, w_down,
+    kh, x_rel, part, sent, got, send_sem, recv_sem, pair_send, pair_recv, own_sem,
+):
+    length = xh.shape[0]
+    half = length // 2
+    width = xh.shape[1]
+    pairs = q.shape[1] // 128
+    rows = 256
+    peers = partners()
+    sems = (send_sem, recv_sem)
+    n = Gather.MESSAGES
+    whole, low, high = pl.ds(0, 64), pl.ds(0, 32), pl.ds(32, 32)
+    one = [
+        Gather(a_own, w_qk, whole, "xy", peers, sems, 0),
+        Gather(b_own, w_vo, whole, "yx", peers, sems, n),
+    ]
+    two = [
+        Gather(g_own, w_gate, whole, "xy", peers, sems, 2 * n),
+        Gather(u_own, w_up, whole, "yx", peers, sems, 3 * n),
+    ]
+    three = [
+        Gather(d_own, w_down, low, "xy", peers, sems, 4 * n),
+        Gather(d_own, w_down, high, "yx", peers, sems, 5 * n),
+    ]
+    owns = [
+        pltpu.make_async_copy(src, dst.at[0, 0, 0], own_sem.at[i])
+        for i, (src, dst) in enumerate(
+            ((a_own, w_qk), (b_own, w_vo), (g_own, w_gate), (u_own, w_up), (d_own, w_down))
+        )
+    ]
+    for copy in owns:
+        copy.start()
+    meet(peers)
+    for gather in one:
+        gather.start_z()
+    for gather in one:
+        gather.relay_z(0)
+
+    def first_norm(i, carry):
+        here = pl.ds(pl.multiple_of(i * 128, 128), 128)
+        values = to_place(x_half[here, :].astype(F32))
+        x_rel[here, :] = values.astype(BF)
+        xh[here, :] = normalize(values)[0].astype(BF)
+        return carry
+
+    lax.fori_loop(0, half // 128, first_norm, 0)
+    for z in (1, 2, 3):
+        for gather in one:
+            gather.relay_z(z)
+    swap_xh = remote(
+        xh.at[pl.ds(0, half)], xh.at[pl.ds(half, half)], pair_send.at[0], pair_recv.at[0], peers["c"]
+    )
+    swap_xh.start()
+    for gather in two:
+        gather.start_z()
+    for z in range(4):
+        for gather in one:
+            gather.relay_first(z)
+    for gather in three:
+        gather.start_z()
+    swap_xh.wait()
+    for gather in one:
+        gather.finish()
+    for copy in owns:
+        copy.wait()
+
+    events = {}
+    for z in range(4):
+        events.setdefault(1 + z, []).extend((g.relay_z, z) for g in two)
+        events.setdefault(6 + z, []).extend((g.relay_first, z) for g in two)
+        events.setdefault(9 + z, []).extend((g.relay_z, z) for g in three)
+    first = lax.broadcasted_iota(jnp.int32, (length, 128), 1) < HD
+
+    def pair(h, carry):
+        lanes = pl.ds(pl.multiple_of(h * 128, 128), 128)
+        lanes_k = pl.ds(pl.multiple_of((h + pairs) * 128, 128), 128)
+        weight = lambda ref, cols: ref[:, :, :, :, cols].reshape(width, 128)
+        tokens = xh[...]
+        qf = dotf(tokens, weight(w_qk, lanes), NN)
+        qf = qf * cos[...] + turn(qf, upper[...], lower[...])
+        q[:, lanes] = (qf * (1.0 / math.sqrt(HD))).astype(BF)
+        kf = dotf(tokens, weight(w_qk, lanes_k), NN)
+        kf = (kf * cos[...] + turn(kf, upper[...], lower[...])).astype(BF)
+        k[:, lanes] = kf
+        kh[0] = jnp.where(first, kf, jnp.zeros_like(kf))
+        kh[1] = jnp.where(first, jnp.zeros_like(kf), kf)
+        v[:, lanes] = dotf(tokens, weight(w_vo, lanes), NN).astype(BF)
+
+        def block(i, carry):
+            for step, calls in events.items():
+
+                @pl.when(h * (length // rows) + i == step)
+                def _():
+                    for call, z in calls:
+                        call(z)
+
+            at = pl.multiple_of(i * rows, rows)
+            q_rows = q[pl.ds(at, rows), lanes]
+            same = seg_col[pl.ds(at, rows), :] == seg_row[...]
+            outs = []
+            for head in range(2):
+                scores = dotf(q_rows, kh[head], NT)
+                scores = jnp.where(same, scores, -1e30)
+                top = jnp.max(scores, axis=-1, keepdims=True)
+                expv = jnp.exp(scores - top)
+                total = jnp.sum(expv, axis=-1, keepdims=True)
+                low_probs = (expv * (1.0 / total)).astype(BF)
+                outs.append(dotf(low_probs, v[:, lanes], NN))
+                level = top + jnp.log(total)
+                flat = jnp.transpose(jnp.broadcast_to(level, (rows, 128)))
+                lse[h, pl.ds(head, 1), pl.ds(at, rows)] = flat[0:1, :]
+            o[pl.ds(at, rows), lanes] = jnp.where(first[:rows], outs[0], outs[1]).astype(BF)
+            return carry
+
+        return lax.fori_loop(0, length // rows, block, carry)
+
+    lax.fori_loop(0, pairs, pair, 0)
+    w_o = w_vo[:, :, :, :, pairs * 128 :].reshape(width, pairs * 128)
+
+    def project(i, carry):
+        at = pl.multiple_of(half + i * rows, rows)
+        sent[pl.ds(pl.multiple_of(i * rows, rows), rows), :] = dotf(
+            o[pl.ds(at, rows), :], w_o, NT
+        ).astype(BF)
+        return carry
+
+    lax.fori_loop(0, half // rows, project, 0)
+
+    def project_own(i, carry):
+        here = pl.ds(pl.multiple_of(i * rows, rows), rows)
+        part[here, :] = dotf(o[here, :], w_o, NT)
+        return carry
+
+    give = remote(sent, got, pair_send.at[1], pair_recv.at[1], peers["c"])
+    lax.fori_loop(0, half // rows, project_own, 0)
+    give.start()
+    for gather in two + three:
+        for z in range(4):
+            if gather in three:
+                gather.relay_first(z)
+    give.wait()
+
+    def second_norm(i, carry):
+        here = pl.ds(pl.multiple_of(i * 128, 128), 128)
+        values = x_rel[here, :].astype(F32) + (part[here, :] + got[here, :].astype(F32))
+        resid[here, :] = values
+        xn[here, :] = normalize(values)[0].astype(BF)
+        return carry
+
+    lax.fori_loop(0, half // 128, second_norm, 0)
+    swap_xn = remote(
+        xn.at[pl.ds(0, half)], xn.at[pl.ds(half, half)], pair_send.at[2], pair_recv.at[2], peers["c"]
+    )
+    swap_xn.start()
+    for gather in two + three:
+        gather.finish()
+    swap_xn.wait()
+
+
+def forward_block(owned, x_half, tables, seg_col, seg_row):
+    half, width = x_half.shape
+    length = 2 * half
+    cols = owned[0].shape[1] // 2
+    pairs = cols // 128
+    units = owned[2].shape[1]
+    vmem = pl.BlockSpec(memory_space=pltpu.VMEM)
+    any_ = pl.BlockSpec(memory_space=pl.ANY)
+    gathered = lambda n: jax.ShapeDtypeStruct(SHARD + (width // 16, n), BF)
+    heads = jax.ShapeDtypeStruct((length, cols), BF)
+    return pl.pallas_call(
+        forward_kernel,
+        in_specs=[any_] * 5 + [vmem] * 6,
+        out_specs=[vmem] * 10 + [any_] * 3,
+        out_shape=[heads] * 4
+        + [
+            jax.ShapeDtypeStruct((pairs, 2, length), F32),
+            jax.ShapeDtypeStruct((length, width), BF),
+            gathered(2 * cols),
+            gathered(2 * cols),
+            jax.ShapeDtypeStruct((half, width), F32),
+            jax.ShapeDtypeStruct((length, width), BF),
+        ]
+        + [gathered(units)] * 3,
+        scratch_shapes=[
+            pltpu.VMEM((2, length, 128), BF),
+            pltpu.VMEM((half, width), BF),
+            pltpu.VMEM((half, width), F32),
+            pltpu.VMEM((half, width), BF),
+            pltpu.VMEM((half, width), BF),
+            pltpu.SemaphoreType.DMA((6 * Gather.MESSAGES,)),
+            pltpu.SemaphoreType.DMA((6 * Gather.MESSAGES,)),
+            pltpu.SemaphoreType.DMA((3,)),
+            pltpu.SemaphoreType.DMA((3,)),
+            pltpu.SemaphoreType.DMA((5,)),
+        ],
+        compiler_params=pltpu.CompilerParams(collective_id=0, has_side_effects=True),
+        name="forward_block",
+    )(*owned, x_half, *tables, seg_col, seg_row)
+
+
 class Chips:
     def __init__(self):
         self.axes = ("dp", "tensor")
@@ -215,20 +512,14 @@
         ]
         return lax.ppermute(value, self.axes, pairs)
 
-    def flips(self, blocks):
-        for axis, bit in ((1, self.y), (2, self.x), (3, self.z // 2), (4, self.z % 2)):
-            blocks = jnp.where(bit == 1, jnp.flip(blocks, axis), blocks)
-        return blocks
-
     def to_relative(self, value):
         rows, width = value.shape
-        blocks = value.reshape(rows, 2, 2, 2, 2, width // 16).transpose(0, 4, 3, 1, 2, 5)
-        return self.flips(blocks).reshape(rows, width)
-
-    def from_relative(self, value):
-        rows, width = value.shape
-        blocks = self.flips(value.reshape(rows, 2, 2, 2, 2, width // 16))
-        return blocks.transpose(0, 3, 4, 2, 1, 5).reshape(rows, width)
+        blocks = value.reshape(rows, 2, 2, 2, 2, width // 16)
+        for axis, bit in ((4, self.y), (3, self.x), (2, self.z % 2), (1, self.z // 2)):
+            blocks = jnp.where(bit == 1, jnp.flip(blocks, axis), blocks)
+        return blocks.reshape(rows, width)
+
+    from_relative = to_relative
 
     def positions(self, half):
         near = jnp.arange(half, dtype=jnp.int32)
@@ -245,22 +536,9 @@
         half = value.shape[0] // 2
         return value[:half] + self.send(value[half:].astype(BF), dc=1).astype(F32)
 
-    def gather(self, a, b):
-        parts = [(a, b)] + [(self.send(a, dz=k), self.send(b, dz=k)) for k in (1, 2, 3)]
-        za = jnp.stack([p[0] for p in parts])
-        zb = jnp.stack([p[1] for p in parts])
-        xa = jnp.concatenate([za, self.send(za, dx=1)])
-        ya = self.send(xa, dy=1)
-        yb = self.send(zb, dy=1)
-        xb = self.send(jnp.concatenate([zb, yb]), dx=1)
-        full_a = jnp.concatenate([xa, ya])
-        full_b = jnp.concatenate([zb, xb[:4], yb, xb[4:]])
-        flat = lambda f: f.reshape((f.shape[0] * f.shape[1],) + f.shape[2:])
-        return flat(full_a), flat(full_b)
-
     def reduce(self, a, b):
-        a = a.astype(BF).reshape(16, a.shape[0] // 16, a.shape[1])
-        b = b.astype(BF).reshape(16, b.shape[0] // 16, b.shape[1])
+        order = lambda w: w.astype(BF).reshape(4, 2, 2, -1, w.shape[1]).swapaxes(0, 2)
+        a, b = (order(w).reshape(16, -1, w.shape[1]) for w in (a, b))
         add = lambda u, w: (u.astype(F32) + w.astype(F32)).astype(BF)
         a = add(a[:8], self.send(a[8:], dy=1))
         b = add(
@@ -333,6 +611,7 @@
 def make_local(comm_type):
     def local(tokens, segments, w_qkv, w_out, w_in, w_down, g_attn, g_mlp, cotangent):
         comm = comm_type()
+        paired = comm_type is Chips
         shard = w_qkv.shape[0]
         cols = w_qkv.shape[2]
         units = w_in.shape[2]
@@ -345,27 +624,38 @@
         down_rows = w_down.T
         a_one = jnp.concatenate([scaled(w_qkv[:, 0], gain_one), scaled(w_qkv[:, 1], gain_one)], axis=1)
         b_one = jnp.concatenate([scaled(w_qkv[:, 2], gain_one), w_out.T], axis=1)
-        a_two = jnp.concatenate([padded(scaled(w_in[:, 0], gain_two)), down_rows[:, :low]], axis=1)
-        b_two = jnp.concatenate([padded(scaled(w_in[:, 1], gain_two)), down_rows[:, low:]], axis=1)
-        w_qk, w_vo = comm.gather(comm.swap(a_one), comm.swap(b_one))
-        w_gd, w_ud = comm.gather(comm.swap(a_two), comm.swap(b_two))
-        w_o = w_vo[:, cols:]
-        w_gate, w_up = w_gd[:, :units], w_ud[:, :units]
-        w_dn = jnp.concatenate([w_gd[:, units + pad :], w_ud[:, units + pad :]], axis=1)
-
-        x_in = comm.to_relative(comm.swap(tokens[0])).astype(F32)
+        own_gate, own_up = scaled(w_in[:, 0], gain_two), scaled(w_in[:, 1], gain_two)
+
         seg = comm.turn_rows(comm.swap(segments[0]))
         cot = comm.to_relative(comm.swap(cotangent[0]))
         cot_all = comm.gather_rows(cot)
-        tables = rope_tables(comm.positions(x_in.shape[0]))
+        tables = rope_tables(comm.positions(tokens.shape[1]))
         seg_col, seg_row = seg[:, None], seg[None, :]
-
-        xh_one, scale_one = normalize(x_in)
-        xh = comm.gather_rows(xh_one.astype(BF))
-        o, q, k, v, lse = attn_fwd(xh, w_qk, w_vo, tables, seg_col, seg_row)
-        resid = x_in + comm.scatter_rows(dotf(o, w_o, NT))
-        xh_two, scale_two = normalize(resid)
-        xn = comm.gather_rows(xh_two.astype(BF))
+        owned = (a_one, b_one, own_gate, own_up, down_rows)
+        if paired:
+            owned = [comm.swap(w) for w in owned]
+            x_half = comm.swap(tokens[0])
+            q, k, v, o, lse, xh, w_qk, w_vo, resid, xn, w_gate, w_up, w_dn = forward_block(
+                owned, x_half, tables, seg_col, seg_row
+            )
+            w_qk, w_vo, w_gate, w_up, w_dn = (
+                w.reshape(-1, w.shape[-1]) for w in (w_qk, w_vo, w_gate, w_up, w_dn)
+            )
+            xh_one, scale_one = normalize(comm.to_relative(x_half).astype(F32))
+            xh_two, scale_two = normalize(resid)
+            w_o = w_vo[:, cols:]
+        else:
+            w_qk, w_vo, w_gate, w_up, w_dn = (
+                lax.all_gather(w, "dp", axis=0, tiled=True) for w in owned
+            )
+            w_o = w_vo[:, cols:]
+            x_in = tokens[0].astype(F32)
+            xh_one, scale_one = normalize(x_in)
+            xh = comm.gather_rows(xh_one.astype(BF))
+            o, q, k, v, lse = attn_fwd(xh, w_qk, w_vo, tables, seg_col, seg_row)
+            resid = x_in + comm.scatter_rows(dotf(o, w_o, NT))
+            xh_two, scale_two = normalize(resid)
+            xn = comm.gather_rows(xh_two.astype(BF))
         gate, up = dotf(xn, w_gate, NN), dotf(xn, w_up, NN)
         act, slope = gelu_parts(gate)
         hidden = (act * up).astype(BF)

time: 634 us -> 473 us (0.75)
  waiting for transfers between devices: 195 us -> 52.7 us
  Pallas kernels: 68.4 us -> 162 us
  local copies, waits for them, and re-layouts: 108 us -> 58.7 us
  starting transfers between devices: 112 us -> 82 us
  other arithmetic: 66.7 us -> 48.5 us
  matrix products: 74.2 us -> 60.2 us
    ppermute x49 -> x26, waiting for transfers between devices: 195 us -> 52.7 us  [send(): return lax.ppermute(value, self.axes, pairs)]
    pallas_call x1, Pallas kernels: 33.8 us -> 128 us  [forward_block(): pl.pallas_call(forward_kernel, in_specs=[any_] * 5 + [vmem] * 6, out_spec...]
    ppermute x49 -> x26, starting transfers between devices: 90.3 us -> 53.3 us  [send(): return lax.ppermute(value, self.axes, pairs)]
    concatenate x8 -> x0, local copies, waits for them, and re-layouts: 14.8 us -> none  [the longest x2 4.5 us: gather(): full_a = jnp.concatenate([xa, ya])]
    slice x10 -> x0, local copies, waits for them, and re-layouts: 14.3 us -> none  [the longest x2 4.43 us: reduce(): b[4:8]]
    dot_general x18 -> x17, matrix products: 74.2 us -> 60.2 us  [dotf(): return lax.dot_general(a, b, (dims, ((), ())), preferred_element_type=F32)]
    concatenate x7 -> x0, other arithmetic: 9.24 us -> none  [the longest x1 3.54 us: local(): jnp.concatenate([d_q, d_k], axis=1)]
    unnamed x160 -> x95, local copies, waits for them, and re-layouts: 33 us -> 23.7 us
  transfers between devices with their start and end apart: 62 -> 40, of which waited for: 20 -> 8; matrix products, arithmetic and copies ran while one was open for 33% -> 26% of each run, Pallas kernels for 11% -> 35%
where the time goes in v2:
time: 473 us; the launch traced here: 467 us
  Pallas kernels  162 us (34%)
  starting transfers between devices  82 us (17%)
  matrix products  60.2 us (13%)
  local copies, waits for them, and re-layouts  58.7 us (12%)
  waiting for transfers between devices  52.7 us (11%)
  other arithmetic  48.5 us (10%)
    pallas_call x1, Pallas kernels, forward_block(): pl.pallas_call(forward_kernel, in_specs=[any_] * 5 + [vmem] * 6, out_spec...  128 us
    dot_general x17, matrix products, dotf(): return lax.dot_general(a, b, (dims, ((), ())), preferred_element_type=F32)  60.2 us
    ppermute x26, starting transfers between devices, send(): return lax.ppermute(value, self.axes, pairs)  53.3 us
    ppermute x26, waiting for transfers between devices, send(): return lax.ppermute(value, self.axes, pairs)  52.7 us
    pallas_call x1, Pallas kernels, attn_bwd(): pl.pallas_call(attn_bwd_kernel, grid=(pairs,), in_specs=[col] * 5 + [pl.B...  34.8 us
    ppermute x14, starting transfers between devices, swap(): return lax.ppermute(value, self.axes, pairs)  28.7 us
    unnamed x95, local copies, waits for them, and re-layouts  23.7 us
    convert_element_type x8, other arithmetic, reduce(): add = lambda u, w: (u.astype(F32) + w.astype(F32)).astype(BF)  11.6 us
  transfers between devices with their start and end apart: 40, of which 8 were waited for; matrix products, arithmetic and copies ran while one was open for 26% of the time, Pallas kernels for 35%

profile of v2, /device:TPU:0, one launch (start us, length us, event | category | flops | bytes accessed | tf_op | source)
XLA Modules:
  0.0 466.6 jit_solution(1945116852085624583)
XLA Ops:
  3.0 2.1 collective-permute-start
  6.7 2.2 collective-permute-start.1
  8.8 1.9 collective-permute-start.5
  12.0 2.3 copy.69
  14.3 1.9 collective-permute-start.9
  17.7 1.9 multiply_sine_fusion
  19.6 1.9 pad_maximum_fusion.11
  22.8 1.6 collective-permute-start.2
  25.4 1.6 collective-permute-start.3
  27.8 3.2 collective-permute-start.4
  33.1 2.3 copy.70
  35.6 1.6 fusion.11
  37.5 12.1 %collective-permute-start.10 = (bf16[512,1024]{0,1:T(8,128)(2,1)}, bf16[512,1024]{0,1:T(8,128)(2,1)}, u32[]{:S(2)}, u32[]{:S(2)}) collective-permute-start(bf16[512,1024]{0,1:T(8,128)(2,1)} %bitcast.19), channel_id=1, source_target_pairs={{0,2},{1,3},{2,0},{3,1},{4,6},{5,7},{6,4},{7,5},{8,10},{9,11},{10,... | collective-permute-start | bytes 3145736 | tf_op jit(solution)/shard_map/ppermute | solution.py:503
  50.3 127.5 %forward_block.1 = (bf16[1024,512]{1,0:T(8,128)(2,1)}, bf16[1024,512]{1,0:T(8,128)(2,1)}, bf16[1024,512]{1,0:T(8,128)(2,1)}, bf16[1024,512]{1,0:T(8,128)(2,1)}, ...) custom-call(bf16[64,1024]{1,0:T(8,128)(2,1)} %collective-permute-don, ...), custom_call_target="tpu_custom_call" | custom-call | tf_op jit(solution)/shard_map/forward_block/pallas_call | solution.py:453
  177.8 1.9 reduce_sum.90
  180.4 2.9 copy.78
  183.7 4.4 copy.80
  188.2 5.6 %fusion.64 = f32[1024,1312]{0,1:T(8,128)S(1)} fusion(bf16[1024,1024]{1,0:T(8,128)(2,1)} %get-tuple-element.22, bf16[1024,1312]{1,0:T(8,128)(2,1)} %bitcast.212), kind=kOutput, calls=%fused_computation.189 | convolution fusion | flops 2751463424 | bytes 10158080 | tf_op jit(solution)/shard_map/dot_general | solution.py:18
  193.8 6.3 %convolution_convert_fusion.3 = bf16[1024,1312]{0,1:T(8,128)(2,1)} fusion(bf16[1024,1312]{1,0:T(8,128)(2,1)S(1)} %bitcast.210, bf16[512,1024]{0,1:T(8,128)(2,1)} %collective-permute-done.10, bf16[512,1024]{0,1:T(8,128)(2,1)} %bitcast.19), kind=kOutput, calls=%fused_computation.21 | convolution fusion | flops 2757001216 | bytes 7471104 | tf_op jit(solution)/shard_map/dot_general | solution.py:18
  200.1 8.1 %fusion.1 = (bf16[1024,1312]{0,1:T(8,128)(2,1)S(1)}, bf16[1024,1312]{0,1:T(8,128)(2,1)S(1)}, bf16[1024,1312]{0,1:T(8,128)(2,1)S(1)}) fusion(bf16[1024,1312]{0,1:T(8,128)(2,1)} %convolution_convert_fusion.3, f32[1024,1312]{0,1:T(8,128)S(1)} %fusion.64, bf16[1024,1024]{1,0:T(8,128)(2,1)S(1)} %copy-done.38, bf16[1024,1312]{1,0:T(8,128)(2,1)S(1)} %bitcast.214), kind=kOutput, calls=%fused_computation.4 | convolution fusion | flops 2774302720 | bytes 20905984 | tf_op jit(solution)/shard_map/dot_general | solution.py:18
  208.3 3.5 fusion.66
  211.8 4.4 convolution_convert_fusion
  216.2 3.5 convolution_add_fusion
  221.0 3.5 fusion.65
  226.3 4.7 %convolution_convert_fusion.2 = bf16[1024,1312]{0,1:T(8,128)(2,1)S(1)} fusion(bf16[1024,1312]{0,1:T(8,128)(2,1)S(1)} %get-tuple-element.65, bf16[512,1024]{0,1:T(8,128)(2,1)} %collective-permute-done.10, bf16[512,1024]{0,1:T(8,128)(2,1)} %bitcast.19), kind=kOutput, calls=%fused_computation.20 | convolution fusion | flops 2757001216 | bytes 7471104 | tf_op jit(solution)/shard_map/dot_general | solution.py:18
  234.2 4.5 copy.105
  238.7 2.2 pad.10.clone
  242.0 1.8 fusion.59
  245.6 4.4 convolution_convert_fusion.1
  250.0 2.1 fusion.34
  252.8 3.9 fusion.58
  260.0 9.5 %collective-permute-start.8 = (bf16[512,1024]{0,1:T(8,128)(2,1)}, bf16[512,1024]{0,1:T(8,128)(2,1)}, u32[]{:S(2)}, u32[]{:S(2)}) collective-permute-start(bf16[512,1024]{0,1:T(8,128)(2,1)} %bitcast.15), channel_id=1, source_target_pairs={{0,0},{1,2},{2,1},{3,3},{4,4},{5,6},{6,5},{7,7},{8,8},{9,10},{10,9... | collective-permute-start | bytes 3145736 | tf_op jit(solution)/shard_map/ppermute | solution.py:513
  269.5 1.6 pad_maximum_fusion
  274.1 3.3 copy.104
  279.9 2.5 copy.86
  282.5 1.9 collective-permute-start.27
  284.4 2.3 copy.92
  286.7 4.1 convolution_convert_fusion.8.do
  290.7 34.8 %attn_bwd.1 = bf16[3,1024,512]{2,1,0:T(8,128)(2,1)} custom-call(bf16[1024,512]{1,0:T(8,128)(2,1)} %get-tuple-element.26.q, bf16[1024,512]{1,0:T(8,128)(2,1)} %get-tuple-element.27.k, bf16[1024,512]{1,0:T(8,128)(2,1)} %get-tuple-element.28.v, bf16[1024,512]{1,0:T(8,128)(2,1)} %get-tuple-element.29.o, bf16[1024,512]{1,0:T(8,128)(2,1)} %convolution_convert_fusion.8.do, ...), custom_call_target="tpu_custom_call" | custom-call | flops 10737418240 | bytes 10485760 | tf_op jit(solution)/shard_map/attn_bwd/pallas_call | solution.py:164
  325.6 3.0 fusion.15
  332.5 2.5 fusion.7
  338.5 2.8 convolution_convert_fusion.4
  351.1 2.2 add_convert_fusion
  354.4 1.8 collective-permute-start.34
  359.2 2.0 reverse_select_fusion.3
  363.1 1.6 add_convert_fusion.2
  364.8 2.8 collective-permute-start.31
  367.6 16.4 %collective-permute-done.21 = bf16[8,64,1024]{2,1,0:T(8,128)(2,1)} collective-permute-done((bf16[8,64,1024]{2,1,0:T(8,128)(2,1)}, bf16[8,64,1024]{2,1,0:T(8,128)(2,1)}, u32[]{:S(2)}, u32[]{:S(2)}) %collective-permute-start.21) | collective-permute-done | bytes 1048608 | tf_op jit(solution)/shard_map/ppermute | solution.py:503
  384.0 1.6 add_convert_fusion.3
  385.7 3.4 collective-permute-start.29
  389.1 1.7 fusion.10
  390.8 8.6 %collective-permute-done.34 = bf16[4,64,2080]{2,1,0:T(8,128)(2,1)} collective-permute-done((bf16[4,64,2080]{2,1,0:T(8,128)(2,1)}, bf16[4,64,2080]{2,1,0:T(8,128)(2,1)}, u32[]{:S(2)}, u32[]{:S(2)}) %collective-permute-start.34) | collective-permute-done | bytes 1064992 | tf_op jit(solution)/shard_map/ppermute | solution.py:503
  399.4 1.9 collective-permute-start.22
  402.9 3.3 collective-permute-start.37
  407.5 6.8 %collective-permute-done.37 = bf16[64,2080]{1,0:T(8,128)(2,1)S(1)} collective-permute-done((bf16[64,2080]{1,0:T(8,128)(2,1)S(1)}, bf16[64,2080]{1,0:T(8,128)(2,1)S(1)}, u32[]{:S(2)}, u32[]{:S(2)}) %collective-permute-start.37) | collective-permute-done | bytes 266272 | tf_op jit(solution)/shard_map/ppermute | solution.py:503
  415.6 10.3 %collective-permute-done.36 = bf16[64,2080]{1,0:T(8,128)(2,1)S(1)} collective-permute-done((bf16[64,2080]{1,0:T(8,128)(2,1)S(1)}, bf16[64,2080]{1,0:T(8,128)(2,1)S(1)}, u32[]{:S(2)}, u32[]{:S(2)}) %collective-permute-start.36) | collective-permute-done | bytes 266272 | tf_op jit(solution)/shard_map/ppermute | solution.py:503
  427.7 2.2 collective-permute-start.25
  430.2 1.7 collective-permute-start.19
  431.9 2.0 collective-permute-start.18
  435.1 2.8 collective-permute-done.19
  437.9 8.3 %collective-permute-start.24 = (bf16[64,1024]{1,0:T(8,128)(2,1)S(1)}, bf16[64,1024]{1,0:T(8,128)(2,1)S(1)}, u32[]{:S(2)}, u32[]{:S(2)}) collective-permute-start(bf16[64,1024]{1,0:T(8,128)(2,1)S(1)} %get-tuple-element.93), channel_id=1, source_target_pairs={{0,16},{1,17},{2,18},{3,19},{4,20},{5,21},{6,22},{7,23},{8,24},{9,... | collective-permute-start | bytes 393224 | tf_op jit(solution)/shard_map/ppermute | solution.py:503
  448.6 4.8 %collective-permute-done.24 = bf16[64,1024]{1,0:T(8,128)(2,1)S(1)} collective-permute-done((bf16[64,1024]{1,0:T(8,128)(2,1)S(1)}, bf16[64,1024]{1,0:T(8,128)(2,1)S(1)}, u32[]{:S(2)}, u32[]{:S(2)}) %collective-permute-start.24) | collective-permute-done | bytes 131104 | tf_op jit(solution)/shard_map/ppermute | solution.py:503
  457.3 4.2 collective-permute-start.39
  464.6 1.8 copy.93
  (246 shorter events, 72.3 us)
Async XLA Ops:
  0.6 15.6 %copy-start.22 = (bf16[64,2,1312]{2,1,0:T(2,128)(2,1)S(1)}, bf16[64,2,1312]{2,1,0:T(2,128)(2,1)}, u32[]{:S(2)}) copy-start(bf16[64,2,1312]{2,1,0:T(2,128)(2,1)} %param.13) | copy-start | bytes 1007620
  0.6 15.6 %copy-start.41 = (bf16[64]{0:T(256)(128)(2,1)S(1)}, bf16[64]{0:T(256)(128)(2,1)}, u32[]{:S(2)}) copy-start(bf16[64]{0:T(256)(128)(2,1)} %param.16) | copy-start | bytes 388
  1.4 9.3 %copy-start.30 = (f32[64]{0:T(128)}, f32[64]{0:T(128)S(1)}, u32[]{:S(2)}) copy-start(f32[64]{0:T(128)S(1)} %convert_element_type.299) | copy-start | bytes 772
  3.0 34.5 %collective-permute-start = (bf16[64,1024]{1,0:T(8,128)(2,1)}, bf16[64,1024]{1,0:T(8,128)(2,1)}, u32[]{:S(2)}, u32[]{:S(2)}) collective-permute-start(bf16[64,1024]{1,0:T(8,128)(2,1)} %pad_maximum_fusion.13), channel_id=1, source_target_pairs={{0,0},{1,2},{2,1},{3,3},{4,4},{5,6},{6,5},{7,7},{8,8},{9,10},{10,9... | collective-permute-start | bytes 393224 | tf_op jit(solution)/shard_map/ppermute | solution.py:513
  6.7 42.9 %collective-permute-start.1 = (bf16[64,1024]{1,0:T(8,128)(2,1)}, bf16[64,1024]{1,0:T(8,128)(2,1)}, u32[]{:S(2)}, u32[]{:S(2)}) collective-permute-start(bf16[64,1024]{1,0:T(8,128)(2,1)} %pad_maximum_fusion.14), channel_id=1, source_target_pairs={{0,0},{1,2},{2,1},{3,3},{4,4},{5,6},{6,5},{7,7},{8,8},{9,10},{10,9... | collective-permute-start | bytes 393224 | tf_op jit(solution)/shard_map/ppermute | solution.py:513
  8.8 16.6 %collective-permute-start.5 = (bf16[512,1024]{1,0:T(8,128)(2,1)}, bf16[512,1024]{1,0:T(8,128)(2,1)S(1)}, u32[]{:S(2)}, u32[]{:S(2)}) collective-permute-start(bf16[512,1024]{1,0:T(8,128)(2,1)} %bitcast.218), channel_id=1, source_target_pairs={{0,0},{1,2},{2,1},{3,3},{4,4},{5,6},{6,5},{7,7},{8,8},{9,10},{10,9... | collective-permute-start | bytes 3145736 | tf_op jit(solution)/shard_map/ppermute | solution.py:513
  10.7 12.0 %collective-permute-start.6 = (s32[1024]{0:T(1024)}, s32[1024]{0:T(1024)S(1)}, u32[]{:S(2)}, u32[]{:S(2)}) collective-permute-start(s32[1024]{0:T(1024)} %bitcast.220), channel_id=1, source_target_pairs={{0,0},{1,2},{2,1},{3,3},{4,4},{5,6},{6,5},{7,7},{8,8},{9,10},{10,9... | collective-permute-start | bytes 12296 | tf_op jit(solution)/shard_map/ppermute | solution.py:513
  14.3 13.4 %collective-permute-start.9 = (bf16[512,1024]{0,1:T(8,128)(2,1)}, bf16[512,1024]{0,1:T(8,128)(2,1)S(1)}, u32[]{:S(2)}, u32[]{:S(2)}) collective-permute-start(bf16[512,1024]{0,1:T(8,128)(2,1)} %bitcast.198), channel_id=1, source_target_pairs={{0,0},{1,2},{2,1},{3,3},{4,4},{5,6},{6,5},{7,7},{8,8},{9,10},{10,9... | collective-permute-start | bytes 3145736 | tf_op jit(solution)/shard_map/ppermute | solution.py:513
  22.8 26.8 %collective-permute-start.2 = (bf16[64,1312]{1,0:T(8,128)(2,1)}, bf16[64,1312]{1,0:T(8,128)(2,1)S(1)}, u32[]{:S(2)}, u32[]{:S(2)}) collective-permute-start(bf16[64,1312]{1,0:T(8,128)(2,1)} %get-tuple-element.99), channel_id=1, source_target_pairs={{0,0},{1,2},{2,1},{3,3},{4,4},{5,6},{6,5},{7,7},{8,8},{9,10},{10,9... | collective-permute-start | bytes 503816 | tf_op jit(solution)/shard_map/ppermute | solution.py:513
  24.3 3.4 copy-start.29
  25.4 5.8 %copy-start.15 = (bf16[512,1024]{1,0:T(8,128)(2,1)}, bf16[512,1024]{1,0:T(8,128)(2,1)S(1)}, u32[]{:S(2)}) copy-start(bf16[512,1024]{1,0:T(8,128)(2,1)S(1)} %collective-permute-done.5.x_half) | copy-start | bytes 3145732
  25.4 24.2 %collective-permute-start.3 = (bf16[64,1312]{1,0:T(8,128)(2,1)}, bf16[64,1312]{1,0:T(8,128)(2,1)S(1)}, u32[]{:S(2)}, u32[]{:S(2)}) collective-permute-start(bf16[64,1312]{1,0:T(8,128)(2,1)} %get-tuple-element.98), channel_id=1, source_target_pairs={{0,0},{1,2},{2,1},{3,3},{4,4},{5,6},{6,5},{7,7},{8,8},{9,10},{10,9... | collective-permute-start | bytes 503816 | tf_op jit(solution)/shard_map/ppermute | solution.py:513
  27.8 21.8 %collective-permute-start.4 = (bf16[64,1312]{1,0:T(8,128)(2,1)}, bf16[64,1312]{1,0:T(8,128)(2,1)}, u32[]{:S(2)}, u32[]{:S(2)}) collective-permute-start(bf16[64,1312]{1,0:T(8,128)(2,1)} %bitcast.219), channel_id=1, source_target_pairs={{0,0},{1,2},{2,1},{3,3},{4,4},{5,6},{6,5},{7,7},{8,8},{9,10},{10,9... | collective-permute-start | bytes 503816 | tf_op jit(solution)/shard_map/ppermute | solution.py:513
  37.5 156.3 %collective-permute-start.10 = (bf16[512,1024]{0,1:T(8,128)(2,1)}, bf16[512,1024]{0,1:T(8,128)(2,1)}, u32[]{:S(2)}, u32[]{:S(2)}) collective-permute-start(bf16[512,1024]{0,1:T(8,128)(2,1)} %bitcast.19), channel_id=1, source_target_pairs={{0,2},{1,3},{2,0},{3,1},{4,6},{5,7},{6,4},{7,5},{8,10},{9,11},{10,... | collective-permute-start | bytes 3145736 | tf_op jit(solution)/shard_map/ppermute | solution.py:503
  188.2 5.6 %copy-start.34 = (bf16[4,2,2,64,1312]{4,3,2,1,0:T(8,128)(2,1)S(1)}, bf16[4,2,2,64,1312]{4,3,2,1,0:T(8,128)(2,1)}, u32[]{:S(2)}) copy-start(bf16[4,2,2,64,1312]{4,3,2,1,0:T(8,128)(2,1)} %get-tuple-element.25) | copy-start | bytes 8060932
  193.8 6.3 %copy-start.36 = (bf16[4,2,2,64,1312]{4,3,2,1,0:T(8,128)(2,1)S(1)}, bf16[4,2,2,64,1312]{4,3,2,1,0:T(8,128)(2,1)}, u32[]{:S(2)}) copy-start(bf16[4,2,2,64,1312]{4,3,2,1,0:T(8,128)(2,1)} %get-tuple-element.24) | copy-start | bytes 8060932
  193.8 6.3 %copy-start.38 = (bf16[1024,1024]{1,0:T(8,128)(2,1)S(1)}, bf16[1024,1024]{1,0:T(8,128)(2,1)}, u32[]{:S(2)}) copy-start(bf16[1024,1024]{1,0:T(8,128)(2,1)} %get-tuple-element.22) | copy-start | bytes 6291460
  208.3 7.9 %copy-start.42 = (bf16[1024,1312]{0,1:T(8,128)(2,1)}, bf16[1024,1312]{0,1:T(8,128)(2,1)S(1)}, u32[]{:S(2)}) copy-start(bf16[1024,1312]{0,1:T(8,128)(2,1)S(1)} %get-tuple-element.64) | copy-start | bytes 8060932
  211.7 4.4 copy-start.35
  219.7 4.8 %copy-start.7 = (f32[1024,1024]{1,0:T(8,128)}, f32[1024,1024]{1,0:T(8,128)S(1)}, u32[]{:S(2)}) copy-start(f32[1024,1024]{1,0:T(8,128)S(1)} %convolution_add_fusion) | copy-start | bytes 12582916
  221.0 28.9 %collective-permute-start.11 = (bf16[512,1024]{1,0:T(8,128)(2,1)}, bf16[512,1024]{1,0:T(8,128)(2,1)}, u32[]{:S(2)}, u32[]{:S(2)}) collective-permute-start(bf16[512,1024]{1,0:T(8,128)(2,1)} %slice.453), channel_id=1, source_target_pairs={{0,2},{1,3},{2,0},{3,1},{4,6},{5,7},{6,4},{7,5},{8,10},{9,11},{10,... | collective-permute-start | bytes 3145736 | tf_op jit(solution)/shard_map/ppermute | solution.py:503
  224.5 6.5 %copy-start.17 = (f32[1024,1024]{1,0:T(8,128)}, f32[1024,1024]{1,0:T(8,128)S(1)}, u32[]{:S(2)}) copy-start(f32[1024,1024]{1,0:T(8,128)S(1)} %fusion.65) | copy-start | bytes 12582916
  225.8 26.3 %collective-permute-start.7 = (bf16[512,1024]{1,0:T(8,128)(2,1)}, bf16[512,1024]{1,0:T(8,128)(2,1)}, u32[]{:S(2)}, u32[]{:S(2)}) collective-permute-start(bf16[512,1024]{1,0:T(8,128)(2,1)} %slice.454), channel_id=1, source_target_pairs={{0,2},{1,3},{2,0},{3,1},{4,6},{5,7},{6,4},{7,5},{8,10},{9,11},{10,... | collective-permute-start | bytes 3145736 | tf_op jit(solution)/shard_map/ppermute | solution.py:503
  242.0 3.6 copy-start.43
  245.6 4.4 copy-start.8
  258.6 10.9 %copy-start.14 = (bf16[4,64,2080]{2,1,0:T(8,128)(2,1)S(1)}, bf16[4,64,2080]{2,1,0:T(8,128)(2,1)}, u32[]{:S(2)}) copy-start(bf16[4,64,2080]{2,1,0:T(8,128)(2,1)} %get-tuple-element.69) | copy-start | bytes 3194884
  260.0 24.4 %collective-permute-start.8 = (bf16[512,1024]{0,1:T(8,128)(2,1)}, bf16[512,1024]{0,1:T(8,128)(2,1)}, u32[]{:S(2)}, u32[]{:S(2)}) collective-permute-start(bf16[512,1024]{0,1:T(8,128)(2,1)} %bitcast.15), channel_id=1, source_target_pairs={{0,0},{1,2},{2,1},{3,3},{4,4},{5,6},{6,5},{7,7},{8,8},{9,10},{10,9... | collective-permute-start | bytes 3145736 | tf_op jit(solution)/shard_map/ppermute | solution.py:513
  269.5 17.2 %collective-permute-start.12 = (bf16[512,1024]{1,0:T(8,128)(2,1)}, bf16[512,1024]{1,0:T(8,128)(2,1)}, u32[]{:S(2)}, u32[]{:S(2)}) collective-permute-start(bf16[512,1024]{1,0:T(8,128)(2,1)} %get-tuple-element.62), channel_id=1, source_target_pairs={{0,2},{1,3},{2,0},{3,1},{4,6},{5,7},{6,4},{7,5},{8,10},{9,11},{10,... | collective-permute-start | bytes 3145736 | tf_op jit(solution)/shard_map/ppermute | solution.py:503
  271.1 80.0 %collective-permute-start.33 = (bf16[8,64,2080]{2,1,0:T(8,128)(2,1)}, bf16[8,64,2080]{2,1,0:T(8,128)(2,1)}, u32[]{:S(2)}, u32[]{:S(2)}) collective-permute-start(bf16[8,64,2080]{2,1,0:T(8,128)(2,1)} %pad_maximum_fusion), channel_id=1, source_target_pairs={{0,4},{1,5},{2,6},{3,7},{4,0},{5,1},{6,2},{7,3},{8,12},{9,13},{10,... | collective-permute-start | bytes 6389768 | tf_op jit(solution)/shard_map/ppermute | solution.py:503
  282.5 49.3 %collective-permute-start.27 = (bf16[8,64,2048]{2,1,0:T(8,128)(2,1)S(1)}, bf16[8,64,2048]{2,1,0:T(8,128)(2,1)}, u32[]{:S(2)}, u32[]{:S(2)}) collective-permute-start(bf16[8,64,2048]{2,1,0:T(8,128)(2,1)S(1)} %bitcast.194), channel_id=1, source_target_pairs={{0,1},{1,0},{2,3},{3,2},{4,5},{5,4},{6,7},{7,6},{8,9},{9,8},{10,11... | collective-permute-start | bytes 6291464 | tf_op jit(solution)/shard_map/ppermute | solution.py:503
  331.8 5.5 %copy-start.19 = (bf16[1024,1024]{1,0:T(8,128)(2,1)S(1)}, bf16[1024,1024]{1,0:T(8,128)(2,1)}, u32[]{:S(2)}) copy-start(bf16[1024,1024]{1,0:T(8,128)(2,1)} %copy.80) | copy-start | bytes 6291460
  331.8 24.4 %collective-permute-start.13 = (bf16[512,1024]{1,0:T(8,128)(2,1)S(1)}, bf16[512,1024]{1,0:T(8,128)(2,1)S(1)}, u32[]{:S(2)}, u32[]{:S(2)}) collective-permute-start(bf16[512,1024]{1,0:T(8,128)(2,1)S(1)} %slice.452), channel_id=1, source_target_pairs={{0,2},{1,3},{2,0},{3,1},{4,6},{5,7},{6,4},{7,5},{8,10},{9,11},{10,... | collective-permute-start | bytes 3145736 | tf_op jit(solution)/shard_map/ppermute | solution.py:503
  335.1 3.4 copy-start.4
  336.3 26.6 %collective-permute-start.28 = (bf16[4,64,2048]{2,1,0:T(8,128)(2,1)}, bf16[4,64,2048]{2,1,0:T(8,128)(2,1)}, u32[]{:S(2)}, u32[]{:S(2)}) collective-permute-start(bf16[4,64,2048]{2,1,0:T(8,128)(2,1)} %slice.330), channel_id=1, source_target_pairs={{0,4},{1,5},{2,6},{3,7},{4,0},{5,1},{6,2},{7,3},{8,12},{9,13},{10,... | collective-permute-start | bytes 3145736 | tf_op jit(solution)/shard_map/ppermute | solution.py:503
  344.1 39.9 %collective-permute-start.21 = (bf16[8,64,1024]{2,1,0:T(8,128)(2,1)}, bf16[8,64,1024]{2,1,0:T(8,128)(2,1)}, u32[]{:S(2)}, u32[]{:S(2)}) collective-permute-start(bf16[8,64,1024]{2,1,0:T(8,128)(2,1)} %pad_maximum_fusion.7), channel_id=1, source_target_pairs={{0,4},{1,5},{2,6},{3,7},{4,0},{5,1},{6,2},{7,3},{8,12},{9,13},{10,... | collective-permute-start | bytes 3145736 | tf_op jit(solution)/shard_map/ppermute | solution.py:503
  350.8 34.8 %collective-permute-start.15 = (bf16[8,64,1024]{2,1,0:T(8,128)(2,1)}, bf16[8,64,1024]{2,1,0:T(8,128)(2,1)}, u32[]{:S(2)}, u32[]{:S(2)}) collective-permute-start(bf16[8,64,1024]{2,1,0:T(8,128)(2,1)} %bitcast.38), channel_id=1, source_target_pairs={{0,1},{1,0},{2,3},{3,2},{4,5},{5,4},{6,7},{7,6},{8,9},{9,8},{10,11... | collective-permute-start | bytes 3145736 | tf_op jit(solution)/shard_map/ppermute | solution.py:503
  354.4 45.0 %collective-permute-start.34 = (bf16[4,64,2080]{2,1,0:T(8,128)(2,1)}, bf16[4,64,2080]{2,1,0:T(8,128)(2,1)}, u32[]{:S(2)}, u32[]{:S(2)}) collective-permute-start(bf16[4,64,2080]{2,1,0:T(8,128)(2,1)} %slice.342), channel_id=1, source_target_pairs={{0,1},{1,0},{2,3},{3,2},{4,5},{5,4},{6,7},{7,6},{8,9},{9,8},{10,11... | collective-permute-start | bytes 3194888 | tf_op jit(solution)/shard_map/ppermute | solution.py:503
  362.0 22.0 %copy-start.20 = (bf16[4,64,1024]{2,1,0:T(8,128)(2,1)S(1)}, bf16[4,64,1024]{2,1,0:T(8,128)(2,1)}, u32[]{:S(2)}) copy-start(bf16[4,64,1024]{2,1,0:T(8,128)(2,1)} %get-tuple-element.75) | copy-start | bytes 1572868
  362.0 22.0 %copy-start.21 = (bf16[4,64,1024]{2,1,0:T(8,128)(2,1)S(1)}, bf16[4,64,1024]{2,1,0:T(8,128)(2,1)}, u32[]{:S(2)}) copy-start(bf16[4,64,1024]{2,1,0:T(8,128)(2,1)} %get-tuple-element.78) | copy-start | bytes 1572868
  362.0 102.3 %collective-permute-start.14 = (bf16[512,1024]{0,1:T(8,128)(2,1)S(1)}, bf16[512,1024]{0,1:T(8,128)(2,1)S(1)}, u32[]{:S(2)}, u32[]{:S(2)}) collective-permute-start(bf16[512,1024]{0,1:T(8,128)(2,1)S(1)} %bitcast.196), channel_id=1, source_target_pairs={{0,0},{1,2},{2,1},{3,3},{4,4},{5,6},{6,5},{7,7},{8,8},{9,10},{10,9... | collective-permute-start | bytes 3145736 | tf_op jit(solution)/shard_map/ppermute | solution.py:513
  364.8 24.3 %copy-start.6 = (f32[1,2,4,64,1024]{4,3,2,1,0:T(8,128)S(1)}, f32[1,2,4,64,1024]{4,3,2,1,0:T(8,128)}, u32[]{:S(2)}) copy-start(f32[1,2,4,64,1024]{4,3,2,1,0:T(8,128)} %copy.81) | copy-start | bytes 6291460
  364.8 38.1 %collective-permute-start.31 = (bf16[64,2048]{1,0:T(8,128)(2,1)S(1)}, bf16[64,2048]{1,0:T(8,128)(2,1)S(1)}, u32[]{:S(2)}, u32[]{:S(2)}) collective-permute-start(bf16[64,2048]{1,0:T(8,128)(2,1)S(1)} %get-tuple-element.84), channel_id=1, source_target_pairs={{0,24},{1,25},{2,26},{3,27},{4,28},{5,29},{6,30},{7,31},{8,16},{9,... | collective-permute-start | bytes 786440 | tf_op jit(solution)/shard_map/ppermute | solution.py:503
  384.0 22.3 %collective-permute-start.30 = (bf16[64,2048]{1,0:T(8,128)(2,1)S(1)}, bf16[64,2048]{1,0:T(8,128)(2,1)S(1)}, u32[]{:S(2)}, u32[]{:S(2)}) collective-permute-start(bf16[64,2048]{1,0:T(8,128)(2,1)S(1)} %get-tuple-element.85), channel_id=1, source_target_pairs={{0,16},{1,17},{2,18},{3,19},{4,20},{5,21},{6,22},{7,23},{8,24},{9,... | collective-permute-start | bytes 786440 | tf_op jit(solution)/shard_map/ppermute | solution.py:503
  385.7 20.6 %collective-permute-start.29 = (bf16[64,2048]{1,0:T(8,128)(2,1)S(1)}, bf16[64,2048]{1,0:T(8,128)(2,1)S(1)}, u32[]{:S(2)}, u32[]{:S(2)}) collective-permute-start(bf16[64,2048]{1,0:T(8,128)(2,1)S(1)} %get-tuple-element.83), channel_id=1, source_target_pairs={{0,8},{1,9},{2,10},{3,11},{4,12},{5,13},{6,14},{7,15},{8,0},{9,1},... | collective-permute-start | bytes 786440 | tf_op jit(solution)/shard_map/ppermute | solution.py:503
  399.4 28.0 %collective-permute-start.22 = (bf16[4,64,1024]{2,1,0:T(8,128)(2,1)S(1)}, bf16[4,64,1024]{2,1,0:T(8,128)(2,1)S(1)}, u32[]{:S(2)}, u32[]{:S(2)}) collective-permute-start(bf16[4,64,1024]{2,1,0:T(8,128)(2,1)S(1)} %slice.320), channel_id=1, source_target_pairs={{0,1},{1,0},{2,3},{3,2},{4,5},{5,4},{6,7},{7,6},{8,9},{9,8},{10,11... | collective-permute-start | bytes 1572872 | tf_op jit(solution)/shard_map/ppermute | solution.py:503
  402.9 11.4 %collective-permute-start.37 = (bf16[64,2080]{1,0:T(8,128)(2,1)S(1)}, bf16[64,2080]{1,0:T(8,128)(2,1)S(1)}, u32[]{:S(2)}, u32[]{:S(2)}) collective-permute-start(bf16[64,2080]{1,0:T(8,128)(2,1)S(1)} %get-tuple-element.81), channel_id=1, source_target_pairs={{0,24},{1,25},{2,26},{3,27},{4,28},{5,29},{6,30},{7,31},{8,16},{9,... | collective-permute-start | bytes 798728 | tf_op jit(solution)/shard_map/ppermute | solution.py:503
  406.2 19.6 %collective-permute-start.36 = (bf16[64,2080]{1,0:T(8,128)(2,1)S(1)}, bf16[64,2080]{1,0:T(8,128)(2,1)S(1)}, u32[]{:S(2)}, u32[]{:S(2)}) collective-permute-start(bf16[64,2080]{1,0:T(8,128)(2,1)S(1)} %get-tuple-element.82), channel_id=1, source_target_pairs={{0,16},{1,17},{2,18},{3,19},{4,20},{5,21},{6,22},{7,23},{8,24},{9,... | collective-permute-start | bytes 798728 | tf_op jit(solution)/shard_map/ppermute | solution.py:503
  406.3 20.3 %collective-permute-start.35 = (bf16[64,2080]{1,0:T(8,128)(2,1)S(1)}, bf16[64,2080]{1,0:T(8,128)(2,1)S(1)}, u32[]{:S(2)}, u32[]{:S(2)}) collective-permute-start(bf16[64,2080]{1,0:T(8,128)(2,1)S(1)} %get-tuple-element.80), channel_id=1, source_target_pairs={{0,8},{1,9},{2,10},{3,11},{4,12},{5,13},{6,14},{7,15},{8,0},{9,1},... | collective-permute-start | bytes 798728 | tf_op jit(solution)/shard_map/ppermute | solution.py:503
  414.3 15.6 %collective-permute-start.16 = (bf16[4,64,1024]{2,1,0:T(8,128)(2,1)S(1)}, bf16[4,64,1024]{2,1,0:T(8,128)(2,1)S(1)}, u32[]{:S(2)}, u32[]{:S(2)}) collective-permute-start(bf16[4,64,1024]{2,1,0:T(8,128)(2,1)S(1)} %slice.308), channel_id=1, source_target_pairs={{0,4},{1,5},{2,6},{3,7},{4,0},{5,1},{6,2},{7,3},{8,12},{9,13},{10,... | collective-permute-start | bytes 1572872 | tf_op jit(solution)/shard_map/ppermute | solution.py:503
  425.9 6.0 %collective-permute-start.32 = (bf16[64,2048]{1,0:T(8,128)(2,1)S(1)}, bf16[64,2048]{1,0:T(8,128)(2,1)S(1)}, u32[]{:S(2)}, u32[]{:S(2)}) collective-permute-start(bf16[64,2048]{1,0:T(8,128)(2,1)S(1)} %fusion.39), channel_id=1, source_target_pairs={{0,0},{1,2},{2,1},{3,3},{4,4},{5,6},{6,5},{7,7},{8,8},{9,10},{10,9... | collective-permute-start | bytes 786440 | tf_op jit(solution)/shard_map/ppermute | solution.py:513
  426.7 7.3 %collective-permute-start.38 = (bf16[64,2080]{1,0:T(8,128)(2,1)S(1)}, bf16[64,2080]{1,0:T(8,128)(2,1)S(1)}, u32[]{:S(2)}, u32[]{:S(2)}) collective-permute-start(bf16[64,2080]{1,0:T(8,128)(2,1)S(1)} %fusion.33), channel_id=1, source_target_pairs={{0,0},{1,2},{2,1},{3,3},{4,4},{5,6},{6,5},{7,7},{8,8},{9,10},{10,9... | collective-permute-start | bytes 798728 | tf_op jit(solution)/shard_map/ppermute | solution.py:513
  427.7 20.9 %collective-permute-start.25 = (bf16[64,1024]{1,0:T(8,128)(2,1)S(1)}, bf16[64,1024]{1,0:T(8,128)(2,1)S(1)}, u32[]{:S(2)}, u32[]{:S(2)}) collective-permute-start(bf16[64,1024]{1,0:T(8,128)(2,1)S(1)} %get-tuple-element.92), channel_id=1, source_target_pairs={{0,24},{1,25},{2,26},{3,27},{4,28},{5,29},{6,30},{7,31},{8,16},{9,... | collective-permute-start | bytes 393224 | tf_op jit(solution)/shard_map/ppermute | solution.py:503
  430.1 4.8 %copy-start.23 = (bf16[64,2,1312]{2,1,0:T(2,128)(2,1)S(1)}, bf16[64,2,1312]{2,1,0:T(2,128)(2,1)}, u32[]{:S(2)}) copy-start(bf16[64,2,1312]{2,1,0:T(2,128)(2,1)} %param.13) | copy-start | bytes 1007620
  430.1 4.8 %copy-start.33 = (f32[64]{0:T(128)S(1)}, f32[64]{0:T(128)}, u32[]{:S(2)}) copy-start(f32[64]{0:T(128)} %copy-done.32) | copy-start | bytes 772
  430.2 7.8 %collective-permute-start.19 = (bf16[64,1024]{1,0:T(8,128)(2,1)S(1)}, bf16[64,1024]{1,0:T(8,128)(2,1)S(1)}, u32[]{:S(2)}, u32[]{:S(2)}) collective-permute-start(bf16[64,1024]{1,0:T(8,128)(2,1)S(1)} %get-tuple-element.89), channel_id=1, source_target_pairs={{0,24},{1,25},{2,26},{3,27},{4,28},{5,29},{6,30},{7,31},{8,16},{9,... | collective-permute-start | bytes 393224 | tf_op jit(solution)/shard_map/ppermute | solution.py:503
  431.9 15.9 %collective-permute-start.18 = (bf16[64,1024]{1,0:T(8,128)(2,1)S(1)}, bf16[64,1024]{1,0:T(8,128)(2,1)S(1)}, u32[]{:S(2)}, u32[]{:S(2)}) collective-permute-start(bf16[64,1024]{1,0:T(8,128)(2,1)S(1)} %get-tuple-element.90), channel_id=1, source_target_pairs={{0,16},{1,17},{2,18},{3,19},{4,20},{5,21},{6,22},{7,23},{8,24},{9,... | collective-permute-start | bytes 393224 | tf_op jit(solution)/shard_map/ppermute | solution.py:503
  434.0 13.8 %collective-permute-start.17 = (bf16[64,1024]{1,0:T(8,128)(2,1)S(1)}, bf16[64,1024]{1,0:T(8,128)(2,1)S(1)}, u32[]{:S(2)}, u32[]{:S(2)}) collective-permute-start(bf16[64,1024]{1,0:T(8,128)(2,1)S(1)} %get-tuple-element.88), channel_id=1, source_target_pairs={{0,8},{1,9},{2,10},{3,11},{4,12},{5,13},{6,14},{7,15},{8,0},{9,1},... | collective-permute-start | bytes 393224 | tf_op jit(solution)/shard_map/ppermute | solution.py:503
  434.9 21.5 %copy-start.24 = (bf16[64,3,512]{2,0,1:T(8,128)(2,1)S(1)}, bf16[64,3,512]{2,0,1:T(8,128)(2,1)}, u32[]{:S(2)}) copy-start(bf16[64,3,512]{2,0,1:T(8,128)(2,1)} %param.11) | copy-start | bytes 589828
  434.9 21.4 %copy-start.31 = (f32[64]{0:T(128)S(1)}, f32[64]{0:T(128)}, u32[]{:S(2)}) copy-start(f32[64]{0:T(128)} %copy-done.30) | copy-start | bytes 772
  437.9 15.4 %collective-permute-start.24 = (bf16[64,1024]{1,0:T(8,128)(2,1)S(1)}, bf16[64,1024]{1,0:T(8,128)(2,1)S(1)}, u32[]{:S(2)}, u32[]{:S(2)}) collective-permute-start(bf16[64,1024]{1,0:T(8,128)(2,1)S(1)} %get-tuple-element.93), channel_id=1, source_target_pairs={{0,16},{1,17},{2,18},{3,19},{4,20},{5,21},{6,22},{7,23},{8,24},{9,... | collective-permute-start | bytes 393224 | tf_op jit(solution)/shard_map/ppermute | solution.py:503
  447.8 7.0 %collective-permute-start.23 = (bf16[64,1024]{1,0:T(8,128)(2,1)S(1)}, bf16[64,1024]{1,0:T(8,128)(2,1)S(1)}, u32[]{:S(2)}, u32[]{:S(2)}) collective-permute-start(bf16[64,1024]{1,0:T(8,128)(2,1)S(1)} %get-tuple-element.91), channel_id=1, source_target_pairs={{0,8},{1,9},{2,10},{3,11},{4,12},{5,13},{6,14},{7,15},{8,0},{9,1},... | collective-permute-start | bytes 393224 | tf_op jit(solution)/shard_map/ppermute | solution.py:503
  447.9 7.7 %collective-permute-start.20 = (bf16[64,1024]{1,0:T(8,128)(2,1)S(1)}, bf16[64,1024]{1,0:T(8,128)(2,1)S(1)}, u32[]{:S(2)}, u32[]{:S(2)}) collective-permute-start(bf16[64,1024]{1,0:T(8,128)(2,1)S(1)} %fusion.48), channel_id=1, source_target_pairs={{0,0},{1,2},{2,1},{3,3},{4,4},{5,6},{6,5},{7,7},{8,8},{9,10},{10,9... | collective-permute-start | bytes 393224 | tf_op jit(solution)/shard_map/ppermute | solution.py:513
  454.9 0.7 collective-permute-start.26
  457.3 6.4 %collective-permute-start.39 = (f32[2,64]{1,0:T(2,128)S(1)}, f32[2,64]{1,0:T(2,128)S(1)}, u32[]{:S(2)}, u32[]{:S(2)}) collective-permute-start(f32[2,64]{1,0:T(2,128)S(1)} %pad_maximum_fusion.15), channel_id=1, source_target_pairs={{0,1},{1,0},{2,3},{3,2},{4,5},{5,4},{6,7},{7,6},{8,9},{9,8},{10,11... | collective-permute-start | bytes 1544 | tf_op jit(solution)/shard_map/ppermute | solution.py:503
  (21 other events, 42.3 us)

commit v3 on v2

--- a/solution.py
+++ b/solution.py
@@ -481,6 +481,113 @@
     )(*owned, x_half, *tables, seg_col, seg_row)
 
 
+def in_chunks(total, size, body):
+    def step(j, carry):
+        body(pl.ds(pl.multiple_of(j * size, size), size))
+        return carry
+
+    lax.fori_loop(0, total // size, step, 0)
+    if total % size:
+        body(pl.ds(total - total % size, total % size))
+
+
+def mlp_kernel(
+    xn, cot, w_gate, w_up, w_down, resid,
+    result, resid_grad, attn_cot, d_gate, d_up, d_down,
+    hidden, gate_grad, up_grad, own, sent, got, send_sem, recv_sem,
+):
+    length, width = xn.shape
+    half = length // 2
+    units = w_gate.shape[1]
+    peer = partners()["c"]
+    meet({"c": peer})
+
+    def units_of(rows, cols):
+        gate = dotf(xn[rows, :], w_gate[:, cols], NN)
+        up = dotf(xn[rows, :], w_up[:, cols], NN)
+        grad = dotf(cot[rows, :], w_down[:, cols], NN).astype(BF).astype(F32)
+        act, slope = gelu_parts(gate)
+        hidden[rows, cols] = (act * up).astype(BF)
+        gate_grad[rows, cols] = (grad * up * slope).astype(BF)
+        up_grad[rows, cols] = (grad * act).astype(BF)
+
+    def phase(rows, put):
+        in_chunks(units, 256, lambda cols: units_of(rows, cols))
+
+        def sums(here):
+            put[0, :, here] = dotf(hidden[rows, :], w_down[here, :], NT).astype(put.dtype)
+            both = dotf(gate_grad[rows, :], w_gate[here, :], NT)
+            both = both + dotf(up_grad[rows, :], w_up[here, :], NT)
+            put[1, :, here] = both.astype(put.dtype)
+
+        in_chunks(width, 256, sums)
+
+    phase(pl.ds(half, half), sent)
+    give = remote(sent, got, send_sem.at[0], recv_sem.at[0], peer)
+    give.start()
+    phase(pl.ds(0, half), own)
+    give.wait()
+
+    def finish(here):
+        values = resid[here, :]
+        mlp = own[0, here, :] + got[0, here, :].astype(F32)
+        result[here, :] = to_place(values + mlp).astype(BF)
+        xhat, scale = normalize(values)
+        back = normalize_back(own[1, here, :] + got[1, here, :].astype(F32), xhat, scale)
+        grad = cot[here, :].astype(F32) + back
+        resid_grad[here, :] = grad
+        attn_cot[here, :] = grad.astype(BF)
+
+    in_chunks(half, 64, finish)
+    swap = remote(
+        attn_cot.at[pl.ds(0, half)], attn_cot.at[pl.ds(half, half)], send_sem.at[1], recv_sem.at[1], peer
+    )
+    swap.start()
+
+    def weights(here):
+        left = jnp.transpose(cot[:, here])
+        d_down[here, :] = dotf(left, hidden[...], NN).astype(BF)
+        left = jnp.transpose(xn[:, here])
+        d_gate[here, :] = dotf(left, gate_grad[...], NN).astype(BF)
+        d_up[here, :] = dotf(left, up_grad[...], NN).astype(BF)
+
+    in_chunks(width, 256, weights)
+    swap.wait()
+
+
+def mlp_block(xn, cot, w_gate, w_up, w_down, resid):
+    length, width = xn.shape
+    half = length // 2
+    units = w_gate.shape[1]
+    vmem = pl.BlockSpec(memory_space=pltpu.VMEM)
+    grads = jax.ShapeDtypeStruct((width, units), BF)
+    return pl.pallas_call(
+        mlp_kernel,
+        in_specs=[vmem] * 6,
+        out_specs=[vmem] * 6,
+        out_shape=[
+            jax.ShapeDtypeStruct((half, width), BF),
+            jax.ShapeDtypeStruct((half, width), F32),
+            jax.ShapeDtypeStruct((length, width), BF),
+            grads,
+            grads,
+            grads,
+        ],
+        scratch_shapes=[pltpu.VMEM((length, units), BF)] * 3
+        + [
+            pltpu.VMEM((2, half, width), F32),
+            pltpu.VMEM((2, half, width), BF),
+            pltpu.VMEM((2, half, width), BF),
+            pltpu.SemaphoreType.DMA((2,)),
+            pltpu.SemaphoreType.DMA((2,)),
+        ],
+        compiler_params=pltpu.CompilerParams(
+            collective_id=1, has_side_effects=True, vmem_limit_bytes=60 << 20
+        ),
+        name="mlp_block",
+    )(xn, cot, w_gate, w_up, w_down, resid)
+
+
 class Chips:
     def __init__(self):
         self.axes = ("dp", "tensor")
@@ -633,7 +740,7 @@
         seg_col, seg_row = seg[:, None], seg[None, :]
         owned = (a_one, b_one, own_gate, own_up, down_rows)
         if paired:
-            owned = [comm.swap(w) for w in owned]
+            owned = [comm.swap(w) for w in owned[:2] + tuple(padded(w) for w in owned[2:])]
             x_half = comm.swap(tokens[0])
             q, k, v, o, lse, xh, w_qk, w_vo, resid, xn, w_gate, w_up, w_dn = forward_block(
                 owned, x_half, tables, seg_col, seg_row
@@ -642,7 +749,6 @@
                 w.reshape(-1, w.shape[-1]) for w in (w_qk, w_vo, w_gate, w_up, w_dn)
             )
             xh_one, scale_one = normalize(comm.to_relative(x_half).astype(F32))
-            xh_two, scale_two = normalize(resid)
             w_o = w_vo[:, cols:]
         else:
             w_qk, w_vo, w_gate, w_up, w_dn = (
@@ -656,23 +762,28 @@
             resid = x_in + comm.scatter_rows(dotf(o, w_o, NT))
             xh_two, scale_two = normalize(resid)
             xn = comm.gather_rows(xh_two.astype(BF))
-        gate, up = dotf(xn, w_gate, NN), dotf(xn, w_up, NN)
-        act, slope = gelu_parts(gate)
-        hidden = (act * up).astype(BF)
-        mlp = comm.scatter_rows(dotf(hidden, w_dn, NT))
-        result = comm.swap(comm.from_relative((resid + mlp).astype(BF)))
-
-        hidden_grad = dotf(cot_all, w_dn, NN).astype(BF).astype(F32)
-        gate_grad = (hidden_grad * up * slope).astype(BF)
-        up_grad = (hidden_grad * act).astype(BF)
-        f_two = comm.scatter_rows(dotf(gate_grad, w_gate, NT) + dotf(up_grad, w_up, NT))
-        resid_grad = cot.astype(F32) + normalize_back(f_two, xh_two, scale_two)
-        attn_cot = comm.gather_rows(resid_grad.astype(BF))
-
-        d_down = dotf(cot_all, hidden, TN)
-        d_gate, d_up = dotf(xn, gate_grad, TN), dotf(xn, up_grad, TN)
-        wide = lambda g, d: jnp.concatenate([padded(g), d], axis=1)
-        two_a, two_b = comm.reduce(wide(d_gate, d_down[:, :low]), wide(d_up, d_down[:, low:]))
+        if paired:
+            placed, resid_grad, attn_cot, d_gate, d_up, d_down = mlp_block(
+                xn, cot_all, w_gate, w_up, w_dn, resid
+            )
+            result = comm.swap(placed)
+        else:
+            gate, up = dotf(xn, w_gate, NN), dotf(xn, w_up, NN)
+            act, slope = gelu_parts(gate)
+            hidden = (act * up).astype(BF)
+            mlp = comm.scatter_rows(dotf(hidden, w_dn, NT))
+            result = comm.swap(comm.from_relative((resid + mlp).astype(BF)))
+            hidden_grad = dotf(cot_all, w_dn, NN).astype(BF).astype(F32)
+            gate_grad = (hidden_grad * up * slope).astype(BF)
+            up_grad = (hidden_grad * act).astype(BF)
+            f_two = comm.scatter_rows(dotf(gate_grad, w_gate, NT) + dotf(up_grad, w_up, NT))
+            resid_grad = cot.astype(F32) + normalize_back(f_two, xh_two, scale_two)
+            attn_cot = comm.gather_rows(resid_grad.astype(BF))
+            d_down = dotf(cot_all, hidden, TN)
+            d_gate, d_up = dotf(xn, gate_grad, TN), dotf(xn, up_grad, TN)
+
+        wide = lambda g, d: jnp.concatenate([g if paired else padded(g), d], axis=1)
+        two_a, two_b = comm.reduce(wide(d_gate, d_down[:, :low]), wide(d_up, d_down[:, low:units]))
 
         heads_grad = dotf(attn_cot, w_o, NN).astype(BF)
         pg = attn_bwd(q, k, v, o, heads_grad, lse, tables, seg_col, seg_row)

time: 473 us -> 515 us (1.089)
  waiting for transfers between devices: 52.7 us -> 110 us
  Pallas kernels: 162 us -> 210 us
  matrix products: 60.2 us -> 17.4 us
  local copies, waits for them, and re-layouts: 58.7 us -> 42.8 us
  other arithmetic: 48.5 us -> 40.2 us
    ppermute x26 -> x23, waiting for transfers between devices: 52.7 us -> 109 us  [send(): return lax.ppermute(value, self.axes, pairs)]
    pallas_call x0 -> x1, Pallas kernels: none -> 47.6 us  [mlp_block(): pl.pallas_call(mlp_kernel, in_specs=[vmem] * 6, out_specs=[vmem] * 6, out...]
    dot_general x17 -> x8, matrix products: 60.2 us -> 17.4 us  [dotf(): return lax.dot_general(a, b, (dims, ((), ())), preferred_element_type=F32)]
    unnamed x95 -> x75, local copies, waits for them, and re-layouts: 23.7 us -> 13.8 us
    concatenate x0 -> x3, other arithmetic: none -> 5.78 us  [the longest x1 3.03 us: gather_rows(): return jnp.concatenate([value, self.send(value, dc=1)], axis=0)]
    ppermute x26 -> x23, starting transfers between devices: 53.3 us -> 57.1 us  [send(): return lax.ppermute(value, self.axes, pairs)]
  transfers between devices with their start and end apart: 40 -> 37, of which waited for: 8 -> 10; matrix products, arithmetic and copies ran while one was open for 26% -> 13% of each run, Pallas kernels for 35% -> 25%
where the time goes in v3:
time: 515 us; the launch traced here: 507 us
  Pallas kernels  210 us (41%)
  waiting for transfers between devices  110 us (21%)
  starting transfers between devices  85.4 us (17%)
  local copies, waits for them, and re-layouts  42.8 us (8%)
  other arithmetic  40.2 us (8%)
  matrix products  17.4 us (3%)
    pallas_call x1, Pallas kernels, forward_block(): pl.pallas_call(forward_kernel, in_specs=[any_] * 5 + [vmem] * 6, out_spec...  127 us
    ppermute x23, waiting for transfers between devices, send(): return lax.ppermute(value, self.axes, pairs)  109 us
    ppermute x23, starting transfers between devices, send(): return lax.ppermute(value, self.axes, pairs)  57.1 us
    pallas_call x1, Pallas kernels, mlp_block(): pl.pallas_call(mlp_kernel, in_specs=[vmem] * 6, out_specs=[vmem] * 6, out...  47.6 us
    pallas_call x1, Pallas kernels, attn_bwd(): pl.pallas_call(attn_bwd_kernel, grid=(pairs,), in_specs=[col] * 5 + [pl.B...  34.6 us
    ppermute x14, starting transfers between devices, swap(): return lax.ppermute(value, self.axes, pairs)  28.3 us
    dot_general x8, matrix products, dotf(): return lax.dot_general(a, b, (dims, ((), ())), preferred_element_type=F32)  17.4 us
    unnamed x75, local copies, waits for them, and re-layouts  13.8 us
  transfers between devices with their start and end apart: 37, of which 10 were waited for; matrix products, arithmetic and copies ran while one was open for 13% of the time, Pallas kernels for 25%

profile of v3, /device:TPU:0, one launch (start us, length us, event | category | flops | bytes accessed | tf_op | source)
XLA Modules:
  0.0 506.9 jit_solution(15631062575987970799)
XLA Ops:
  0.7 2.0 collective-permute-start.5
  2.7 2.3 copy.33
  5.0 1.9 collective-permute-start.7
  8.3 2.1 collective-permute-start
  11.1 2.1 collective-permute-start.1
  13.3 1.9 multiply_sine_fusion
  15.3 1.8 pad_maximum_fusion.8
  20.6 1.6 collective-permute-start.2
  23.2 1.6 collective-permute-start.3
  25.4 3.0 collective-permute-start.4
  28.3 2.2 reverse_select_fusion.7
  31.2 1.6 copy.35
  32.8 12.3 %collective-permute-start.8 = (bf16[512,1024]{1,0:T(8,128)(2,1)}, bf16[512,1024]{1,0:T(8,128)(2,1)}, u32[]{:S(2)}, u32[]{:S(2)}) collective-permute-start(bf16[512,1024]{1,0:T(8,128)(2,1)} %copy.35), channel_id=1, source_target_pairs={{0,2},{1,3},{2,0},{3,1},{4,6},{5,7},{6,4},{7,5},{8,10},{9,11},{10,... | collective-permute-start | bytes 3145736 | tf_op jit(solution)/shard_map/ppermute | solution.py:610
  45.9 127.5 %forward_block.1 = (bf16[1024,512]{1,0:T(8,128)(2,1)}, bf16[1024,512]{1,0:T(8,128)(2,1)}, bf16[1024,512]{1,0:T(8,128)(2,1)}, bf16[1024,512]{1,0:T(8,128)(2,1)}, ...) custom-call(bf16[64,1024]{1,0:T(8,128)(2,1)} %collective-permute-don, ...), custom_call_target="tpu_custom_call" | custom-call | tf_op jit(solution)/shard_map/forward_block/pallas_call | solution.py:453
  173.4 3.9 copy.43
  177.8 1.6 fusion.2
  179.4 1.9 copy.41
  182.0 3.0 pad_maximum_fusion.3.cot
  185.0 47.6 %mlp_block.1 = (bf16[512,1024]{1,0:T(8,128)(2,1)}, f32[512,1024]{1,0:T(8,128)}, bf16[1024,1024]{1,0:T(8,128)(2,1)}, bf16[1024,1408]{1,0:T(8,128)(2,1)}, bf16[102...) custom-call(bf16[1024,1024]{1,0:T(8,128)(2,1)} %get-tuple-element.27.xn, bf16[1024,1024]{1,0:T(8,128)(2,1)} %pad_maximum_fusion.3.cot, ...), custom_call_target="tpu_custom_call" | custom-call | tf_op jit(solution)/shard_map/mlp_block/pallas_call | solution.py:564
  232.7 1.6 slice.242
  234.3 2.9 slice.253
  237.1 2.2 convolution_convert_fusion.4.do
  239.4 34.6 %attn_bwd.1 = bf16[3,1024,512]{2,1,0:T(8,128)(2,1)} custom-call(bf16[1024,512]{1,0:T(8,128)(2,1)} %get-tuple-element.34.q, bf16[1024,512]{1,0:T(8,128)(2,1)} %get-tuple-element.35.k, bf16[1024,512]{1,0:T(8,128)(2,1)} %get-tuple-element.36.v, bf16[1024,512]{1,0:T(8,128)(2,1)} %get-tuple-element.37.o, bf16[1024,512]{1,0:T(8,128)(2,1)} %convolution_convert_fusion.4.do, ...), custom_call_target="tpu_custom_call" | custom-call | flops 10737418240 | bytes 10485760 | tf_op jit(solution)/shard_map/attn_bwd/pallas_call | solution.py:164
  274.0 4.2 convolution_convert_fusion.2
  278.3 2.2 convolution_convert_fusion.3
  282.3 2.3 convolution_convert_fusion
  289.1 1.6 copy.48
  290.7 1.5 collective-permute-start.24
  292.2 2.2 pad_maximum_fusion
  300.0 2.6 add_add_fusion
  303.0 1.4 fusion.44
  304.4 2.5 copy.47
  306.9 1.7 pad_maximum_fusion.2
  309.6 51.9 %collective-permute-done.12 = bf16[8,64,1024]{2,1,0:T(8,128)(2,1)} collective-permute-done((bf16[8,64,1024]{2,1,0:T(8,128)(2,1)S(1)}, bf16[8,64,1024]{2,1,0:T(8,128)(2,1)}, u32[]{:S(2)}, u32[]{:S(2)}) %collective-permute-start.12) | collective-permute-done | bytes 1048608 | tf_op jit(solution)/shard_map/ppermute | solution.py:610
  361.5 9.6 %collective-permute-start.9 = (bf16[512,1024]{1,0:T(8,128)(2,1)}, bf16[512,1024]{1,0:T(8,128)(2,1)}, u32[]{:S(2)}, u32[]{:S(2)}) collective-permute-start(bf16[512,1024]{1,0:T(8,128)(2,1)} %get-tuple-element.32), channel_id=1, source_target_pairs={{0,0},{1,2},{2,1},{3,3},{4,4},{5,6},{6,5},{7,7},{8,8},{9,10},{10,9... | collective-permute-start | bytes 3145736 | tf_op jit(solution)/shard_map/ppermute | solution.py:620
  371.1 1.7 fusion.1
  373.7 1.5 collective-permute-start.13
  378.2 1.7 add_convert_fusion.4
  379.9 1.5 copy.42
  381.8 1.4 collective-permute-done.13
  384.8 4.6 collective-permute-done.19
  390.8 3.3 collective-permute-start.16
  394.1 7.3 %collective-permute-done.15 = bf16[64,1024]{1,0:T(8,128)(2,1)S(1)} collective-permute-done((bf16[64,1024]{1,0:T(8,128)(2,1)S(1)}, bf16[64,1024]{1,0:T(8,128)(2,1)S(1)}, u32[]{:S(2)}, u32[]{:S(2)}) %collective-permute-start.15) | collective-permute-done | bytes 131104 | tf_op jit(solution)/shard_map/ppermute | solution.py:610
  401.6 2.2 collective-permute-start.21
  403.8 3.0 collective-permute-done.20
  406.7 1.6 collective-permute-start.22
  408.4 5.2 %collective-permute-done.21 = bf16[64,1024]{1,0:T(8,128)(2,1)S(1)} collective-permute-done((bf16[64,1024]{1,0:T(8,128)(2,1)S(1)}, bf16[64,1024]{1,0:T(8,128)(2,1)S(1)}, u32[]{:S(2)}, u32[]{:S(2)}) %collective-permute-start.21) | collective-permute-done | bytes 131104 | tf_op jit(solution)/shard_map/ppermute | solution.py:610
  418.1 2.5 fusion
  422.7 2.2 add_convert_fusion
  426.0 8.2 %collective-permute-start.31 = (bf16[4,64,2080]{2,1,0:T(8,128)(2,1)}, bf16[4,64,2080]{2,1,0:T(8,128)(2,1)S(1)}, u32[]{:S(2)}, u32[]{:S(2)}) collective-permute-start(bf16[4,64,2080]{2,1,0:T(8,128)(2,1)} %slice.316), channel_id=1, source_target_pairs={{0,1},{1,0},{2,3},{3,2},{4,5},{5,4},{6,7},{7,6},{8,9},{9,8},{10,11... | collective-permute-start | bytes 3194888 | tf_op jit(solution)/shard_map/ppermute | solution.py:610
  434.3 1.6 bitcast_convert_fusion
  435.9 2.9 copy.51
  438.7 1.9 collective-permute-done.25
  440.7 1.9 add_convert_fusion.2
  442.7 3.6 collective-permute-start.26
  447.2 1.5 collective-permute-start.28
  448.7 11.7 %collective-permute-done.31 = bf16[4,64,2080]{2,1,0:T(8,128)(2,1)S(1)} collective-permute-done((bf16[4,64,2080]{2,1,0:T(8,128)(2,1)}, bf16[4,64,2080]{2,1,0:T(8,128)(2,1)S(1)}, u32[]{:S(2)}, u32[]{:S(2)}) %collective-permute-start.31) | collective-permute-done | bytes 1064992 | tf_op jit(solution)/shard_map/ppermute | solution.py:610
  461.2 1.5 collective-permute-start.33
  462.8 2.5 collective-permute-start.34
  466.2 9.1 %collective-permute-done.32 = bf16[64,2080]{1,0:T(8,128)(2,1)S(1)} collective-permute-done((bf16[64,2080]{1,0:T(8,128)(2,1)S(1)}, bf16[64,2080]{1,0:T(8,128)(2,1)S(1)}, u32[]{:S(2)}, u32[]{:S(2)}) %collective-permute-start.32) | collective-permute-done | bytes 266272 | tf_op jit(solution)/shard_map/ppermute | solution.py:610
  475.3 13.3 %collective-permute-done.33 = bf16[64,2080]{1,0:T(8,128)(2,1)S(1)} collective-permute-done((bf16[64,2080]{1,0:T(8,128)(2,1)S(1)}, bf16[64,2080]{1,0:T(8,128)(2,1)S(1)}, u32[]{:S(2)}, u32[]{:S(2)}) %collective-permute-start.33) | collective-permute-done | bytes 266272 | tf_op jit(solution)/shard_map/ppermute | solution.py:610
  489.9 11.8 %collective-permute-start.36 = (f32[2,64]{1,0:T(2,128)S(1)}, f32[2,64]{1,0:T(2,128)S(1)}, u32[]{:S(2)}, u32[]{:S(2)}) collective-permute-start(f32[2,64]{1,0:T(2,128)S(1)} %pad_maximum_fusion.12), channel_id=1, source_target_pairs={{0,1},{1,0},{2,3},{3,2},{4,5},{5,4},{6,7},{7,6},{8,9},{9,8},{10,11... | collective-permute-start | bytes 1544 | tf_op jit(solution)/shard_map/ppermute | solution.py:610
  502.5 1.4 copy.52
  504.4 2.3 copy.61
  (196 shorter events, 43.1 us)
Async XLA Ops:
  0.6 6.2 %copy-start.32 = (s32[1,1024]{1,0:T(1,128)S(1)}, s32[1,1024]{1,0:T(1,128)}, u32[]{:S(2)}) copy-start(s32[1,1024]{1,0:T(1,128)} %param.10) | copy-start | bytes 12292
  0.6 6.9 %copy-start.33 = (bf16[64]{0:T(256)(128)(2,1)S(1)}, bf16[64]{0:T(256)(128)(2,1)}, u32[]{:S(2)}) copy-start(bf16[64]{0:T(256)(128)(2,1)} %param.15) | copy-start | bytes 388
  0.7 6.9 %copy-start.18 = (bf16[64,3,512]{2,0,1:T(8,128)(2,1)S(1)}, bf16[64,3,512]{2,0,1:T(8,128)(2,1)}, u32[]{:S(2)}) copy-start(bf16[64,3,512]{2,0,1:T(8,128)(2,1)} %param.11) | copy-start | bytes 589828
  0.7 9.8 %copy-start.26 = (bf16[512,64]{0,1:T(8,128)(2,1)S(1)}, bf16[512,64]{0,1:T(8,128)(2,1)}, u32[]{:S(2)}) copy-start(bf16[512,64]{0,1:T(8,128)(2,1)} %param.12) | copy-start | bytes 196612
  0.7 22.6 %collective-permute-start.5 = (bf16[512,1024]{1,0:T(8,128)(2,1)}, bf16[512,1024]{1,0:T(8,128)(2,1)S(1)}, u32[]{:S(2)}, u32[]{:S(2)}) collective-permute-start(bf16[512,1024]{1,0:T(8,128)(2,1)} %bitcast.195), channel_id=1, source_target_pairs={{0,0},{1,2},{2,1},{3,3},{4,4},{5,6},{6,5},{7,7},{8,8},{9,10},{10,9... | collective-permute-start | bytes 3145736 | tf_op jit(solution)/shard_map/ppermute | solution.py:620
  5.0 20.4 %collective-permute-start.7 = (bf16[512,1024]{0,1:T(8,128)(2,1)}, bf16[512,1024]{0,1:T(8,128)(2,1)S(1)}, u32[]{:S(2)}, u32[]{:S(2)}) collective-permute-start(bf16[512,1024]{0,1:T(8,128)(2,1)} %bitcast.11), channel_id=1, source_target_pairs={{0,0},{1,2},{2,1},{3,3},{4,4},{5,6},{6,5},{7,7},{8,8},{9,10},{10,9... | collective-permute-start | bytes 3145736 | tf_op jit(solution)/shard_map/ppermute | solution.py:620
  6.8 13.8 %collective-permute-start.6 = (s32[1024]{0:T(1024)S(1)}, s32[1024]{0:T(1024)S(1)}, u32[]{:S(2)}, u32[]{:S(2)}) collective-permute-start(s32[1024]{0:T(1024)S(1)} %bitcast.196), channel_id=1, source_target_pairs={{0,0},{1,2},{2,1},{3,3},{4,4},{5,6},{6,5},{7,7},{8,8},{9,10},{10,9... | collective-permute-start | bytes 12296 | tf_op jit(solution)/shard_map/ppermute | solution.py:620
  8.3 24.5 %collective-permute-start = (bf16[64,1024]{1,0:T(8,128)(2,1)}, bf16[64,1024]{1,0:T(8,128)(2,1)}, u32[]{:S(2)}, u32[]{:S(2)}) collective-permute-start(bf16[64,1024]{1,0:T(8,128)(2,1)} %pad_maximum_fusion.10), channel_id=1, source_target_pairs={{0,0},{1,2},{2,1},{3,3},{4,4},{5,6},{6,5},{7,7},{8,8},{9,10},{10,9... | collective-permute-start | bytes 393224 | tf_op jit(solution)/shard_map/ppermute | solution.py:620
  11.1 34.1 %collective-permute-start.1 = (bf16[64,1024]{1,0:T(8,128)(2,1)}, bf16[64,1024]{1,0:T(8,128)(2,1)}, u32[]{:S(2)}, u32[]{:S(2)}) collective-permute-start(bf16[64,1024]{1,0:T(8,128)(2,1)} %pad_maximum_fusion.11), channel_id=1, source_target_pairs={{0,0},{1,2},{2,1},{3,3},{4,4},{5,6},{6,5},{7,7},{8,8},{9,10},{10,9... | collective-permute-start | bytes 393224 | tf_op jit(solution)/shard_map/ppermute | solution.py:620
  13.3 3.8 copy-start.34
  13.3 3.8 copy-start.12
  17.1 2.8 copy-start.25
  20.6 24.5 %collective-permute-start.2 = (bf16[64,1408]{1,0:T(8,128)(2,1)}, bf16[64,1408]{1,0:T(8,128)(2,1)S(1)}, u32[]{:S(2)}, u32[]{:S(2)}) collective-permute-start(bf16[64,1408]{1,0:T(8,128)(2,1)} %pad.10), channel_id=1, source_target_pairs={{0,0},{1,2},{2,1},{3,3},{4,4},{5,6},{6,5},{7,7},{8,8},{9,10},{10,9... | collective-permute-start | bytes 540680 | tf_op jit(solution)/shard_map/ppermute | solution.py:620
  22.2 8.3 %copy-start.27 = (s32[1024]{0:T(1024)}, s32[1024]{0:T(1024)S(1)}, u32[]{:S(2)}) copy-start(s32[1024]{0:T(1024)S(1)} %add_select_fusion) | copy-start | bytes 12292
  23.2 7.3 %copy-start.6 = (bf16[512,1024]{1,0:T(8,128)(2,1)}, bf16[512,1024]{1,0:T(8,128)(2,1)S(1)}, u32[]{:S(2)}) copy-start(bf16[512,1024]{1,0:T(8,128)(2,1)S(1)} %collective-permute-done.5.x_half) | copy-start | bytes 3145732
  23.2 21.9 %collective-permute-start.3 = (bf16[64,1408]{1,0:T(8,128)(2,1)}, bf16[64,1408]{1,0:T(8,128)(2,1)S(1)}, u32[]{:S(2)}, u32[]{:S(2)}) collective-permute-start(bf16[64,1408]{1,0:T(8,128)(2,1)} %pad.11), channel_id=1, source_target_pairs={{0,0},{1,2},{2,1},{3,3},{4,4},{5,6},{6,5},{7,7},{8,8},{9,10},{10,9... | collective-permute-start | bytes 540680 | tf_op jit(solution)/shard_map/ppermute | solution.py:620
  25.4 3.0 copy-start.14
  25.4 19.8 %collective-permute-start.4 = (bf16[64,1408]{1,0:T(8,128)(2,1)}, bf16[64,1408]{1,0:T(8,128)(2,1)}, u32[]{:S(2)}, u32[]{:S(2)}) collective-permute-start(bf16[64,1408]{1,0:T(8,128)(2,1)} %pad.12), channel_id=1, source_target_pairs={{0,0},{1,2},{2,1},{3,3},{4,4},{5,6},{6,5},{7,7},{8,8},{9,10},{10,9... | collective-permute-start | bytes 540680 | tf_op jit(solution)/shard_map/ppermute | solution.py:620
  32.8 149.1 %collective-permute-start.8 = (bf16[512,1024]{1,0:T(8,128)(2,1)}, bf16[512,1024]{1,0:T(8,128)(2,1)}, u32[]{:S(2)}, u32[]{:S(2)}) collective-permute-start(bf16[512,1024]{1,0:T(8,128)(2,1)} %copy.35), channel_id=1, source_target_pairs={{0,2},{1,3},{2,0},{3,1},{4,6},{5,7},{6,4},{7,5},{8,10},{9,11},{10,... | collective-permute-start | bytes 3145736 | tf_op jit(solution)/shard_map/ppermute | solution.py:610
  232.7 4.5 copy-start.29
  234.3 2.9 copy-start.20
  274.0 4.3 copy-start.11
  274.0 4.3 copy-start.22
  280.5 1.9 copy-start.31
  282.3 2.3 copy-start.28
  285.9 1.8 copy-start.9
  289.1 3.1 copy-start.2
  290.7 127.4 %collective-permute-start.24 = (bf16[8,64,2048]{2,1,0:T(8,128)(2,1)}, bf16[8,64,2048]{2,1,0:T(8,128)(2,1)}, u32[]{:S(2)}, u32[]{:S(2)}) collective-permute-start(bf16[8,64,2048]{2,1,0:T(8,128)(2,1)} %bitcast.58), channel_id=1, source_target_pairs={{0,1},{1,0},{2,3},{3,2},{4,5},{5,4},{6,7},{7,6},{8,9},{9,8},{10,11... | collective-permute-start | bytes 6291464 | tf_op jit(solution)/shard_map/ppermute | solution.py:610
  296.6 64.9 %collective-permute-start.12 = (bf16[8,64,1024]{2,1,0:T(8,128)(2,1)S(1)}, bf16[8,64,1024]{2,1,0:T(8,128)(2,1)}, u32[]{:S(2)}, u32[]{:S(2)}) collective-permute-start(bf16[8,64,1024]{2,1,0:T(8,128)(2,1)S(1)} %bitcast.180), channel_id=1, source_target_pairs={{0,1},{1,0},{2,3},{3,2},{4,5},{5,4},{6,7},{7,6},{8,9},{9,8},{10,11... | collective-permute-start | bytes 3145736 | tf_op jit(solution)/shard_map/ppermute | solution.py:610
  298.4 1.6 copy-start.21
  298.5 75.2 %collective-permute-start.18 = (bf16[8,64,1024]{2,1,0:T(8,128)(2,1)S(1)}, bf16[8,64,1024]{2,1,0:T(8,128)(2,1)S(1)}, u32[]{:S(2)}, u32[]{:S(2)}) collective-permute-start(bf16[8,64,1024]{2,1,0:T(8,128)(2,1)S(1)} %pad_maximum_fusion.4), channel_id=1, source_target_pairs={{0,4},{1,5},{2,6},{3,7},{4,0},{5,1},{6,2},{7,3},{8,12},{9,13},{10,... | collective-permute-start | bytes 3145736 | tf_op jit(solution)/shard_map/ppermute | solution.py:610
  302.8 73.8 %collective-permute-start.10 = (bf16[512,1024]{1,0:T(8,128)(2,1)S(1)}, bf16[512,1024]{1,0:T(8,128)(2,1)S(1)}, u32[]{:S(2)}, u32[]{:S(2)}) collective-permute-start(bf16[512,1024]{1,0:T(8,128)(2,1)S(1)} %slice.412), channel_id=1, source_target_pairs={{0,2},{1,3},{2,0},{3,1},{4,6},{5,7},{6,4},{7,5},{8,10},{9,11},{10,... | collective-permute-start | bytes 3145736 | tf_op jit(solution)/shard_map/ppermute | solution.py:610
  308.6 114.1 %collective-permute-start.30 = (bf16[8,64,2080]{2,1,0:T(8,128)(2,1)}, bf16[8,64,2080]{2,1,0:T(8,128)(2,1)}, u32[]{:S(2)}, u32[]{:S(2)}) collective-permute-start(bf16[8,64,2080]{2,1,0:T(8,128)(2,1)} %pad_maximum_fusion.2), channel_id=1, source_target_pairs={{0,4},{1,5},{2,6},{3,7},{4,0},{5,1},{6,2},{7,3},{8,12},{9,13},{10,... | collective-permute-start | bytes 6389768 | tf_op jit(solution)/shard_map/ppermute | solution.py:610
  361.5 53.9 %collective-permute-start.9 = (bf16[512,1024]{1,0:T(8,128)(2,1)}, bf16[512,1024]{1,0:T(8,128)(2,1)}, u32[]{:S(2)}, u32[]{:S(2)}) collective-permute-start(bf16[512,1024]{1,0:T(8,128)(2,1)} %get-tuple-element.32), channel_id=1, source_target_pairs={{0,0},{1,2},{2,1},{3,3},{4,4},{5,6},{6,5},{7,7},{8,8},{9,10},{10,9... | collective-permute-start | bytes 3145736 | tf_op jit(solution)/shard_map/ppermute | solution.py:620
  372.8 2.8 copy-start.7
  373.7 9.5 %collective-permute-start.13 = (bf16[4,64,1024]{2,1,0:T(8,128)(2,1)}, bf16[4,64,1024]{2,1,0:T(8,128)(2,1)}, u32[]{:S(2)}, u32[]{:S(2)}) collective-permute-start(bf16[4,64,1024]{2,1,0:T(8,128)(2,1)} %slice.284), channel_id=1, source_target_pairs={{0,4},{1,5},{2,6},{3,7},{4,0},{5,1},{6,2},{7,3},{8,12},{9,13},{10,... | collective-permute-start | bytes 1572872 | tf_op jit(solution)/shard_map/ppermute | solution.py:610
  376.8 12.6 %collective-permute-start.19 = (bf16[4,64,1024]{2,1,0:T(8,128)(2,1)}, bf16[4,64,1024]{2,1,0:T(8,128)(2,1)}, u32[]{:S(2)}, u32[]{:S(2)}) collective-permute-start(bf16[4,64,1024]{2,1,0:T(8,128)(2,1)} %slice.296), channel_id=1, source_target_pairs={{0,1},{1,0},{2,3},{3,2},{4,5},{5,4},{6,7},{7,6},{8,9},{9,8},{10,11... | collective-permute-start | bytes 1572872 | tf_op jit(solution)/shard_map/ppermute | solution.py:610
  381.4 1.9 copy-start.8
  381.6 7.9 %copy-start.5 = (bf16[8,64,1024]{2,1,0:T(8,128)(2,1)S(1)}, bf16[8,64,1024]{2,1,0:T(8,128)(2,1)}, u32[]{:S(2)}) copy-start(bf16[8,64,1024]{2,1,0:T(8,128)(2,1)} %copy-done.4) | copy-start | bytes 3145732
  384.5 6.3 %collective-permute-start.14 = (bf16[64,1024]{1,0:T(8,128)(2,1)S(1)}, bf16[64,1024]{1,0:T(8,128)(2,1)S(1)}, u32[]{:S(2)}, u32[]{:S(2)}) collective-permute-start(bf16[64,1024]{1,0:T(8,128)(2,1)S(1)} %get-tuple-element.84), channel_id=1, source_target_pairs={{0,8},{1,9},{2,10},{3,11},{4,12},{5,13},{6,14},{7,15},{8,0},{9,1},... | collective-permute-start | bytes 393224 | tf_op jit(solution)/shard_map/ppermute | solution.py:610
  389.4 11.9 %collective-permute-start.15 = (bf16[64,1024]{1,0:T(8,128)(2,1)S(1)}, bf16[64,1024]{1,0:T(8,128)(2,1)S(1)}, u32[]{:S(2)}, u32[]{:S(2)}) collective-permute-start(bf16[64,1024]{1,0:T(8,128)(2,1)S(1)} %get-tuple-element.86), channel_id=1, source_target_pairs={{0,16},{1,17},{2,18},{3,19},{4,20},{5,21},{6,22},{7,23},{8,24},{9,... | collective-permute-start | bytes 393224 | tf_op jit(solution)/shard_map/ppermute | solution.py:610
  390.8 10.8 %collective-permute-start.16 = (bf16[64,1024]{1,0:T(8,128)(2,1)S(1)}, bf16[64,1024]{1,0:T(8,128)(2,1)S(1)}, u32[]{:S(2)}, u32[]{:S(2)}) collective-permute-start(bf16[64,1024]{1,0:T(8,128)(2,1)S(1)} %get-tuple-element.85), channel_id=1, source_target_pairs={{0,24},{1,25},{2,26},{3,27},{4,28},{5,29},{6,30},{7,31},{8,16},{9,... | collective-permute-start | bytes 393224 | tf_op jit(solution)/shard_map/ppermute | solution.py:610
  401.4 5.4 %collective-permute-start.20 = (bf16[64,1024]{1,0:T(8,128)(2,1)S(1)}, bf16[64,1024]{1,0:T(8,128)(2,1)S(1)}, u32[]{:S(2)}, u32[]{:S(2)}) collective-permute-start(bf16[64,1024]{1,0:T(8,128)(2,1)S(1)} %get-tuple-element.87), channel_id=1, source_target_pairs={{0,8},{1,9},{2,10},{3,11},{4,12},{5,13},{6,14},{7,15},{8,0},{9,1},... | collective-permute-start | bytes 393224 | tf_op jit(solution)/shard_map/ppermute | solution.py:610
  401.6 12.0 %collective-permute-start.21 = (bf16[64,1024]{1,0:T(8,128)(2,1)S(1)}, bf16[64,1024]{1,0:T(8,128)(2,1)S(1)}, u32[]{:S(2)}, u32[]{:S(2)}) collective-permute-start(bf16[64,1024]{1,0:T(8,128)(2,1)S(1)} %get-tuple-element.89), channel_id=1, source_target_pairs={{0,16},{1,17},{2,18},{3,19},{4,20},{5,21},{6,22},{7,23},{8,24},{9,... | collective-permute-start | bytes 393224 | tf_op jit(solution)/shard_map/ppermute | solution.py:610
  406.7 7.6 %collective-permute-start.22 = (bf16[64,1024]{1,0:T(8,128)(2,1)S(1)}, bf16[64,1024]{1,0:T(8,128)(2,1)S(1)}, u32[]{:S(2)}, u32[]{:S(2)}) collective-permute-start(bf16[64,1024]{1,0:T(8,128)(2,1)S(1)} %get-tuple-element.88), channel_id=1, source_target_pairs={{0,24},{1,25},{2,26},{3,27},{4,28},{5,29},{6,30},{7,31},{8,16},{9,... | collective-permute-start | bytes 393224 | tf_op jit(solution)/shard_map/ppermute | solution.py:610
  413.6 2.7 collective-permute-start.17
  414.3 2.8 copy-start.19
  414.4 3.7 copy-start
  414.4 1.9 collective-permute-start.23
  415.5 18.8 %collective-permute-start.11 = (bf16[512,1024]{0,1:T(8,128)(2,1)S(1)}, bf16[512,1024]{0,1:T(8,128)(2,1)S(1)}, u32[]{:S(2)}, u32[]{:S(2)}) collective-permute-start(bf16[512,1024]{0,1:T(8,128)(2,1)S(1)} %bitcast.179), channel_id=1, source_target_pairs={{0,0},{1,2},{2,1},{3,3},{4,4},{5,6},{6,5},{7,7},{8,8},{9,10},{10,9... | collective-permute-start | bytes 3145736 | tf_op jit(solution)/shard_map/ppermute | solution.py:620
  420.6 4.3 copy-start.1
  420.6 2.1 copy-start.3
  421.7 19.0 %collective-permute-start.25 = (bf16[4,64,2048]{2,1,0:T(8,128)(2,1)}, bf16[4,64,2048]{2,1,0:T(8,128)(2,1)}, u32[]{:S(2)}, u32[]{:S(2)}) collective-permute-start(bf16[4,64,2048]{2,1,0:T(8,128)(2,1)} %slice.305), channel_id=1, source_target_pairs={{0,4},{1,5},{2,6},{3,7},{4,0},{5,1},{6,2},{7,3},{8,12},{9,13},{10,... | collective-permute-start | bytes 3145736 | tf_op jit(solution)/shard_map/ppermute | solution.py:610
  426.0 34.4 %collective-permute-start.31 = (bf16[4,64,2080]{2,1,0:T(8,128)(2,1)}, bf16[4,64,2080]{2,1,0:T(8,128)(2,1)S(1)}, u32[]{:S(2)}, u32[]{:S(2)}) collective-permute-start(bf16[4,64,2080]{2,1,0:T(8,128)(2,1)} %slice.316), channel_id=1, source_target_pairs={{0,1},{1,0},{2,3},{3,2},{4,5},{5,4},{6,7},{7,6},{8,9},{9,8},{10,11... | collective-permute-start | bytes 3194888 | tf_op jit(solution)/shard_map/ppermute | solution.py:610
  442.7 20.1 %collective-permute-start.26 = (bf16[64,2048]{1,0:T(8,128)(2,1)S(1)}, bf16[64,2048]{1,0:T(8,128)(2,1)S(1)}, u32[]{:S(2)}, u32[]{:S(2)}) collective-permute-start(bf16[64,2048]{1,0:T(8,128)(2,1)S(1)} %get-tuple-element.79), channel_id=1, source_target_pairs={{0,8},{1,9},{2,10},{3,11},{4,12},{5,13},{6,14},{7,15},{8,0},{9,1},... | collective-permute-start | bytes 786440 | tf_op jit(solution)/shard_map/ppermute | solution.py:610
  446.3 19.0 %collective-permute-start.27 = (bf16[64,2048]{1,0:T(8,128)(2,1)S(1)}, bf16[64,2048]{1,0:T(8,128)(2,1)S(1)}, u32[]{:S(2)}, u32[]{:S(2)}) collective-permute-start(bf16[64,2048]{1,0:T(8,128)(2,1)S(1)} %get-tuple-element.81), channel_id=1, source_target_pairs={{0,16},{1,17},{2,18},{3,19},{4,20},{5,21},{6,22},{7,23},{8,24},{9,... | collective-permute-start | bytes 786440 | tf_op jit(solution)/shard_map/ppermute | solution.py:610
  447.2 18.1 %collective-permute-start.28 = (bf16[64,2048]{1,0:T(8,128)(2,1)S(1)}, bf16[64,2048]{1,0:T(8,128)(2,1)S(1)}, u32[]{:S(2)}, u32[]{:S(2)}) collective-permute-start(bf16[64,2048]{1,0:T(8,128)(2,1)S(1)} %get-tuple-element.80), channel_id=1, source_target_pairs={{0,24},{1,25},{2,26},{3,27},{4,28},{5,29},{6,30},{7,31},{8,16},{9,... | collective-permute-start | bytes 786440 | tf_op jit(solution)/shard_map/ppermute | solution.py:610
  460.8 14.5 %collective-permute-start.32 = (bf16[64,2080]{1,0:T(8,128)(2,1)S(1)}, bf16[64,2080]{1,0:T(8,128)(2,1)S(1)}, u32[]{:S(2)}, u32[]{:S(2)}) collective-permute-start(bf16[64,2080]{1,0:T(8,128)(2,1)S(1)} %get-tuple-element.76), channel_id=1, source_target_pairs={{0,8},{1,9},{2,10},{3,11},{4,12},{5,13},{6,14},{7,15},{8,0},{9,1},... | collective-permute-start | bytes 798728 | tf_op jit(solution)/shard_map/ppermute | solution.py:610
  461.2 27.4 %collective-permute-start.33 = (bf16[64,2080]{1,0:T(8,128)(2,1)S(1)}, bf16[64,2080]{1,0:T(8,128)(2,1)S(1)}, u32[]{:S(2)}, u32[]{:S(2)}) collective-permute-start(bf16[64,2080]{1,0:T(8,128)(2,1)S(1)} %get-tuple-element.78), channel_id=1, source_target_pairs={{0,16},{1,17},{2,18},{3,19},{4,20},{5,21},{6,22},{7,23},{8,24},{9,... | collective-permute-start | bytes 798728 | tf_op jit(solution)/shard_map/ppermute | solution.py:610
  462.8 25.9 %collective-permute-start.34 = (bf16[64,2080]{1,0:T(8,128)(2,1)S(1)}, bf16[64,2080]{1,0:T(8,128)(2,1)S(1)}, u32[]{:S(2)}, u32[]{:S(2)}) collective-permute-start(bf16[64,2080]{1,0:T(8,128)(2,1)S(1)} %get-tuple-element.77), channel_id=1, source_target_pairs={{0,24},{1,25},{2,26},{3,27},{4,28},{5,29},{6,30},{7,31},{8,16},{9,... | collective-permute-start | bytes 798728 | tf_op jit(solution)/shard_map/ppermute | solution.py:610
  465.4 24.3 %copy-start.13 = (bf16[64,2,1312]{2,1,0:T(2,128)(2,1)S(1)}, bf16[64,2,1312]{2,1,0:T(2,128)(2,1)}, u32[]{:S(2)}) copy-start(bf16[64,2,1312]{2,1,0:T(2,128)(2,1)} %param.13) | copy-start | bytes 1007620
  465.4 24.0 %collective-permute-start.29 = (bf16[64,2048]{1,0:T(8,128)(2,1)S(1)}, bf16[64,2048]{1,0:T(8,128)(2,1)S(1)}, u32[]{:S(2)}, u32[]{:S(2)}) collective-permute-start(bf16[64,2048]{1,0:T(8,128)(2,1)S(1)} %fusion.29), channel_id=1, source_target_pairs={{0,0},{1,2},{2,1},{3,3},{4,4},{5,6},{6,5},{7,7},{8,8},{9,10},{10,9... | collective-permute-start | bytes 786440 | tf_op jit(solution)/shard_map/ppermute | solution.py:620
  488.8 0.8 collective-permute-start.35
  489.9 14.0 %collective-permute-start.36 = (f32[2,64]{1,0:T(2,128)S(1)}, f32[2,64]{1,0:T(2,128)S(1)}, u32[]{:S(2)}, u32[]{:S(2)}) collective-permute-start(f32[2,64]{1,0:T(2,128)S(1)} %pad_maximum_fusion.12), channel_id=1, source_target_pairs={{0,1},{1,0},{2,3},{3,2},{4,5},{5,4},{6,7},{7,6},{8,9},{9,8},{10,11... | collective-permute-start | bytes 1544 | tf_op jit(solution)/shard_map/ppermute | solution.py:610
  (8 other events, 9.7 us)

commit v4 on v3

--- a/solution.py
+++ b/solution.py
@@ -205,11 +205,28 @@
     }
 
 
-def meet(peers):
+def meet(peers, other=None):
     barrier = pltpu.get_barrier_semaphore()
+    greet = lambda peer: pl.semaphore_signal(
+        barrier, inc=1, device_id=peer, device_id_type=pl.DeviceIdType.MESH
+    )
     for peer in peers.values():
-        pl.semaphore_signal(barrier, inc=1, device_id=peer, device_id_type=pl.DeviceIdType.MESH)
-    pl.semaphore_wait(barrier, len(peers))
+        greet(peer)
+    if other is None:
+        pl.semaphore_wait(barrier, len(peers))
+    else:
+        moved, peer = other
+
+        @pl.when(moved)
+        def _():
+            greet(peer)
+
+        pl.semaphore_wait(barrier, len(peers) + jnp.where(moved, 1, 0))
+
+
+def exchanged():
+    z, x, c, y = place()
+    return c != y, ((z * 2 + x) * 2 + y, c)
 
 
 def remote(src, dst, send_sem, recv_sem, peer):
@@ -588,6 +605,320 @@
     )(xn, cot, w_gate, w_up, w_down, resid)
 
 
+class Reduce:
+    MESSAGES = 12
+    ORDER = (2, 3, 1, 0)
+
+    def __init__(self, parts, near, rows, axes, peers, sems, base, bufs, out):
+        self.parts, self.near, self.rows, self.axes, self.peers = parts, near, rows, axes, peers
+        self.send_sem, self.recv_sem = sems
+        self.base = base
+        self.one, self.two, self.three, self.sum = bufs
+        self.out = out
+
+    def link(self, i, src, dst, peer):
+        n = self.base + i
+        return remote(src, dst, self.send_sem.at[n], self.recv_sem.at[n], peer)
+
+    def first(self, z):
+        if self.axes == "xy":
+            src = self.parts.at[z, :, 1, self.rows]
+        else:
+            src = self.parts.at[z, 1, :, self.rows]
+        return self.link(z, src, self.one.at[z], self.peers[self.axes[1]])
+
+    def second(self, z):
+        return self.link(4 + z, self.one.at[z, 1], self.two.at[z], self.peers[self.axes[0]])
+
+    def third(self, z):
+        return self.link(7 + z, self.two.at[z], self.three.at[z - 1], self.peers["z%d" % z])
+
+    def start(self):
+        for z in self.ORDER:
+            self.first(z).start()
+
+    def relay_first(self, z):
+        self.first(z).wait_recv()
+        self.one[z] = (self.one[z].astype(F32) + self.near(z).astype(F32)).astype(BF)
+        self.second(z).start()
+
+    def relay_second(self, z):
+        self.second(z).wait_recv()
+        self.two[z] = (self.two[z].astype(F32) + self.one[z, 0].astype(F32)).astype(BF)
+        if z:
+            self.third(z).start()
+
+    def last(self):
+        moved, peer = exchanged()
+        return moved, self.link(11, self.sum, self.out, peer)
+
+    def finish(self):
+        total = self.two[0].astype(F32)
+        for z in (1, 2, 3):
+            self.third(z).wait_recv()
+            total = total + self.three[z - 1].astype(F32)
+        self.sum[...] = total.astype(BF)
+        moved, copy = self.last()
+
+        @pl.when(moved)
+        def _():
+            copy.start()
+
+        @pl.when(jnp.logical_not(moved))
+        def _():
+            self.out[...] = self.sum[...]
+
+    def close(self):
+        for z in range(4):
+            self.first(z).wait_send()
+            self.second(z).wait_send()
+            if z:
+                self.third(z).wait_send()
+        moved, copy = self.last()
+
+        @pl.when(moved)
+        def _():
+            copy.wait()
+
+
+def backward_kernel(
+    d_gate, d_up, d_down, q, k, v, o, lse, attn_cot, w_qk, w_vo, xh, x_half, resid_grad,
+    cos, upper, lower, seg_col, seg_row,
+    token_grad, s_gate, s_up, s_down_low, s_down_high, s_qk, s_vo,
+    d_qk, d_vo, pg, heads_grad, kh, dk, dv, own, sent, got, near_gate, near_up, near_low, near_high,
+    *rest,
+):
+    bufs = [rest[4 * i : 4 * i + 4] for i in range(6)]
+    send_sem, recv_sem, pair_send, pair_recv, near_sem = rest[24:]
+    length, width = xh.shape
+    half = length // 2
+    cols = q.shape[1]
+    pairs = cols // 128
+    rows = 256
+    peers = partners()
+    sems = (send_sem, recv_sem)
+    n = Reduce.MESSAGES
+    whole, low, high = pl.ds(0, 64), pl.ds(0, 32), pl.ds(32, 32)
+    held = lambda ref: (lambda z: ref[z])
+    gate = Reduce(d_gate, held(near_gate), whole, "xy", peers, sems, 0, bufs[0], s_gate)
+    up = Reduce(d_up, held(near_up), whole, "yx", peers, sems, n, bufs[1], s_up)
+    down = [
+        Reduce(d_down, held(near_low), low, "xy", peers, sems, 2 * n, bufs[2], s_down_low),
+        Reduce(d_down, held(near_high), high, "yx", peers, sems, 3 * n, bufs[3], s_down_high),
+    ]
+    one = [gate, up]
+    last = [
+        Reduce(d_qk, lambda z: d_qk[z, :, 0], whole, "xy", peers, sems, 4 * n, bufs[4], s_qk),
+        Reduce(d_vo, lambda z: d_vo[z, 0], whole, "yx", peers, sems, 5 * n, bufs[5], s_vo),
+    ]
+    nears = [
+        pltpu.make_async_copy(src, dst, near_sem.at[i])
+        for i, (src, dst) in enumerate(
+            (
+                (d_gate.at[:, :, 0], near_gate),
+                (d_up.at[:, 0], near_up),
+                (d_down.at[:, :, 0, low], near_low),
+                (d_down.at[:, 0, :, high], near_high),
+            )
+        )
+    ]
+    for copy in nears:
+        copy.start()
+    meet(peers, exchanged())
+    for part in one:
+        part.start()
+
+    def heads(here):
+        heads_grad[here, :] = dotf(attn_cot[here, :], w_vo[:, cols:], NN).astype(BF)
+
+    in_chunks(length, 256, heads)
+
+    def out_weights(z, carry):
+        here = pl.ds(pl.multiple_of(z * 256, 256), 256)
+        value = dotf(jnp.transpose(attn_cot[:, here]), o[...], NN).astype(BF)
+        d_vo[z, :, :, :, cols:] = value.reshape(2, 2, 64, cols)
+        return carry
+
+    lax.fori_loop(0, width // 256, out_weights, 0)
+    for copy in nears:
+        copy.wait()
+
+    events = {}
+    for i, z in enumerate(Reduce.ORDER):
+        events.setdefault(2 + 4 * i, []).extend((lambda r=r, z=z: r.relay_first(z)) for r in one)
+    events.setdefault(11, []).extend(r.start for r in down)
+    lane = lax.broadcasted_iota(jnp.int32, (length, 128), 1)
+    first = lane < HD
+
+    def pair(h, carry):
+        lanes = pl.ds(pl.multiple_of(h * 128, 128), 128)
+        kf = k[:, lanes]
+        none = jnp.zeros_like(kf)
+        kh[0] = jnp.where(first, kf, none)
+        kh[1] = jnp.where(first, none, kf)
+        dk[...] = jnp.zeros_like(dk)
+        dv[...] = jnp.zeros_like(dv)
+
+        def block(i, carry):
+            for step, calls in events.items():
+
+                @pl.when(h * (length // rows) + i == step)
+                def _():
+                    for call in calls:
+                        call()
+
+            at = pl.multiple_of(i * rows, rows)
+            here = pl.ds(at, rows)
+            q_rows = q[here, lanes]
+            g_rows = heads_grad[here, lanes]
+            same = seg_col[...] == seg_row[:, here]
+            prod = g_rows.astype(F32) * o[here, lanes].astype(F32)
+            f = first[:rows]
+            blank = jnp.zeros_like(q_rows)
+            dq = jnp.zeros((rows, 128), F32)
+            for head in range(2):
+                mine = f if head == 0 else jnp.logical_not(f)
+                q_head = jnp.where(mine, q_rows, blank)
+                g_head = jnp.where(mine, g_rows, blank)
+                delta = lax.dot_general(
+                    jnp.ones((8, 128), F32),
+                    jnp.where(mine, prod, 0.0),
+                    (NT, ((), ())),
+                    precision=lax.Precision.HIGHEST,
+                    preferred_element_type=F32,
+                )[0:1, :]
+                scores = dotf(k[:, lanes], q_head, NT)
+                level = lse[h, pl.ds(head, 1), here]
+                probs = jnp.where(same, jnp.exp(scores - level), 0.0)
+                dv[...] += dotf(probs.astype(BF), g_head, NN)
+                dp = dotf(v[:, lanes], g_head, NT)
+                ds = (probs * (dp - delta)).astype(BF)
+                dk[...] += dotf(ds, q_head, NN)
+                dq = dq + dotf(ds, kh[head], TN)
+            dq = dq * (1.0 / math.sqrt(HD))
+            c, a, b = cos[here, :], upper[here, :], lower[here, :]
+            pg[0, here, lanes] = (dq * c - turn(dq, a, b)).astype(BF)
+            return carry
+
+        lax.fori_loop(0, length // rows, block, 0)
+        dkf = dk[...]
+        pg[1, :, lanes] = (dkf * cos[...] - turn(dkf, upper[...], lower[...])).astype(BF)
+        pg[2, :, lanes] = dv[...].astype(BF)
+        return carry
+
+    lax.fori_loop(0, pairs, pair, 0)
+
+    def weights(z, carry):
+        left = jnp.transpose(xh[:, pl.ds(pl.multiple_of(z * 256, 256), 256)])
+        for i, (ref, at) in enumerate(((d_qk, 0), (d_qk, cols), (d_vo, 0))):
+            value = dotf(left, pg[i], NN).astype(BF)
+            ref[z, :, :, :, at : at + cols] = value.reshape(2, 2, 64, cols)
+        return carry
+
+    lax.fori_loop(0, width // 256, weights, 0)
+
+    def back(tokens, put):
+        def step(here):
+            total = dotf(pg[0, tokens, :], w_qk[here, :cols], NT)
+            total = total + dotf(pg[1, tokens, :], w_qk[here, cols:], NT)
+            put[:, here] = (total + dotf(pg[2, tokens, :], w_vo[here, :cols], NT)).astype(put.dtype)
+
+        in_chunks(width, 256, step)
+
+    back(pl.ds(half, half), sent)
+    for part in last:
+        part.start()
+    give = remote(sent, got, pair_send.at[0], pair_recv.at[0], peers["c"])
+    give.start()
+    back(pl.ds(0, half), own)
+    for z in Reduce.ORDER:
+        for part in one:
+            part.relay_second(z)
+    give.wait()
+
+    def finish(here):
+        xhat, scale = normalize(to_place(x_half[here, :].astype(F32)))
+        f = own[here, :] + got[here, :].astype(F32)
+        value = resid_grad[here, :] + normalize_back(f, xhat, scale)
+        token_grad[here, :] = to_place(value).astype(BF)
+
+    in_chunks(half, 64, finish)
+    for z in Reduce.ORDER:
+        for part in down:
+            part.relay_first(z)
+    for part in one:
+        part.finish()
+    for z in Reduce.ORDER:
+        for part in down:
+            part.relay_second(z)
+        for part in last:
+            part.relay_first(z)
+    for part in down:
+        part.finish()
+    for z in Reduce.ORDER:
+        for part in last:
+            part.relay_second(z)
+    for part in last:
+        part.finish()
+    for part in one + down + last:
+        part.close()
+
+
+def backward_block(grads, heads, lse, attn_cot, w_qk, w_vo, xh, x_half, resid_grad, tables, seg_col, seg_row):
+    length, width = xh.shape
+    half = length // 2
+    cols = heads[0].shape[1]
+    units = grads[0].shape[1]
+    shard = width // 16
+    vmem = pl.BlockSpec(memory_space=pltpu.VMEM)
+    any_ = pl.BlockSpec(memory_space=pl.ANY)
+    sizes = [(shard, units), (shard, units), (shard // 2, units), (shard // 2, units)]
+    sizes += [(shard, 2 * cols)] * 2
+    bufs = []
+    for size in sizes:
+        bufs += [
+            pltpu.VMEM((4, 2) + size, BF),
+            pltpu.VMEM((4,) + size, BF),
+            pltpu.VMEM((3,) + size, BF),
+            pltpu.VMEM(size, BF),
+        ]
+    messages = 6 * Reduce.MESSAGES
+    return pl.pallas_call(
+        backward_kernel,
+        in_specs=[any_] * 3 + [vmem] * 16,
+        out_specs=[vmem] * 7,
+        out_shape=[jax.ShapeDtypeStruct((half, width), BF)]
+        + [jax.ShapeDtypeStruct(size, BF) for size in sizes],
+        scratch_shapes=[pltpu.VMEM(SHARD + (shard, 2 * cols), BF)] * 2
+        + [
+            pltpu.VMEM((3, length, cols), BF),
+            pltpu.VMEM((length, cols), BF),
+            pltpu.VMEM((2, length, 128), BF),
+            pltpu.VMEM((length, 128), F32),
+            pltpu.VMEM((length, 128), F32),
+            pltpu.VMEM((half, width), F32),
+            pltpu.VMEM((half, width), BF),
+            pltpu.VMEM((half, width), BF),
+        ]
+        + [pltpu.VMEM((4, 2) + size, BF) for size in sizes[:4]]
+        + bufs
+        + [
+            pltpu.SemaphoreType.DMA((messages,)),
+            pltpu.SemaphoreType.DMA((messages,)),
+            pltpu.SemaphoreType.DMA((1,)),
+            pltpu.SemaphoreType.DMA((1,)),
+            pltpu.SemaphoreType.DMA((4,)),
+        ],
+        compiler_params=pltpu.CompilerParams(
+            collective_id=2, has_side_effects=True, vmem_limit_bytes=60 << 20
+        ),
+        name="backward_block",
+    )(
+        *(g.reshape(SHARD + (shard, units)) for g in grads),
+        *heads, lse, attn_cot, w_qk, w_vo, xh, x_half, resid_grad, *tables, seg_col, seg_row,
+    )
+
+
 class Chips:
     def __init__(self):
         self.axes = ("dp", "tensor")
@@ -638,27 +969,6 @@
 
     def gather_rows(self, value):
         return jnp.concatenate([value, self.send(value, dc=1)], axis=0)
-
-    def scatter_rows(self, value):
-        half = value.shape[0] // 2
-        return value[:half] + self.send(value[half:].astype(BF), dc=1).astype(F32)
-
-    def reduce(self, a, b):
-        order = lambda w: w.astype(BF).reshape(4, 2, 2, -1, w.shape[1]).swapaxes(0, 2)
-        a, b = (order(w).reshape(16, -1, w.shape[1]) for w in (a, b))
-        add = lambda u, w: (u.astype(F32) + w.astype(F32)).astype(BF)
-        a = add(a[:8], self.send(a[8:], dy=1))
-        b = add(
-            jnp.concatenate([b[:4], b[8:12]]),
-            self.send(jnp.concatenate([b[4:8], b[12:]]), dx=1),
-        )
-        a = add(a[:4], self.send(a[4:], dx=1))
-        b = add(b[:4], self.send(b[4:], dy=1))
-        sum_a, sum_b = a[0].astype(F32), b[0].astype(F32)
-        for k in (1, 2, 3):
-            sum_a = sum_a + self.send(a[k], dz=k).astype(F32)
-            sum_b = sum_b + self.send(b[k], dz=k).astype(F32)
-        return self.swap(sum_a.astype(BF)).astype(F32), self.swap(sum_b.astype(BF)).astype(F32)
 
     def sum_tensor(self, value):
         return value + self.send(value, dy=1)
@@ -748,8 +1058,6 @@
             w_qk, w_vo, w_gate, w_up, w_dn = (
                 w.reshape(-1, w.shape[-1]) for w in (w_qk, w_vo, w_gate, w_up, w_dn)
             )
-            xh_one, scale_one = normalize(comm.to_relative(x_half).astype(F32))
-            w_o = w_vo[:, cols:]
         else:
             w_qk, w_vo, w_gate, w_up, w_dn = (
                 lax.all_gather(w, "dp", axis=0, tiled=True) for w in owned
@@ -782,27 +1090,36 @@
             d_down = dotf(cot_all, hidden, TN)
             d_gate, d_up = dotf(xn, gate_grad, TN), dotf(xn, up_grad, TN)
 
-        wide = lambda g, d: jnp.concatenate([g if paired else padded(g), d], axis=1)
-        two_a, two_b = comm.reduce(wide(d_gate, d_down[:, :low]), wide(d_up, d_down[:, low:units]))
-
-        heads_grad = dotf(attn_cot, w_o, NN).astype(BF)
-        pg = attn_bwd(q, k, v, o, heads_grad, lse, tables, seg_col, seg_row)
-        d_out = dotf(attn_cot, o, TN)
-        d_q, d_k, d_v = (dotf(xh, pg[i], TN) for i in range(3))
-        one_a, one_b = comm.reduce(
-            jnp.concatenate([d_q, d_k], axis=1), jnp.concatenate([d_v, d_out], axis=1)
-        )
-        f_one = comm.scatter_rows(
-            dotf(pg[0], w_qk[:, :cols], NT)
-            + dotf(pg[1], w_qk[:, cols:], NT)
-            + dotf(pg[2], w_vo[:, :cols], NT)
-        )
-        token_grad = resid_grad + normalize_back(f_one, xh_one, scale_one)
-        token_grad = comm.swap(comm.from_relative(token_grad.astype(BF))).astype(F32)
+        if paired:
+            placed, *sums = backward_block(
+                (d_gate, d_up, d_down), (q, k, v, o), lse, attn_cot, w_qk, w_vo, xh, x_half,
+                resid_grad, tables, seg_col, seg_row,
+            )
+            token_grad = comm.swap(placed).astype(F32)
+            s_gate, s_up, s_low, s_high, one_a, one_b = (w.astype(F32) for w in sums)
+            in_raw = jnp.stack([s_gate[:, :units], s_up[:, :units]], axis=1)
+            down_sum = jnp.concatenate([s_low[:, :units], s_high[:, :units]], axis=0).T
+        else:
+            wide = lambda g, d: jnp.concatenate([padded(g), d], axis=1)
+            two_a, two_b = comm.reduce(wide(d_gate, d_down[:, :low]), wide(d_up, d_down[:, low:]))
+
+            heads_grad = dotf(attn_cot, w_o, NN).astype(BF)
+            pg = attn_bwd(q, k, v, o, heads_grad, lse, tables, seg_col, seg_row)
+            d_out = dotf(attn_cot, o, TN)
+            d_q, d_k, d_v = (dotf(xh, pg[i], TN) for i in range(3))
+            one_a, one_b = comm.reduce(
+                jnp.concatenate([d_q, d_k], axis=1), jnp.concatenate([d_v, d_out], axis=1)
+            )
+            f_one = comm.scatter_rows(
+                dotf(pg[0], w_qk[:, :cols], NT)
+                + dotf(pg[1], w_qk[:, cols:], NT)
+                + dotf(pg[2], w_vo[:, :cols], NT)
+            )
+            token_grad = resid_grad + normalize_back(f_one, xh_one, scale_one)
+            in_raw = jnp.stack([two_a[:, :units], two_b[:, :units]], axis=1)
+            down_sum = jnp.concatenate([two_a[:, units + pad :], two_b[:, units + pad :]], axis=1).T
 
         qkv_raw = jnp.stack([one_a[:, :cols], one_a[:, cols:], one_b[:, :cols]], axis=1)
-        in_raw = jnp.stack([two_a[:, :units], two_b[:, :units]], axis=1)
-        down_sum = jnp.concatenate([two_a[:, units + pad :], two_b[:, units + pad :]], axis=1).T
         gains = jnp.stack(
             [
                 jnp.sum(qkv_raw * w_qkv.astype(F32), axis=(1, 2)),

time: 515 us -> 407 us (0.79); the launches traced: 507 us -> 404 us
  Pallas kernels: 210 us -> 318 us
  waiting for transfers between devices: 110 us -> 18.7 us
  starting transfers between devices: 85.4 us -> 33.7 us
  local copies, waits for them, and re-layouts: 42.8 us -> 14.6 us
  other arithmetic: 40.2 us -> 18.6 us
  matrix products: 17.4 us -> 0 us
    pallas_call x1, Pallas kernels: 34.6 us -> 138 us  [backward_block(): pl.pallas_call(backward_kernel, in_specs=[any_] * 3 + [vmem] * 16, out_sp...]
    ppermute x23 -> x2, waiting for transfers between devices: 109 us -> 18.6 us  [send(): return lax.ppermute(value, self.axes, pairs)]
    ppermute x23 -> x2, starting transfers between devices: 57.1 us -> 15.1 us  [send(): return lax.ppermute(value, self.axes, pairs)]
    dot_general x8 -> x0, matrix products: 17.4 us -> none  [dotf(): return lax.dot_general(a, b, (dims, ((), ())), preferred_element_type=F32)]
    convert_element_type x18 -> x2, other arithmetic: 15.4 us -> 1.88 us  [local(): s_gate, s_up, s_low, s_high, one_a, one_b = (w.astype(F32) for w in sums)]
    slice x13 -> x0, local copies, waits for them, and re-layouts: 11.8 us -> none  [the longest x1 2.86 us: local(): d_down[:, low:units]]
    ppermute x14 -> x10, starting transfers between devices: 28.3 us -> 18.7 us  [swap(): return lax.ppermute(value, self.axes, pairs)]
    unnamed x75 -> x30, local copies, waits for them, and re-layouts: 13.8 us -> 4.94 us
  transfers between devices with their start and end apart: 37 -> 12, of which waited for: 10 -> 1; matrix products, arithmetic and copies ran while one was open for 13% -> 6% of each run, Pallas kernels for 25% -> 33%
where the time goes in v4:
time: 407 us; the launch traced here: 404 us
  Pallas kernels  318 us (78%)
  starting transfers between devices  33.7 us (8%)
  waiting for transfers between devices  18.7 us (5%)
  other arithmetic  18.6 us (5%)
  local copies, waits for them, and re-layouts  14.6 us (4%)
    pallas_call x1, Pallas kernels, backward_block(): pl.pallas_call(backward_kernel, in_specs=[any_] * 3 + [vmem] * 16, out_sp...  138 us
    pallas_call x1, Pallas kernels, forward_block(): pl.pallas_call(forward_kernel, in_specs=[any_] * 5 + [vmem] * 6, out_spec...  132 us
    pallas_call x1, Pallas kernels, mlp_block(): pl.pallas_call(mlp_kernel, in_specs=[vmem] * 6, out_specs=[vmem] * 6, out...  47.4 us
    ppermute x10, starting transfers between devices, swap(): return lax.ppermute(value, self.axes, pairs)  18.7 us
    ppermute x2, waiting for transfers between devices, send(): return lax.ppermute(value, self.axes, pairs)  18.6 us
    ppermute x2, starting transfers between devices, send(): return lax.ppermute(value, self.axes, pairs)  15.1 us
  transfers between devices with their start and end apart: 12, of which 1 were waited for; matrix products, arithmetic and copies ran while one was open for 6% of the time, Pallas kernels for 33%

profile of v4, /device:TPU:0, one launch (start us, length us, event | category | flops | bytes accessed | tf_op | source)
XLA Modules:
  0.0 404.4 jit_solution(17509797583894331731)
XLA Ops:
  0.6 0.0 copy-start.2
  0.7 1.5 collective-permute-start.6
  2.1 1.6 pad.12
  3.7 2.9 collective-permute-start.4
  6.7 1.5 copy.24
  8.2 0.7 collective-permute-start.7
  9.0 0.7 fusion.5
  9.7 0.7 pad_maximum_fusion.6
  10.4 2.1 collective-permute-start
  12.5 1.9 collective-permute-start.5
  14.4 3.0 multiply_sine_fusion
  17.4 1.9 pad_maximum_fusion.3
  19.3 0.0 collective-permute-done.7
  19.3 0.2 reverse_select_fusion.3
  19.5 0.2 reverse_select_fusion.2
  19.7 0.2 reverse_select_fusion.1
  20.0 0.2 reverse_select_fusion
  20.2 0.0 copy-start.12
  20.2 0.0 copy-start.1
  20.2 0.5 copy.26
  20.7 0.0 copy-start.4
  20.7 0.0 copy-start.7
  20.8 7.7 %collective-permute-start.8 = (bf16[512,1024]{1,0:T(8,128)(2,1)S(1)}, bf16[512,1024]{1,0:T(8,128)(2,1)S(1)}, u32[]{:S(2)}, u32[]{:S(2)}) collective-permute-start(bf16[512,1024]{1,0:T(8,128)(2,1)S(1)} %copy.26), channel_id=1, source_target_pairs={{0,2},{1,3},{2,0},{3,1},{4,6},{5,7},{6,4},{7,5},{8,10},{9,11},{10,... | collective-permute-start | bytes 3145736 | tf_op jit(solution)/shard_map/ppermute | solution.py:941
  28.5 3.0 pad_maximum_fusion.1.cos
  31.6 0.9 fusion.1
  32.5 0.7 pad_maximum_fusion.7
  33.1 1.6 pad.11
  34.7 1.6 pad.10
  36.3 0.0 collective-permute-done.6
  36.3 2.1 collective-permute-start.1
  38.5 0.0 collective-permute-done.a_own
  38.5 3.0 collective-permute-start.2
  41.5 0.0 collective-permute-done.1.b_own
  41.5 2.9 collective-permute-start.3
  44.4 0.0 copy-start.8
  44.4 1.0 copy.23.seg_col
  45.4 0.0 collective-permute-done.4.d_own
  45.5 0.0 collective-permute-done.2.g_own
  45.5 0.0 collective-permute-done.3.u_own
  45.5 0.0 copy-start
  45.5 1.0 copy-done
  46.4 132.0 %forward_block.1 = (bf16[1024,512]{1,0:T(8,128)(2,1)}, bf16[1024,512]{1,0:T(8,128)(2,1)}, bf16[1024,512]{1,0:T(8,128)(2,1)}, bf16[1024,512]{1,0:T(8,128)(2,1)}, ...) custom-call(bf16[64,1024]{1,0:T(8,128)(2,1)} %collective-permute-don, ...), custom_call_target="tpu_custom_call" | custom-call | tf_op jit(solution)/shard_map/forward_block/pallas_call | solution.py:470
  178.5 0.0 collective-permute-done.8
  178.5 1.5 pad_maximum_fusion.cot
  180.0 47.4 %mlp_block.1 = (bf16[512,1024]{1,0:T(8,128)(2,1)}, f32[512,1024]{1,0:T(8,128)}, bf16[1024,1024]{1,0:T(8,128)(2,1)}, bf16[1024,1408]{1,0:T(8,128)(2,1)}, bf16[102...) custom-call(bf16[1024,1024]{1,0:T(8,128)(2,1)} %get-tuple-element.34.xn, bf16[1024,1024]{1,0:T(8,128)(2,1)} %pad_maximum_fusion.cot, ...), custom_call_target="tpu_custom_call" | custom-call | tf_op jit(solution)/shard_map/mlp_block/pallas_call | solution.py:581
  227.4 138.4 %backward_block.1 = (bf16[512,1024]{1,0:T(8,128)(2,1)}, bf16[64,1408]{1,0:T(8,128)(2,1)}, bf16[64,1408]{1,0:T(8,128)(2,1)}, bf16[32,1408]{1,0:T(8,128)(2,1)}, bf...) custom-call(bf16[4,2,2,64,1408]{4,3,2,1,0:T(8,128)(2,1)} %bitcast.66, ...), custom_call_target="tpu_custom_call" | custom-call | tf_op jit(solution)/shard_map/backward_block/pallas_call | solution.py:886
  365.8 0.0 copy-start.3
  365.8 1.1 slice_bitcast_fusion.3
  366.9 0.9 slice_bitcast_fusion.2
  367.9 1.0 convert_element_type.105
  368.9 0.9 convert_element_type.106
  369.8 0.7 slice_bitcast_fusion.4
  370.5 0.7 collective-permute-start.10
  371.2 0.7 collective-permute-start.9
  372.0 0.9 fusion.3
  372.9 0.2 convert_multiply_fusion
  373.2 7.3 %collective-permute-start.11 = (f32[2,64]{1,0:T(2,128)S(1)}, f32[2,64]{1,0:T(2,128)S(1)}, u32[]{:S(2)}, u32[]{:S(2)}) collective-permute-start(f32[2,64]{1,0:T(2,128)S(1)} %pad_maximum_fusion.8), channel_id=1, source_target_pairs={{0,1},{1,0},{2,3},{3,2},{4,5},{5,4},{6,7},{7,6},{8,9},{9,8},{10,11... | collective-permute-start | bytes 1544 | tf_op jit(solution)/shard_map/ppermute | solution.py:941
  380.5 0.8 convert_bitcast_fusion
  381.3 1.4 copy.29
  382.7 18.6 %collective-permute-done.11 = f32[2,64]{1,0:T(2,128)S(1)} collective-permute-done((f32[2,64]{1,0:T(2,128)S(1)}, f32[2,64]{1,0:T(2,128)S(1)}, u32[]{:S(2)}, u32[]{:S(2)}) %collective-permute-start.11) | collective-permute-done | bytes 544 | tf_op jit(solution)/shard_map/ppermute | solution.py:941
  401.3 0.5 slice_bitcast_fusion.8
  401.8 0.0 collective-permute-done.9
  401.8 1.6 bitcast_convert_fusion
  403.4 1.0 copy.32
  (31 shorter events, 0.2 us)
Async XLA Ops:
  0.6 8.3 %copy-start.11 = (bf16[64]{0:T(256)(128)(2,1)S(1)}, bf16[64]{0:T(256)(128)(2,1)}, u32[]{:S(2)}) copy-start(bf16[64]{0:T(256)(128)(2,1)} %param.15) | copy-start | bytes 388
  0.6 8.3 %copy-start.2 = (bf16[64,3,512]{2,0,1:T(8,128)(2,1)S(1)}, bf16[64,3,512]{2,0,1:T(8,128)(2,1)}, u32[]{:S(2)}) copy-start(bf16[64,3,512]{2,0,1:T(8,128)(2,1)} %param.11) | copy-start | bytes 589828
  0.7 35.7 %collective-permute-start.6 = (s32[1024]{0:T(1024)}, s32[1024]{0:T(1024)S(1)}, u32[]{:S(2)}, u32[]{:S(2)}) collective-permute-start(s32[1024]{0:T(1024)} %bitcast.86), channel_id=1, source_target_pairs={{0,0},{1,2},{2,1},{3,3},{4,4},{5,6},{6,5},{7,7},{8,8},{9,10},{10,9... | collective-permute-start | bytes 12296 | tf_op jit(solution)/shard_map/ppermute | solution.py:951
  3.7 41.7 %collective-permute-start.4 = (bf16[64,1408]{1,0:T(8,128)(2,1)}, bf16[64,1408]{1,0:T(8,128)(2,1)}, u32[]{:S(2)}, u32[]{:S(2)}) collective-permute-start(bf16[64,1408]{1,0:T(8,128)(2,1)} %pad.12), channel_id=1, source_target_pairs={{0,0},{1,2},{2,1},{3,3},{4,4},{5,6},{6,5},{7,7},{8,8},{9,10},{10,9... | collective-permute-start | bytes 540680 | tf_op jit(solution)/shard_map/ppermute | solution.py:951
  8.2 11.1 %collective-permute-start.7 = (bf16[512,1024]{0,1:T(8,128)(2,1)S(1)}, bf16[512,1024]{0,1:T(8,128)(2,1)S(1)}, u32[]{:S(2)}, u32[]{:S(2)}) collective-permute-start(bf16[512,1024]{0,1:T(8,128)(2,1)S(1)} %bitcast.72), channel_id=1, source_target_pairs={{0,0},{1,2},{2,1},{3,3},{4,4},{5,6},{6,5},{7,7},{8,8},{9,10},{10,9... | collective-permute-start | bytes 3145736 | tf_op jit(solution)/shard_map/ppermute | solution.py:951
  10.4 28.1 %collective-permute-start = (bf16[64,1024]{1,0:T(8,128)(2,1)}, bf16[64,1024]{1,0:T(8,128)(2,1)}, u32[]{:S(2)}, u32[]{:S(2)}) collective-permute-start(bf16[64,1024]{1,0:T(8,128)(2,1)} %pad_maximum_fusion.6), channel_id=1, source_target_pairs={{0,0},{1,2},{2,1},{3,3},{4,4},{5,6},{6,5},{7,7},{8,8},{9,10},{10,9... | collective-permute-start | bytes 393224 | tf_op jit(solution)/shard_map/ppermute | solution.py:951
  12.5 33.0 %collective-permute-start.5 = (bf16[512,1024]{1,0:T(8,128)(2,1)}, bf16[512,1024]{1,0:T(8,128)(2,1)S(1)}, u32[]{:S(2)}, u32[]{:S(2)}) collective-permute-start(bf16[512,1024]{1,0:T(8,128)(2,1)} %bitcast.85), channel_id=1, source_target_pairs={{0,0},{1,2},{2,1},{3,3},{4,4},{5,6},{6,5},{7,7},{8,8},{9,10},{10,9... | collective-permute-start | bytes 3145736 | tf_op jit(solution)/shard_map/ppermute | solution.py:951
  20.2 11.4 %copy-start.12 = (bf16[64]{0:T(256)(128)(2,1)S(1)}, bf16[64]{0:T(256)(128)(2,1)}, u32[]{:S(2)}) copy-start(bf16[64]{0:T(256)(128)(2,1)} %param.16) | copy-start | bytes 388
  20.2 11.4 %copy-start.1 = (bf16[64,2,1312]{2,1,0:T(2,128)(2,1)S(1)}, bf16[64,2,1312]{2,1,0:T(2,128)(2,1)}, u32[]{:S(2)}) copy-start(bf16[64,2,1312]{2,1,0:T(2,128)(2,1)} %param.13) | copy-start | bytes 1007620
  20.7 11.7 %copy-start.4 = (bf16[64,512]{1,0:T(8,128)(2,1)S(1)}, bf16[64,512]{1,0:T(8,128)(2,1)}, u32[]{:S(2)}) copy-start(bf16[64,512]{1,0:T(8,128)(2,1)} %get-tuple-element.88) | copy-start | bytes 196612
  20.7 11.7 %copy-start.7 = (bf16[512,64]{0,1:T(8,128)(2,1)S(1)}, bf16[512,64]{0,1:T(8,128)(2,1)}, u32[]{:S(2)}) copy-start(bf16[512,64]{0,1:T(8,128)(2,1)} %param.12) | copy-start | bytes 196612
  20.8 157.7 %collective-permute-start.8 = (bf16[512,1024]{1,0:T(8,128)(2,1)S(1)}, bf16[512,1024]{1,0:T(8,128)(2,1)S(1)}, u32[]{:S(2)}, u32[]{:S(2)}) collective-permute-start(bf16[512,1024]{1,0:T(8,128)(2,1)S(1)} %copy.26), channel_id=1, source_target_pairs={{0,2},{1,3},{2,0},{3,1},{4,6},{5,7},{6,4},{7,5},{8,10},{9,11},{10,... | collective-permute-start | bytes 3145736 | tf_op jit(solution)/shard_map/ppermute | solution.py:941
  36.3 5.1 %collective-permute-start.1 = (bf16[64,1024]{1,0:T(8,128)(2,1)}, bf16[64,1024]{1,0:T(8,128)(2,1)}, u32[]{:S(2)}, u32[]{:S(2)}) collective-permute-start(bf16[64,1024]{1,0:T(8,128)(2,1)} %pad_maximum_fusion.7), channel_id=1, source_target_pairs={{0,0},{1,2},{2,1},{3,3},{4,4},{5,6},{6,5},{7,7},{8,8},{9,10},{10,9... | collective-permute-start | bytes 393224 | tf_op jit(solution)/shard_map/ppermute | solution.py:951
  38.5 7.0 %collective-permute-start.2 = (bf16[64,1408]{1,0:T(8,128)(2,1)}, bf16[64,1408]{1,0:T(8,128)(2,1)}, u32[]{:S(2)}, u32[]{:S(2)}) collective-permute-start(bf16[64,1408]{1,0:T(8,128)(2,1)} %pad.10), channel_id=1, source_target_pairs={{0,0},{1,2},{2,1},{3,3},{4,4},{5,6},{6,5},{7,7},{8,8},{9,10},{10,9... | collective-permute-start | bytes 540680 | tf_op jit(solution)/shard_map/ppermute | solution.py:951
  41.5 4.0 collective-permute-start.3
  44.4 1.1 copy-start.8
  45.5 1.0 copy-start
  365.8 4.7 %copy-start.10 = (bf16[512,1024]{1,0:T(8,128)(2,1)S(1)}, bf16[512,1024]{1,0:T(8,128)(2,1)}, u32[]{:S(2)}) copy-start(bf16[512,1024]{1,0:T(8,128)(2,1)} %get-tuple-element.53) | copy-start | bytes 3145732
  365.8 5.4 %copy-start.9 = (bf16[512,1024]{1,0:T(8,128)(2,1)S(1)}, bf16[512,1024]{1,0:T(8,128)(2,1)}, u32[]{:S(2)}) copy-start(bf16[512,1024]{1,0:T(8,128)(2,1)} %get-tuple-element.39) | copy-start | bytes 3145732
  365.8 6.1 %copy-start.3 = (bf16[64,3,512]{2,0,1:T(8,128)(2,1)S(1)}, bf16[64,3,512]{2,0,1:T(8,128)(2,1)}, u32[]{:S(2)}) copy-start(bf16[64,3,512]{2,0,1:T(8,128)(2,1)} %param.11) | copy-start | bytes 589828
  367.9 12.6 %copy-start.5 = (bf16[32,1408]{1,0:T(8,128)(2,1)S(1)}, bf16[32,1408]{1,0:T(8,128)(2,1)}, u32[]{:S(2)}) copy-start(bf16[32,1408]{1,0:T(8,128)(2,1)} %get-tuple-element.58) | copy-start | bytes 270340
  367.9 12.6 %copy-start.6 = (bf16[32,1408]{1,0:T(8,128)(2,1)S(1)}, bf16[32,1408]{1,0:T(8,128)(2,1)}, u32[]{:S(2)}) copy-start(bf16[32,1408]{1,0:T(8,128)(2,1)} %get-tuple-element.59) | copy-start | bytes 270340
  370.5 31.3 %collective-permute-start.10 = (bf16[512,1024]{1,0:T(8,128)(2,1)S(1)}, bf16[512,1024]{1,0:T(8,128)(2,1)S(1)}, u32[]{:S(2)}, u32[]{:S(2)}) collective-permute-start(bf16[512,1024]{1,0:T(8,128)(2,1)S(1)} %copy-done.10), channel_id=1, source_target_pairs={{0,0},{1,2},{2,1},{3,3},{4,4},{5,6},{6,5},{7,7},{8,8},{9,10},{10,9... | collective-permute-start | bytes 3145736 | tf_op jit(solution)/shard_map/ppermute | solution.py:951
  371.2 30.6 %collective-permute-start.9 = (bf16[512,1024]{1,0:T(8,128)(2,1)S(1)}, bf16[512,1024]{1,0:T(8,128)(2,1)S(1)}, u32[]{:S(2)}, u32[]{:S(2)}) collective-permute-start(bf16[512,1024]{1,0:T(8,128)(2,1)S(1)} %copy-done.9), channel_id=1, source_target_pairs={{0,0},{1,2},{2,1},{3,3},{4,4},{5,6},{6,5},{7,7},{8,8},{9,10},{10,9... | collective-permute-start | bytes 3145736 | tf_op jit(solution)/shard_map/ppermute | solution.py:951
  373.2 28.1 %collective-permute-start.11 = (f32[2,64]{1,0:T(2,128)S(1)}, f32[2,64]{1,0:T(2,128)S(1)}, u32[]{:S(2)}, u32[]{:S(2)}) collective-permute-start(f32[2,64]{1,0:T(2,128)S(1)} %pad_maximum_fusion.8), channel_id=1, source_target_pairs={{0,1},{1,0},{2,3},{3,2},{4,5},{5,4},{6,7},{7,6},{8,9},{9,8},{10,11... | collective-permute-start | bytes 1544 | tf_op jit(solution)/shard_map/ppermute | solution.py:941

commit v5 on v4

--- a/solution.py
+++ b/solution.py
@@ -23,10 +23,12 @@
 TN = ((0,), (0,))
 
 
+def rope_rates():
+    return 1.0 / ROTARY_BASE ** (jnp.arange(HD // 2).astype(F32) * (2.0 / HD))
+
+
 def rope_tables(positions):
-    half = HD // 2
-    inverse = 1.0 / ROTARY_BASE ** (jnp.arange(half).astype(F32) * (2.0 / HD))
-    angles = positions.astype(F32)[:, None] * inverse[None, :]
+    angles = positions.astype(F32)[:, None] * rope_rates()[None, :]
     cos, sin = jnp.cos(angles), jnp.sin(angles)
     zero = jnp.zeros_like(sin)
     cosine = jnp.concatenate([cos] * 4, axis=-1)
@@ -184,6 +186,16 @@
     )(q, k, v, o, do, lse, *tables, seg_col, seg_row)
 
 
+def in_chunks(total, size, body):
+    def step(j, carry):
+        body(pl.ds(pl.multiple_of(j * size, size), size))
+        return carry
+
+    lax.fori_loop(0, total // size, step, 0)
+    if total % size:
+        body(pl.ds(total - total % size, total % size))
+
+
 SHARD = (4, 2, 2)
 
 
@@ -240,7 +252,37 @@
     )
 
 
-def to_place(values, inverse=False):
+class Move:
+    def __init__(self, src, dst, sems, i):
+        send_sem, recv_sem, near_sem = sems
+        self.moved, peer = exchanged()
+        self.far = remote(src, dst, send_sem.at[i], recv_sem.at[i], peer)
+        self.near = pltpu.make_async_copy(src, dst, near_sem.at[i])
+
+    def start(self):
+        @pl.when(self.moved)
+        def _():
+            self.far.start()
+
+        @pl.when(jnp.logical_not(self.moved))
+        def _():
+            self.near.start()
+
+    def wait(self):
+        @pl.when(self.moved)
+        def _():
+            self.far.wait()
+
+        @pl.when(jnp.logical_not(self.moved))
+        def _():
+            self.near.wait()
+
+
+def move_sems(n):
+    return [pltpu.SemaphoreType.DMA((n,))] * 3
+
+
+def to_place(values):
     z, x, _, y = place()
     tiles = [values[:, j * 128 : (j + 1) * 128] for j in range(8)]
     tiles = [jnp.where(y == 1, pltpu.roll(t, 64, 1), t) for t in tiles]
@@ -297,15 +339,18 @@
 
 
 def forward_kernel(
-    a_own, b_own, g_own, u_own, d_own, x_half, cos, upper, lower, seg_col, seg_row,
-    q, k, v, o, lse, xh, w_qk, w_vo, resid, xn, w_gate, w_up, w_down,
-    kh, x_rel, part, sent, got, send_sem, recv_sem, pair_send, pair_recv, own_sem,
+    a_in, b_in, g_in, u_in, d_in, x_in, c_in, seg_in, inverse,
+    q, k, v, o, lse, xh, w_qk, w_vo, resid, xn, x_half, cot, cos, upper, lower, seg_col, seg_row,
+    w_gate, w_up, w_down,
+    a_own, b_own, g_own, u_own, d_own, c_own, seg_own,
+    kh, x_rel, part, sent, got, send_sem, recv_sem, pair_send, pair_recv, own_sem, *moving,
 ):
     length = xh.shape[0]
     half = length // 2
     width = xh.shape[1]
     pairs = q.shape[1] // 128
     rows = 256
+    core = place()[2]
     peers = partners()
     sems = (send_sem, recv_sem)
     n = Gather.MESSAGES
@@ -328,13 +373,51 @@
             ((a_own, w_qk), (b_own, w_vo), (g_own, w_gate), (u_own, w_up), (d_own, w_down))
         )
     ]
-    for copy in owns:
-        copy.start()
-    meet(peers)
+    move_a, move_b, move_x, move_seg, move_g, move_u, move_d, move_c = (
+        Move(src, dst, moving, i)
+        for i, (src, dst) in enumerate(
+            (
+                (a_in, a_own),
+                (b_in, b_own),
+                (x_in, x_half),
+                (seg_in, seg_own),
+                (g_in, g_own),
+                (u_in, u_own),
+                (d_in, d_own),
+                (c_in, c_own),
+            )
+        )
+    )
+    meet(peers, exchanged())
+    for move in (move_a, move_b, move_seg, move_x, move_g, move_u, move_d):
+        move.start()
+
+    def tables(here):
+        shape = (here.size, 128)
+        row = here.start + lax.broadcasted_iota(jnp.int32, shape, 0) + core * half
+        row = jnp.where(row >= length, row - length, row)
+        angle = row.astype(F32) * inverse[0:1, :]
+        front = lax.broadcasted_iota(jnp.int32, shape, 1) % HD < HD // 2
+        sin = jnp.sin(angle)
+        cos[here, :] = jnp.cos(angle)
+        upper[here, :] = jnp.where(front, -sin, 0.0)
+        lower[here, :] = jnp.where(front, 0.0, sin)
+
+    move_a.wait()
+    move_b.wait()
     for gather in one:
         gather.start_z()
     for gather in one:
         gather.relay_z(0)
+    for copy in owns[:2]:
+        copy.start()
+    in_chunks(length, 64, tables)
+    move_seg.wait()
+    ids = seg_own[...]
+    ids = jnp.where(core == 0, ids, jnp.concatenate([ids[:, half:], ids[:, :half]], axis=1))
+    seg_row[...] = ids
+    seg_col[...] = jnp.transpose(jnp.broadcast_to(ids[0:1, :], (128, length)))
+    move_x.wait()
 
     def first_norm(i, carry):
         here = pl.ds(pl.multiple_of(i * 128, 128), 128)
@@ -351,17 +434,22 @@
         xh.at[pl.ds(0, half)], xh.at[pl.ds(half, half)], pair_send.at[0], pair_recv.at[0], peers["c"]
     )
     swap_xh.start()
+    move_g.wait()
+    move_u.wait()
     for gather in two:
         gather.start_z()
     for z in range(4):
         for gather in one:
             gather.relay_first(z)
+    move_d.wait()
     for gather in three:
         gather.start_z()
+    for copy in owns[2:]:
+        copy.start()
     swap_xh.wait()
     for gather in one:
         gather.finish()
-    for copy in owns:
+    for copy in owns[:2]:
         copy.wait()
 
     events = {}
@@ -369,6 +457,7 @@
         events.setdefault(1 + z, []).extend((g.relay_z, z) for g in two)
         events.setdefault(6 + z, []).extend((g.relay_first, z) for g in two)
         events.setdefault(9 + z, []).extend((g.relay_z, z) for g in three)
+    events.setdefault(5, []).append((lambda _: move_c.start(), 0))
     first = lax.broadcasted_iota(jnp.int32, (length, 128), 1) < HD
 
     def pair(h, carry):
@@ -396,7 +485,7 @@
 
             at = pl.multiple_of(i * rows, rows)
             q_rows = q[pl.ds(at, rows), lanes]
-            same = seg_col[pl.ds(at, rows), :] == seg_row[...]
+            same = seg_col[pl.ds(at, rows), 0:1] == seg_row[0:1, :]
             outs = []
             for head in range(2):
                 scores = dotf(q_rows, kh[head], NT)
@@ -434,10 +523,19 @@
     give = remote(sent, got, pair_send.at[1], pair_recv.at[1], peers["c"])
     lax.fori_loop(0, half // rows, project_own, 0)
     give.start()
-    for gather in two + three:
+    move_c.wait()
+
+    def turn_cot(here):
+        cot[here, :] = to_place(c_own[here, :].astype(F32)).astype(BF)
+
+    in_chunks(half, 128, turn_cot)
+    swap_cot = remote(
+        cot.at[pl.ds(0, half)], cot.at[pl.ds(half, half)], pair_send.at[3], pair_recv.at[3], peers["c"]
+    )
+    swap_cot.start()
+    for gather in three:
         for z in range(4):
-            if gather in three:
-                gather.relay_first(z)
+            gather.relay_first(z)
     give.wait()
 
     def second_norm(i, carry):
@@ -454,34 +552,48 @@
     swap_xn.start()
     for gather in two + three:
         gather.finish()
+    for copy in owns[2:]:
+        copy.wait()
+    swap_cot.wait()
     swap_xn.wait()
 
 
-def forward_block(owned, x_half, tables, seg_col, seg_row):
+def forward_block(owned, x_half, cot_half, seg, inverse):
     half, width = x_half.shape
     length = 2 * half
     cols = owned[0].shape[1] // 2
     pairs = cols // 128
     units = owned[2].shape[1]
+    shard = width // 16
     vmem = pl.BlockSpec(memory_space=pltpu.VMEM)
     any_ = pl.BlockSpec(memory_space=pl.ANY)
-    gathered = lambda n: jax.ShapeDtypeStruct(SHARD + (width // 16, n), BF)
+    gathered = lambda n: jax.ShapeDtypeStruct(SHARD + (shard, n), BF)
     heads = jax.ShapeDtypeStruct((length, cols), BF)
+    flat = jax.ShapeDtypeStruct((length, width), BF)
+    table = jax.ShapeDtypeStruct((length, 128), F32)
     return pl.pallas_call(
         forward_kernel,
-        in_specs=[any_] * 5 + [vmem] * 6,
-        out_specs=[vmem] * 10 + [any_] * 3,
+        in_specs=[any_] * 8 + [vmem],
+        out_specs=[vmem] * 17 + [any_] * 3,
         out_shape=[heads] * 4
         + [
             jax.ShapeDtypeStruct((pairs, 2, length), F32),
-            jax.ShapeDtypeStruct((length, width), BF),
+            flat,
             gathered(2 * cols),
             gathered(2 * cols),
             jax.ShapeDtypeStruct((half, width), F32),
-            jax.ShapeDtypeStruct((length, width), BF),
+            flat,
+            jax.ShapeDtypeStruct((half, width), BF),
+            flat,
         ]
+        + [table] * 4
+        + [jax.ShapeDtypeStruct((8, length), F32)]
         + [gathered(units)] * 3,
-        scratch_shapes=[
+        scratch_shapes=[pltpu.VMEM((shard, 2 * cols), BF)] * 2
+        + [pltpu.VMEM((shard, units), BF)] * 3
+        + [
+            pltpu.VMEM((half, width), BF),
+            pltpu.VMEM((8, length), F32),
             pltpu.VMEM((2, length, 128), BF),
             pltpu.VMEM((half, width), BF),
             pltpu.VMEM((half, width), F32),
@@ -489,35 +601,29 @@
             pltpu.VMEM((half, width), BF),
             pltpu.SemaphoreType.DMA((6 * Gather.MESSAGES,)),
             pltpu.SemaphoreType.DMA((6 * Gather.MESSAGES,)),
-            pltpu.SemaphoreType.DMA((3,)),
-            pltpu.SemaphoreType.DMA((3,)),
+            pltpu.SemaphoreType.DMA((4,)),
+            pltpu.SemaphoreType.DMA((4,)),
             pltpu.SemaphoreType.DMA((5,)),
-        ],
-        compiler_params=pltpu.CompilerParams(collective_id=0, has_side_effects=True),
+        ]
+        + move_sems(8),
+        compiler_params=pltpu.CompilerParams(
+            collective_id=0, has_side_effects=True, vmem_limit_bytes=60 << 20
+        ),
         name="forward_block",
-    )(*owned, x_half, *tables, seg_col, seg_row)
-
-
-def in_chunks(total, size, body):
-    def step(j, carry):
-        body(pl.ds(pl.multiple_of(j * size, size), size))
-        return carry
-
-    lax.fori_loop(0, total // size, step, 0)
-    if total % size:
-        body(pl.ds(total - total % size, total % size))
+    )(*owned, x_half, cot_half, seg, inverse)
 
 
 def mlp_kernel(
     xn, cot, w_gate, w_up, w_down, resid,
     result, resid_grad, attn_cot, d_gate, d_up, d_down,
-    hidden, gate_grad, up_grad, own, sent, got, send_sem, recv_sem,
+    hidden, gate_grad, up_grad, own, sent, got, placed, send_sem, recv_sem, *moving,
 ):
     length, width = xn.shape
     half = length // 2
     units = w_gate.shape[1]
     peer = partners()["c"]
-    meet({"c": peer})
+    meet({"c": peer}, exchanged())
+    move = Move(placed, result, moving, 0)
 
     def units_of(rows, cols):
         gate = dotf(xn[rows, :], w_gate[:, cols], NN)
@@ -548,7 +654,7 @@
     def finish(here):
         values = resid[here, :]
         mlp = own[0, here, :] + got[0, here, :].astype(F32)
-        result[here, :] = to_place(values + mlp).astype(BF)
+        placed[here, :] = to_place(values + mlp).astype(BF)
         xhat, scale = normalize(values)
         back = normalize_back(own[1, here, :] + got[1, here, :].astype(F32), xhat, scale)
         grad = cot[here, :].astype(F32) + back
@@ -560,6 +666,7 @@
         attn_cot.at[pl.ds(0, half)], attn_cot.at[pl.ds(half, half)], send_sem.at[1], recv_sem.at[1], peer
     )
     swap.start()
+    move.start()
 
     def weights(here):
         left = jnp.transpose(cot[:, here])
@@ -570,6 +677,7 @@
 
     in_chunks(width, 256, weights)
     swap.wait()
+    move.wait()
 
 
 def mlp_block(xn, cot, w_gate, w_up, w_down, resid):
@@ -595,9 +703,11 @@
             pltpu.VMEM((2, half, width), F32),
             pltpu.VMEM((2, half, width), BF),
             pltpu.VMEM((2, half, width), BF),
+            pltpu.VMEM((half, width), BF),
             pltpu.SemaphoreType.DMA((2,)),
             pltpu.SemaphoreType.DMA((2,)),
-        ],
+        ]
+        + move_sems(1),
         compiler_params=pltpu.CompilerParams(
             collective_id=1, has_side_effects=True, vmem_limit_bytes=60 << 20
         ),
@@ -685,11 +795,11 @@
     d_gate, d_up, d_down, q, k, v, o, lse, attn_cot, w_qk, w_vo, xh, x_half, resid_grad,
     cos, upper, lower, seg_col, seg_row,
     token_grad, s_gate, s_up, s_down_low, s_down_high, s_qk, s_vo,
-    d_qk, d_vo, pg, heads_grad, kh, dk, dv, own, sent, got, near_gate, near_up, near_low, near_high,
+    d_qk, d_vo, pg, heads_grad, kh, dk, dv, own, sent, got, placed, near_gate, near_up, near_low, near_high,
     *rest,
 ):
     bufs = [rest[4 * i : 4 * i + 4] for i in range(6)]
-    send_sem, recv_sem, pair_send, pair_recv, near_sem = rest[24:]
+    send_sem, recv_sem, pair_send, pair_recv, near_sem, *moving = rest[24:]
     length, width = xh.shape
     half = length // 2
     cols = q.shape[1]
@@ -771,7 +881,7 @@
             here = pl.ds(at, rows)
             q_rows = q[here, lanes]
             g_rows = heads_grad[here, lanes]
-            same = seg_col[...] == seg_row[:, here]
+            same = seg_col[:, 0:1] == seg_row[0:1, here]
             prod = g_rows.astype(F32) * o[here, lanes].astype(F32)
             f = first[:rows]
             blank = jnp.zeros_like(q_rows)
@@ -840,9 +950,11 @@
         xhat, scale = normalize(to_place(x_half[here, :].astype(F32)))
         f = own[here, :] + got[here, :].astype(F32)
         value = resid_grad[here, :] + normalize_back(f, xhat, scale)
-        token_grad[here, :] = to_place(value).astype(BF)
+        placed[here, :] = to_place(value).astype(BF)
 
     in_chunks(half, 64, finish)
+    move = Move(placed, token_grad, moving, 0)
+    move.start()
     for z in Reduce.ORDER:
         for part in down:
             part.relay_first(z)
@@ -862,6 +974,7 @@
         part.finish()
     for part in one + down + last:
         part.close()
+    move.wait()
 
 
 def backward_block(grads, heads, lse, attn_cot, w_qk, w_vo, xh, x_half, resid_grad, tables, seg_col, seg_row):
@@ -899,6 +1012,7 @@
             pltpu.VMEM((half, width), F32),
             pltpu.VMEM((half, width), BF),
             pltpu.VMEM((half, width), BF),
+            pltpu.VMEM((half, width), BF),
         ]
         + [pltpu.VMEM((4, 2) + size, BF) for size in sizes[:4]]
         + bufs
@@ -908,7 +1022,8 @@
             pltpu.SemaphoreType.DMA((1,)),
             pltpu.SemaphoreType.DMA((1,)),
             pltpu.SemaphoreType.DMA((4,)),
-        ],
+        ]
+        + move_sems(1),
         compiler_params=pltpu.CompilerParams(
             collective_id=2, has_side_effects=True, vmem_limit_bytes=60 << 20
         ),
@@ -920,80 +1035,17 @@
 
 
 class Chips:
-    def __init__(self):
-        self.axes = ("dp", "tensor")
-        dp = lax.axis_index("dp")
-        self.z, self.x, self.core = dp // 4, (dp // 2) % 2, dp % 2
-        self.y = lax.axis_index("tensor")
-
-    @staticmethod
-    def place(z, x, c, y):
-        return ((z * 2 + x) * 2 + c) * 2 + y
-
-    def send(self, value, dz=0, dx=0, dy=0, dc=0):
-        pairs = [
-            (self.place(z, x, c, y), self.place(z ^ dz, x ^ dx, c ^ dc, y ^ dy))
-            for z in range(4)
-            for x in range(2)
-            for c in range(2)
-            for y in range(2)
-        ]
-        return lax.ppermute(value, self.axes, pairs)
-
-    def swap(self, value):
-        pairs = [
-            (self.place(z, x, c, y), self.place(z, x, y, c))
-            for z in range(4)
-            for x in range(2)
-            for c in range(2)
-            for y in range(2)
-        ]
-        return lax.ppermute(value, self.axes, pairs)
-
-    def to_relative(self, value):
-        rows, width = value.shape
-        blocks = value.reshape(rows, 2, 2, 2, 2, width // 16)
-        for axis, bit in ((4, self.y), (3, self.x), (2, self.z % 2), (1, self.z // 2)):
-            blocks = jnp.where(bit == 1, jnp.flip(blocks, axis), blocks)
-        return blocks.reshape(rows, width)
-
-    from_relative = to_relative
-
-    def positions(self, half):
-        near = jnp.arange(half, dtype=jnp.int32)
-        return jnp.concatenate([near + self.core * half, near + (1 - self.core) * half])
-
-    def turn_rows(self, value):
-        half = value.shape[0] // 2
-        return jnp.where(self.core == 0, value, jnp.concatenate([value[half:], value[:half]]))
-
-    def gather_rows(self, value):
-        return jnp.concatenate([value, self.send(value, dc=1)], axis=0)
-
     def sum_tensor(self, value):
-        return value + self.send(value, dy=1)
+        pairs = [(2 * i + y, 2 * i + 1 - y) for i in range(16) for y in range(2)]
+        return value + lax.ppermute(value, ("dp", "tensor"), pairs)
 
 
 class Axes:
-    def swap(self, value):
-        return value
-
-    to_relative = from_relative = swap
-
-    def positions(self, half):
-        return jnp.arange(half * lax.axis_size("tensor"), dtype=jnp.int32)
-
-    def turn_rows(self, value):
-        return value
-
     def gather_rows(self, value):
         return lax.all_gather(value, "tensor", axis=0, tiled=True)
 
     def scatter_rows(self, value):
         return lax.psum_scatter(value.astype(BF), "tensor", scatter_dimension=0, tiled=True).astype(F32)
-
-    def gather(self, a, b):
-        return tuple(lax.all_gather(w, "dp", axis=0, tiled=True) for w in (a, b))
 
     def reduce(self, a, b):
         return tuple(
@@ -1043,18 +1095,15 @@
         b_one = jnp.concatenate([scaled(w_qkv[:, 2], gain_one), w_out.T], axis=1)
         own_gate, own_up = scaled(w_in[:, 0], gain_two), scaled(w_in[:, 1], gain_two)
 
-        seg = comm.turn_rows(comm.swap(segments[0]))
-        cot = comm.to_relative(comm.swap(cotangent[0]))
-        cot_all = comm.gather_rows(cot)
-        tables = rope_tables(comm.positions(tokens.shape[1]))
-        seg_col, seg_row = seg[:, None], seg[None, :]
         owned = (a_one, b_one, own_gate, own_up, down_rows)
         if paired:
-            owned = [comm.swap(w) for w in owned[:2] + tuple(padded(w) for w in owned[2:])]
-            x_half = comm.swap(tokens[0])
-            q, k, v, o, lse, xh, w_qk, w_vo, resid, xn, w_gate, w_up, w_dn = forward_block(
-                owned, x_half, tables, seg_col, seg_row
-            )
+            owned = owned[:2] + tuple(padded(w) for w in owned[2:])
+            seg = jnp.broadcast_to(segments.astype(F32), (8, segments.shape[1]))
+            inverse = jnp.broadcast_to(jnp.tile(rope_rates(), 4), (8, 128))
+            (
+                q, k, v, o, lse, xh, w_qk, w_vo, resid, xn, x_half, cot_all, *tables, seg_col, seg_row,
+                w_gate, w_up, w_dn,
+            ) = forward_block(owned, tokens[0], cotangent[0], seg, inverse)
             w_qk, w_vo, w_gate, w_up, w_dn = (
                 w.reshape(-1, w.shape[-1]) for w in (w_qk, w_vo, w_gate, w_up, w_dn)
             )
@@ -1063,6 +1112,10 @@
                 lax.all_gather(w, "dp", axis=0, tiled=True) for w in owned
             )
             w_o = w_vo[:, cols:]
+            seg_col, seg_row = segments[0][:, None], segments
+            cot = cotangent[0]
+            cot_all = comm.gather_rows(cot)
+            tables = rope_tables(jnp.arange(segments.shape[1]))
             x_in = tokens[0].astype(F32)
             xh_one, scale_one = normalize(x_in)
             xh = comm.gather_rows(xh_one.astype(BF))
@@ -1071,16 +1124,15 @@
             xh_two, scale_two = normalize(resid)
             xn = comm.gather_rows(xh_two.astype(BF))
         if paired:
-            placed, resid_grad, attn_cot, d_gate, d_up, d_down = mlp_block(
+            result, resid_grad, attn_cot, d_gate, d_up, d_down = mlp_block(
                 xn, cot_all, w_gate, w_up, w_dn, resid
             )
-            result = comm.swap(placed)
         else:
             gate, up = dotf(xn, w_gate, NN), dotf(xn, w_up, NN)
             act, slope = gelu_parts(gate)
             hidden = (act * up).astype(BF)
             mlp = comm.scatter_rows(dotf(hidden, w_dn, NT))
-            result = comm.swap(comm.from_relative((resid + mlp).astype(BF)))
+            result = (resid + mlp).astype(BF)
             hidden_grad = dotf(cot_all, w_dn, NN).astype(BF).astype(F32)
             gate_grad = (hidden_grad * up * slope).astype(BF)
             up_grad = (hidden_grad * act).astype(BF)
@@ -1091,11 +1143,11 @@
             d_gate, d_up = dotf(xn, gate_grad, TN), dotf(xn, up_grad, TN)
 
         if paired:
-            placed, *sums = backward_block(
+            token_grad, *sums = backward_block(
                 (d_gate, d_up, d_down), (q, k, v, o), lse, attn_cot, w_qk, w_vo, xh, x_half,
                 resid_grad, tables, seg_col, seg_row,
             )
-            token_grad = comm.swap(placed).astype(F32)
+            token_grad = token_grad.astype(F32)
             s_gate, s_up, s_low, s_high, one_a, one_b = (w.astype(F32) for w in sums)
             in_raw = jnp.stack([s_gate[:, :units], s_up[:, :units]], axis=1)
             down_sum = jnp.concatenate([s_low[:, :units], s_high[:, :units]], axis=0).T

time: 407 us -> 366 us (0.90)
  starting transfers between devices: 33.7 us -> 0.07 us
  Pallas kernels: 318 us -> 345 us
  waiting for transfers between devices: 18.7 us -> 0.01 us
  other arithmetic: 18.6 us -> 8.46 us
    ppermute x12 -> x1, starting transfers between devices: 33.7 us -> 0.07 us  [sum_tensor(): return value + lax.ppermute(value, ('dp', 'tensor'), pairs)]
    pallas_call x1, Pallas kernels: 132 us -> 157 us  [forward_block(): pl.pallas_call(forward_kernel, in_specs=[any_] * 8 + [vmem], out_specs=[v...]
    ppermute x12 -> x1, waiting for transfers between devices: 18.7 us -> 0.01 us  [sum_tensor(): return value + lax.ppermute(value, ('dp', 'tensor'), pairs)]
    concatenate x4 -> x0, other arithmetic: 7.06 us -> none  [the longest x1 3.03 us: rope_tables(): cosine = jnp.concatenate([cos] * 4, axis=-1)]
  transfers between devices with their start and end apart: 12 -> 1, of which waited for: 1 -> 0; matrix products, arithmetic and copies ran while one was open for 6% -> 1% of each run, Pallas kernels for 33% -> 0%
where the time goes in v5:
time: 366 us; the launch traced here: 365 us
  Pallas kernels  345 us (94%)
  local copies, waits for them, and re-layouts  10.9 us (3%)
  other arithmetic  8.46 us (2%)
    pallas_call x1, Pallas kernels, forward_block(): pl.pallas_call(forward_kernel, in_specs=[any_] * 8 + [vmem], out_specs=[v...  157 us
    pallas_call x1, Pallas kernels, backward_block(): pl.pallas_call(backward_kernel, in_specs=[any_] * 3 + [vmem] * 16, out_sp...  141 us
    pallas_call x1, Pallas kernels, mlp_block(): pl.pallas_call(mlp_kernel, in_specs=[vmem] * 6, out_specs=[vmem] * 6, out...  47.4 us
  transfers between devices with their start and end apart: 1, of which 0 were waited for; matrix products, arithmetic and copies ran while one was open for 1% of the time, Pallas kernels for 0%

profile of v5, /device:TPU:0, one launch (start us, length us, event | category | flops | bytes accessed | tf_op | source)
XLA Modules:
  0.0 365.4 jit_solution(8981660319822292993)
XLA Ops:
  0.6 0.0 copy-start.3
  0.6 0.0 copy-start.6
  0.7 0.7 convert_element_type.84
  1.4 0.7 convert_element_type.94
  2.0 0.1 tile.10
  2.1 0.7 convert_element_type.99
  2.8 1.0 copy.17
  3.8 1.6 pad.12.d_in
  5.4 0.1 fusion.1
  5.6 0.7 pad.11.u_in
  6.3 0.7 pad.10.g_in
  7.0 0.0 copy-done.3
  7.0 0.1 fusion.4
  7.1 0.0 copy-done.6
  7.1 0.7 pad_maximum_fusion.2
  7.8 0.6 broadcast_in_dim.23.inverse
  8.4 0.6 broadcast_in_dim.22.seg_in
  9.0 156.8 %forward_block.1 = (bf16[1024,512]{1,0:T(8,128)(2,1)}, bf16[1024,512]{1,0:T(8,128)(2,1)}, bf16[1024,512]{1,0:T(8,128)(2,1)}, bf16[1024,512]{1,0:T(8,128)(2,1)}, ...) custom-call(bf16[64,1024]{1,0:T(8,128)(2,1)} %get-tuple-element.97.a, ...), custom_call_target="tpu_custom_call" | custom-call | tf_op jit(solution)/shard_map/forward_block/pallas_call | solution.py:574
  165.8 47.4 %mlp_block.1 = (bf16[512,1024]{1,0:T(8,128)(2,1)}, f32[512,1024]{1,0:T(8,128)}, bf16[1024,1024]{1,0:T(8,128)(2,1)}, bf16[1024,1408]{1,0:T(8,128)(2,1)}, bf16[102...) custom-call(bf16[1024,1024]{1,0:T(8,128)(2,1)} %get-tuple-element.41.xn, bf16[1024,1024]{1,0:T(8,128)(2,1)} %get-tuple-element.42.cot, ...), custom_call_target="tpu_custom_call" | custom-call | tf_op jit(solution)/shard_map/mlp_block/pallas_call | solution.py:689
  213.2 141.0 %backward_block.1 = (bf16[512,1024]{1,0:T(8,128)(2,1)}, bf16[64,1408]{1,0:T(8,128)(2,1)}, bf16[64,1408]{1,0:T(8,128)(2,1)}, bf16[32,1408]{1,0:T(8,128)(2,1)}, bf...) custom-call(bf16[4,2,2,64,1408]{4,3,2,1,0:T(8,128)(2,1)} %bitcast.58, ...), custom_call_target="tpu_custom_call" | custom-call | tf_op jit(solution)/shard_map/backward_block/pallas_call | solution.py:999
  354.2 0.0 copy-start
  354.2 1.0 slice_bitcast_fusion.3
  355.2 0.9 slice_bitcast_fusion.2
  356.2 0.0 copy-start.1
  356.2 1.0 convert_element_type.101
  357.2 0.9 convert_element_type.102
  358.1 0.7 slice_bitcast_fusion.4
  358.8 0.0 copy-done
  358.8 0.2 convert_multiply_fusion
  359.0 0.0 copy-start.4
  359.0 0.0 copy-start.5
  359.1 0.9 fusion.3
  360.0 0.1 collective-permute-start
  360.1 0.0 copy-done.1
  360.1 0.0 copy-start.2
  360.1 1.6 bitcast_convert_fusion
  361.7 0.0 copy-done.4
  361.7 0.0 copy-done.5
  361.7 0.8 convert_bitcast_fusion
  362.4 1.4 copy.20
  363.9 0.0 collective-permute-done
  363.9 0.5 slice_bitcast_fusion.8
  364.4 0.0 copy-done.2
  364.4 1.0 copy.23
  (5 shorter events, 0.0 us)
Async XLA Ops:
  0.6 6.3 %copy-start.3 = (bf16[64,3,512]{2,0,1:T(8,128)(2,1)S(1)}, bf16[64,3,512]{2,0,1:T(8,128)(2,1)}, u32[]{:S(2)}) copy-start(bf16[64,3,512]{2,0,1:T(8,128)(2,1)} %param.11) | copy-start | bytes 589828
  0.6 6.4 %copy-start.6 = (bf16[512,64]{0,1:T(8,128)(2,1)S(1)}, bf16[512,64]{0,1:T(8,128)(2,1)}, u32[]{:S(2)}) copy-start(bf16[512,64]{0,1:T(8,128)(2,1)} %param.12) | copy-start | bytes 196612
  354.2 4.6 %copy-start = (bf16[64,2,1312]{2,1,0:T(2,128)(2,1)S(1)}, bf16[64,2,1312]{2,1,0:T(2,128)(2,1)}, u32[]{:S(2)}) copy-start(bf16[64,2,1312]{2,1,0:T(2,128)(2,1)} %param.13) | copy-start | bytes 1007620
  356.2 3.9 %copy-start.1 = (bf16[512,1024]{1,0:T(8,128)(2,1)S(1)}, bf16[512,1024]{1,0:T(8,128)(2,1)}, u32[]{:S(2)}) copy-start(bf16[512,1024]{1,0:T(8,128)(2,1)} %get-tuple-element.67) | copy-start | bytes 3145732
  359.0 2.6 copy-start.4
  359.0 2.6 copy-start.5
  360.0 3.9 %collective-permute-start = (f32[2,64]{1,0:T(2,128)S(1)}, f32[2,64]{1,0:T(2,128)S(1)}, u32[]{:S(2)}, u32[]{:S(2)}) collective-permute-start(f32[2,64]{1,0:T(2,128)S(1)} %pad_maximum_fusion.4), channel_id=1, source_target_pairs={{0,1},{1,0},{2,3},{3,2},{4,5},{5,4},{6,7},{7,6},{8,9},{9,8},{10,11... | collective-permute-start | bytes 1544 | tf_op jit(solution)/shard_map/ppermute | solution.py:1040
  360.1 4.3 %copy-start.2 = (bf16[512,1024]{1,0:T(8,128)(2,1)S(1)}, bf16[512,1024]{1,0:T(8,128)(2,1)}, u32[]{:S(2)}) copy-start(bf16[512,1024]{1,0:T(8,128)(2,1)} %get-tuple-element.47) | copy-start | bytes 3145732

commit v6 on v5

--- a/solution.py
+++ b/solution.py
@@ -291,51 +291,66 @@
     return jnp.concatenate(tiles, axis=1)
 
 
+AXIS = {"z": 4, "x": 2, "y": 2}
+
+
+def partner(peers, axis, step):
+    return peers["z%d" % step if axis == "z" else axis]
+
+
 class Gather:
     MESSAGES = 15
 
-    def __init__(self, own, buf, rows, axes, peers, sems, base):
-        self.buf, self.rows, self.axes, self.peers = buf, rows, axes, peers
+    def __init__(self, own, buf, rows, order, peers, sems, base):
+        self.buf, self.rows, self.order, self.peers = buf, rows, order, peers
         self.own = own.at[rows]
         self.send_sem, self.recv_sem = sems
         self.base = base
-
-    def slot(self, z, first, second):
-        x, y = (first, second) if self.axes[0] == "x" else (second, first)
-        return self.buf.at[z, x, y, self.rows]
-
-    def copy(self, i):
-        if i < 3:
-            src, dst, peer = self.own, self.slot(i + 1, 0, 0), "z%d" % (i + 1)
-        elif i < 7:
-            src, dst, peer = self.slot(i - 3, 0, 0), self.slot(i - 3, 1, 0), self.axes[0]
-        else:
-            f, z = divmod(i - 7, 4)
-            src, dst, peer = self.slot(z, f, 0), self.slot(z, f, 1), self.axes[1]
-        if i in (3, 7):
-            src = self.own
-        n = self.base + i
-        return remote(src, dst, self.send_sem.at[n], self.recv_sem.at[n], self.peers[peer])
-
-    def start_z(self):
-        for i in range(3):
-            self.copy(i).start()
-
-    def relay_z(self, z):
-        if z:
-            self.copy(z - 1).wait_recv()
-        self.copy(3 + z).start()
-        self.copy(7 + z).start()
-
-    def relay_first(self, z):
-        self.copy(3 + z).wait_recv()
-        self.copy(11 + z).start()
+        n, m, p = (AXIS[axis] for axis in order)
+        self.outer, self.middle = range(n), range(1, m)
+        self.stages = [
+            [(i, 0, 0) for i in range(1, n)],
+            [(i, j, 0) for i in range(n) for j in range(1, m)],
+            [(i, j, k) for i in range(n) for j in range(m) for k in range(1, p)],
+        ]
+        self.numbers = {at: n for n, at in enumerate(sum(self.stages, []))}
+
+    def slot(self, at):
+        where = dict(zip(self.order, at))
+        return self.buf.at[where["z"], where["x"], where["y"], self.rows]
+
+    def copy(self, at):
+        hop = max(i for i in range(3) if at[i])
+        source = at[:hop] + (0,) * (3 - hop)
+        src = self.slot(source) if any(source) else self.own
+        n = self.base + self.numbers[at]
+        peer = partner(self.peers, self.order[hop], at[hop])
+        return remote(src, self.slot(at), self.send_sem.at[n], self.recv_sem.at[n], peer)
+
+    def send(self, stage, *prefix):
+        for at in self.stages[stage]:
+            if at[: len(prefix)] == prefix:
+                self.copy(at).start()
+
+    def start(self):
+        self.send(0)
+
+    def relay(self, i):
+        if i:
+            self.copy((i, 0, 0)).wait_recv()
+        self.send(1, i)
+        self.send(2, i, 0)
+
+    def relay_again(self, i):
+        for j in self.middle:
+            self.copy((i, j, 0)).wait_recv()
+            self.send(2, i, j)
 
     def finish(self):
-        for i in range(7, 15):
-            self.copy(i).wait_recv()
-        for i in range(15):
-            self.copy(i).wait_send()
+        for at in self.stages[2]:
+            self.copy(at).wait_recv()
+        for at in self.numbers:
+            self.copy(at).wait_send()
 
 
 def forward_kernel(
@@ -355,18 +370,18 @@
     sems = (send_sem, recv_sem)
     n = Gather.MESSAGES
     whole, low, high = pl.ds(0, 64), pl.ds(0, 32), pl.ds(32, 32)
-    one = [
-        Gather(a_own, w_qk, whole, "xy", peers, sems, 0),
-        Gather(b_own, w_vo, whole, "yx", peers, sems, n),
-    ]
-    two = [
-        Gather(g_own, w_gate, whole, "xy", peers, sems, 2 * n),
-        Gather(u_own, w_up, whole, "yx", peers, sems, 3 * n),
-    ]
-    three = [
-        Gather(d_own, w_down, low, "xy", peers, sems, 4 * n),
-        Gather(d_own, w_down, high, "yx", peers, sems, 5 * n),
-    ]
+    plan = (
+        (a_own, w_qk, whole, "zyx"),
+        (b_own, w_vo, low, "zyx"),
+        (b_own, w_vo, high, "xyz"),
+        (g_own, w_gate, whole, "zyx"),
+        (u_own, w_up, low, "zyx"),
+        (u_own, w_up, high, "zxy"),
+        (d_own, w_down, low, "zyx"),
+        (d_own, w_down, high, "xyz"),
+    )
+    gathers = [Gather(*piece, peers, sems, i * n) for i, piece in enumerate(plan)]
+    one, early, two, three, late = gathers[:2], gathers[2], gathers[3:6], gathers[6], gathers[7]
     owns = [
         pltpu.make_async_copy(src, dst.at[0, 0, 0], own_sem.at[i])
         for i, (src, dst) in enumerate(
@@ -405,18 +420,24 @@
 
     move_a.wait()
     move_b.wait()
+    early.start()
     for gather in one:
-        gather.start_z()
-    for gather in one:
-        gather.relay_z(0)
+        gather.start()
+    for gather in [early] + one:
+        gather.relay(0)
     for copy in owns[:2]:
         copy.start()
     in_chunks(length, 64, tables)
+    early.relay(1)
     move_seg.wait()
     ids = seg_own[...]
     ids = jnp.where(core == 0, ids, jnp.concatenate([ids[:, half:], ids[:, :half]], axis=1))
     seg_row[...] = ids
     seg_col[...] = jnp.transpose(jnp.broadcast_to(ids[0:1, :], (128, length)))
+    early.relay_again(0)
+    for gather in one:
+        gather.relay(1)
+    early.relay_again(1)
     move_x.wait()
 
     def first_norm(i, carry):
@@ -427,9 +448,9 @@
         return carry
 
     lax.fori_loop(0, half // 128, first_norm, 0)
-    for z in (1, 2, 3):
+    for z in (2, 3):
         for gather in one:
-            gather.relay_z(z)
+            gather.relay(z)
     swap_xh = remote(
         xh.at[pl.ds(0, half)], xh.at[pl.ds(half, half)], pair_send.at[0], pair_recv.at[0], peers["c"]
     )
@@ -437,27 +458,36 @@
     move_g.wait()
     move_u.wait()
     for gather in two:
-        gather.start_z()
+        gather.start()
     for z in range(4):
         for gather in one:
-            gather.relay_first(z)
+            gather.relay_again(z)
+    for gather in two:
+        gather.relay(0)
     move_d.wait()
-    for gather in three:
-        gather.start_z()
+    late.start()
+    three.start()
     for copy in owns[2:]:
         copy.start()
     swap_xh.wait()
-    for gather in one:
+    for gather in one + [early]:
         gather.finish()
     for copy in owns[:2]:
         copy.wait()
 
     events = {}
+    at_step = lambda step, call, *args: events.setdefault(step, []).append((call, args))
     for z in range(4):
-        events.setdefault(1 + z, []).extend((g.relay_z, z) for g in two)
-        events.setdefault(6 + z, []).extend((g.relay_first, z) for g in two)
-        events.setdefault(9 + z, []).extend((g.relay_z, z) for g in three)
-    events.setdefault(5, []).append((lambda _: move_c.start(), 0))
+        for gather in two:
+            if z:
+                at_step(1 + z, gather.relay, z)
+            at_step(6 + z, gather.relay_again, z)
+        at_step(9 + z, three.relay, z)
+    at_step(1, late.relay, 0)
+    at_step(5, late.relay, 1)
+    at_step(5, move_c.start)
+    at_step(9, late.relay_again, 0)
+    at_step(12, late.relay_again, 1)
     first = lax.broadcasted_iota(jnp.int32, (length, 128), 1) < HD
 
     def pair(h, carry):
@@ -480,8 +510,8 @@
 
                 @pl.when(h * (length // rows) + i == step)
                 def _():
-                    for call, z in calls:
-                        call(z)
+                    for call, args in calls:
+                        call(*args)
 
             at = pl.multiple_of(i * rows, rows)
             q_rows = q[pl.ds(at, rows), lanes]
@@ -533,9 +563,8 @@
         cot.at[pl.ds(0, half)], cot.at[pl.ds(half, half)], pair_send.at[3], pair_recv.at[3], peers["c"]
     )
     swap_cot.start()
-    for gather in three:
-        for z in range(4):
-            gather.relay_first(z)
+    for z in range(4):
+        three.relay_again(z)
     give.wait()
 
     def second_norm(i, carry):
@@ -550,7 +579,7 @@
         xn.at[pl.ds(0, half)], xn.at[pl.ds(half, half)], pair_send.at[2], pair_recv.at[2], peers["c"]
     )
     swap_xn.start()
-    for gather in two + three:
+    for gather in two + [three, late]:
         gather.finish()
     for copy in owns[2:]:
         copy.wait()
@@ -599,8 +628,8 @@
             pltpu.VMEM((half, width), F32),
             pltpu.VMEM((half, width), BF),
             pltpu.VMEM((half, width), BF),
-            pltpu.SemaphoreType.DMA((6 * Gather.MESSAGES,)),
-            pltpu.SemaphoreType.DMA((6 * Gather.MESSAGES,)),
+            pltpu.SemaphoreType.DMA((8 * Gather.MESSAGES,)),
+            pltpu.SemaphoreType.DMA((8 * Gather.MESSAGES,)),
             pltpu.SemaphoreType.DMA((4,)),
             pltpu.SemaphoreType.DMA((4,)),
             pltpu.SemaphoreType.DMA((5,)),
@@ -762,12 +791,15 @@
         moved, peer = exchanged()
         return moved, self.link(11, self.sum, self.out, peer)
 
-    def finish(self):
+    def total(self):
         total = self.two[0].astype(F32)
         for z in (1, 2, 3):
             self.third(z).wait_recv()
             total = total + self.three[z - 1].astype(F32)
-        self.sum[...] = total.astype(BF)
+        return total
+
+    def finish(self):
+        self.sum[...] = self.total().astype(BF)
         moved, copy = self.last()
 
         @pl.when(moved)
@@ -778,12 +810,13 @@
         def _():
             self.out[...] = self.sum[...]
 
+    def sent(self):
+        thirds = [self.third(z) for z in (1, 2, 3)]
+        return [hop(z) for z in range(4) for hop in (self.first, self.second)] + thirds
+
     def close(self):
-        for z in range(4):
-            self.first(z).wait_send()
-            self.second(z).wait_send()
-            if z:
-                self.third(z).wait_send()
+        for copy in self.sent():
+            copy.wait_send()
         moved, copy = self.last()
 
         @pl.when(moved)
@@ -791,15 +824,53 @@
             copy.wait()
 
 
+class ReduceAlongZ(Reduce):
+    def first(self, z):
+        src = self.parts.at[z, :, :, self.rows]
+        return self.link(z - 1, src, self.one.at[z - 1], self.peers["z%d" % z])
+
+    def second(self):
+        return self.link(3, self.two.at[:, 1], self.three.at[0:2], self.peers["y"])
+
+    def third(self):
+        return self.link(4, self.three.at[1], self.three.at[2], self.peers["x"])
+
+    def start(self):
+        for z in (2, 3, 1):
+            self.first(z).start()
+
+    def relay_first(self):
+        total = self.near().astype(F32)
+        for z in (1, 2, 3):
+            self.first(z).wait_recv()
+            total = total + self.one[z - 1].astype(F32)
+        self.two[...] = total.astype(BF)
+        self.second().start()
+
+    def relay_second(self):
+        self.second().wait_recv()
+        for x in (0, 1):
+            self.three[x] = (self.three[x].astype(F32) + self.two[x, 0].astype(F32)).astype(BF)
+        self.third().start()
+
+    def total(self):
+        self.third().wait_recv()
+        return self.three[0].astype(F32) + self.three[2].astype(F32)
+
+    def sent(self):
+        return [self.first(z) for z in (1, 2, 3)] + [self.second(), self.third()]
+
+
 def backward_kernel(
     d_gate, d_up, d_down, q, k, v, o, lse, attn_cot, w_qk, w_vo, xh, x_half, resid_grad,
     cos, upper, lower, seg_col, seg_row,
-    token_grad, s_gate, s_up, s_down_low, s_down_high, s_qk, s_vo,
-    d_qk, d_vo, pg, heads_grad, kh, dk, dv, own, sent, got, placed, near_gate, near_up, near_low, near_high,
+    token_grad, s_gate, s_up_low, s_up_high, s_down_low, s_down_high, s_qk, s_vo_low, s_vo_high,
+    d_qk, d_vo, pg, heads_grad, kh, dk, dv, own, sent, got, placed,
+    near_gate, near_up_low, near_up_high, near_low, near_high,
     *rest,
 ):
-    bufs = [rest[4 * i : 4 * i + 4] for i in range(6)]
-    send_sem, recv_sem, pair_send, pair_recv, near_sem, *moving = rest[24:]
+    bufs = [rest[4 * i : 4 * i + 4] for i in range(8)]
+    send_sem, recv_sem, pair_send, pair_recv, near_sem, *moving = rest[32:]
     length, width = xh.shape
     half = length // 2
     cols = q.shape[1]
@@ -809,33 +880,39 @@
     sems = (send_sem, recv_sem)
     n = Reduce.MESSAGES
     whole, low, high = pl.ds(0, 64), pl.ds(0, 32), pl.ds(32, 32)
+    most, few = pl.ds(0, 48), pl.ds(48, 16)
     held = lambda ref: (lambda z: ref[z])
-    gate = Reduce(d_gate, held(near_gate), whole, "xy", peers, sems, 0, bufs[0], s_gate)
-    up = Reduce(d_up, held(near_up), whole, "yx", peers, sems, n, bufs[1], s_up)
-    down = [
-        Reduce(d_down, held(near_low), low, "xy", peers, sems, 2 * n, bufs[2], s_down_low),
-        Reduce(d_down, held(near_high), high, "yx", peers, sems, 3 * n, bufs[3], s_down_high),
+    plan = (
+        (Reduce, d_gate, held(near_gate), whole, "yx", s_gate),
+        (Reduce, d_up, held(near_up_low), low, "yx", s_up_low),
+        (Reduce, d_up, held(near_up_high), high, "xy", s_up_high),
+        (Reduce, d_down, held(near_low), low, "yx", s_down_low),
+        (ReduceAlongZ, d_down, lambda: near_high[...], high, None, s_down_high),
+        (Reduce, d_qk, lambda z: d_qk[z, 0], whole, "yx", s_qk),
+        (Reduce, d_vo, lambda z: d_vo[z, :, 0, 0:48], most, "xy", s_vo_low),
+        (ReduceAlongZ, d_vo, lambda: d_vo[0, :, :, 48:64], few, None, s_vo_high),
+    )
+    parts = [
+        kind(src, near, rows_, axes, peers, sems, i * n, bufs[i], out)
+        for i, (kind, src, near, rows_, axes, out) in enumerate(plan)
     ]
-    one = [gate, up]
-    last = [
-        Reduce(d_qk, lambda z: d_qk[z, :, 0], whole, "xy", peers, sems, 4 * n, bufs[4], s_qk),
-        Reduce(d_vo, lambda z: d_vo[z, 0], whole, "yx", peers, sems, 5 * n, bufs[5], s_vo),
-    ]
+    gate, up_low, up_high, down_low, down_high, qk, vo_low, vo_high = parts
     nears = [
         pltpu.make_async_copy(src, dst, near_sem.at[i])
         for i, (src, dst) in enumerate(
             (
-                (d_gate.at[:, :, 0], near_gate),
-                (d_up.at[:, 0], near_up),
-                (d_down.at[:, :, 0, low], near_low),
-                (d_down.at[:, 0, :, high], near_high),
+                (d_gate.at[:, 0], near_gate),
+                (d_up.at[:, 0, :, low], near_up_low),
+                (d_up.at[:, :, 0, high], near_up_high),
+                (d_down.at[:, 0, :, low], near_low),
+                (d_down.at[0, :, :, high], near_high),
             )
         )
     ]
     for copy in nears:
         copy.start()
     meet(peers, exchanged())
-    for part in one:
+    for part in (down_high, up_high, gate, up_low):
         part.start()
 
     def heads(here):
@@ -855,8 +932,10 @@
 
     events = {}
     for i, z in enumerate(Reduce.ORDER):
-        events.setdefault(2 + 4 * i, []).extend((lambda r=r, z=z: r.relay_first(z)) for r in one)
-    events.setdefault(11, []).extend(r.start for r in down)
+        events.setdefault(2 + 4 * i, []).append(lambda z=z: gate.relay_first(z))
+        events.setdefault(3 + 2 * i, []).append(lambda z=z: up_high.relay_first(z))
+    events.setdefault(11, []).append(down_low.start)
+    events.setdefault(12, []).append(down_high.relay_first)
     lane = lax.broadcasted_iota(jnp.int32, (length, 128), 1)
     first = lane < HD
 
@@ -935,15 +1014,15 @@
 
         in_chunks(width, 256, step)
 
+    for part in (qk, vo_low, vo_high):
+        part.start()
     back(pl.ds(half, half), sent)
-    for part in last:
-        part.start()
     give = remote(sent, got, pair_send.at[0], pair_recv.at[0], peers["c"])
     give.start()
     back(pl.ds(0, half), own)
     for z in Reduce.ORDER:
-        for part in one:
-            part.relay_second(z)
+        gate.relay_second(z)
+    down_high.relay_second()
     give.wait()
 
     def finish(here):
@@ -956,23 +1035,31 @@
     move = Move(placed, token_grad, moving, 0)
     move.start()
     for z in Reduce.ORDER:
-        for part in down:
-            part.relay_first(z)
-    for part in one:
-        part.finish()
+        up_low.relay_first(z)
+        up_high.relay_second(z)
+    gate.finish()
     for z in Reduce.ORDER:
-        for part in down:
-            part.relay_second(z)
-        for part in last:
-            part.relay_first(z)
-    for part in down:
-        part.finish()
+        down_low.relay_first(z)
+        vo_low.relay_first(z)
+    up_high.finish()
+    vo_high.relay_first()
     for z in Reduce.ORDER:
-        for part in last:
-            part.relay_second(z)
-    for part in last:
-        part.finish()
-    for part in one + down + last:
+        up_low.relay_second(z)
+    down_high.finish()
+    for z in Reduce.ORDER:
+        qk.relay_first(z)
+        down_low.relay_second(z)
+    up_low.finish()
+    vo_high.relay_second()
+    for z in Reduce.ORDER:
+        vo_low.relay_second(z)
+    down_low.finish()
+    for z in Reduce.ORDER:
+        qk.relay_second(z)
+    vo_high.finish()
+    vo_low.finish()
+    qk.finish()
+    for part in parts:
         part.close()
     move.wait()
 
@@ -985,21 +1072,22 @@
     shard = width // 16
     vmem = pl.BlockSpec(memory_space=pltpu.VMEM)
     any_ = pl.BlockSpec(memory_space=pl.ANY)
-    sizes = [(shard, units), (shard, units), (shard // 2, units), (shard // 2, units)]
-    sizes += [(shard, 2 * cols)] * 2
+    sizes = [(shard, units)] + [(shard // 2, units)] * 4
+    sizes += [(shard, 2 * cols), (shard * 3 // 4, 2 * cols), (shard // 4, 2 * cols)]
+    along_z = (4, 7)
     bufs = []
-    for size in sizes:
-        bufs += [
-            pltpu.VMEM((4, 2) + size, BF),
-            pltpu.VMEM((4,) + size, BF),
-            pltpu.VMEM((3,) + size, BF),
-            pltpu.VMEM(size, BF),
-        ]
-    messages = 6 * Reduce.MESSAGES
+    for i, size in enumerate(sizes):
+        if i in along_z:
+            lead = (3, 2, 2), (2, 2), (3,)
+        else:
+            lead = (4, 2), (4,), (3,)
+        bufs += [pltpu.VMEM(n + size, BF) for n in lead + ((),)]
+    nears = [pltpu.VMEM(((2, 2) if i in along_z else (4, 2)) + size, BF) for i, size in enumerate(sizes[:5])]
+    messages = 8 * Reduce.MESSAGES
     return pl.pallas_call(
         backward_kernel,
         in_specs=[any_] * 3 + [vmem] * 16,
-        out_specs=[vmem] * 7,
+        out_specs=[vmem] * 9,
         out_shape=[jax.ShapeDtypeStruct((half, width), BF)]
         + [jax.ShapeDtypeStruct(size, BF) for size in sizes],
         scratch_shapes=[pltpu.VMEM(SHARD + (shard, 2 * cols), BF)] * 2
@@ -1014,14 +1102,14 @@
             pltpu.VMEM((half, width), BF),
             pltpu.VMEM((half, width), BF),
         ]
-        + [pltpu.VMEM((4, 2) + size, BF) for size in sizes[:4]]
+        + nears
         + bufs
         + [
             pltpu.SemaphoreType.DMA((messages,)),
             pltpu.SemaphoreType.DMA((messages,)),
             pltpu.SemaphoreType.DMA((1,)),
             pltpu.SemaphoreType.DMA((1,)),
-            pltpu.SemaphoreType.DMA((4,)),
+            pltpu.SemaphoreType.DMA((5,)),
         ]
         + move_sems(1),
         compiler_params=pltpu.CompilerParams(
@@ -1148,7 +1236,9 @@
                 resid_grad, tables, seg_col, seg_row,
             )
             token_grad = token_grad.astype(F32)
-            s_gate, s_up, s_low, s_high, one_a, one_b = (w.astype(F32) for w in sums)
+            s_gate, up_low, up_high, s_low, s_high, one_a, vo_low, vo_high = (w.astype(F32) for w in sums)
+            s_up = jnp.concatenate([up_low, up_high], axis=0)
+            one_b = jnp.concatenate([vo_low, vo_high], axis=0)
             in_raw = jnp.stack([s_gate[:, :units], s_up[:, :units]], axis=1)
             down_sum = jnp.concatenate([s_low[:, :units], s_high[:, :units]], axis=0).T
         else:

time: 366 us -> 354 us (0.967)
  Pallas kernels: 345 us -> 329 us
  starting transfers between devices: 0.07 us -> 4.36 us
    pallas_call x1, Pallas kernels: 157 us -> 142 us  [forward_block(): pl.pallas_call(forward_kernel, in_specs=[any_] * 8 + [vmem], out_specs=[v...]
    pallas_call x1, Pallas kernels: 141 us -> 136 us  [backward_block(): pl.pallas_call(backward_kernel, in_specs=[any_] * 3 + [vmem] * 16, out_sp...]
    ppermute x1, starting transfers between devices: 0.07 us -> 4.36 us  [sum_tensor(): return value + lax.ppermute(value, ('dp', 'tensor'), pairs)]
where the time goes in v6:
time: 354 us; the launch traced here: 353 us
  Pallas kernels  329 us (93%)
  local copies, waits for them, and re-layouts  9.94 us (3%)
  other arithmetic  8.48 us (2%)
  starting transfers between devices  4.36 us (1%)
    pallas_call x1, Pallas kernels, forward_block(): pl.pallas_call(forward_kernel, in_specs=[any_] * 8 + [vmem], out_specs=[v...  142 us
    pallas_call x1, Pallas kernels, backward_block(): pl.pallas_call(backward_kernel, in_specs=[any_] * 3 + [vmem] * 16, out_sp...  136 us
    pallas_call x1, Pallas kernels, mlp_block(): pl.pallas_call(mlp_kernel, in_specs=[vmem] * 6, out_specs=[vmem] * 6, out...  51 us
  transfers between devices with their start and end apart: 1, of which 0 were waited for; matrix products, arithmetic and copies ran while one was open for 1% of the time, Pallas kernels for 0%

profile of v6, /device:TPU:0, one launch (start us, length us, event | category | flops | bytes accessed | tf_op | source)
XLA Modules:
  0.0 352.6 jit_solution(3773188935227971191)
XLA Ops:
  0.6 0.0 copy-start.3
  0.6 0.0 copy-start.8
  0.7 0.7 convert_element_type.84
  1.4 0.7 convert_element_type.94
  2.0 0.1 tile.10
  2.1 0.7 convert_element_type.99
  2.8 1.0 copy.17
  3.8 1.6 pad.12.d_in
  5.4 0.1 fusion.1
  5.6 0.7 pad.11.u_in
  6.3 0.7 pad.10.g_in
  7.0 0.0 copy-done.3
  7.0 0.1 fusion.5
  7.1 0.0 copy-done.8
  7.1 0.7 pad_maximum_fusion.3
  7.8 0.6 broadcast_in_dim.23.inverse
  8.4 0.6 broadcast_in_dim.22.seg_in
  9.0 142.3 %forward_block.1 = (bf16[1024,512]{1,0:T(8,128)(2,1)}, bf16[1024,512]{1,0:T(8,128)(2,1)}, bf16[1024,512]{1,0:T(8,128)(2,1)}, bf16[1024,512]{1,0:T(8,128)(2,1)}, ...) custom-call(bf16[64,1024]{1,0:T(8,128)(2,1)} %get-tuple-element.101., ...), custom_call_target="tpu_custom_call" | custom-call | tf_op jit(solution)/shard_map/forward_block/pallas_call | solution.py:603
  151.3 51.0 %mlp_block.1 = (bf16[512,1024]{1,0:T(8,128)(2,1)}, f32[512,1024]{1,0:T(8,128)}, bf16[1024,1024]{1,0:T(8,128)(2,1)}, bf16[1024,1408]{1,0:T(8,128)(2,1)}, bf16[102...) custom-call(bf16[1024,1024]{1,0:T(8,128)(2,1)} %get-tuple-element.43.xn, bf16[1024,1024]{1,0:T(8,128)(2,1)} %get-tuple-element.44.cot, ...), custom_call_target="tpu_custom_call" | custom-call | tf_op jit(solution)/shard_map/mlp_block/pallas_call | solution.py:718
  202.3 135.8 %backward_block.1 = (bf16[512,1024]{1,0:T(8,128)(2,1)}, bf16[64,1408]{1,0:T(8,128)(2,1)}, bf16[32,1408]{1,0:T(8,128)(2,1)}, bf16[32,1408]{1,0:T(8,128)(2,1)}, bf...) custom-call(bf16[4,2,2,64,1408]{4,3,2,1,0:T(8,128)(2,1)} %bitcast.58, ...), custom_call_target="tpu_custom_call" | custom-call | tf_op jit(solution)/shard_map/backward_block/pallas_call | solution.py:1087
  338.1 0.0 copy-start.6
  338.1 0.0 copy-start.7
  338.1 0.0 copy-start
  338.1 1.0 slice_bitcast_fusion.2
  339.1 0.9 convert_element_type.101
  340.1 0.0 copy-start.1
  340.1 1.0 maximum_convert_fusion
  341.1 0.7 slice_bitcast_fusion.3
  341.8 0.0 copy-done.6
  341.8 0.0 copy-done.7
  341.8 0.0 copy-done
  341.8 0.2 convert_multiply_fusion
  342.0 0.0 copy-start.4
  342.0 0.0 copy-start.5
  342.1 0.9 fusion.3
  343.0 4.4 %collective-permute-start = (f32[2,64]{1,0:T(2,128)S(1)}, f32[2,64]{1,0:T(2,128)S(1)}, u32[]{:S(2)}, u32[]{:S(2)}) collective-permute-start(f32[2,64]{1,0:T(2,128)S(1)} %pad_maximum_fusion.5), channel_id=1, source_target_pairs={{0,1},{1,0},{2,3},{3,2},{4,5},{5,4},{6,7},{7,6},{8,9},{9,8},{10,11... | collective-permute-start | bytes 1544 | tf_op jit(solution)/shard_map/ppermute | solution.py:1128
  347.4 0.0 copy-done.1
  347.4 0.0 copy-start.2
  347.4 1.6 bitcast_convert_fusion
  348.9 0.0 copy-done.4
  349.0 0.0 copy-done.5
  349.0 0.8 convert_bitcast_fusion
  349.7 1.4 copy.20
  351.1 0.0 collective-permute-done
  351.1 0.5 slice_bitcast_fusion.7
  351.7 0.0 copy-done.2
  351.7 1.0 copy.23
  (6 shorter events, 0.1 us)
Async XLA Ops:
  0.6 6.3 %copy-start.3 = (bf16[64,3,512]{2,0,1:T(8,128)(2,1)S(1)}, bf16[64,3,512]{2,0,1:T(8,128)(2,1)}, u32[]{:S(2)}) copy-start(bf16[64,3,512]{2,0,1:T(8,128)(2,1)} %param.11) | copy-start | bytes 589828
  0.6 6.4 %copy-start.8 = (bf16[512,64]{0,1:T(8,128)(2,1)S(1)}, bf16[512,64]{0,1:T(8,128)(2,1)}, u32[]{:S(2)}) copy-start(bf16[512,64]{0,1:T(8,128)(2,1)} %param.12) | copy-start | bytes 196612
  338.1 3.7 %copy-start.6 = (bf16[32,1408]{1,0:T(8,128)(2,1)S(1)}, bf16[32,1408]{1,0:T(8,128)(2,1)}, u32[]{:S(2)}) copy-start(bf16[32,1408]{1,0:T(8,128)(2,1)} %get-tuple-element.74) | copy-start | bytes 270340
  338.1 3.7 %copy-start.7 = (bf16[32,1408]{1,0:T(8,128)(2,1)S(1)}, bf16[32,1408]{1,0:T(8,128)(2,1)}, u32[]{:S(2)}) copy-start(bf16[32,1408]{1,0:T(8,128)(2,1)} %get-tuple-element.75) | copy-start | bytes 270340
  338.1 3.7 %copy-start = (bf16[64,2,1312]{2,1,0:T(2,128)(2,1)S(1)}, bf16[64,2,1312]{2,1,0:T(2,128)(2,1)}, u32[]{:S(2)}) copy-start(bf16[64,2,1312]{2,1,0:T(2,128)(2,1)} %param.13) | copy-start | bytes 1007620
  340.1 7.3 %copy-start.1 = (bf16[512,1024]{1,0:T(8,128)(2,1)S(1)}, bf16[512,1024]{1,0:T(8,128)(2,1)}, u32[]{:S(2)}) copy-start(bf16[512,1024]{1,0:T(8,128)(2,1)} %get-tuple-element.69) | copy-start | bytes 3145732
  342.0 6.9 %copy-start.4 = (bf16[32,1408]{1,0:T(8,128)(2,1)S(1)}, bf16[32,1408]{1,0:T(8,128)(2,1)}, u32[]{:S(2)}) copy-start(bf16[32,1408]{1,0:T(8,128)(2,1)} %get-tuple-element.76) | copy-start | bytes 270340
  342.0 6.9 %copy-start.5 = (bf16[32,1408]{1,0:T(8,128)(2,1)S(1)}, bf16[32,1408]{1,0:T(8,128)(2,1)}, u32[]{:S(2)}) copy-start(bf16[32,1408]{1,0:T(8,128)(2,1)} %get-tuple-element.77) | copy-start | bytes 270340
  343.0 8.1 %collective-permute-start = (f32[2,64]{1,0:T(2,128)S(1)}, f32[2,64]{1,0:T(2,128)S(1)}, u32[]{:S(2)}, u32[]{:S(2)}) collective-permute-start(f32[2,64]{1,0:T(2,128)S(1)} %pad_maximum_fusion.5), channel_id=1, source_target_pairs={{0,1},{1,0},{2,3},{3,2},{4,5},{5,4},{6,7},{7,6},{8,9},{9,8},{10,11... | collective-permute-start | bytes 1544 | tf_op jit(solution)/shard_map/ppermute | solution.py:1128
  347.4 4.3 %copy-start.2 = (bf16[512,1024]{1,0:T(8,128)(2,1)S(1)}, bf16[512,1024]{1,0:T(8,128)(2,1)}, u32[]{:S(2)}) copy-start(bf16[512,1024]{1,0:T(8,128)(2,1)} %get-tuple-element.49) | copy-start | bytes 3145732

commit v7 on v6

--- a/solution.py
+++ b/solution.py
@@ -301,8 +301,8 @@
 class Gather:
     MESSAGES = 15
 
-    def __init__(self, own, buf, rows, order, peers, sems, base):
-        self.buf, self.rows, self.order, self.peers = buf, rows, order, peers
+    def __init__(self, own, buf, rows, order, hops, peers, sems, base):
+        self.buf, self.rows, self.order, self.hops, self.peers = buf, rows, order, hops, peers
         self.own = own.at[rows]
         self.send_sem, self.recv_sem = sems
         self.base = base
@@ -313,6 +313,7 @@
             [(i, j, 0) for i in range(n) for j in range(1, m)],
             [(i, j, k) for i in range(n) for j in range(m) for k in range(1, p)],
         ]
+        self.stages = self.stages[:hops]
         self.numbers = {at: n for n, at in enumerate(sum(self.stages, []))}
 
     def slot(self, at):
@@ -339,7 +340,8 @@
         if i:
             self.copy((i, 0, 0)).wait_recv()
         self.send(1, i)
-        self.send(2, i, 0)
+        if self.hops == 3:
+            self.send(2, i, 0)
 
     def relay_again(self, i):
         for j in self.middle:
@@ -347,7 +349,7 @@
             self.send(2, i, j)
 
     def finish(self):
-        for at in self.stages[2]:
+        for at in self.stages[-1]:
             self.copy(at).wait_recv()
         for at in self.numbers:
             self.copy(at).wait_send()
@@ -370,18 +372,20 @@
     sems = (send_sem, recv_sem)
     n = Gather.MESSAGES
     whole, low, high = pl.ds(0, 64), pl.ds(0, 32), pl.ds(32, 32)
+    third, fourth = pl.ds(32, 16), pl.ds(48, 16)
     plan = (
-        (a_own, w_qk, whole, "zyx"),
-        (b_own, w_vo, low, "zyx"),
-        (b_own, w_vo, high, "xyz"),
-        (g_own, w_gate, whole, "zyx"),
-        (u_own, w_up, low, "zyx"),
-        (u_own, w_up, high, "zxy"),
-        (d_own, w_down, low, "zyx"),
-        (d_own, w_down, high, "xyz"),
+        (a_own, w_qk, whole, "zyx", 3),
+        (b_own, w_vo, low, "zyx", 3),
+        (b_own, w_vo, high, "xyz", 3),
+        (g_own, w_gate, whole, "zyx", 3),
+        (u_own, w_up, low, "zyx", 3),
+        (u_own, w_up, third, "zxy", 3),
+        (u_own, w_up, fourth, "xyz", 3),
+        (d_own, w_down, low, "zyx", 2),
+        (d_own, w_down, high, "zxy", 2),
     )
     gathers = [Gather(*piece, peers, sems, i * n) for i, piece in enumerate(plan)]
-    one, early, two, three, late = gathers[:2], gathers[2], gathers[3:6], gathers[6], gathers[7]
+    one, early, two, late, three = gathers[:2], gathers[2], gathers[3:6], gathers[6], gathers[7:]
     owns = [
         pltpu.make_async_copy(src, dst.at[0, 0, 0], own_sem.at[i])
         for i, (src, dst) in enumerate(
@@ -464,9 +468,10 @@
             gather.relay_again(z)
     for gather in two:
         gather.relay(0)
+    late.start()
     move_d.wait()
-    late.start()
-    three.start()
+    for gather in three:
+        gather.start()
     for copy in owns[2:]:
         copy.start()
     swap_xh.wait()
@@ -482,7 +487,8 @@
             if z:
                 at_step(1 + z, gather.relay, z)
             at_step(6 + z, gather.relay_again, z)
-        at_step(9 + z, three.relay, z)
+        for gather in three:
+            at_step(9 + z, gather.relay, z)
     at_step(1, late.relay, 0)
     at_step(5, late.relay, 1)
     at_step(5, move_c.start)
@@ -563,8 +569,6 @@
         cot.at[pl.ds(0, half)], cot.at[pl.ds(half, half)], pair_send.at[3], pair_recv.at[3], peers["c"]
     )
     swap_cot.start()
-    for z in range(4):
-        three.relay_again(z)
     give.wait()
 
     def second_norm(i, carry):
@@ -579,7 +583,7 @@
         xn.at[pl.ds(0, half)], xn.at[pl.ds(half, half)], pair_send.at[2], pair_recv.at[2], peers["c"]
     )
     swap_xn.start()
-    for gather in two + [three, late]:
+    for gather in two + three + [late]:
         gather.finish()
     for copy in owns[2:]:
         copy.wait()
@@ -628,8 +632,8 @@
             pltpu.VMEM((half, width), F32),
             pltpu.VMEM((half, width), BF),
             pltpu.VMEM((half, width), BF),
-            pltpu.SemaphoreType.DMA((8 * Gather.MESSAGES,)),
-            pltpu.SemaphoreType.DMA((8 * Gather.MESSAGES,)),
+            pltpu.SemaphoreType.DMA((9 * Gather.MESSAGES,)),
+            pltpu.SemaphoreType.DMA((9 * Gather.MESSAGES,)),
             pltpu.SemaphoreType.DMA((4,)),
             pltpu.SemaphoreType.DMA((4,)),
             pltpu.SemaphoreType.DMA((5,)),
@@ -642,42 +646,222 @@
     )(*owned, x_half, cot_half, seg, inverse)
 
 
+class Reduce:
+    MESSAGES = 12
+    ORDER = (2, 3, 1, 0)
+
+    def __init__(self, parts, near, rows, axes, peers, sems, base, bufs, out):
+        self.parts, self.near, self.rows, self.axes, self.peers = parts, near, rows, axes, peers
+        self.send_sem, self.recv_sem = sems
+        self.base = base
+        self.one, self.two, self.three, self.sum = bufs
+        self.out = out
+
+    def link(self, i, src, dst, peer):
+        n = self.base + i
+        return remote(src, dst, self.send_sem.at[n], self.recv_sem.at[n], peer)
+
+    def first(self, z):
+        if self.axes == "xy":
+            src = self.parts.at[z, :, 1, self.rows]
+        else:
+            src = self.parts.at[z, 1, :, self.rows]
+        return self.link(z, src, self.one.at[z], self.peers[self.axes[1]])
+
+    def second(self, z):
+        return self.link(4 + z, self.one.at[z, 1], self.two.at[z], self.peers[self.axes[0]])
+
+    def third(self, z):
+        return self.link(7 + z, self.two.at[z], self.three.at[z - 1], self.peers["z%d" % z])
+
+    def start(self):
+        for z in self.ORDER:
+            self.first(z).start()
+
+    def add_first(self, z):
+        self.first(z).wait_recv()
+        self.one[z] = (self.one[z].astype(F32) + self.near(z).astype(F32)).astype(BF)
+
+    def relay_first(self, z):
+        self.add_first(z)
+        self.second(z).start()
+
+    def resume(self):
+        for z in self.ORDER:
+            self.second(z).start()
+
+    def relay_second(self, z):
+        self.second(z).wait_recv()
+        self.two[z] = (self.two[z].astype(F32) + self.one[z, 0].astype(F32)).astype(BF)
+        if z:
+            self.third(z).start()
+
+    def last(self):
+        moved, peer = exchanged()
+        return moved, self.link(11, self.sum, self.out, peer)
+
+    def total(self):
+        total = self.two[0].astype(F32)
+        for z in (1, 2, 3):
+            self.third(z).wait_recv()
+            total = total + self.three[z - 1].astype(F32)
+        return total
+
+    def finish(self):
+        self.sum[...] = self.total().astype(BF)
+        moved, copy = self.last()
+
+        @pl.when(moved)
+        def _():
+            copy.start()
+
+        @pl.when(jnp.logical_not(moved))
+        def _():
+            self.out[...] = self.sum[...]
+
+    def sent(self):
+        hops = (self.second,) if self.parts is None else (self.first, self.second)
+        thirds = [self.third(z) for z in (1, 2, 3)]
+        return [hop(z) for z in range(4) for hop in hops] + thirds
+
+    def close(self):
+        for copy in self.sent():
+            copy.wait_send()
+        moved, copy = self.last()
+
+        @pl.when(moved)
+        def _():
+            copy.wait()
+
+
+class ReduceAlongZ(Reduce):
+    def first(self, z):
+        src = self.parts.at[z, :, :, self.rows]
+        return self.link(z - 1, src, self.one.at[z - 1], self.peers["z%d" % z])
+
+    def second(self):
+        return self.link(3, self.two.at[:, 1], self.three.at[0:2], self.peers["y"])
+
+    def third(self):
+        return self.link(4, self.three.at[1], self.three.at[2], self.peers["x"])
+
+    def start(self):
+        for z in (2, 3, 1):
+            self.first(z).start()
+
+    def relay_first(self):
+        total = self.near().astype(F32)
+        for z in (1, 2, 3):
+            self.first(z).wait_recv()
+            total = total + self.one[z - 1].astype(F32)
+        self.two[...] = total.astype(BF)
+        self.second().start()
+
+    def relay_second(self):
+        self.second().wait_recv()
+        for x in (0, 1):
+            self.three[x] = (self.three[x].astype(F32) + self.two[x, 0].astype(F32)).astype(BF)
+        self.third().start()
+
+    def total(self):
+        self.third().wait_recv()
+        return self.three[0].astype(F32) + self.three[2].astype(F32)
+
+    def sent(self):
+        return [self.first(z) for z in (1, 2, 3)] + [self.second(), self.third()]
+
+
 def mlp_kernel(
-    xn, cot, w_gate, w_up, w_down, resid,
-    result, resid_grad, attn_cot, d_gate, d_up, d_down,
-    hidden, gate_grad, up_grad, own, sent, got, placed, send_sem, recv_sem, *moving,
+    down_in, xn, cot, w_gate, w_up, resid,
+    result, resid_grad, attn_cot, d_gate, d_up, d_low, d_high,
+    w_down, d_down, hidden, act, slope_up, gate_grad, up_grad, own, sent, got, placed,
+    send_sem, recv_sem, last_send, last_recv, first_send, first_recv, own_sem, *moving,
 ):
     length, width = xn.shape
     half = length // 2
     units = w_gate.shape[1]
-    peer = partners()["c"]
-    meet({"c": peer}, exchanged())
+    peers = {axis: partners()[axis] for axis in "xyc"}
     move = Move(placed, result, moving, 0)
-
-    def units_of(rows, cols):
-        gate = dotf(xn[rows, :], w_gate[:, cols], NN)
-        up = dotf(xn[rows, :], w_up[:, cols], NN)
-        grad = dotf(cot[rows, :], w_down[:, cols], NN).astype(BF).astype(F32)
-        act, slope = gelu_parts(gate)
-        hidden[rows, cols] = (act * up).astype(BF)
-        gate_grad[rows, cols] = (grad * up * slope).astype(BF)
-        up_grad[rows, cols] = (grad * act).astype(BF)
-
-    def phase(rows, put):
-        in_chunks(units, 256, lambda cols: units_of(rows, cols))
-
-        def sums(here):
-            put[0, :, here] = dotf(hidden[rows, :], w_down[here, :], NT).astype(put.dtype)
+    low, high = pl.ds(0, 32), pl.ds(32, 32)
+    most, few = pl.ds(0, 48), pl.ds(48, 16)
+    at_low = lambda ref, z, x: ref.at[z, x, :, low]
+    at_high = lambda ref, z, y: ref.at[z, :, y, high]
+    last = []
+    for z in range(4):
+        for i, (part, axis) in enumerate(((at_low, "x"), (at_high, "y"))):
+            n = 2 * z + i
+            last.append(
+                remote(
+                    part(down_in, z, 0), part(w_down, z, 1), last_send.at[n], last_recv.at[n], peers[axis]
+                )
+            )
+    every = pl.ds(0, 4)
+    owns = [
+        pltpu.make_async_copy(part(down_in, every, 0), part(w_down, every, 0), own_sem.at[i])
+        for i, part in enumerate((at_low, at_high))
+    ]
+    sems = (first_send, first_recv)
+    n = Reduce.MESSAGES
+    reduce_low = Reduce(
+        d_down, lambda z: d_down[z, 0, :, 0:48], most, "yx", peers, sems, 0, (d_low, None, None, None), None
+    )
+    reduce_high = Reduce(
+        d_down, lambda z: d_down[z, :, 0, 48:64], few, "xy", peers, sems, n, (d_high, None, None, None), None
+    )
+    meet(peers, exchanged())
+    for copy in last + owns:
+        copy.start()
+    back, front = pl.ds(half, half), pl.ds(0, half)
+
+    def gate_and_up(rows):
+        def step(cols):
+            gate = dotf(xn[rows, :], w_gate[:, cols], NN)
+            up = dotf(xn[rows, :], w_up[:, cols], NN)
+            value, slope = gelu_parts(gate)
+            hidden[rows, cols] = (value * up).astype(BF)
+            act[rows, cols] = value
+            slope_up[rows, cols] = up * slope
+
+        in_chunks(units, 256, step)
+
+    def units_back(rows):
+        def step(cols):
+            down = w_down[:, :, :, :, cols].reshape(width, cols.size)
+            grad = dotf(cot[rows, :], down, NN).astype(BF).astype(F32)
+            gate_grad[rows, cols] = (grad * slope_up[rows, cols]).astype(BF)
+            up_grad[rows, cols] = (grad * act[rows, cols]).astype(BF)
+
+        in_chunks(units, 256, step)
+
+    def sums(rows, put):
+        def step(z, carry):
+            here = pl.ds(pl.multiple_of(z * 256, 256), 256)
+            down = w_down[z].reshape(256, units)
+            put[0, :, here] = dotf(hidden[rows, :], down, NT).astype(put.dtype)
             both = dotf(gate_grad[rows, :], w_gate[here, :], NT)
             both = both + dotf(up_grad[rows, :], w_up[here, :], NT)
             put[1, :, here] = both.astype(put.dtype)
-
-        in_chunks(width, 256, sums)
-
-    phase(pl.ds(half, half), sent)
-    give = remote(sent, got, send_sem.at[0], recv_sem.at[0], peer)
+            return carry
+
+        lax.fori_loop(0, width // 256, step, 0)
+
+    gate_and_up(back)
+    gate_and_up(front)
+    for z in Reduce.ORDER:
+        left = jnp.transpose(cot[:, z * 256 : (z + 1) * 256])
+        d_down[z] = dotf(left, hidden[...], NN).astype(BF).reshape(2, 2, 64, units)
+        reduce_low.first(z).start()
+        reduce_high.first(z).start()
+    for copy in owns:
+        copy.wait()
+    for copy in last:
+        copy.wait()
+    units_back(back)
+    sums(back, sent)
+    give = remote(sent, got, send_sem.at[0], recv_sem.at[0], peers["c"])
     give.start()
-    phase(pl.ds(0, half), own)
+    units_back(front)
+    sums(front, own)
     give.wait()
 
     def finish(here):
@@ -692,185 +876,82 @@
 
     in_chunks(half, 64, finish)
     swap = remote(
-        attn_cot.at[pl.ds(0, half)], attn_cot.at[pl.ds(half, half)], send_sem.at[1], recv_sem.at[1], peer
+        attn_cot.at[pl.ds(0, half)], attn_cot.at[pl.ds(half, half)], send_sem.at[1], recv_sem.at[1], peers["c"]
     )
     swap.start()
     move.start()
 
     def weights(here):
-        left = jnp.transpose(cot[:, here])
-        d_down[here, :] = dotf(left, hidden[...], NN).astype(BF)
         left = jnp.transpose(xn[:, here])
         d_gate[here, :] = dotf(left, gate_grad[...], NN).astype(BF)
         d_up[here, :] = dotf(left, up_grad[...], NN).astype(BF)
 
     in_chunks(width, 256, weights)
+    for z in Reduce.ORDER:
+        reduce_low.add_first(z)
+        reduce_high.add_first(z)
+    for z in range(4):
+        reduce_low.first(z).wait_send()
+        reduce_high.first(z).wait_send()
     swap.wait()
     move.wait()
 
 
-def mlp_block(xn, cot, w_gate, w_up, w_down, resid):
+def mlp_block(down_in, xn, cot, w_gate, w_up, resid):
     length, width = xn.shape
     half = length // 2
     units = w_gate.shape[1]
+    shard = width // 16
     vmem = pl.BlockSpec(memory_space=pltpu.VMEM)
+    any_ = pl.BlockSpec(memory_space=pl.ANY)
     grads = jax.ShapeDtypeStruct((width, units), BF)
+    dma = lambda n: pltpu.SemaphoreType.DMA((n,))
     return pl.pallas_call(
         mlp_kernel,
-        in_specs=[vmem] * 6,
-        out_specs=[vmem] * 6,
+        in_specs=[any_] + [vmem] * 5,
+        out_specs=[any_] + [vmem] * 6,
         out_shape=[
             jax.ShapeDtypeStruct((half, width), BF),
             jax.ShapeDtypeStruct((half, width), F32),
             jax.ShapeDtypeStruct((length, width), BF),
             grads,
             grads,
-            grads,
+            jax.ShapeDtypeStruct((4, 2, shard * 3 // 4, units), BF),
+            jax.ShapeDtypeStruct((4, 2, shard // 4, units), BF),
         ],
-        scratch_shapes=[pltpu.VMEM((length, units), BF)] * 3
+        scratch_shapes=[pltpu.VMEM(SHARD + (shard, units), BF)] * 2
         + [
+            pltpu.VMEM((length, units), BF),
+            pltpu.VMEM((length, units), F32),
+            pltpu.VMEM((length, units), F32),
+            pltpu.VMEM((length, units), BF),
+            pltpu.VMEM((length, units), BF),
             pltpu.VMEM((2, half, width), F32),
             pltpu.VMEM((2, half, width), BF),
             pltpu.VMEM((2, half, width), BF),
             pltpu.VMEM((half, width), BF),
-            pltpu.SemaphoreType.DMA((2,)),
-            pltpu.SemaphoreType.DMA((2,)),
         ]
+        + [dma(2), dma(2), dma(8), dma(8), dma(2 * Reduce.MESSAGES), dma(2 * Reduce.MESSAGES), dma(2)]
         + move_sems(1),
         compiler_params=pltpu.CompilerParams(
-            collective_id=1, has_side_effects=True, vmem_limit_bytes=60 << 20
+            collective_id=1, has_side_effects=True, vmem_limit_bytes=63 << 20
         ),
         name="mlp_block",
-    )(xn, cot, w_gate, w_up, w_down, resid)
-
-
-class Reduce:
-    MESSAGES = 12
-    ORDER = (2, 3, 1, 0)
-
-    def __init__(self, parts, near, rows, axes, peers, sems, base, bufs, out):
-        self.parts, self.near, self.rows, self.axes, self.peers = parts, near, rows, axes, peers
-        self.send_sem, self.recv_sem = sems
-        self.base = base
-        self.one, self.two, self.three, self.sum = bufs
-        self.out = out
-
-    def link(self, i, src, dst, peer):
-        n = self.base + i
-        return remote(src, dst, self.send_sem.at[n], self.recv_sem.at[n], peer)
-
-    def first(self, z):
-        if self.axes == "xy":
-            src = self.parts.at[z, :, 1, self.rows]
-        else:
-            src = self.parts.at[z, 1, :, self.rows]
-        return self.link(z, src, self.one.at[z], self.peers[self.axes[1]])
-
-    def second(self, z):
-        return self.link(4 + z, self.one.at[z, 1], self.two.at[z], self.peers[self.axes[0]])
-
-    def third(self, z):
-        return self.link(7 + z, self.two.at[z], self.three.at[z - 1], self.peers["z%d" % z])
-
-    def start(self):
-        for z in self.ORDER:
-            self.first(z).start()
-
-    def relay_first(self, z):
-        self.first(z).wait_recv()
-        self.one[z] = (self.one[z].astype(F32) + self.near(z).astype(F32)).astype(BF)
-        self.second(z).start()
-
-    def relay_second(self, z):
-        self.second(z).wait_recv()
-        self.two[z] = (self.two[z].astype(F32) + self.one[z, 0].astype(F32)).astype(BF)
-        if z:
-            self.third(z).start()
-
-    def last(self):
-        moved, peer = exchanged()
-        return moved, self.link(11, self.sum, self.out, peer)
-
-    def total(self):
-        total = self.two[0].astype(F32)
-        for z in (1, 2, 3):
-            self.third(z).wait_recv()
-            total = total + self.three[z - 1].astype(F32)
-        return total
-
-    def finish(self):
-        self.sum[...] = self.total().astype(BF)
-        moved, copy = self.last()
-
-        @pl.when(moved)
-        def _():
-            copy.start()
-
-        @pl.when(jnp.logical_not(moved))
-        def _():
-            self.out[...] = self.sum[...]
-
-    def sent(self):
-        thirds = [self.third(z) for z in (1, 2, 3)]
-        return [hop(z) for z in range(4) for hop in (self.first, self.second)] + thirds
-
-    def close(self):
-        for copy in self.sent():
-            copy.wait_send()
-        moved, copy = self.last()
-
-        @pl.when(moved)
-        def _():
-            copy.wait()
-
-
-class ReduceAlongZ(Reduce):
-    def first(self, z):
-        src = self.parts.at[z, :, :, self.rows]
-        return self.link(z - 1, src, self.one.at[z - 1], self.peers["z%d" % z])
-
-    def second(self):
-        return self.link(3, self.two.at[:, 1], self.three.at[0:2], self.peers["y"])
-
-    def third(self):
-        return self.link(4, self.three.at[1], self.three.at[2], self.peers["x"])
-
-    def start(self):
-        for z in (2, 3, 1):
-            self.first(z).start()
-
-    def relay_first(self):
-        total = self.near().astype(F32)
-        for z in (1, 2, 3):
-            self.first(z).wait_recv()
-            total = total + self.one[z - 1].astype(F32)
-        self.two[...] = total.astype(BF)
-        self.second().start()
-
-    def relay_second(self):
-        self.second().wait_recv()
-        for x in (0, 1):
-            self.three[x] = (self.three[x].astype(F32) + self.two[x, 0].astype(F32)).astype(BF)
-        self.third().start()
-
-    def total(self):
-        self.third().wait_recv()
-        return self.three[0].astype(F32) + self.three[2].astype(F32)
-
-    def sent(self):
-        return [self.first(z) for z in (1, 2, 3)] + [self.second(), self.third()]
+    )(down_in, xn, cot, w_gate, w_up, resid)
 
 
 def backward_kernel(
-    d_gate, d_up, d_down, q, k, v, o, lse, attn_cot, w_qk, w_vo, xh, x_half, resid_grad,
+    d_gate, d_up, d_low, d_high, q, k, v, o, lse, attn_cot, w_qk, w_vo, xh, x_half, resid_grad,
     cos, upper, lower, seg_col, seg_row,
     token_grad, s_gate, s_up_low, s_up_high, s_down_low, s_down_high, s_qk, s_vo_low, s_vo_high,
     d_qk, d_vo, pg, heads_grad, kh, dk, dv, own, sent, got, placed,
-    near_gate, near_up_low, near_up_high, near_low, near_high,
+    near_gate, near_up_low, near_up_high,
     *rest,
 ):
-    bufs = [rest[4 * i : 4 * i + 4] for i in range(8)]
-    send_sem, recv_sem, pair_send, pair_recv, near_sem, *moving = rest[32:]
+    bufs = [rest[4 * i : 4 * i + 4] for i in range(3)]
+    bufs += [(first,) + rest[12 + 3 * i : 15 + 3 * i] for i, first in enumerate((d_low, d_high))]
+    bufs += [rest[18 + 4 * i : 22 + 4 * i] for i in range(3)]
+    send_sem, recv_sem, pair_send, pair_recv, near_sem, *moving = rest[30:]
     length, width = xh.shape
     half = length // 2
     cols = q.shape[1]
@@ -879,15 +960,14 @@
     peers = partners()
     sems = (send_sem, recv_sem)
     n = Reduce.MESSAGES
-    whole, low, high = pl.ds(0, 64), pl.ds(0, 32), pl.ds(32, 32)
-    most, few = pl.ds(0, 48), pl.ds(48, 16)
+    whole, most, few = pl.ds(0, 64), pl.ds(0, 48), pl.ds(48, 16)
     held = lambda ref: (lambda z: ref[z])
     plan = (
         (Reduce, d_gate, held(near_gate), whole, "yx", s_gate),
-        (Reduce, d_up, held(near_up_low), low, "yx", s_up_low),
-        (Reduce, d_up, held(near_up_high), high, "xy", s_up_high),
-        (Reduce, d_down, held(near_low), low, "yx", s_down_low),
-        (ReduceAlongZ, d_down, lambda: near_high[...], high, None, s_down_high),
+        (Reduce, d_up, held(near_up_low), most, "yx", s_up_low),
+        (ReduceAlongZ, d_up, lambda: near_up_high[...], few, None, s_up_high),
+        (Reduce, None, None, most, "yx", s_down_low),
+        (Reduce, None, None, few, "xy", s_down_high),
         (Reduce, d_qk, lambda z: d_qk[z, 0], whole, "yx", s_qk),
         (Reduce, d_vo, lambda z: d_vo[z, :, 0, 0:48], most, "xy", s_vo_low),
         (ReduceAlongZ, d_vo, lambda: d_vo[0, :, :, 48:64], few, None, s_vo_high),
@@ -902,18 +982,19 @@
         for i, (src, dst) in enumerate(
             (
                 (d_gate.at[:, 0], near_gate),
-                (d_up.at[:, 0, :, low], near_up_low),
-                (d_up.at[:, :, 0, high], near_up_high),
-                (d_down.at[:, 0, :, low], near_low),
-                (d_down.at[0, :, :, high], near_high),
+                (d_up.at[:, 0, :, most], near_up_low),
+                (d_up.at[0, :, :, few], near_up_high),
             )
         )
     ]
     for copy in nears:
         copy.start()
     meet(peers, exchanged())
-    for part in (down_high, up_high, gate, up_low):
-        part.start()
+    up_high.start()
+    down_low.resume()
+    down_high.resume()
+    gate.start()
+    up_low.start()
 
     def heads(here):
         heads_grad[here, :] = dotf(attn_cot[here, :], w_vo[:, cols:], NN).astype(BF)
@@ -932,10 +1013,12 @@
 
     events = {}
     for i, z in enumerate(Reduce.ORDER):
-        events.setdefault(2 + 4 * i, []).append(lambda z=z: gate.relay_first(z))
-        events.setdefault(3 + 2 * i, []).append(lambda z=z: up_high.relay_first(z))
-    events.setdefault(11, []).append(down_low.start)
-    events.setdefault(12, []).append(down_high.relay_first)
+        if i < 3:
+            events.setdefault(4 + 4 * i, []).append(lambda z=z: gate.relay_first(z))
+        events.setdefault(3 + 3 * i, []).append(lambda z=z: down_low.relay_second(z))
+        events.setdefault(2 + 3 * i, []).append(lambda z=z: down_high.relay_second(z))
+    events.setdefault(7, []).append(up_high.relay_first)
+    events.setdefault(13, []).append(up_high.relay_second)
     lane = lax.broadcasted_iota(jnp.int32, (length, 128), 1)
     first = lane < HD
 
@@ -996,6 +1079,7 @@
         return carry
 
     lax.fori_loop(0, pairs, pair, 0)
+    gate.relay_first(Reduce.ORDER[3])
 
     def weights(z, carry):
         left = jnp.transpose(xh[:, pl.ds(pl.multiple_of(z * 256, 256), 256)])
@@ -1020,9 +1104,8 @@
     give = remote(sent, got, pair_send.at[0], pair_recv.at[0], peers["c"])
     give.start()
     back(pl.ds(0, half), own)
-    for z in Reduce.ORDER:
-        gate.relay_second(z)
-    down_high.relay_second()
+    down_low.finish()
+    down_high.finish()
     give.wait()
 
     def finish(here):
@@ -1034,26 +1117,21 @@
     in_chunks(half, 64, finish)
     move = Move(placed, token_grad, moving, 0)
     move.start()
+    up_high.finish()
     for z in Reduce.ORDER:
         up_low.relay_first(z)
-        up_high.relay_second(z)
+        gate.relay_second(z)
+    vo_high.relay_first()
+    for z in Reduce.ORDER:
+        vo_low.relay_first(z)
     gate.finish()
     for z in Reduce.ORDER:
-        down_low.relay_first(z)
-        vo_low.relay_first(z)
-    up_high.finish()
-    vo_high.relay_first()
-    for z in Reduce.ORDER:
+        qk.relay_first(z)
         up_low.relay_second(z)
-    down_high.finish()
-    for z in Reduce.ORDER:
-        qk.relay_first(z)
-        down_low.relay_second(z)
-    up_low.finish()
     vo_high.relay_second()
     for z in Reduce.ORDER:
         vo_low.relay_second(z)
-    down_low.finish()
+    up_low.finish()
     for z in Reduce.ORDER:
         qk.relay_second(z)
     vo_high.finish()
@@ -1072,21 +1150,22 @@
     shard = width // 16
     vmem = pl.BlockSpec(memory_space=pltpu.VMEM)
     any_ = pl.BlockSpec(memory_space=pl.ANY)
-    sizes = [(shard, units)] + [(shard // 2, units)] * 4
-    sizes += [(shard, 2 * cols), (shard * 3 // 4, 2 * cols), (shard // 4, 2 * cols)]
-    along_z = (4, 7)
+    most, few = shard * 3 // 4, shard // 4
+    sizes = [(shard, units)] + [(most, units), (few, units)] * 2
+    sizes += [(shard, 2 * cols), (most, 2 * cols), (few, 2 * cols)]
+    along_z, begun = (2, 7), (3, 4)
     bufs = []
     for i, size in enumerate(sizes):
         if i in along_z:
             lead = (3, 2, 2), (2, 2), (3,)
         else:
             lead = (4, 2), (4,), (3,)
-        bufs += [pltpu.VMEM(n + size, BF) for n in lead + ((),)]
-    nears = [pltpu.VMEM(((2, 2) if i in along_z else (4, 2)) + size, BF) for i, size in enumerate(sizes[:5])]
+        bufs += [pltpu.VMEM(n + size, BF) for n in lead[i in begun :] + ((),)]
+    nears = [pltpu.VMEM(((2, 2) if i in along_z else (4, 2)) + size, BF) for i, size in enumerate(sizes[:3])]
     messages = 8 * Reduce.MESSAGES
     return pl.pallas_call(
         backward_kernel,
-        in_specs=[any_] * 3 + [vmem] * 16,
+        in_specs=[any_] * 2 + [vmem] * 18,
         out_specs=[vmem] * 9,
         out_shape=[jax.ShapeDtypeStruct((half, width), BF)]
         + [jax.ShapeDtypeStruct(size, BF) for size in sizes],
@@ -1109,7 +1188,7 @@
             pltpu.SemaphoreType.DMA((messages,)),
             pltpu.SemaphoreType.DMA((1,)),
             pltpu.SemaphoreType.DMA((1,)),
-            pltpu.SemaphoreType.DMA((5,)),
+            pltpu.SemaphoreType.DMA((3,)),
         ]
         + move_sems(1),
         compiler_params=pltpu.CompilerParams(
@@ -1117,7 +1196,7 @@
         ),
         name="backward_block",
     )(
-        *(g.reshape(SHARD + (shard, units)) for g in grads),
+        *(g.reshape(SHARD + (shard, units)) for g in grads[:2]), *grads[2:],
         *heads, lse, attn_cot, w_qk, w_vo, xh, x_half, resid_grad, *tables, seg_col, seg_row,
     )
 
@@ -1192,8 +1271,8 @@
                 q, k, v, o, lse, xh, w_qk, w_vo, resid, xn, x_half, cot_all, *tables, seg_col, seg_row,
                 w_gate, w_up, w_dn,
             ) = forward_block(owned, tokens[0], cotangent[0], seg, inverse)
-            w_qk, w_vo, w_gate, w_up, w_dn = (
-                w.reshape(-1, w.shape[-1]) for w in (w_qk, w_vo, w_gate, w_up, w_dn)
+            w_qk, w_vo, w_gate, w_up = (
+                w.reshape(-1, w.shape[-1]) for w in (w_qk, w_vo, w_gate, w_up)
             )
         else:
             w_qk, w_vo, w_gate, w_up, w_dn = (
@@ -1212,9 +1291,7 @@
             xh_two, scale_two = normalize(resid)
             xn = comm.gather_rows(xh_two.astype(BF))
         if paired:
-            result, resid_grad, attn_cot, d_gate, d_up, d_down = mlp_block(
-                xn, cot_all, w_gate, w_up, w_dn, resid
-            )
+            result, resid_grad, attn_cot, *grads = mlp_block(w_dn, xn, cot_all, w_gate, w_up, resid)
         else:
             gate, up = dotf(xn, w_gate, NN), dotf(xn, w_up, NN)
             act, slope = gelu_parts(gate)
@@ -1232,7 +1309,7 @@
 
         if paired:
             token_grad, *sums = backward_block(
-                (d_gate, d_up, d_down), (q, k, v, o), lse, attn_cot, w_qk, w_vo, xh, x_half,
+                grads, (q, k, v, o), lse, attn_cot, w_qk, w_vo, xh, x_half,
                 resid_grad, tables, seg_col, seg_row,
             )
             token_grad = token_grad.astype(F32)

time: 354 us -> 339 us (0.958)
  Pallas kernels: 329 us -> 319 us
  starting transfers between devices: 4.36 us -> 0.07 us
    pallas_call x1, Pallas kernels: 142 us -> 134 us  [forward_block(): pl.pallas_call(forward_kernel, in_specs=[any_] * 8 + [vmem], out_specs=[v...]
    ppermute x1, starting transfers between devices: 4.36 us -> 0.07 us  [sum_tensor(): return value + lax.ppermute(value, ('dp', 'tensor'), pairs)]
where the time goes in v7:
time: 339 us; the launch traced here: 338 us
  Pallas kernels  319 us (94%)
  local copies, waits for them, and re-layouts  9.93 us (3%)
  other arithmetic  8.48 us (3%)
    pallas_call x1, Pallas kernels, forward_block(): pl.pallas_call(forward_kernel, in_specs=[any_] * 8 + [vmem], out_specs=[v...  134 us
    pallas_call x1, Pallas kernels, backward_block(): pl.pallas_call(backward_kernel, in_specs=[any_] * 2 + [vmem] * 18, out_sp...  128 us
    pallas_call x1, Pallas kernels, mlp_block(): pl.pallas_call(mlp_kernel, in_specs=[any_] + [vmem] * 5, out_specs=[any_]...  56.4 us
  transfers between devices with their start and end apart: 1, of which 0 were waited for; matrix products, arithmetic and copies ran while one was open for 1% of the time, Pallas kernels for 0%

profile of v7, /device:TPU:0, one launch (start us, length us, event | category | flops | bytes accessed | tf_op | source)
XLA Modules:
  0.0 338.3 jit_solution(8692559313568907370)
XLA Ops:
  0.6 0.0 copy-start.3
  0.6 0.0 copy-start.6
  0.7 0.7 convert_element_type.84
  1.4 0.7 convert_element_type.94
  2.0 0.1 tile.10
  2.1 0.7 convert_element_type.99
  2.8 1.0 copy.17
  3.8 1.6 pad.12.d_in
  5.4 0.1 fusion.1
  5.6 0.7 pad.11.u_in
  6.3 0.7 pad.10.g_in
  7.0 0.0 copy-done.3
  7.0 0.1 fusion.5
  7.1 0.0 copy-done.6
  7.1 0.7 pad_maximum_fusion.3
  7.8 0.6 broadcast_in_dim.23.inverse
  8.4 0.6 broadcast_in_dim.22.seg_in
  9.0 134.4 %forward_block.1 = (bf16[1024,512]{1,0:T(8,128)(2,1)}, bf16[1024,512]{1,0:T(8,128)(2,1)}, bf16[1024,512]{1,0:T(8,128)(2,1)}, bf16[1024,512]{1,0:T(8,128)(2,1)}, ...) custom-call(bf16[64,1024]{1,0:T(8,128)(2,1)} %get-tuple-element.103., ...), custom_call_target="tpu_custom_call" | custom-call | tf_op jit(solution)/shard_map/forward_block/pallas_call | solution.py:607
  143.4 56.4 %mlp_block.1 = (bf16[512,1024]{1,0:T(8,128)(2,1)}, f32[512,1024]{1,0:T(8,128)}, bf16[1024,1024]{1,0:T(8,128)(2,1)}, bf16[1024,1408]{1,0:T(8,128)(2,1)}, bf16[102...) custom-call(bf16[4,2,2,64,1408]{4,3,2,1,0:T(8,128)(2,1)} %get-tuple-element.44.down_in, ...), custom_call_target="tpu_custom_call" | custom-call | tf_op jit(solution)/shard_map/mlp_block/pallas_call | solution.py:909
  199.8 128.2 %backward_block.1 = (bf16[512,1024]{1,0:T(8,128)(2,1)}, bf16[64,1408]{1,0:T(8,128)(2,1)}, bf16[48,1408]{1,0:T(8,128)(2,1)}, bf16[16,1408]{1,0:T(8,128)(2,1)}, bf...) custom-call(bf16[4,2,2,64,1408]{4,3,2,1,0:T(8,128)(2,1)} %bitcast.56, ...), custom_call_target="tpu_custom_call" | custom-call | tf_op jit(solution)/shard_map/backward_block/pallas_call | solution.py:1166
  328.0 0.0 copy-start.5
  328.0 0.0 copy-start.8
  328.0 0.0 copy-start
  328.1 1.0 slice_bitcast_fusion.2
  329.1 0.9 convert_element_type.101
  330.0 0.0 copy-start.1
  330.0 1.0 maximum_convert_fusion
  331.0 0.7 slice_bitcast_fusion.3
  331.7 0.0 copy-done.5
  331.7 0.0 copy-done.8
  331.7 0.0 copy-done
  331.7 0.2 convert_multiply_fusion
  332.0 0.0 copy-start.4
  332.0 0.0 copy-start.7
  332.0 0.9 fusion.3
  332.9 0.1 collective-permute-start
  333.0 0.0 copy-done.1
  333.0 0.0 copy-start.2
  333.0 1.6 bitcast_convert_fusion
  334.6 0.0 copy-done.4
  334.6 0.0 copy-done.7
  334.6 0.8 convert_bitcast_fusion
  335.4 1.4 copy.20
  336.8 0.0 collective-permute-done
  336.8 0.5 slice_bitcast_fusion.7
  337.3 0.0 copy-done.2
  337.3 1.0 copy.23
  (6 shorter events, 0.1 us)
Async XLA Ops:
  0.6 6.3 %copy-start.3 = (bf16[64,3,512]{2,0,1:T(8,128)(2,1)S(1)}, bf16[64,3,512]{2,0,1:T(8,128)(2,1)}, u32[]{:S(2)}) copy-start(bf16[64,3,512]{2,0,1:T(8,128)(2,1)} %param.11) | copy-start | bytes 589828
  0.6 6.4 %copy-start.6 = (bf16[512,64]{0,1:T(8,128)(2,1)S(1)}, bf16[512,64]{0,1:T(8,128)(2,1)}, u32[]{:S(2)}) copy-start(bf16[512,64]{0,1:T(8,128)(2,1)} %param.12) | copy-start | bytes 196612
  328.0 3.7 %copy-start.5 = (bf16[48,1408]{1,0:T(8,128)(2,1)S(1)}, bf16[48,1408]{1,0:T(8,128)(2,1)}, u32[]{:S(2)}) copy-start(bf16[48,1408]{1,0:T(8,128)(2,1)} %get-tuple-element.76) | copy-start | bytes 405508
  328.0 3.7 %copy-start.8 = (bf16[16,1408]{1,0:T(8,128)(2,1)S(1)}, bf16[16,1408]{1,0:T(8,128)(2,1)}, u32[]{:S(2)}) copy-start(bf16[16,1408]{1,0:T(8,128)(2,1)} %get-tuple-element.77) | copy-start | bytes 135172
  328.0 3.7 %copy-start = (bf16[64,2,1312]{2,1,0:T(2,128)(2,1)S(1)}, bf16[64,2,1312]{2,1,0:T(2,128)(2,1)}, u32[]{:S(2)}) copy-start(bf16[64,2,1312]{2,1,0:T(2,128)(2,1)} %param.13) | copy-start | bytes 1007620
  330.0 3.0 copy-start.1
  332.0 2.6 copy-start.4
  332.0 2.6 copy-start.7
  332.9 3.9 %collective-permute-start = (f32[2,64]{1,0:T(2,128)S(1)}, f32[2,64]{1,0:T(2,128)S(1)}, u32[]{:S(2)}, u32[]{:S(2)}) collective-permute-start(f32[2,64]{1,0:T(2,128)S(1)} %pad_maximum_fusion.5), channel_id=1, source_target_pairs={{0,1},{1,0},{2,3},{3,2},{4,5},{5,4},{6,7},{7,6},{8,9},{9,8},{10,11... | collective-permute-start | bytes 1544 | tf_op jit(solution)/shard_map/ppermute | solution.py:1207
  333.0 4.3 %copy-start.2 = (bf16[512,1024]{1,0:T(8,128)(2,1)S(1)}, bf16[512,1024]{1,0:T(8,128)(2,1)}, u32[]{:S(2)}) copy-start(bf16[512,1024]{1,0:T(8,128)(2,1)} %get-tuple-element.50) | copy-start | bytes 3145732

commit v8 on v7

--- a/solution.py
+++ b/solution.py
@@ -301,9 +301,10 @@
 class Gather:
     MESSAGES = 15
 
-    def __init__(self, own, buf, rows, order, hops, peers, sems, base):
-        self.buf, self.rows, self.order, self.hops, self.peers = buf, rows, order, hops, peers
-        self.own = own.at[rows]
+    def __init__(self, own, buf, rows, cols, order, hops, peers, sems, base):
+        self.buf, self.order, self.hops, self.peers = buf, order, hops, peers
+        self.part = (rows, cols)
+        self.own = own.at[self.part]
         self.send_sem, self.recv_sem = sems
         self.base = base
         n, m, p = (AXIS[axis] for axis in order)
@@ -318,7 +319,7 @@
 
     def slot(self, at):
         where = dict(zip(self.order, at))
-        return self.buf.at[where["z"], where["x"], where["y"], self.rows]
+        return self.buf.at[(where["z"], where["x"], where["y"]) + self.part]
 
     def copy(self, at):
         hop = max(i for i in range(3) if at[i])
@@ -357,7 +358,7 @@
 
 def forward_kernel(
     a_in, b_in, g_in, u_in, d_in, x_in, c_in, seg_in, inverse,
-    q, k, v, o, lse, xh, w_qk, w_vo, resid, xn, x_half, cot, cos, upper, lower, seg_col, seg_row,
+    q, k, v, o, lse, xh, w_qkv, w_out, resid, xn, x_half, cot, cos, upper, lower, seg_col, seg_row,
     w_gate, w_up, w_down,
     a_own, b_own, g_own, u_own, d_own, c_own, seg_own,
     kh, x_rel, part, sent, got, send_sem, recv_sem, pair_send, pair_recv, own_sem, *moving,
@@ -372,24 +373,24 @@
     sems = (send_sem, recv_sem)
     n = Gather.MESSAGES
     whole, low, high = pl.ds(0, 64), pl.ds(0, 32), pl.ds(32, 32)
-    third, fourth = pl.ds(32, 16), pl.ds(48, 16)
+    wide = w_qkv.shape[4] // 2
+    all_ = lambda ref: pl.ds(0, ref.shape[-1])
     plan = (
-        (a_own, w_qk, whole, "zyx", 3),
-        (b_own, w_vo, low, "zyx", 3),
-        (b_own, w_vo, high, "xyz", 3),
-        (g_own, w_gate, whole, "zyx", 3),
-        (u_own, w_up, low, "zyx", 3),
-        (u_own, w_up, third, "zxy", 3),
-        (u_own, w_up, fourth, "xyz", 3),
-        (d_own, w_down, low, "zyx", 2),
-        (d_own, w_down, high, "zxy", 2),
+        (a_own, w_qkv, whole, pl.ds(0, wide), "zyx", 3),
+        (a_own, w_qkv, whole, pl.ds(wide, wide), "zyx", 3),
+        (b_own, w_out, whole, all_(w_out), "zxy", 3),
+        (g_own, w_gate, whole, all_(w_gate), "zyx", 3),
+        (u_own, w_up, low, all_(w_up), "zyx", 3),
+        (u_own, w_up, high, all_(w_up), "xyz", 3),
+        (d_own, w_down, low, all_(w_down), "zyx", 2),
+        (d_own, w_down, high, all_(w_down), "zxy", 2),
     )
     gathers = [Gather(*piece, peers, sems, i * n) for i, piece in enumerate(plan)]
-    one, early, two, late, three = gathers[:2], gathers[2], gathers[3:6], gathers[6], gathers[7:]
+    near, far, out, two, late, three = *gathers[:3], gathers[3:5], gathers[5], gathers[6:]
     owns = [
         pltpu.make_async_copy(src, dst.at[0, 0, 0], own_sem.at[i])
         for i, (src, dst) in enumerate(
-            ((a_own, w_qk), (b_own, w_vo), (g_own, w_gate), (u_own, w_up), (d_own, w_down))
+            ((a_own, w_qkv), (b_own, w_out), (g_own, w_gate), (u_own, w_up), (d_own, w_down))
         )
     ]
     move_a, move_b, move_x, move_seg, move_g, move_u, move_d, move_c = (
@@ -408,7 +409,7 @@
         )
     )
     meet(peers, exchanged())
-    for move in (move_a, move_b, move_seg, move_x, move_g, move_u, move_d):
+    for move in (move_a, move_seg, move_x):
         move.start()
 
     def tables(here):
@@ -423,25 +424,20 @@
         lower[here, :] = jnp.where(front, 0.0, sin)
 
     move_a.wait()
-    move_b.wait()
-    early.start()
-    for gather in one:
-        gather.start()
-    for gather in [early] + one:
-        gather.relay(0)
-    for copy in owns[:2]:
-        copy.start()
+    near.start()
+    far.start()
+    near.relay(0)
+    owns[0].start()
     in_chunks(length, 64, tables)
-    early.relay(1)
+    for z in (1, 2, 3):
+        near.relay(z)
+    for move in (move_b, move_g, move_u, move_d):
+        move.start()
     move_seg.wait()
     ids = seg_own[...]
     ids = jnp.where(core == 0, ids, jnp.concatenate([ids[:, half:], ids[:, :half]], axis=1))
     seg_row[...] = ids
     seg_col[...] = jnp.transpose(jnp.broadcast_to(ids[0:1, :], (128, length)))
-    early.relay_again(0)
-    for gather in one:
-        gather.relay(1)
-    early.relay_again(1)
     move_x.wait()
 
     def first_norm(i, carry):
@@ -452,64 +448,68 @@
         return carry
 
     lax.fori_loop(0, half // 128, first_norm, 0)
-    for z in (2, 3):
-        for gather in one:
-            gather.relay(z)
     swap_xh = remote(
         xh.at[pl.ds(0, half)], xh.at[pl.ds(half, half)], pair_send.at[0], pair_recv.at[0], peers["c"]
     )
     swap_xh.start()
+    for z in range(4):
+        near.relay_again(z)
+        far.relay(z)
+    move_b.wait()
+    out.start()
     move_g.wait()
     move_u.wait()
+    late.start()
     for gather in two:
         gather.start()
-    for z in range(4):
-        for gather in one:
-            gather.relay_again(z)
+    out.relay(0)
+    late.relay(0)
     for gather in two:
         gather.relay(0)
-    late.start()
     move_d.wait()
     for gather in three:
         gather.start()
-    for copy in owns[2:]:
+    for copy in owns[1:]:
         copy.start()
     swap_xh.wait()
-    for gather in one + [early]:
-        gather.finish()
-    for copy in owns[:2]:
-        copy.wait()
+    near.finish()
+    owns[0].wait()
 
     events = {}
     at_step = lambda step, call, *args: events.setdefault(step, []).append((call, args))
     for z in range(4):
+        at_step(z, far.relay_again, z)
+        if z:
+            at_step(z, out.relay, z)
+        at_step(5 + z, out.relay_again, z)
         for gather in two:
             if z:
-                at_step(1 + z, gather.relay, z)
-            at_step(6 + z, gather.relay_again, z)
+                at_step(1 + 2 * z, gather.relay, z)
+            at_step(9 + z, gather.relay_again, z)
         for gather in three:
-            at_step(9 + z, gather.relay, z)
-    at_step(1, late.relay, 0)
-    at_step(5, late.relay, 1)
+            at_step(11 + z, gather.relay, z)
+    at_step(4, late.relay, 1)
     at_step(5, move_c.start)
-    at_step(9, late.relay_again, 0)
-    at_step(12, late.relay_again, 1)
+    at_step(6, late.relay_again, 0)
+    at_step(8, late.relay_again, 1)
+    at_step(length // rows * pairs // 2 - 1, far.finish)
     first = lax.broadcasted_iota(jnp.int32, (length, 128), 1) < HD
 
     def pair(h, carry):
         lanes = pl.ds(pl.multiple_of(h * 128, 128), 128)
-        lanes_k = pl.ds(pl.multiple_of((h + pairs) * 128, 128), 128)
-        weight = lambda ref, cols: ref[:, :, :, :, cols].reshape(width, 128)
+        weight = lambda i: w_qkv[
+            :, :, :, :, pl.ds(pl.multiple_of((3 * h + i) * 128, 128), 128)
+        ].reshape(width, 128)
         tokens = xh[...]
-        qf = dotf(tokens, weight(w_qk, lanes), NN)
+        qf = dotf(tokens, weight(0), NN)
         qf = qf * cos[...] + turn(qf, upper[...], lower[...])
         q[:, lanes] = (qf * (1.0 / math.sqrt(HD))).astype(BF)
-        kf = dotf(tokens, weight(w_qk, lanes_k), NN)
+        kf = dotf(tokens, weight(1), NN)
         kf = (kf * cos[...] + turn(kf, upper[...], lower[...])).astype(BF)
         k[:, lanes] = kf
         kh[0] = jnp.where(first, kf, jnp.zeros_like(kf))
         kh[1] = jnp.where(first, jnp.zeros_like(kf), kf)
-        v[:, lanes] = dotf(tokens, weight(w_vo, lanes), NN).astype(BF)
+        v[:, lanes] = dotf(tokens, weight(2), NN).astype(BF)
 
         def block(i, carry):
             for step, calls in events.items():
@@ -540,7 +540,9 @@
         return lax.fori_loop(0, length // rows, block, carry)
 
     lax.fori_loop(0, pairs, pair, 0)
-    w_o = w_vo[:, :, :, :, pairs * 128 :].reshape(width, pairs * 128)
+    out.finish()
+    owns[1].wait()
+    w_o = w_out[...].reshape(width, pairs * 128)
 
     def project(i, carry):
         at = pl.multiple_of(half + i * rows, rows)
@@ -594,7 +596,7 @@
 def forward_block(owned, x_half, cot_half, seg, inverse):
     half, width = x_half.shape
     length = 2 * half
-    cols = owned[0].shape[1] // 2
+    cols = owned[1].shape[1]
     pairs = cols // 128
     units = owned[2].shape[1]
     shard = width // 16
@@ -612,8 +614,8 @@
         + [
             jax.ShapeDtypeStruct((pairs, 2, length), F32),
             flat,
-            gathered(2 * cols),
-            gathered(2 * cols),
+            gathered(3 * cols),
+            gathered(cols),
             jax.ShapeDtypeStruct((half, width), F32),
             flat,
             jax.ShapeDtypeStruct((half, width), BF),
@@ -622,7 +624,7 @@
         + [table] * 4
         + [jax.ShapeDtypeStruct((8, length), F32)]
         + [gathered(units)] * 3,
-        scratch_shapes=[pltpu.VMEM((shard, 2 * cols), BF)] * 2
+        scratch_shapes=[pltpu.VMEM((shard, 3 * cols), BF), pltpu.VMEM((shard, cols), BF)]
         + [pltpu.VMEM((shard, units), BF)] * 3
         + [
             pltpu.VMEM((half, width), BF),
@@ -632,8 +634,8 @@
             pltpu.VMEM((half, width), F32),
             pltpu.VMEM((half, width), BF),
             pltpu.VMEM((half, width), BF),
-            pltpu.SemaphoreType.DMA((9 * Gather.MESSAGES,)),
-            pltpu.SemaphoreType.DMA((9 * Gather.MESSAGES,)),
+            pltpu.SemaphoreType.DMA((8 * Gather.MESSAGES,)),
+            pltpu.SemaphoreType.DMA((8 * Gather.MESSAGES,)),
             pltpu.SemaphoreType.DMA((4,)),
             pltpu.SemaphoreType.DMA((4,)),
             pltpu.SemaphoreType.DMA((5,)),
@@ -941,10 +943,10 @@
 
 
 def backward_kernel(
-    d_gate, d_up, d_low, d_high, q, k, v, o, lse, attn_cot, w_qk, w_vo, xh, x_half, resid_grad,
+    d_gate, d_up, d_low, d_high, q, k, v, o, lse, attn_cot, w_qkv, w_out, xh, x_half, resid_grad,
     cos, upper, lower, seg_col, seg_row,
-    token_grad, s_gate, s_up_low, s_up_high, s_down_low, s_down_high, s_qk, s_vo_low, s_vo_high,
-    d_qk, d_vo, pg, heads_grad, kh, dk, dv, own, sent, got, placed,
+    token_grad, s_gate, s_up_low, s_up_high, s_down_low, s_down_high, s_out, s_near, s_far,
+    d_out, d_near, d_far, pg, heads_grad, kh, dk, dv, own, sent, got, placed,
     near_gate, near_up_low, near_up_high,
     *rest,
 ):
@@ -960,30 +962,30 @@
     peers = partners()
     sems = (send_sem, recv_sem)
     n = Reduce.MESSAGES
-    whole, most, few = pl.ds(0, 64), pl.ds(0, 48), pl.ds(48, 16)
+    whole, low, high = pl.ds(0, 64), pl.ds(0, 32), pl.ds(32, 32)
     held = lambda ref: (lambda z: ref[z])
     plan = (
         (Reduce, d_gate, held(near_gate), whole, "yx", s_gate),
-        (Reduce, d_up, held(near_up_low), most, "yx", s_up_low),
-        (ReduceAlongZ, d_up, lambda: near_up_high[...], few, None, s_up_high),
-        (Reduce, None, None, most, "yx", s_down_low),
-        (Reduce, None, None, few, "xy", s_down_high),
-        (Reduce, d_qk, lambda z: d_qk[z, 0], whole, "yx", s_qk),
-        (Reduce, d_vo, lambda z: d_vo[z, :, 0, 0:48], most, "xy", s_vo_low),
-        (ReduceAlongZ, d_vo, lambda: d_vo[0, :, :, 48:64], few, None, s_vo_high),
+        (Reduce, d_up, held(near_up_low), low, "yx", s_up_low),
+        (ReduceAlongZ, d_up, lambda: near_up_high[...], high, None, s_up_high),
+        (Reduce, None, None, None, "yx", s_down_low),
+        (Reduce, None, None, None, "xy", s_down_high),
+        (Reduce, d_out, lambda z: d_out[z, 0], whole, "yx", s_out),
+        (Reduce, d_near, lambda z: d_near[z, 0], whole, "yx", s_near),
+        (Reduce, d_far, lambda z: d_far[z, :, 0], whole, "xy", s_far),
     )
     parts = [
         kind(src, near, rows_, axes, peers, sems, i * n, bufs[i], out)
         for i, (kind, src, near, rows_, axes, out) in enumerate(plan)
     ]
-    gate, up_low, up_high, down_low, down_high, qk, vo_low, vo_high = parts
+    gate, up_low, up_high, down_low, down_high, out, near, far = parts
     nears = [
         pltpu.make_async_copy(src, dst, near_sem.at[i])
         for i, (src, dst) in enumerate(
             (
                 (d_gate.at[:, 0], near_gate),
-                (d_up.at[:, 0, :, most], near_up_low),
-                (d_up.at[0, :, :, few], near_up_high),
+                (d_up.at[:, 0, :, low], near_up_low),
+                (d_up.at[0, :, :, high], near_up_high),
             )
         )
     ]
@@ -994,36 +996,50 @@
     down_low.resume()
     down_high.resume()
     gate.start()
-    up_low.start()
 
     def heads(here):
-        heads_grad[here, :] = dotf(attn_cot[here, :], w_vo[:, cols:], NN).astype(BF)
+        heads_grad[here, :] = dotf(attn_cot[here, :], w_out[...], NN).astype(BF)
 
     in_chunks(length, 256, heads)
 
     def out_weights(z, carry):
         here = pl.ds(pl.multiple_of(z * 256, 256), 256)
         value = dotf(jnp.transpose(attn_cot[:, here]), o[...], NN).astype(BF)
-        d_vo[z, :, :, :, cols:] = value.reshape(2, 2, 64, cols)
+        d_out[z] = value.reshape(2, 2, 64, cols)
         return carry
 
     lax.fori_loop(0, width // 256, out_weights, 0)
+    out.start()
+    up_low.start()
     for copy in nears:
         copy.wait()
+    for z in Reduce.ORDER:
+        down_low.relay_second(z)
+        down_high.relay_second(z)
 
     events = {}
     for i, z in enumerate(Reduce.ORDER):
-        if i < 3:
-            events.setdefault(4 + 4 * i, []).append(lambda z=z: gate.relay_first(z))
-        events.setdefault(3 + 3 * i, []).append(lambda z=z: down_low.relay_second(z))
-        events.setdefault(2 + 3 * i, []).append(lambda z=z: down_high.relay_second(z))
-    events.setdefault(7, []).append(up_high.relay_first)
-    events.setdefault(13, []).append(up_high.relay_second)
+        events.setdefault((1, 4, 7, 11)[i], []).append(lambda z=z: gate.relay_first(z))
+        events.setdefault((3, 6, 9, 13)[i], []).append(lambda z=z: gate.relay_second(z))
+        events.setdefault(12 + i, []).append(lambda z=z: out.relay_first(z))
+    events.setdefault(6, []).append(up_high.relay_first)
+    events.setdefault(9, []).append(up_high.relay_second)
+
+    def weights(ref, at):
+        def step(z, carry):
+            left = jnp.transpose(xh[:, pl.ds(pl.multiple_of(z * 256, 256), 256)])
+            value = dotf(left, pg[:, at : at + ref.shape[-1]], NN).astype(BF)
+            ref[z] = value.reshape(2, 2, 64, ref.shape[-1])
+            return carry
+
+        lax.fori_loop(0, width // 256, step, 0)
+
     lane = lax.broadcasted_iota(jnp.int32, (length, 128), 1)
     first = lane < HD
 
     def pair(h, carry):
         lanes = pl.ds(pl.multiple_of(h * 128, 128), 128)
+        third = lambda i: pl.ds(pl.multiple_of((3 * h + i) * 128, 128), 128)
         kf = k[:, lanes]
         none = jnp.zeros_like(kf)
         kh[0] = jnp.where(first, kf, none)
@@ -1069,43 +1085,37 @@
                 dq = dq + dotf(ds, kh[head], TN)
             dq = dq * (1.0 / math.sqrt(HD))
             c, a, b = cos[here, :], upper[here, :], lower[here, :]
-            pg[0, here, lanes] = (dq * c - turn(dq, a, b)).astype(BF)
+            pg[here, third(0)] = (dq * c - turn(dq, a, b)).astype(BF)
             return carry
 
         lax.fori_loop(0, length // rows, block, 0)
         dkf = dk[...]
-        pg[1, :, lanes] = (dkf * cos[...] - turn(dkf, upper[...], lower[...])).astype(BF)
-        pg[2, :, lanes] = dv[...].astype(BF)
+        pg[:, third(1)] = (dkf * cos[...] - turn(dkf, upper[...], lower[...])).astype(BF)
+        pg[:, third(2)] = dv[...].astype(BF)
+
+        @pl.when(h == pairs // 2 - 1)
+        def _():
+            weights(d_near, 0)
+            near.start()
+
         return carry
 
     lax.fori_loop(0, pairs, pair, 0)
-    gate.relay_first(Reduce.ORDER[3])
-
-    def weights(z, carry):
-        left = jnp.transpose(xh[:, pl.ds(pl.multiple_of(z * 256, 256), 256)])
-        for i, (ref, at) in enumerate(((d_qk, 0), (d_qk, cols), (d_vo, 0))):
-            value = dotf(left, pg[i], NN).astype(BF)
-            ref[z, :, :, :, at : at + cols] = value.reshape(2, 2, 64, cols)
-        return carry
-
-    lax.fori_loop(0, width // 256, weights, 0)
+    weights(d_far, d_near.shape[-1])
+    far.start()
 
     def back(tokens, put):
         def step(here):
-            total = dotf(pg[0, tokens, :], w_qk[here, :cols], NT)
-            total = total + dotf(pg[1, tokens, :], w_qk[here, cols:], NT)
-            put[:, here] = (total + dotf(pg[2, tokens, :], w_vo[here, :cols], NT)).astype(put.dtype)
+            put[:, here] = dotf(pg[tokens, :], w_qkv[here, :], NT).astype(put.dtype)
 
         in_chunks(width, 256, step)
 
-    for part in (qk, vo_low, vo_high):
-        part.start()
     back(pl.ds(half, half), sent)
     give = remote(sent, got, pair_send.at[0], pair_recv.at[0], peers["c"])
     give.start()
     back(pl.ds(0, half), own)
-    down_low.finish()
-    down_high.finish()
+    for z in Reduce.ORDER:
+        up_low.relay_first(z)
     give.wait()
 
     def finish(here):
@@ -1117,32 +1127,27 @@
     in_chunks(half, 64, finish)
     move = Move(placed, token_grad, moving, 0)
     move.start()
-    up_high.finish()
     for z in Reduce.ORDER:
-        up_low.relay_first(z)
-        gate.relay_second(z)
-    vo_high.relay_first()
+        out.relay_second(z)
+        near.relay_first(z)
+        far.relay_first(z)
+    for part in (down_low, down_high, gate, up_high):
+        part.finish()
     for z in Reduce.ORDER:
-        vo_low.relay_first(z)
-    gate.finish()
+        up_low.relay_second(z)
+    out.finish()
     for z in Reduce.ORDER:
-        qk.relay_first(z)
-        up_low.relay_second(z)
-    vo_high.relay_second()
-    for z in Reduce.ORDER:
-        vo_low.relay_second(z)
+        far.relay_second(z)
+        near.relay_second(z)
     up_low.finish()
-    for z in Reduce.ORDER:
-        qk.relay_second(z)
-    vo_high.finish()
-    vo_low.finish()
-    qk.finish()
+    far.finish()
+    near.finish()
     for part in parts:
         part.close()
     move.wait()
 
 
-def backward_block(grads, heads, lse, attn_cot, w_qk, w_vo, xh, x_half, resid_grad, tables, seg_col, seg_row):
+def backward_block(grads, heads, lse, attn_cot, w_qkv, w_out, xh, x_half, resid_grad, tables, seg_col, seg_row):
     length, width = xh.shape
     half = length // 2
     cols = heads[0].shape[1]
@@ -1150,10 +1155,11 @@
     shard = width // 16
     vmem = pl.BlockSpec(memory_space=pltpu.VMEM)
     any_ = pl.BlockSpec(memory_space=pl.ANY)
-    most, few = shard * 3 // 4, shard // 4
-    sizes = [(shard, units)] + [(most, units), (few, units)] * 2
-    sizes += [(shard, 2 * cols), (most, 2 * cols), (few, 2 * cols)]
-    along_z, begun = (2, 7), (3, 4)
+    wide = 3 * cols // 2
+    sizes = [(shard, units), (shard // 2, units), (shard // 2, units)]
+    sizes += [g.shape[2:] for g in grads[2:]]
+    sizes += [(shard, cols), (shard, wide), (shard, wide)]
+    along_z, begun = (2,), (3, 4)
     bufs = []
     for i, size in enumerate(sizes):
         if i in along_z:
@@ -1169,9 +1175,9 @@
         out_specs=[vmem] * 9,
         out_shape=[jax.ShapeDtypeStruct((half, width), BF)]
         + [jax.ShapeDtypeStruct(size, BF) for size in sizes],
-        scratch_shapes=[pltpu.VMEM(SHARD + (shard, 2 * cols), BF)] * 2
+        scratch_shapes=[pltpu.VMEM(SHARD + (shard, n), BF) for n in (cols, wide, wide)]
         + [
-            pltpu.VMEM((3, length, cols), BF),
+            pltpu.VMEM((length, 3 * cols), BF),
             pltpu.VMEM((length, cols), BF),
             pltpu.VMEM((2, length, 128), BF),
             pltpu.VMEM((length, 128), F32),
@@ -1197,7 +1203,7 @@
         name="backward_block",
     )(
         *(g.reshape(SHARD + (shard, units)) for g in grads[:2]), *grads[2:],
-        *heads, lse, attn_cot, w_qk, w_vo, xh, x_half, resid_grad, *tables, seg_col, seg_row,
+        *heads, lse, attn_cot, w_qkv, w_out, xh, x_half, resid_grad, *tables, seg_col, seg_row,
     )
 
 
@@ -1264,15 +1270,16 @@
 
         owned = (a_one, b_one, own_gate, own_up, down_rows)
         if paired:
-            owned = owned[:2] + tuple(padded(w) for w in owned[2:])
+            by_pair = scaled(w_qkv, gain_one[:, None]).reshape(shard, 3, cols // 128, 128).swapaxes(1, 2)
+            owned = (by_pair.reshape(shard, 3 * cols), w_out.T) + tuple(padded(w) for w in owned[2:])
             seg = jnp.broadcast_to(segments.astype(F32), (8, segments.shape[1]))
             inverse = jnp.broadcast_to(jnp.tile(rope_rates(), 4), (8, 128))
             (
-                q, k, v, o, lse, xh, w_qk, w_vo, resid, xn, x_half, cot_all, *tables, seg_col, seg_row,
+                q, k, v, o, lse, xh, qkv_all, out_all, resid, xn, x_half, cot_all, *tables, seg_col, seg_row,
                 w_gate, w_up, w_dn,
             ) = forward_block(owned, tokens[0], cotangent[0], seg, inverse)
-            w_qk, w_vo, w_gate, w_up = (
-                w.reshape(-1, w.shape[-1]) for w in (w_qk, w_vo, w_gate, w_up)
+            qkv_all, out_all, w_gate, w_up = (
+                w.reshape(-1, w.shape[-1]) for w in (qkv_all, out_all, w_gate, w_up)
             )
         else:
             w_qk, w_vo, w_gate, w_up, w_dn = (
@@ -1309,13 +1316,14 @@
 
         if paired:
             token_grad, *sums = backward_block(
-                grads, (q, k, v, o), lse, attn_cot, w_qk, w_vo, xh, x_half,
+                grads, (q, k, v, o), lse, attn_cot, qkv_all, out_all, xh, x_half,
                 resid_grad, tables, seg_col, seg_row,
             )
             token_grad = token_grad.astype(F32)
-            s_gate, up_low, up_high, s_low, s_high, one_a, vo_low, vo_high = (w.astype(F32) for w in sums)
+            s_gate, up_low, up_high, s_low, s_high, s_out, near, far = (w.astype(F32) for w in sums)
             s_up = jnp.concatenate([up_low, up_high], axis=0)
-            one_b = jnp.concatenate([vo_low, vo_high], axis=0)
+            qkv_raw = jnp.concatenate([near, far], axis=1).reshape(shard, cols // 128, 3, 128)
+            qkv_raw = qkv_raw.swapaxes(1, 2).reshape(shard, 3, cols)
             in_raw = jnp.stack([s_gate[:, :units], s_up[:, :units]], axis=1)
             down_sum = jnp.concatenate([s_low[:, :units], s_high[:, :units]], axis=0).T
         else:
@@ -1337,8 +1345,9 @@
             token_grad = resid_grad + normalize_back(f_one, xh_one, scale_one)
             in_raw = jnp.stack([two_a[:, :units], two_b[:, :units]], axis=1)
             down_sum = jnp.concatenate([two_a[:, units + pad :], two_b[:, units + pad :]], axis=1).T
-
-        qkv_raw = jnp.stack([one_a[:, :cols], one_a[:, cols:], one_b[:, :cols]], axis=1)
+            s_out = one_b[:, cols:]
+            qkv_raw = jnp.stack([one_a[:, :cols], one_a[:, cols:], one_b[:, :cols]], axis=1)
+
         gains = jnp.stack(
             [
                 jnp.sum(qkv_raw * w_qkv.astype(F32), axis=(1, 2)),
@@ -1352,7 +1361,7 @@
             gains[0],
             gains[1],
             qkv_raw * gain_one[:, :, None],
-            one_b[:, cols:].T,
+            s_out.T,
             in_raw * gain_two[:, :, None],
             down_sum,
         )

time: 339 us -> 346 us (1.021)
  Pallas kernels: 319 us -> 324 us
    pallas_call x1, Pallas kernels: 128 us -> 141 us  [backward_block(): pl.pallas_call(backward_kernel, in_specs=[any_] * 2 + [vmem] * 18, out_sp...]
    pallas_call x1, Pallas kernels: 134 us -> 127 us  [forward_block(): pl.pallas_call(forward_kernel, in_specs=[any_] * 8 + [vmem], out_specs=[v...]
where the time goes in v8:
time: 346 us; the launch traced here: 342 us
  Pallas kernels  324 us (94%)
  local copies, waits for them, and re-layouts  8.96 us (3%)
  other arithmetic  8.44 us (2%)
    pallas_call x1, Pallas kernels, backward_block(): pl.pallas_call(backward_kernel, in_specs=[any_] * 2 + [vmem] * 18, out_sp...  141 us
    pallas_call x1, Pallas kernels, forward_block(): pl.pallas_call(forward_kernel, in_specs=[any_] * 8 + [vmem], out_specs=[v...  127 us
    pallas_call x1, Pallas kernels, mlp_block(): pl.pallas_call(mlp_kernel, in_specs=[any_] + [vmem] * 5, out_specs=[any_]...  56 us
  transfers between devices with their start and end apart: 1, of which 0 were waited for; matrix products, arithmetic and copies ran while one was open for 1% of the time, Pallas kernels for 0%

profile of v8, /device:TPU:0, one launch (start us, length us, event | category | flops | bytes accessed | tf_op | source)
XLA Modules:
  0.0 342.0 jit_solution(16101163013770248025)
XLA Ops:
  0.6 0.0 copy-start.4
  0.7 0.7 convert_element_type.58
  1.4 0.7 convert_element_type.62
  2.0 0.1 tile.10
  2.1 0.7 convert_element_type.67
  2.8 1.0 fusion.1
  3.8 0.1 reshape.64
  3.9 0.2 copy.36
  4.1 0.8 reshape.65.a_in
  4.9 1.0 copy.29
  5.9 0.0 copy-done.4
  5.9 0.7 pad.12.d_in
  6.6 0.1 fusion.3
  6.8 0.7 pad.11.u_in
  7.5 0.7 pad.10.g_in
  8.1 0.6 broadcast_in_dim.22.inverse
  8.7 0.6 broadcast_in_dim.21.seg_in
  9.3 126.6 %forward_block.1 = (bf16[1024,512]{1,0:T(8,128)(2,1)}, bf16[1024,512]{1,0:T(8,128)(2,1)}, bf16[1024,512]{1,0:T(8,128)(2,1)}, bf16[1024,512]{1,0:T(8,128)(2,1)}, ...) custom-call(bf16[64,1536]{1,0:T(8,128)(2,1)} %reshape.65.a_in, ...), custom_call_target="tpu_custom_call" | custom-call | tf_op jit(solution)/shard_map/forward_block/pallas_call | solution.py:609
  136.0 56.0 %mlp_block.1 = (bf16[512,1024]{1,0:T(8,128)(2,1)}, f32[512,1024]{1,0:T(8,128)}, bf16[1024,1024]{1,0:T(8,128)(2,1)}, bf16[1024,1408]{1,0:T(8,128)(2,1)}, bf16[102...) custom-call(bf16[4,2,2,64,1408]{4,3,2,1,0:T(8,128)(2,1)} %get-tuple-element.44.down_in, ...), custom_call_target="tpu_custom_call" | custom-call | tf_op jit(solution)/shard_map/mlp_block/pallas_call | solution.py:911
  191.9 141.1 %backward_block.1 = (bf16[512,1024]{1,0:T(8,128)(2,1)}, bf16[64,1408]{1,0:T(8,128)(2,1)}, bf16[32,1408]{1,0:T(8,128)(2,1)}, bf16[32,1408]{1,0:T(8,128)(2,1)}, bf...) custom-call(bf16[4,2,2,64,1408]{4,3,2,1,0:T(8,128)(2,1)} %bitcast.50, ...), custom_call_target="tpu_custom_call" | custom-call | tf_op jit(solution)/shard_map/backward_block/pallas_call | solution.py:1172
  333.0 0.0 copy-start.3
  333.0 0.0 copy-start.5
  333.0 0.0 copy-start.7
  333.0 0.0 copy-start.8
  333.0 1.0 maximum_convert_fusion
  334.1 0.0 copy-start
  334.1 0.3 reshape.82
  334.4 0.1 copy.31
  334.5 0.0 copy-start.1
  334.5 0.2 reshape.79
  334.7 0.0 copy-done.3
  334.7 0.9 broadcast_multiply_fusion
  335.6 0.0 copy-done.5
  335.6 0.0 copy-done.7
  335.6 0.0 copy-done.8
  335.7 0.0 copy-done
  335.7 0.0 copy-start.6
  335.7 0.0 copy-start.10
  335.7 0.2 convert_multiply_fusion
  335.9 0.0 copy-start.9
  335.9 0.1 collective-permute-start
  336.0 0.0 copy-done.1
  336.0 0.0 copy-start.2
  336.0 1.6 bitcast_convert_fusion
  337.6 0.0 copy-done.6
  337.6 0.0 copy-done.10
  337.6 0.8 convert_bitcast_fusion
  338.4 0.0 copy-done.9
  338.4 0.7 convert_bitcast_fusion.1
  339.1 1.4 copy.33
  340.5 0.0 collective-permute-done
  340.5 0.5 slice_bitcast_fusion.3
  341.0 0.0 copy-done.2
  341.0 1.0 copy.38
  (5 shorter events, 0.1 us)
Async XLA Ops:
  0.6 5.3 %copy-start.4 = (bf16[1312,64]{0,1:T(8,128)(2,1)S(1)}, bf16[1312,64]{0,1:T(8,128)(2,1)}, u32[]{:S(2)}) copy-start(bf16[1312,64]{0,1:T(8,128)(2,1)} %param.14) | copy-start | bytes 503812
  333.0 1.7 copy-start.3
  333.0 2.6 copy-start.5
  333.0 2.6 copy-start.7
  333.0 2.6 copy-start.8
  334.1 1.6 copy-start
  334.5 1.5 copy-start.1
  335.7 1.9 copy-start.6
  335.7 1.9 copy-start.10
  335.9 2.5 copy-start.9
  335.9 4.5 %collective-permute-start = (f32[2,64]{1,0:T(2,128)S(1)}, f32[2,64]{1,0:T(2,128)S(1)}, u32[]{:S(2)}, u32[]{:S(2)}) collective-permute-start(f32[2,64]{1,0:T(2,128)S(1)} %pad_maximum_fusion.2), channel_id=1, source_target_pairs={{0,1},{1,0},{2,3},{3,2},{4,5},{5,4},{6,7},{7,6},{8,9},{9,8},{10,11... | collective-permute-start | bytes 1544 | tf_op jit(solution)/shard_map/ppermute | solution.py:1213
  336.0 5.0 %copy-start.2 = (bf16[512,1024]{1,0:T(8,128)(2,1)S(1)}, bf16[512,1024]{1,0:T(8,128)(2,1)}, u32[]{:S(2)}) copy-start(bf16[512,1024]{1,0:T(8,128)(2,1)} %get-tuple-element.50) | copy-start | bytes 3145732

commit v9 on v8

--- a/solution.py
+++ b/solution.py
@@ -966,13 +966,13 @@
     held = lambda ref: (lambda z: ref[z])
     plan = (
         (Reduce, d_gate, held(near_gate), whole, "yx", s_gate),
-        (Reduce, d_up, held(near_up_low), low, "yx", s_up_low),
+        (Reduce, d_up, held(near_up_low), low, "xy", s_up_low),
         (ReduceAlongZ, d_up, lambda: near_up_high[...], high, None, s_up_high),
         (Reduce, None, None, None, "yx", s_down_low),
         (Reduce, None, None, None, "xy", s_down_high),
         (Reduce, d_out, lambda z: d_out[z, 0], whole, "yx", s_out),
         (Reduce, d_near, lambda z: d_near[z, 0], whole, "yx", s_near),
-        (Reduce, d_far, lambda z: d_far[z, :, 0], whole, "xy", s_far),
+        (Reduce, d_far, lambda z: d_far[z, 0], whole, "yx", s_far),
     )
     parts = [
         kind(src, near, rows_, axes, peers, sems, i * n, bufs[i], out)
@@ -984,7 +984,7 @@
         for i, (src, dst) in enumerate(
             (
                 (d_gate.at[:, 0], near_gate),
-                (d_up.at[:, 0, :, low], near_up_low),
+                (d_up.at[:, :, 0, low], near_up_low),
                 (d_up.at[0, :, :, high], near_up_high),
             )
         )
@@ -996,6 +996,7 @@
     down_low.resume()
     down_high.resume()
     gate.start()
+    up_low.start()
 
     def heads(here):
         heads_grad[here, :] = dotf(attn_cot[here, :], w_out[...], NN).astype(BF)
@@ -1010,7 +1011,6 @@
 
     lax.fori_loop(0, width // 256, out_weights, 0)
     out.start()
-    up_low.start()
     for copy in nears:
         copy.wait()
     for z in Reduce.ORDER:
@@ -1019,11 +1019,12 @@
 
     events = {}
     for i, z in enumerate(Reduce.ORDER):
-        events.setdefault((1, 4, 7, 11)[i], []).append(lambda z=z: gate.relay_first(z))
-        events.setdefault((3, 6, 9, 13)[i], []).append(lambda z=z: gate.relay_second(z))
-        events.setdefault(12 + i, []).append(lambda z=z: out.relay_first(z))
-    events.setdefault(6, []).append(up_high.relay_first)
-    events.setdefault(9, []).append(up_high.relay_second)
+        events.setdefault((3, 6, 10, 13)[i], []).append(lambda z=z: gate.relay_first(z))
+        events.setdefault((5, 7, 8, 10)[i], []).append(lambda z=z: up_low.relay_first(z))
+    for z in Reduce.ORDER[:2]:
+        events.setdefault(14, []).append(lambda z=z: gate.relay_second(z))
+    events.setdefault(9, []).append(up_high.relay_first)
+    events.setdefault(13, []).append(up_high.relay_second)
 
     def weights(ref, at):
         def step(z, carry):
@@ -1110,12 +1111,20 @@
 
         in_chunks(width, 256, step)
 
+    for z in Reduce.ORDER[2:]:
+        gate.relay_second(z)
+    for z in Reduce.ORDER:
+        out.relay_first(z)
     back(pl.ds(half, half), sent)
     give = remote(sent, got, pair_send.at[0], pair_recv.at[0], peers["c"])
     give.start()
+    for z in Reduce.ORDER:
+        up_low.relay_second(z)
     back(pl.ds(0, half), own)
     for z in Reduce.ORDER:
-        up_low.relay_first(z)
+        out.relay_second(z)
+    for part in (down_low, down_high):
+        part.finish()
     give.wait()
 
     def finish(here):
@@ -1128,20 +1137,17 @@
     move = Move(placed, token_grad, moving, 0)
     move.start()
     for z in Reduce.ORDER:
-        out.relay_second(z)
         near.relay_first(z)
-        far.relay_first(z)
-    for part in (down_low, down_high, gate, up_high):
+    for part in (gate, up_high, up_low):
         part.finish()
     for z in Reduce.ORDER:
-        up_low.relay_second(z)
+        far.relay_first(z)
+        near.relay_second(z)
     out.finish()
     for z in Reduce.ORDER:
         far.relay_second(z)
-        near.relay_second(z)
-    up_low.finish()
+    near.finish()
     far.finish()
-    near.finish()
     for part in parts:
         part.close()
     move.wait()

time: 346 us -> 334 us (0.965)
  Pallas kernels: 324 us -> 315 us
    pallas_call x1, Pallas kernels: 141 us -> 132 us  [backward_block(): pl.pallas_call(backward_kernel, in_specs=[any_] * 2 + [vmem] * 18, out_sp...]
where the time goes in v9:
time: 334 us; the launch traced here: 333 us
  Pallas kernels  315 us (94%)
  local copies, waits for them, and re-layouts  8.96 us (3%)
  other arithmetic  8.44 us (3%)
    pallas_call x1, Pallas kernels, backward_block(): pl.pallas_call(backward_kernel, in_specs=[any_] * 2 + [vmem] * 18, out_sp...  132 us
    pallas_call x1, Pallas kernels, forward_block(): pl.pallas_call(forward_kernel, in_specs=[any_] * 8 + [vmem], out_specs=[v...  127 us
    pallas_call x1, Pallas kernels, mlp_block(): pl.pallas_call(mlp_kernel, in_specs=[any_] + [vmem] * 5, out_specs=[any_]...  56 us
  transfers between devices with their start and end apart: 1, of which 0 were waited for; matrix products, arithmetic and copies ran while one was open for 1% of the time, Pallas kernels for 0%

profile of v9, /device:TPU:0, one launch (start us, length us, event | category | flops | bytes accessed | tf_op | source)
XLA Modules:
  0.0 333.4 jit_solution(942302902695644281)
XLA Ops:
  0.6 0.0 copy-start.4
  0.7 0.7 convert_element_type.58
  1.4 0.7 convert_element_type.62
  2.0 0.1 tile.10
  2.1 0.7 convert_element_type.67
  2.8 1.0 fusion.1
  3.8 0.1 reshape.64
  3.9 0.2 copy.36
  4.1 0.8 reshape.65.a_in
  4.9 1.0 copy.29
  5.9 0.0 copy-done.4
  5.9 0.7 pad.12.d_in
  6.6 0.1 fusion.3
  6.8 0.7 pad.11.u_in
  7.5 0.7 pad.10.g_in
  8.1 0.6 broadcast_in_dim.22.inverse
  8.7 0.6 broadcast_in_dim.21.seg_in
  9.3 126.6 %forward_block.1 = (bf16[1024,512]{1,0:T(8,128)(2,1)}, bf16[1024,512]{1,0:T(8,128)(2,1)}, bf16[1024,512]{1,0:T(8,128)(2,1)}, bf16[1024,512]{1,0:T(8,128)(2,1)}, ...) custom-call(bf16[64,1536]{1,0:T(8,128)(2,1)} %reshape.65.a_in, ...), custom_call_target="tpu_custom_call" | custom-call | tf_op jit(solution)/shard_map/forward_block/pallas_call | solution.py:609
  136.0 56.0 %mlp_block.1 = (bf16[512,1024]{1,0:T(8,128)(2,1)}, f32[512,1024]{1,0:T(8,128)}, bf16[1024,1024]{1,0:T(8,128)(2,1)}, bf16[1024,1408]{1,0:T(8,128)(2,1)}, bf16[102...) custom-call(bf16[4,2,2,64,1408]{4,3,2,1,0:T(8,128)(2,1)} %get-tuple-element.44.down_in, ...), custom_call_target="tpu_custom_call" | custom-call | tf_op jit(solution)/shard_map/mlp_block/pallas_call | solution.py:911
  191.9 132.1 %backward_block.1 = (bf16[512,1024]{1,0:T(8,128)(2,1)}, bf16[64,1408]{1,0:T(8,128)(2,1)}, bf16[32,1408]{1,0:T(8,128)(2,1)}, bf16[32,1408]{1,0:T(8,128)(2,1)}, bf...) custom-call(bf16[4,2,2,64,1408]{4,3,2,1,0:T(8,128)(2,1)} %bitcast.50, ...), custom_call_target="tpu_custom_call" | custom-call | tf_op jit(solution)/shard_map/backward_block/pallas_call | solution.py:1178
  324.0 0.0 copy-start.3
  324.0 0.0 copy-start.5
  324.0 0.0 copy-start.7
  324.0 0.0 copy-start.8
  324.1 1.0 maximum_convert_fusion
  325.1 0.0 copy-start
  325.1 0.3 reshape.82
  325.4 0.1 copy.31
  325.5 0.0 copy-start.1
  325.5 0.2 reshape.79
  325.7 0.0 copy-done.3
  325.7 0.9 broadcast_multiply_fusion
  326.6 0.0 copy-done.5
  326.6 0.0 copy-done.7
  326.7 0.0 copy-done.8
  326.7 0.0 copy-done
  326.7 0.0 copy-start.6
  326.7 0.0 copy-start.10
  326.7 0.2 convert_multiply_fusion
  327.0 0.0 copy-start.9
  327.0 0.5 collective-permute-start
  327.4 0.0 copy-done.1
  327.4 0.0 copy-start.2
  327.4 1.6 bitcast_convert_fusion
  329.0 0.0 copy-done.6
  329.0 0.0 copy-done.10
  329.0 0.8 convert_bitcast_fusion
  329.8 0.0 copy-done.9
  329.8 0.7 convert_bitcast_fusion.1
  330.4 1.4 copy.33
  331.9 0.0 collective-permute-done
  331.9 0.5 slice_bitcast_fusion.3
  332.4 0.0 copy-done.2
  332.4 1.0 copy.38
  (5 shorter events, 0.1 us)
Async XLA Ops:
  0.6 5.3 %copy-start.4 = (bf16[1312,64]{0,1:T(8,128)(2,1)S(1)}, bf16[1312,64]{0,1:T(8,128)(2,1)}, u32[]{:S(2)}) copy-start(bf16[1312,64]{0,1:T(8,128)(2,1)} %param.14) | copy-start | bytes 503812
  324.0 1.7 copy-start.3
  324.0 2.6 copy-start.5
  324.0 2.6 copy-start.7
  324.0 2.6 copy-start.8
  325.1 1.6 copy-start
  325.5 1.9 copy-start.1
  326.7 2.3 copy-start.6
  326.7 2.3 copy-start.10
  327.0 2.8 copy-start.9
  327.0 4.9 %collective-permute-start = (f32[2,64]{1,0:T(2,128)S(1)}, f32[2,64]{1,0:T(2,128)S(1)}, u32[]{:S(2)}, u32[]{:S(2)}) collective-permute-start(f32[2,64]{1,0:T(2,128)S(1)} %pad_maximum_fusion.2), channel_id=1, source_target_pairs={{0,1},{1,0},{2,3},{3,2},{4,5},{5,4},{6,7},{7,6},{8,9},{9,8},{10,11... | collective-permute-start | bytes 1544 | tf_op jit(solution)/shard_map/ppermute | solution.py:1219
  327.4 5.0 %copy-start.2 = (bf16[512,1024]{1,0:T(8,128)(2,1)S(1)}, bf16[512,1024]{1,0:T(8,128)(2,1)}, u32[]{:S(2)}) copy-start(bf16[512,1024]{1,0:T(8,128)(2,1)} %get-tuple-element.50) | copy-start | bytes 3145732

commit v10 on v9

--- a/solution.py
+++ b/solution.py
@@ -357,7 +357,7 @@
 
 
 def forward_kernel(
-    a_in, b_in, g_in, u_in, d_in, x_in, c_in, seg_in, inverse,
+    writes, a_in, b_in, g_in, u_in, d_in, x_in, c_in, seg_in, inverse,
     q, k, v, o, lse, xh, w_qkv, w_out, resid, xn, x_half, cot, cos, upper, lower, seg_col, seg_row,
     w_gate, w_up, w_down,
     a_own, b_own, g_own, u_own, d_own, c_own, seg_own,
@@ -561,6 +561,8 @@
     give = remote(sent, got, pair_send.at[1], pair_recv.at[1], peers["c"])
     lax.fori_loop(0, half // rows, project_own, 0)
     give.start()
+    for copy in writes:
+        copy.start()
     move_c.wait()
 
     def turn_cot(here):
@@ -591,6 +593,22 @@
         copy.wait()
     swap_cot.wait()
     swap_xn.wait()
+    for copy in writes:
+        copy.wait()
+
+
+WRITTEN = (0, 1, 2, 3, 5, 6, 7, 10, 12, 13, 14, 15)
+
+
+def forward_written(*refs):
+    count = len(WRITTEN)
+    ins, outs, scratch = refs[:9], list(refs[9:29]), refs[29 : -count - 1]
+    held, sem = refs[-count - 1 : -1], refs[-1]
+    writes = []
+    for i, (n, ref) in enumerate(zip(WRITTEN, held)):
+        writes.append(pltpu.make_async_copy(ref, outs[n], sem.at[i]))
+        outs[n] = ref
+    forward_kernel(writes, *ins, *outs, *scratch)
 
 
 def forward_block(owned, x_half, cot_half, seg, inverse):
@@ -606,24 +624,22 @@
     heads = jax.ShapeDtypeStruct((length, cols), BF)
     flat = jax.ShapeDtypeStruct((length, width), BF)
     table = jax.ShapeDtypeStruct((length, 128), F32)
+    shapes = [heads] * 4 + [
+        jax.ShapeDtypeStruct((pairs, 2, length), F32),
+        flat,
+        gathered(3 * cols),
+        gathered(cols),
+        jax.ShapeDtypeStruct((half, width), F32),
+        flat,
+        jax.ShapeDtypeStruct((half, width), BF),
+        flat,
+    ]
+    shapes += [table] * 4 + [jax.ShapeDtypeStruct((8, length), F32)] + [gathered(units)] * 3
     return pl.pallas_call(
-        forward_kernel,
+        forward_written,
         in_specs=[any_] * 8 + [vmem],
-        out_specs=[vmem] * 17 + [any_] * 3,
-        out_shape=[heads] * 4
-        + [
-            jax.ShapeDtypeStruct((pairs, 2, length), F32),
-            flat,
-            gathered(3 * cols),
-            gathered(cols),
-            jax.ShapeDtypeStruct((half, width), F32),
-            flat,
-            jax.ShapeDtypeStruct((half, width), BF),
-            flat,
-        ]
-        + [table] * 4
-        + [jax.ShapeDtypeStruct((8, length), F32)]
-        + [gathered(units)] * 3,
+        out_specs=[any_ if i in WRITTEN + (17, 18, 19) else vmem for i in range(20)],
+        out_shape=shapes,
         scratch_shapes=[pltpu.VMEM((shard, 3 * cols), BF), pltpu.VMEM((shard, cols), BF)]
         + [pltpu.VMEM((shard, units), BF)] * 3
         + [
@@ -640,7 +656,9 @@
             pltpu.SemaphoreType.DMA((4,)),
             pltpu.SemaphoreType.DMA((5,)),
         ]
-        + move_sems(8),
+        + move_sems(8)
+        + [pltpu.VMEM(shapes[i].shape, shapes[i].dtype) for i in WRITTEN]
+        + [pltpu.SemaphoreType.DMA((len(WRITTEN),))],
         compiler_params=pltpu.CompilerParams(
             collective_id=0, has_side_effects=True, vmem_limit_bytes=60 << 20
         ),
@@ -774,7 +792,7 @@
 
 
 def mlp_kernel(
-    down_in, xn, cot, w_gate, w_up, resid,
+    reads, writes, down_in, xn, cot, w_gate, w_up, resid,
     result, resid_grad, attn_cot, d_gate, d_up, d_low, d_high,
     w_down, d_down, hidden, act, slope_up, gate_grad, up_grad, own, sent, got, placed,
     send_sem, recv_sem, last_send, last_recv, first_send, first_recv, own_sem, *moving,
@@ -810,9 +828,13 @@
     reduce_high = Reduce(
         d_down, lambda z: d_down[z, :, 0, 48:64], few, "xy", peers, sems, n, (d_high, None, None, None), None
     )
+    for copy in reads:
+        copy.start()
     meet(peers, exchanged())
     for copy in last + owns:
         copy.start()
+    for copy in reads:
+        copy.wait()
     back, front = pl.ds(half, half), pl.ds(0, half)
 
     def gate_and_up(rows):
@@ -889,14 +911,30 @@
         d_up[here, :] = dotf(left, up_grad[...], NN).astype(BF)
 
     in_chunks(width, 256, weights)
+    writes[0].start()
     for z in Reduce.ORDER:
         reduce_low.add_first(z)
         reduce_high.add_first(z)
     for z in range(4):
         reduce_low.first(z).wait_send()
         reduce_high.first(z).wait_send()
+    for copy in writes[1:]:
+        copy.start()
     swap.wait()
     move.wait()
+    for copy in writes:
+        copy.wait()
+
+
+def mlp_staged(*refs):
+    ins, outs, scratch = refs[1:6], list(refs[6:13]), refs[13:-10]
+    held, read_sem, write_sem = refs[-10:-2], refs[-2], refs[-1]
+    reads = [pltpu.make_async_copy(a, b, read_sem.at[i]) for i, (a, b) in enumerate(zip(ins, held))]
+    writes = []
+    for i, (n, ref) in enumerate(zip((1, 3, 4), held[5:])):
+        writes.append(pltpu.make_async_copy(ref, outs[n], write_sem.at[i]))
+        outs[n] = ref
+    mlp_kernel(reads, writes, refs[0], *held[:5], *outs, *scratch)
 
 
 def mlp_block(down_in, xn, cot, w_gate, w_up, resid):
@@ -909,9 +947,9 @@
     grads = jax.ShapeDtypeStruct((width, units), BF)
     dma = lambda n: pltpu.SemaphoreType.DMA((n,))
     return pl.pallas_call(
-        mlp_kernel,
-        in_specs=[any_] + [vmem] * 5,
-        out_specs=[any_] + [vmem] * 6,
+        mlp_staged,
+        in_specs=[any_] * 6,
+        out_specs=[any_, any_, vmem, any_, any_, vmem, vmem],
         out_shape=[
             jax.ShapeDtypeStruct((half, width), BF),
             jax.ShapeDtypeStruct((half, width), F32),
@@ -934,7 +972,11 @@
             pltpu.VMEM((half, width), BF),
         ]
         + [dma(2), dma(2), dma(8), dma(8), dma(2 * Reduce.MESSAGES), dma(2 * Reduce.MESSAGES), dma(2)]
-        + move_sems(1),
+        + move_sems(1)
+        + [pltpu.VMEM(a.shape, a.dtype) for a in (xn, cot, w_gate, w_up, resid)]
+        + [pltpu.VMEM((half, width), F32)]
+        + [pltpu.VMEM((width, units), BF)] * 2
+        + [dma(5), dma(3)],
         compiler_params=pltpu.CompilerParams(
             collective_id=1, has_side_effects=True, vmem_limit_bytes=63 << 20
         ),
@@ -943,7 +985,7 @@
 
 
 def backward_kernel(
-    d_gate, d_up, d_low, d_high, q, k, v, o, lse, attn_cot, w_qkv, w_out, xh, x_half, resid_grad,
+    reads, d_gate, d_up, d_low, d_high, q, k, v, o, lse, attn_cot, w_qkv, w_out, xh, x_half, resid_grad,
     cos, upper, lower, seg_col, seg_row,
     token_grad, s_gate, s_up_low, s_up_high, s_down_low, s_down_high, s_out, s_near, s_far,
     d_out, d_near, d_far, pg, heads_grad, kh, dk, dv, own, sent, got, placed,
@@ -989,7 +1031,7 @@
             )
         )
     ]
-    for copy in nears:
+    for copy in nears + reads:
         copy.start()
     meet(peers, exchanged())
     up_high.start()
@@ -997,6 +1039,8 @@
     down_high.resume()
     gate.start()
     up_low.start()
+    for copy in reads:
+        copy.wait()
 
     def heads(here):
         heads_grad[here, :] = dotf(attn_cot[here, :], w_out[...], NN).astype(BF)
@@ -1153,6 +1197,12 @@
     move.wait()
 
 
+def backward_staged(*refs):
+    held, sem = refs[-17:-1], refs[-1]
+    reads = [pltpu.make_async_copy(a, b, sem.at[i]) for i, (a, b) in enumerate(zip(refs[4:20], held))]
+    backward_kernel(reads, *refs[:4], *held, *refs[20:-17])
+
+
 def backward_block(grads, heads, lse, attn_cot, w_qkv, w_out, xh, x_half, resid_grad, tables, seg_col, seg_row):
     length, width = xh.shape
     half = length // 2
@@ -1175,9 +1225,10 @@
         bufs += [pltpu.VMEM(n + size, BF) for n in lead[i in begun :] + ((),)]
     nears = [pltpu.VMEM(((2, 2) if i in along_z else (4, 2)) + size, BF) for i, size in enumerate(sizes[:3])]
     messages = 8 * Reduce.MESSAGES
+    operands = (*heads, lse, attn_cot, w_qkv, w_out, xh, x_half, resid_grad, *tables, seg_col, seg_row)
     return pl.pallas_call(
-        backward_kernel,
-        in_specs=[any_] * 2 + [vmem] * 18,
+        backward_staged,
+        in_specs=[any_] * 2 + [vmem] * 2 + [any_] * 16,
         out_specs=[vmem] * 9,
         out_shape=[jax.ShapeDtypeStruct((half, width), BF)]
         + [jax.ShapeDtypeStruct(size, BF) for size in sizes],
@@ -1202,14 +1253,16 @@
             pltpu.SemaphoreType.DMA((1,)),
             pltpu.SemaphoreType.DMA((3,)),
         ]
-        + move_sems(1),
+        + move_sems(1)
+        + [pltpu.VMEM(a.shape, a.dtype) for a in operands]
+        + [pltpu.SemaphoreType.DMA((16,))],
         compiler_params=pltpu.CompilerParams(
             collective_id=2, has_side_effects=True, vmem_limit_bytes=60 << 20
         ),
         name="backward_block",
     )(
         *(g.reshape(SHARD + (shard, units)) for g in grads[:2]), *grads[2:],
-        *heads, lse, attn_cot, w_qkv, w_out, xh, x_half, resid_grad, *tables, seg_col, seg_row,
+        *operands,
     )
 
 

time: 334 us -> 318 us (0.952)
  Pallas kernels: 315 us -> 299 us
    pallas_call x3, Pallas kernels: 315 us -> 299 us  [the longest x1 125 us: backward_block(): pl.pallas_call(backward_staged, in_specs=[any_] * 2 + [vmem] * 2 + [any_]...]
where the time goes in v10:
time: 318 us; the launch traced here: 317 us
  Pallas kernels  299 us (94%)
  local copies, waits for them, and re-layouts  8.96 us (3%)
  other arithmetic  8.44 us (3%)
    pallas_call x1, Pallas kernels, backward_block(): pl.pallas_call(backward_staged, in_specs=[any_] * 2 + [vmem] * 2 + [any_]...  125 us
    pallas_call x1, Pallas kernels, forward_block(): pl.pallas_call(forward_written, in_specs=[any_] * 8 + [vmem], out_specs=[...  123 us
    pallas_call x1, Pallas kernels, mlp_block(): pl.pallas_call(mlp_staged, in_specs=[any_] * 6, out_specs=[any_, any_, vm...  51.5 us
  transfers between devices with their start and end apart: 1, of which 0 were waited for; matrix products, arithmetic and copies ran while one was open for 1% of the time, Pallas kernels for 0%

profile of v10, /device:TPU:0, one launch (start us, length us, event | category | flops | bytes accessed | tf_op | source)
XLA Modules:
  0.0 317.4 jit_solution(14070323733131602389)
XLA Ops:
  0.6 0.0 copy-start.4
  0.7 0.7 convert_element_type.58
  1.4 0.7 convert_element_type.62
  2.0 0.1 tile.10
  2.1 0.7 convert_element_type.67
  2.8 1.0 fusion.1
  3.8 0.1 reshape.64
  3.9 0.2 copy.36
  4.1 0.8 reshape.65.refs_0_
  4.9 1.0 copy.29
  5.9 0.0 copy-done.4
  5.9 0.7 pad.12.refs_4_
  6.6 0.1 fusion.3
  6.8 0.7 pad.11.refs_3_
  7.5 0.7 pad.10.refs_2_
  8.1 0.6 broadcast_in_dim.22.refs_8_
  8.7 0.6 broadcast_in_dim.21.refs_7_
  9.3 122.5 %forward_block.1 = (bf16[1024,512]{1,0:T(8,128)(2,1)}, bf16[1024,512]{1,0:T(8,128)(2,1)}, bf16[1024,512]{1,0:T(8,128)(2,1)}, bf16[1024,512]{1,0:T(8,128)(2,1)}, ...) custom-call(bf16[64,1536]{1,0:T(8,128)(2,1)} %reshape.65.refs_0_, ...), custom_call_target="tpu_custom_call" | custom-call | tf_op jit(solution)/shard_map/forward_block/pallas_call | solution.py:638
  131.9 51.5 %mlp_block.1 = (bf16[512,1024]{1,0:T(8,128)(2,1)}, f32[512,1024]{1,0:T(8,128)}, bf16[1024,1024]{1,0:T(8,128)(2,1)}, bf16[1024,1408]{1,0:T(8,128)(2,1)}, bf16[102...) custom-call(bf16[4,2,2,64,1408]{4,3,2,1,0:T(8,128)(2,1)} %get-tuple-element.44.refs_0_, ...), custom_call_target="tpu_custom_call" | custom-call | tf_op jit(solution)/shard_map/mlp_block/pallas_call | solution.py:949
  183.4 124.6 %backward_block.1 = (bf16[512,1024]{1,0:T(8,128)(2,1)}, bf16[64,1408]{1,0:T(8,128)(2,1)}, bf16[32,1408]{1,0:T(8,128)(2,1)}, bf16[32,1408]{1,0:T(8,128)(2,1)}, bf...) custom-call(bf16[4,2,2,64,1408]{4,3,2,1,0:T(8,128)(2,1)} %bitcast.50, ...), custom_call_target="tpu_custom_call" | custom-call | tf_op jit(solution)/shard_map/backward_block/pallas_call | solution.py:1229
  308.0 0.0 copy-start.3
  308.0 0.0 copy-start.5
  308.0 0.0 copy-start.7
  308.0 0.0 copy-start.8
  308.0 1.0 maximum_convert_fusion
  309.0 0.0 copy-start
  309.1 0.3 reshape.82
  309.3 0.1 copy.31
  309.5 0.0 copy-start.1
  309.5 0.2 reshape.79
  309.6 0.0 copy-done.3
  309.6 0.9 broadcast_multiply_fusion
  310.6 0.0 copy-done.5
  310.6 0.0 copy-done.7
  310.6 0.0 copy-done.8
  310.7 0.0 copy-done
  310.7 0.0 copy-start.6
  310.7 0.0 copy-start.10
  310.7 0.2 convert_multiply_fusion
  310.9 0.0 copy-start.9
  310.9 0.5 collective-permute-start
  311.4 0.0 copy-done.1
  311.4 0.0 copy-start.2
  311.4 1.6 bitcast_convert_fusion
  313.0 0.0 copy-done.6
  313.0 0.0 copy-done.10
  313.0 0.8 convert_bitcast_fusion
  313.8 0.0 copy-done.9
  313.8 0.7 convert_bitcast_fusion.1
  314.4 1.4 copy.33
  315.9 0.0 collective-permute-done
  315.9 0.5 slice_bitcast_fusion.3
  316.4 0.0 copy-done.2
  316.4 1.0 copy.38
  (5 shorter events, 0.1 us)
Async XLA Ops:
  0.6 5.3 %copy-start.4 = (bf16[1312,64]{0,1:T(8,128)(2,1)S(1)}, bf16[1312,64]{0,1:T(8,128)(2,1)}, u32[]{:S(2)}) copy-start(bf16[1312,64]{0,1:T(8,128)(2,1)} %param.14) | copy-start | bytes 503812
  308.0 1.7 copy-start.3
  308.0 2.6 copy-start.5
  308.0 2.6 copy-start.7
  308.0 2.6 copy-start.8
  309.0 1.6 copy-start
  309.5 2.0 copy-start.1
  310.7 2.3 copy-start.6
  310.7 2.3 copy-start.10
  310.9 2.9 copy-start.9
  310.9 4.9 %collective-permute-start = (f32[2,64]{1,0:T(2,128)S(1)}, f32[2,64]{1,0:T(2,128)S(1)}, u32[]{:S(2)}, u32[]{:S(2)}) collective-permute-start(f32[2,64]{1,0:T(2,128)S(1)} %pad_maximum_fusion.2), channel_id=1, source_target_pairs={{0,1},{1,0},{2,3},{3,2},{4,5},{5,4},{6,7},{7,6},{8,9},{9,8},{10,11... | collective-permute-start | bytes 1544 | tf_op jit(solution)/shard_map/ppermute | solution.py:1272
  311.4 5.0 %copy-start.2 = (bf16[512,1024]{1,0:T(8,128)(2,1)S(1)}, bf16[512,1024]{1,0:T(8,128)(2,1)}, u32[]{:S(2)}) copy-start(bf16[512,1024]{1,0:T(8,128)(2,1)} %get-tuple-element.50) | copy-start | bytes 3145732

commit v11 on v10

--- a/solution.py
+++ b/solution.py
@@ -987,15 +987,15 @@
 def backward_kernel(
     reads, d_gate, d_up, d_low, d_high, q, k, v, o, lse, attn_cot, w_qkv, w_out, xh, x_half, resid_grad,
     cos, upper, lower, seg_col, seg_row,
-    token_grad, s_gate, s_up_low, s_up_high, s_down_low, s_down_high, s_out, s_near, s_far,
+    token_grad, s_gate, s_up_low, s_up_high, s_down_low, s_down_high, s_out, s_near, s_far_low, s_far_high,
     d_out, d_near, d_far, pg, heads_grad, kh, dk, dv, own, sent, got, placed,
     near_gate, near_up_low, near_up_high,
     *rest,
 ):
     bufs = [rest[4 * i : 4 * i + 4] for i in range(3)]
     bufs += [(first,) + rest[12 + 3 * i : 15 + 3 * i] for i, first in enumerate((d_low, d_high))]
-    bufs += [rest[18 + 4 * i : 22 + 4 * i] for i in range(3)]
-    send_sem, recv_sem, pair_send, pair_recv, near_sem, *moving = rest[30:]
+    bufs += [rest[18 + 4 * i : 22 + 4 * i] for i in range(4)]
+    send_sem, recv_sem, pair_send, pair_recv, near_sem, *moving = rest[34:]
     length, width = xh.shape
     half = length // 2
     cols = q.shape[1]
@@ -1014,13 +1014,14 @@
         (Reduce, None, None, None, "xy", s_down_high),
         (Reduce, d_out, lambda z: d_out[z, 0], whole, "yx", s_out),
         (Reduce, d_near, lambda z: d_near[z, 0], whole, "yx", s_near),
-        (Reduce, d_far, lambda z: d_far[z, 0], whole, "yx", s_far),
+        (Reduce, d_far, lambda z: d_far[z, 0, :, 0:32], low, "yx", s_far_low),
+        (Reduce, d_far, lambda z: d_far[z, :, 0, 32:64], high, "xy", s_far_high),
     )
     parts = [
         kind(src, near, rows_, axes, peers, sems, i * n, bufs[i], out)
         for i, (kind, src, near, rows_, axes, out) in enumerate(plan)
     ]
-    gate, up_low, up_high, down_low, down_high, out, near, far = parts
+    gate, up_low, up_high, down_low, down_high, out, near, far_low, far_high = parts
     nears = [
         pltpu.make_async_copy(src, dst, near_sem.at[i])
         for i, (src, dst) in enumerate(
@@ -1147,7 +1148,8 @@
 
     lax.fori_loop(0, pairs, pair, 0)
     weights(d_far, d_near.shape[-1])
-    far.start()
+    far_low.start()
+    far_high.start()
 
     def back(tokens, put):
         def step(here):
@@ -1185,13 +1187,17 @@
     for part in (gate, up_high, up_low):
         part.finish()
     for z in Reduce.ORDER:
-        far.relay_first(z)
+        far_high.relay_first(z)
+    for z in Reduce.ORDER:
+        far_low.relay_first(z)
         near.relay_second(z)
     out.finish()
     for z in Reduce.ORDER:
-        far.relay_second(z)
+        far_high.relay_second(z)
+        far_low.relay_second(z)
     near.finish()
-    far.finish()
+    far_high.finish()
+    far_low.finish()
     for part in parts:
         part.close()
     move.wait()
@@ -1214,7 +1220,7 @@
     wide = 3 * cols // 2
     sizes = [(shard, units), (shard // 2, units), (shard // 2, units)]
     sizes += [g.shape[2:] for g in grads[2:]]
-    sizes += [(shard, cols), (shard, wide), (shard, wide)]
+    sizes += [(shard, cols), (shard, wide), (shard // 2, wide), (shard // 2, wide)]
     along_z, begun = (2,), (3, 4)
     bufs = []
     for i, size in enumerate(sizes):
@@ -1224,12 +1230,12 @@
             lead = (4, 2), (4,), (3,)
         bufs += [pltpu.VMEM(n + size, BF) for n in lead[i in begun :] + ((),)]
     nears = [pltpu.VMEM(((2, 2) if i in along_z else (4, 2)) + size, BF) for i, size in enumerate(sizes[:3])]
-    messages = 8 * Reduce.MESSAGES
+    messages = 9 * Reduce.MESSAGES
     operands = (*heads, lse, attn_cot, w_qkv, w_out, xh, x_half, resid_grad, *tables, seg_col, seg_row)
     return pl.pallas_call(
         backward_staged,
         in_specs=[any_] * 2 + [vmem] * 2 + [any_] * 16,
-        out_specs=[vmem] * 9,
+        out_specs=[vmem] * 10,
         out_shape=[jax.ShapeDtypeStruct((half, width), BF)]
         + [jax.ShapeDtypeStruct(size, BF) for size in sizes],
         scratch_shapes=[pltpu.VMEM(SHARD + (shard, n), BF) for n in (cols, wide, wide)]
@@ -1379,9 +1385,9 @@
                 resid_grad, tables, seg_col, seg_row,
             )
             token_grad = token_grad.astype(F32)
-            s_gate, up_low, up_high, s_low, s_high, s_out, near, far = (w.astype(F32) for w in sums)
+            s_gate, up_low, up_high, s_low, s_high, s_out, near, *far = (w.astype(F32) for w in sums)
             s_up = jnp.concatenate([up_low, up_high], axis=0)
-            qkv_raw = jnp.concatenate([near, far], axis=1).reshape(shard, cols // 128, 3, 128)
+            qkv_raw = jnp.concatenate([near, jnp.concatenate(far, axis=0)], axis=1).reshape(shard, cols // 128, 3, 128)
             qkv_raw = qkv_raw.swapaxes(1, 2).reshape(shard, 3, cols)
             in_raw = jnp.stack([s_gate[:, :units], s_up[:, :units]], axis=1)
             down_sum = jnp.concatenate([s_low[:, :units], s_high[:, :units]], axis=0).T

time: 318 us -> 314 us (0.987)
  Pallas kernels: 299 us -> 295 us
    pallas_call x1, Pallas kernels: 125 us -> 121 us  [backward_block(): pl.pallas_call(backward_staged, in_specs=[any_] * 2 + [vmem] * 2 + [any_]...]
where the time goes in v11:
time: 314 us; the launch traced here: 313 us
  Pallas kernels  295 us (94%)
  local copies, waits for them, and re-layouts  8.96 us (3%)
  other arithmetic  8.44 us (3%)
    pallas_call x1, Pallas kernels, forward_block(): pl.pallas_call(forward_written, in_specs=[any_] * 8 + [vmem], out_specs=[...  123 us
    pallas_call x1, Pallas kernels, backward_block(): pl.pallas_call(backward_staged, in_specs=[any_] * 2 + [vmem] * 2 + [any_]...  121 us
    pallas_call x1, Pallas kernels, mlp_block(): pl.pallas_call(mlp_staged, in_specs=[any_] * 6, out_specs=[any_, any_, vm...  51.5 us
  transfers between devices with their start and end apart: 1, of which 0 were waited for; matrix products, arithmetic and copies ran while one was open for 1% of the time, Pallas kernels for 0%

profile of v11, /device:TPU:0, one launch (start us, length us, event | category | flops | bytes accessed | tf_op | source)
XLA Modules:
  0.0 313.4 jit_solution(1984539625767200587)
XLA Ops:
  0.6 0.0 copy-start.4
  0.7 0.7 convert_element_type.59
  1.4 0.7 convert_element_type.63
  2.0 0.1 tile.10
  2.1 0.7 convert_element_type.68
  2.8 1.0 fusion.1
  3.8 0.1 reshape.64
  3.9 0.2 copy.36
  4.1 0.8 reshape.65.refs_0_
  4.9 1.0 copy.29
  5.9 0.0 copy-done.4
  5.9 0.7 pad.12.refs_4_
  6.6 0.1 fusion.3
  6.8 0.7 pad.11.refs_3_
  7.5 0.7 pad.10.refs_2_
  8.1 0.6 broadcast_in_dim.22.refs_8_
  8.7 0.6 broadcast_in_dim.21.refs_7_
  9.3 122.5 %forward_block.1 = (bf16[1024,512]{1,0:T(8,128)(2,1)}, bf16[1024,512]{1,0:T(8,128)(2,1)}, bf16[1024,512]{1,0:T(8,128)(2,1)}, bf16[1024,512]{1,0:T(8,128)(2,1)}, ...) custom-call(bf16[64,1536]{1,0:T(8,128)(2,1)} %reshape.65.refs_0_, ...), custom_call_target="tpu_custom_call" | custom-call | tf_op jit(solution)/shard_map/forward_block/pallas_call | solution.py:638
  131.9 51.5 %mlp_block.1 = (bf16[512,1024]{1,0:T(8,128)(2,1)}, f32[512,1024]{1,0:T(8,128)}, bf16[1024,1024]{1,0:T(8,128)(2,1)}, bf16[1024,1408]{1,0:T(8,128)(2,1)}, bf16[102...) custom-call(bf16[4,2,2,64,1408]{4,3,2,1,0:T(8,128)(2,1)} %get-tuple-element.45.refs_0_, ...), custom_call_target="tpu_custom_call" | custom-call | tf_op jit(solution)/shard_map/mlp_block/pallas_call | solution.py:949
  183.4 120.6 %backward_block.1 = (bf16[512,1024]{1,0:T(8,128)(2,1)}, bf16[64,1408]{1,0:T(8,128)(2,1)}, bf16[32,1408]{1,0:T(8,128)(2,1)}, bf16[32,1408]{1,0:T(8,128)(2,1)}, bf...) custom-call(bf16[4,2,2,64,1408]{4,3,2,1,0:T(8,128)(2,1)} %bitcast.50, ...), custom_call_target="tpu_custom_call" | custom-call | tf_op jit(solution)/shard_map/backward_block/pallas_call | solution.py:1235
  304.0 0.0 copy-start.3
  304.0 0.0 copy-start.5
  304.0 0.0 copy-start.7
  304.0 0.0 copy-start.8
  304.0 1.0 maximum_convert_fusion
  305.0 0.0 copy-start
  305.0 0.3 reshape.82
  305.3 0.1 copy.31
  305.4 0.0 copy-start.1
  305.5 0.2 reshape.79
  305.6 0.0 copy-done.3
  305.6 0.9 broadcast_multiply_fusion
  306.6 0.0 copy-done.5
  306.6 0.0 copy-done.7
  306.6 0.0 copy-done.8
  306.6 0.0 copy-done
  306.7 0.0 copy-start.6
  306.7 0.0 copy-start.10
  306.7 0.2 convert_multiply_fusion
  306.9 0.0 copy-start.9
  306.9 0.6 collective-permute-start
  307.5 0.0 copy-done.1
  307.5 0.0 copy-start.2
  307.5 1.6 bitcast_convert_fusion
  309.0 0.0 copy-done.6
  309.0 0.0 copy-done.10
  309.0 0.8 convert_bitcast_fusion
  309.8 0.0 copy-done.9
  309.8 0.7 convert_bitcast_fusion.1
  310.5 1.4 copy.33
  311.9 0.0 collective-permute-done
  311.9 0.5 slice_bitcast_fusion.3
  312.4 0.0 copy-done.2
  312.4 1.0 copy.38
  (5 shorter events, 0.1 us)
Async XLA Ops:
  0.6 5.3 %copy-start.4 = (bf16[1312,64]{0,1:T(8,128)(2,1)S(1)}, bf16[1312,64]{0,1:T(8,128)(2,1)}, u32[]{:S(2)}) copy-start(bf16[1312,64]{0,1:T(8,128)(2,1)} %param.14) | copy-start | bytes 503812
  304.0 1.7 copy-start.3
  304.0 2.6 copy-start.5
  304.0 2.6 copy-start.7
  304.0 2.6 copy-start.8
  305.0 1.6 copy-start
  305.4 2.0 copy-start.1
  306.7 2.4 copy-start.6
  306.7 2.4 copy-start.10
  306.9 2.9 copy-start.9
  306.9 5.0 %collective-permute-start = (f32[2,64]{1,0:T(2,128)S(1)}, f32[2,64]{1,0:T(2,128)S(1)}, u32[]{:S(2)}, u32[]{:S(2)}) collective-permute-start(f32[2,64]{1,0:T(2,128)S(1)} %pad_maximum_fusion.2), channel_id=1, source_target_pairs={{0,1},{1,0},{2,3},{3,2},{4,5},{5,4},{6,7},{7,6},{8,9},{9,8},{10,11... | collective-permute-start | bytes 1544 | tf_op jit(solution)/shard_map/ppermute | solution.py:1278
  307.5 5.0 %copy-start.2 = (bf16[512,1024]{1,0:T(8,128)(2,1)S(1)}, bf16[512,1024]{1,0:T(8,128)(2,1)}, u32[]{:S(2)}) copy-start(bf16[512,1024]{1,0:T(8,128)(2,1)} %get-tuple-element.51) | copy-start | bytes 3145732

commit v12 on v11

--- a/solution.py
+++ b/solution.py
@@ -1040,8 +1040,8 @@
     down_high.resume()
     gate.start()
     up_low.start()
-    for copy in reads:
-        copy.wait()
+    for i in (3, 5, 7):
+        reads[i].wait()
 
     def heads(here):
         heads_grad[here, :] = dotf(attn_cot[here, :], w_out[...], NN).astype(BF)
@@ -1056,7 +1056,7 @@
 
     lax.fori_loop(0, width // 256, out_weights, 0)
     out.start()
-    for copy in nears:
+    for copy in nears + [copy for i, copy in enumerate(reads) if i not in (3, 5, 7)]:
         copy.wait()
     for z in Reduce.ORDER:
         down_low.relay_second(z)
@@ -1184,13 +1184,13 @@
     move.start()
     for z in Reduce.ORDER:
         near.relay_first(z)
-    for part in (gate, up_high, up_low):
-        part.finish()
     for z in Reduce.ORDER:
         far_high.relay_first(z)
     for z in Reduce.ORDER:
         far_low.relay_first(z)
         near.relay_second(z)
+    for part in (gate, up_high, up_low):
+        part.finish()
     out.finish()
     for z in Reduce.ORDER:
         far_high.relay_second(z)

time: 314 us -> 314 us (level)
  no operation moved by 1% of the time
where the time goes in v12:
time: 314 us; the launch traced here: 313 us
  Pallas kernels  292 us (93%)
  local copies, waits for them, and re-layouts  8.96 us (3%)
  other arithmetic  8.44 us (3%)
  starting transfers between devices  3.35 us (1%)
    pallas_call x1, Pallas kernels, forward_block(): pl.pallas_call(forward_written, in_specs=[any_] * 8 + [vmem], out_specs=[...  123 us
    pallas_call x1, Pallas kernels, backward_block(): pl.pallas_call(backward_staged, in_specs=[any_] * 2 + [vmem] * 2 + [any_]...  118 us
    pallas_call x1, Pallas kernels, mlp_block(): pl.pallas_call(mlp_staged, in_specs=[any_] * 6, out_specs=[any_, any_, vm...  51.5 us
  transfers between devices with their start and end apart: 1, of which 0 were waited for; matrix products, arithmetic and copies ran while one was open for 1% of the time, Pallas kernels for 0%

profile of v12, /device:TPU:0, one launch (start us, length us, event | category | flops | bytes accessed | tf_op | source)
XLA Modules:
  0.0 313.4 jit_solution(7546366722165477058)
XLA Ops:
  0.6 0.0 copy-start.4
  0.7 0.7 convert_element_type.59
  1.4 0.7 convert_element_type.63
  2.0 0.1 tile.10
  2.1 0.7 convert_element_type.68
  2.8 1.0 fusion.1
  3.8 0.1 reshape.64
  3.9 0.2 copy.36
  4.1 0.8 reshape.65.refs_0_
  4.9 1.0 copy.29
  5.9 0.0 copy-done.4
  5.9 0.7 pad.12.refs_4_
  6.6 0.1 fusion.3
  6.8 0.7 pad.11.refs_3_
  7.5 0.7 pad.10.refs_2_
  8.1 0.6 broadcast_in_dim.22.refs_8_
  8.7 0.6 broadcast_in_dim.21.refs_7_
  9.3 122.5 %forward_block.1 = (bf16[1024,512]{1,0:T(8,128)(2,1)}, bf16[1024,512]{1,0:T(8,128)(2,1)}, bf16[1024,512]{1,0:T(8,128)(2,1)}, bf16[1024,512]{1,0:T(8,128)(2,1)}, ...) custom-call(bf16[64,1536]{1,0:T(8,128)(2,1)} %reshape.65.refs_0_, ...), custom_call_target="tpu_custom_call" | custom-call | tf_op jit(solution)/shard_map/forward_block/pallas_call | solution.py:638
  131.9 51.5 %mlp_block.1 = (bf16[512,1024]{1,0:T(8,128)(2,1)}, f32[512,1024]{1,0:T(8,128)}, bf16[1024,1024]{1,0:T(8,128)(2,1)}, bf16[1024,1408]{1,0:T(8,128)(2,1)}, bf16[102...) custom-call(bf16[4,2,2,64,1408]{4,3,2,1,0:T(8,128)(2,1)} %get-tuple-element.45.refs_0_, ...), custom_call_target="tpu_custom_call" | custom-call | tf_op jit(solution)/shard_map/mlp_block/pallas_call | solution.py:949
  183.4 117.8 %backward_block.1 = (bf16[512,1024]{1,0:T(8,128)(2,1)}, bf16[64,1408]{1,0:T(8,128)(2,1)}, bf16[32,1408]{1,0:T(8,128)(2,1)}, bf16[32,1408]{1,0:T(8,128)(2,1)}, bf...) custom-call(bf16[4,2,2,64,1408]{4,3,2,1,0:T(8,128)(2,1)} %bitcast.50, ...), custom_call_target="tpu_custom_call" | custom-call | tf_op jit(solution)/shard_map/backward_block/pallas_call | solution.py:1235
  301.2 0.0 copy-start.3
  301.2 0.0 copy-start.5
  301.2 0.0 copy-start.7
  301.2 0.0 copy-start.8
  301.2 1.0 maximum_convert_fusion
  302.2 0.0 copy-start
  302.2 0.3 reshape.82
  302.5 0.1 copy.31
  302.6 0.0 copy-start.1
  302.7 0.2 reshape.79
  302.8 0.0 copy-done.3
  302.8 0.9 broadcast_multiply_fusion
  303.8 0.0 copy-done.5
  303.8 0.0 copy-done.7
  303.8 0.0 copy-done.8
  303.8 0.0 copy-done
  303.9 0.0 copy-start.6
  303.9 0.0 copy-start.10
  303.9 0.2 convert_multiply_fusion
  304.1 0.0 copy-start.9
  304.1 3.4 %collective-permute-start = (f32[2,64]{1,0:T(2,128)S(1)}, f32[2,64]{1,0:T(2,128)S(1)}, u32[]{:S(2)}, u32[]{:S(2)}) collective-permute-start(f32[2,64]{1,0:T(2,128)S(1)} %pad_maximum_fusion.2), channel_id=1, source_target_pairs={{0,1},{1,0},{2,3},{3,2},{4,5},{5,4},{6,7},{7,6},{8,9},{9,8},{10,11... | collective-permute-start | bytes 1544 | tf_op jit(solution)/shard_map/ppermute | solution.py:1278
  307.5 0.0 copy-done.1
  307.5 0.0 copy-start.2
  307.5 1.6 bitcast_convert_fusion
  309.0 0.0 copy-done.6
  309.0 0.0 copy-done.10
  309.0 0.8 convert_bitcast_fusion
  309.8 0.0 copy-done.9
  309.8 0.7 convert_bitcast_fusion.1
  310.5 1.4 copy.33
  311.9 0.0 collective-permute-done
  311.9 0.5 slice_bitcast_fusion.3
  312.4 0.0 copy-done.2
  312.4 1.0 copy.38
  (5 shorter events, 0.1 us)
Async XLA Ops:
  0.6 5.3 %copy-start.4 = (bf16[1312,64]{0,1:T(8,128)(2,1)S(1)}, bf16[1312,64]{0,1:T(8,128)(2,1)}, u32[]{:S(2)}) copy-start(bf16[1312,64]{0,1:T(8,128)(2,1)} %param.14) | copy-start | bytes 503812
  301.2 1.7 copy-start.3
  301.2 2.6 copy-start.5
  301.2 2.6 copy-start.7
  301.2 2.6 copy-start.8
  302.2 1.6 copy-start
  302.6 4.8 %copy-start.1 = (bf16[512,1024]{1,0:T(8,128)(2,1)S(1)}, bf16[512,1024]{1,0:T(8,128)(2,1)}, u32[]{:S(2)}) copy-start(bf16[512,1024]{1,0:T(8,128)(2,1)} %get-tuple-element.72) | copy-start | bytes 3145732
  303.9 5.2 %copy-start.6 = (bf16[48,1408]{1,0:T(8,128)(2,1)S(1)}, bf16[48,1408]{1,0:T(8,128)(2,1)}, u32[]{:S(2)}) copy-start(bf16[48,1408]{1,0:T(8,128)(2,1)} %get-tuple-element.80) | copy-start | bytes 405508
  303.9 5.2 %copy-start.10 = (bf16[16,1408]{1,0:T(8,128)(2,1)S(1)}, bf16[16,1408]{1,0:T(8,128)(2,1)}, u32[]{:S(2)}) copy-start(bf16[16,1408]{1,0:T(8,128)(2,1)} %get-tuple-element.81) | copy-start | bytes 135172
  304.1 5.7 %copy-start.9 = (bf16[64,512]{1,0:T(8,128)(2,1)S(1)}, bf16[64,512]{1,0:T(8,128)(2,1)}, u32[]{:S(2)}) copy-start(bf16[64,512]{1,0:T(8,128)(2,1)} %get-tuple-element.79) | copy-start | bytes 196612
  304.1 7.8 %collective-permute-start = (f32[2,64]{1,0:T(2,128)S(1)}, f32[2,64]{1,0:T(2,128)S(1)}, u32[]{:S(2)}, u32[]{:S(2)}) collective-permute-start(f32[2,64]{1,0:T(2,128)S(1)} %pad_maximum_fusion.2), channel_id=1, source_target_pairs={{0,1},{1,0},{2,3},{3,2},{4,5},{5,4},{6,7},{7,6},{8,9},{9,8},{10,11... | collective-permute-start | bytes 1544 | tf_op jit(solution)/shard_map/ppermute | solution.py:1278
  307.5 5.0 %copy-start.2 = (bf16[512,1024]{1,0:T(8,128)(2,1)S(1)}, bf16[512,1024]{1,0:T(8,128)(2,1)}, u32[]{:S(2)}) copy-start(bf16[512,1024]{1,0:T(8,128)(2,1)} %get-tuple-element.51) | copy-start | bytes 3145732
